TPU v7x, 32 devices: a whole 2x2x4 slice. The times are simulated.
32 devices in a mesh: req: 16 (over z, y, core), grp: 2 (over x).
Axes of the slice: x: 2, y: 2, z: 4, core: 2. Of those that a mesh axis runs over, the one named last changes fastest.
Arguments:
- tokens: bfloat16 [8192, 1024], P('req'), may hold values from -6 to 6
- norm_attn: float32 [1024], replicated, may hold values from 0.25 to 1.75
- w_query: bfloat16 [1024, 1024], P(None, 'grp'), may hold values from -0.1875 to 0.1875
- w_key: bfloat16 [1024, 1024], P(None, 'grp'), may hold values from -0.1875 to 0.1875
- w_value: bfloat16 [1024, 1024], P(None, 'grp'), may hold values from -0.1875 to 0.1875
- w_out: bfloat16 [1024, 1024], P('grp'), may hold values from -0.1875 to 0.1875
- persist_keys: bfloat16 [16, 1024], P(None, 'grp'), may hold values from -5 to 5
- persist_values: bfloat16 [16, 1024], P(None, 'grp'), may hold values from -5 to 5
- kv_cache: bfloat16 [768, 2, 128, 1024], P('req', None, None, 'grp'), may hold values from -160 to 160
- slot_request: int32 [768], P('req'), may hold values from 0 to 255, as said below
- slot_page: int32 [768], P('req'), may hold values from 0 to 48, as said below
- cache_len: int32 [256], P('req'), may hold values from 1 to 2304
- tree_mask: int32 [256, 32, 32], P('req'), may hold values from 0 to 1, as said below
- accept_path: int32 [256, 8], P('req'), may hold values from 0 to 31, as said below
- accept_len: int32 [256], P('req'), may hold values from 1 to 8
- memory: float32 [256, 8, 128, 128], P('req', 'grp'), may hold values from -4 to 4
- momentum: float32 [256, 8, 128, 128], P('req', 'grp'), may hold values from -1.2 to 1.2
- momentum_code: int32 [256, 8, 8], P('req', None, 'grp'), may hold values from 0 to 15
- forget_code: int32 [256, 8, 8], P('req', None, 'grp'), may hold values from 0 to 15
- norm_ffn: float32 [1024], replicated, may hold values from 0.25 to 1.75
- w_gate_up: bfloat16 [2, 1024, 2816], P(None, None, 'grp'), may hold values from -0.1875 to 0.1875
- w_down: bfloat16 [2816, 1024], P('grp'), may hold values from -0.109375 to 0.109375
Outputs:
- layer_out: bfloat16 [8192, 1024], P(('req', 'grp'))
- memory_out: float32 [256, 8, 128, 128], P('req', 'grp')
- momentum_out: float32 [256, 8, 128, 128], P('req', 'grp')
Inputs may be any that keep to these rules, and one draw needn't show every extreme that they name: `slot_request`: slot s lies with index s // 48 of req; slots s with (s % 48) // 3 = j hold pages of requests j * 16 to (j + 1) * 16 - 1 only. The live pages 0 .. ceil(cache_len[r] / 128) - 1 of every request stand each in exactly one slot; every other slot has page number 16 * 3. `slot_page`: see slot_request. `tree_mask`: each node's parent precedes it; node 0 is the root; rows include the node itself. `accept_path`: entry n is the node at depth n on the root path of one draft node.
All inputs are finite; a program needn't handle non-finite values.
Results may differ from a plain program's by a relative error of at most 0.015.
Values may be sent and summed in bfloat16 or wider, within the bound.
No kernel may reach another device: no remote copies, remote signals or barrier semaphores. Data moves between devices by JAX's collectives and lax.ppermute only.
A program may use at most 192 MiB of HBM per device.

v0:
```python
import math

import jax
import jax.numpy as jnp
from jax import lax
from jax.sharding import PartitionSpec as P

HD = 128


EPS = 1e-06
THETA = 0.5
NEG = -1e30


def rms_norm(rows, gain):
    values = rows.astype(jnp.float32)
    factor = lax.rsqrt(jnp.mean(values * values, axis=-1, keepdims=True) + EPS)
    return (values * factor * gain).astype(jnp.bfloat16)


def unit_rows(vectors):
    return vectors * lax.rsqrt(jnp.sum(vectors * vectors, axis=-1, keepdims=True) + EPS)


def page_partials(pages, page_queries, page_first, page_limit, scale):
    count = pages.shape[0]
    page_len = pages.shape[2]
    width = pages.shape[3]
    heads = width // HD
    draft = page_queries.shape[1]
    query_four = page_queries.reshape(count, draft, heads, HD)
    key_four = pages[:, 0].reshape(count, page_len, heads, HD)
    value_four = pages[:, 1].reshape(count, page_len, heads, HD)
    scores = (
        jnp.einsum("sihd,sthd->shit", query_four, key_four, preferred_element_type=jnp.float32)
        * scale
    )
    position = page_first[:, None] + jnp.arange(page_len, dtype=jnp.int32)[None, :]
    valid = (position < page_limit[:, None])[:, None, None, :]
    masked = jnp.where(valid, scores, NEG)
    top = jnp.max(masked, axis=3)
    weight = jnp.where(valid, jnp.exp(masked - top[..., None]), 0.0)
    total = jnp.sum(weight, axis=3)
    numer = jnp.einsum(
        "shit,sthd->sihd",
        weight.astype(jnp.bfloat16),
        value_four,
        preferred_element_type=jnp.float32,
    )
    return (numer.reshape(count, draft, width), top, total)


def on_device(
    tokens,
    norm_attn,
    w_query,
    w_key,
    w_value,
    w_out,
    persist_keys,
    persist_values,
    kv_cache,
    slot_request,
    slot_page,
    cache_len,
    tree_mask,
    accept_path,
    accept_len,
    memory,
    momentum,
    momentum_code,
    forget_code,
    norm_ffn,
    w_gate_up,
    w_down,
):
    group_rows = tokens.shape[0]
    reqs = cache_len.shape[0]
    draft = tree_mask.shape[1]
    width = w_query.shape[1]
    heads = width // HD
    fixed_count = persist_keys.shape[0]
    page_len = kv_cache.shape[2]
    scale = 1.0 / math.sqrt(HD)
    normed = rms_norm(tokens, norm_attn)
    queries = jnp.dot(normed, w_query, preferred_element_type=jnp.float32).astype(jnp.bfloat16)
    keys = jnp.dot(normed, w_key, preferred_element_type=jnp.float32).astype(jnp.bfloat16)
    values = jnp.dot(normed, w_value, preferred_element_type=jnp.float32).astype(jnp.bfloat16)
    query_four = queries.reshape(reqs, draft, heads, HD)
    key_four = keys.reshape(reqs, draft, heads, HD)
    value_four = values.reshape(reqs, draft, heads, HD)
    fixed_keys = persist_keys.reshape(fixed_count, heads, HD)
    fixed_values = persist_values.reshape(fixed_count, heads, HD)
    tree_scores = (
        jnp.einsum("rihd,rjhd->rhij", query_four, key_four, preferred_element_type=jnp.float32)
        * scale
    )
    tree_scores = jnp.where(tree_mask[:, None] == 1, tree_scores, NEG)
    fixed_scores = (
        jnp.einsum("rihd,phd->rhip", query_four, fixed_keys, preferred_element_type=jnp.float32)
        * scale
    )
    local_scores = jnp.concatenate([fixed_scores, tree_scores], axis=3)
    local_top = jnp.max(local_scores, axis=3)
    local_weight = jnp.exp(local_scores - local_top[..., None])
    local_total = jnp.sum(local_weight, axis=3)
    local_rounded = local_weight.astype(jnp.bfloat16)
    local_numer = jnp.einsum(
        "rhip,phd->rihd",
        local_rounded[..., :fixed_count],
        fixed_values,
        preferred_element_type=jnp.float32,
    )
    local_numer = local_numer + jnp.einsum(
        "rhij,rjhd->rihd",
        local_rounded[..., fixed_count:],
        value_four,
        preferred_element_type=jnp.float32,
    )
    first_request = lax.axis_index("req") * reqs
    request_ids = jnp.arange(reqs, dtype=jnp.int32)
    moved_pages, moved_request, moved_page = (
        lax.all_to_all(kv_cache, "req", split_axis=0, concat_axis=0, tiled=True),
        lax.all_to_all(slot_request, "req", split_axis=0, concat_axis=0, tiled=True),
        lax.all_to_all(slot_page, "req", split_axis=0, concat_axis=0, tiled=True),
    )
    local_request = moved_request - first_request
    pick = local_request[:, None] == request_ids[None, :]
    limits = jnp.sum(jnp.where(pick, cache_len[None, :], 0), axis=1)
    page_queries = queries.reshape(reqs, draft, width)[local_request]
    numer, top, total = page_partials(
        moved_pages, page_queries, moved_page * page_len, limits, scale
    )
    slot_count = numer.shape[0]
    pick_weight = pick.astype(jnp.float32)
    request_top = jnp.max(jnp.where(pick[:, :, None, None], top[:, None], NEG), axis=0)
    best = jnp.maximum(request_top, local_top)
    slot_best = jnp.einsum("sr,rhi->shi", pick_weight, best, precision=lax.Precision.HIGHEST)
    factor = jnp.exp(top - slot_best)
    scaled = (
        numer.reshape(slot_count, draft, heads, HD) * jnp.transpose(factor, (0, 2, 1))[..., None]
    )
    page_numer = jnp.einsum("sr,sihd->rihd", pick_weight, scaled, precision=lax.Precision.HIGHEST)
    page_total = jnp.einsum(
        "sr,shi->rhi", pick_weight, total * factor, precision=lax.Precision.HIGHEST
    )
    local_factor = jnp.exp(local_top - best)
    numer_all = local_numer * jnp.transpose(local_factor, (0, 2, 1))[..., None] + page_numer
    total_all = local_total * local_factor + page_total
    attention = numer_all / jnp.transpose(total_all, (0, 2, 1))[..., None]
    unit_query = unit_rows(query_four.astype(jnp.float32))
    retrieved = jnp.einsum("rihd,rhde->rihe", unit_query, memory, precision=lax.Precision.HIGHEST)
    mixed = (attention + retrieved).reshape(group_rows, width).astype(jnp.bfloat16)
    rows = group_rows // lax.axis_size("grp")
    head_sum = lax.psum_scatter(
        jnp.dot(mixed, w_out, preferred_element_type=jnp.float32).astype(jnp.bfloat16),
        "grp",
        scatter_dimension=0,
        tiled=True,
    ).astype(jnp.float32)
    own_rows = lax.dynamic_slice_in_dim(tokens, lax.axis_index("grp") * rows, rows, 0)
    residual = (own_rows.astype(jnp.float32) + head_sum).astype(jnp.bfloat16)
    ffn_in = rms_norm(residual, norm_ffn)
    piece = lax.all_gather(ffn_in, "grp", axis=0, tiled=True)
    gate = jnp.dot(piece, w_gate_up[0], preferred_element_type=jnp.float32)
    up = jnp.dot(piece, w_gate_up[1], preferred_element_type=jnp.float32)
    hidden = (jax.nn.silu(gate) * up).astype(jnp.bfloat16)
    ffn_out = lax.psum_scatter(
        jnp.dot(hidden, w_down, preferred_element_type=jnp.float32).astype(jnp.bfloat16),
        "grp",
        scatter_dimension=0,
        tiled=True,
    ).astype(jnp.float32)
    layer_out = (residual.astype(jnp.float32) + ffn_out).astype(jnp.bfloat16)
    req_rows = request_ids[:, None]
    path_keys = unit_rows(key_four[req_rows, accept_path].astype(jnp.float32))
    path_values = value_four[req_rows, accept_path].astype(jnp.float32)
    eta = 0.97 - 0.06 * momentum_code.astype(jnp.float32)
    forget = 0.01 + 0.02 * forget_code.astype(jnp.float32)
    for step in range(accept_path.shape[1]):
        unit = path_keys[:, step]
        predicted = jnp.einsum("rhd,rhde->rhe", unit, memory, precision=lax.Precision.HIGHEST)
        grad = jnp.einsum(
            "rhd,rhe->rhde", unit, predicted - path_values[:, step], precision=lax.Precision.HIGHEST
        )
        new_mom = eta[:, step, :, None, None] * momentum - THETA * grad
        new_mem = (1.0 - forget[:, step, :, None, None]) * memory + new_mom
        live = (step < accept_len)[:, None, None, None]
        momentum = jnp.where(live, new_mom, momentum)
        memory = jnp.where(live, new_mem, memory)
    return (layer_out, memory, momentum)


def solution(mesh):
    return jax.shard_map(
        on_device,
        mesh=mesh,
        in_specs=(
            P("req", None),
            P(),
            P(None, "grp"),
            P(None, "grp"),
            P(None, "grp"),
            P("grp", None),
            P(None, "grp"),
            P(None, "grp"),
            P("req", None, None, "grp"),
            P("req"),
            P("req"),
            P("req"),
            P("req", None, None),
            P("req", None),
            P("req"),
            P("req", "grp", None, None),
            P("req", "grp", None, None),
            P("req", None, "grp"),
            P("req", None, "grp"),
            P(),
            P(None, None, "grp"),
            P("grp", None),
        ),
        out_specs=(
            P(("req", "grp"), None),
            P("req", "grp", None, None),
            P("req", "grp", None, None),
        ),
        check_vma=False,
    )
```

profile of v0, /device:TPU:0, one launch (start us, length us, event | category | flops | bytes accessed | tf_op | source)
XLA Modules:
  0.0 470.6 jit_solution(17253716148561162837)
XLA Ops:
  8.7 7.4 %all-to-all-start = ((s32[16,3,1]{1,2,0:T(1,128)}), s32[16,3,1]{1,2,0:T(1,128)S(1)}, u32[]{:S(2)}, u32[]{:S(2)}) async-start(s32[16,3,1]{1,2,0:T(1,128)} %bitcast.6), calls=%async_computation | async-start | bytes 16384 | tf_op jit(solution)/shard_map/all_to_all | solution.py:125
  17.4 5.0 %all-to-all-done = s32[16,3,1]{1,2,0:T(1,128)S(1)} async-done(((s32[16,3,1]{1,2,0:T(1,128)}), s32[16,3,1]{1,2,0:T(1,128)S(1)}, u32[]{:S(2)}, u32[]{:S(2)}) %all-to-all-start) | async-done | bytes 224 | tf_op jit(solution)/shard_map/all_to_all | solution.py:125
  22.4 3.5 all-to-all-start.1
  25.9 16.7 %copy.234 = bf16[48,2,128,512]{2,3,1,0:T(8,128)(2,1)} copy(bf16[48,2,128,512]{3,2,1,0:T(8,128)(2,1)} %param.30) | data formatting | bytes 25165824 | tf_op args[8]
  43.2 6.0 %all-to-all-start.2 = ((bf16[48,2,128,512]{2,3,1,0:T(8,128)(2,1)}), bf16[48,2,128,512]{2,3,1,0:T(8,128)(2,1)}, u32[]{:S(2)}, u32[]{:S(2)}) async-start(bf16[48,2,128,512]{2,3,1,0:T(8,128)(2,1)} %copy.234), calls=%async_computation.2 | async-start | bytes 25165824 | tf_op jit(solution)/shard_map/all_to_all | solution.py:124
  51.4 3.1 convolution_convert_fusion.4
  55.7 3.1 convolution_convert_fusion.3
  58.8 2.0 reshape.250
  60.7 2.2 fusion.143
  62.9 2.4 copy.225
  65.3 3.1 convolution_convert_fusion.2
  68.4 2.0 reshape.252
  70.5 2.0 gather_fusion.1
  72.5 2.6 gather_fusion.2
  94.5 5.8 %fusion.145 = f32[16,4,1,128]{3,2,1,0:T(1,128)S(1)} fusion(f32[16,4,128,1]{2,3,1,0:T(1,128)S(1)} %bitcast.263, f32[16,4,128,128]{3,2,1,0:T(8,128)} %param.37), kind=kOutput, calls=%fused_computation.235 | convolution fusion | flops 12582912 | bytes 4259840 | tf_op jit(solution)/shard_map/rhd,rhde->rhe/dot_general | solution.py:183
  100.4 6.6 %fusion.36 = f32[16,4,1,128]{3,2,1,0:T(1,128)S(1)} fusion(f32[16,4,128,1]{2,3,1,0:T(1,128)S(1)} %bitcast.262, f32[16,4,128,128]{3,2,1,0:T(8,128)} %param.37, f32[16,4,128,128]{3,2,1,0:T(8,128)S(1)} %copy-done.1, f32[16,4,128]{2,1,0:T(4,128)S(1)} %fusion.104, f32[16,4,128]{2,1,0:T(4,128)S(1)} %get-tuple-element.14, f32[16,4]{1,0:T(8,128)S(1)} %copy.260, ...), kind=kOutput, calls=%fused_computation.61 | convolution fusion | flops 19922944 | bytes 8520208 | tf_op jit(solution)/shard_map/rhd,rhde->rhe/dot_general | solution.py:183
  107.0 3.6 add_select_fusion.6
  110.6 3.7 fusion.146
  114.4 7.9 %fusion.30 = f32[16,4,1,128]{3,2,1,0:T(1,128)S(1)} fusion(f32[16,4,128,1]{2,3,1,0:T(1,128)S(1)} %bitcast.272, f32[16,4,128,128]{3,2,1,0:T(8,128)S(1)} %add_select_fusion.6, f32[16,4,128]{2,1,0:T(4,128)S(1)} %fusion.102, f32[16,4,128]{2,1,0:T(4,128)S(1)} %get-tuple-element.16, f32[16,4]{1,0:T(8,128)S(1)} %copy-done.30, f32[16,4]{1,0:T(8,128)S(1)} %copy-done.50, ...), kind=kOutput, calls=%fused_computation.55 | convolution fusion | flops 30408704 | bytes 8651824 | tf_op jit(solution)/shard_map/rhd,rhde->rhe/dot_general | solution.py:183
  122.4 6.4 %add_select_fusion.4 = f32[16,4,128,128]{3,2,1,0:T(8,128)S(1)} fusion(f32[16,4,128]{2,1,0:T(4,128)S(1)} %fusion.101, f32[16,4,128]{2,1,0:T(4,128)S(1)} %get-tuple-element.17, f32[16,4]{1,0:T(8,128)S(1)} %copy-done.32, f32[16,4,128]{2,1,0:T(4,128)S(1)} %fusion.102, f32[16,4,128,128]{3,2,1,0:T(8,128)S(1)} %add_select_fusion.6, ...), kind=kLoop, calls=%fused_computation.17 | loop fusion | flops 26214400 | bytes 12846656 | tf_op jit(solution)/shard_map/jit(_where)/select_n | solution.py:191
  128.8 3.6 fusion.147
  132.5 2.0 fusion.144
  134.5 5.7 %fusion.6 = f32[16,4,128,128]{3,2,1,0:T(8,128)S(1)} fusion(f32[16,4,128]{2,1,0:T(4,128)S(1)} %fusion.101, f32[16,4,128]{2,1,0:T(4,128)S(1)} %get-tuple-element.17, f32[16,4]{1,0:T(8,128)S(1)} %copy-done.32, f32[16,4,128]{2,1,0:T(4,128)S(1)} %fusion.102, f32[16,4,128]{2,1,0:T(4,128)S(1)} %get-tuple-element.16, f32[16,4]{1,0:T(8,128)S(1)} %copy-done.30, ...), kind=kLoop, calls=%fused_computation.19 | loop fusion | flops 20971520 | bytes 8651840 | tf_op jit(solution)/shard_map/jit(_where)/select_n | solution.py:190
  140.3 2.0 copy-done.7
  142.3 4.9 %fusion.27 = f32[16,4,1,128]{3,2,1,0:T(1,128)} fusion(f32[16,4,128,1]{2,3,1,0:T(1,128)S(1)} %bitcast.259, f32[16,4,128,128]{3,2,1,0:T(8,128)S(1)} %add_select_fusion.4, f32[16,4,128,128]{3,2,1,0:T(8,128)S(1)} %fusion.6, f32[16,4,128]{2,1,0:T(4,128)S(1)} %fusion.100, f32[16,4,128]{2,1,0:T(4,128)S(1)} %get-tuple-element.18, f32[16,4]{1,0:T(8,128)S(1)} %copy-done.36, ...), kind=kOutput, calls=%fused_computation.52 | convolution fusion | flops 19922944 | bytes 8520208 | tf_op jit(solution)/shard_map/rhd,rhde->rhe/dot_general | solution.py:183
  147.7 2.5 fusion.141
  156.3 3.0 gather_fusion
  161.8 111.1 %all-to-all-done.2 = bf16[48,2,128,512]{2,3,1,0:T(8,128)(2,1)} async-done(((bf16[48,2,128,512]{2,3,1,0:T(8,128)(2,1)}), bf16[48,2,128,512]{2,3,1,0:T(8,128)(2,1)}, u32[]{:S(2)}, u32[]{:S(2)}) %all-to-all-start.2) | async-done | bytes 12582944 | tf_op jit(solution)/shard_map/all_to_all | solution.py:124
  272.9 8.6 %fusion.142 = (bf16[48,1,128,512]{2,3,1,0:T(8,128)(2,1)}, bf16[48,1,128,512]{2,3,1,0:T(8,128)(2,1)S(1)}) fusion(bf16[48,2,128,512]{2,3,1,0:T(8,128)(2,1)} %all-to-all-done.2), kind=kLoop, calls=%fused_computation.232 | loop fusion | bytes 25165824 | tf_op jit(solution)/shard_map/slice | solution.py:34
  281.6 4.1 fusion.18
  293.7 4.3 fusion.19
  298.1 5.9 %bitcast_multiply_fusion = f32[48,32,4,128]{3,1,2,0:T(8,128)S(1)} fusion(bf16[48,128,4,128]{1,3,2,0:T(8,128)(2,1)} %bitcast.250, f32[48,4,32,128]{3,2,1,0:T(8,128)S(1)} %copy-done.6, f32[48,32,4]{1,2,0:T(4,128)} %copy.244, f32[48,4,32]{2,1,0:T(4,128)} %get-tuple-element.53, pred[48,128]{1,0:T(8,128)(4,1)} %add_compare_fusion), kind=kOutput, calls=%fused_computation.30 | convolution fusion | flops 206045184 | bytes 12638208 | tf_op jit(solution)/shard_map/shit,sthd->sihd/dot_general | solution.py:45
  304.0 4.7 fusion.10
  310.3 2.6 fusion.93
  314.4 1.9 fusion.66
  316.3 3.9 fusion.70
  320.9 1.7 convolution_convert_fusion.1
  325.9 10.3 %add_select_fusion.2 = f32[16,4,128,128]{3,2,1,0:T(8,128)S(1)} fusion(f32[16,4,128]{2,1,0:T(4,128)S(1)} %fusion.99, f32[16,4,128]{2,1,0:T(4,128)S(1)} %copy-done.26, f32[16,4]{1,0:T(8,128)S(1)} %copy.271, f32[16,4,128]{2,1,0:T(4,128)S(1)} %copy-done.22, f32[16,4,128,128]{3,2,1,0:T(8,128)} %copy-done.4, f32[16,4,128]{2,1,0:T(4,128)S(1)} %copy-done.20, ...), kind=kLoop, calls=%fused_computation.11 | loop fusion | flops 36700160 | bytes 12978272 | tf_op jit(solution)/shard_map/jit(_where)/select_n | solution.py:191
  336.2 2.0 copy-done.5
  338.2 3.7 fusion.148
  343.3 48.5 %reduce-scatter.3.cloned.1.call-done = bf16[256,1024]{1,0:T(8,128)(2,1)} async-done(((bf16[512,1024]{1,0:T(8,128)(2,1)}), bf16[256,1024]{1,0:T(8,128)(2,1)}) %reduce-scatter.3.cloned.1.call-update) | async-done | bytes 524304 | tf_op jit(solution)/shard_map/reduce_scatter | solution.py:156
  395.0 9.2 %fusion.24 = f32[16,4,1,128]{3,2,1,0:T(1,128)S(1)} fusion(f32[16,4,128,1]{2,3,1,0:T(1,128)} %bitcast.271, f32[16,4,128,128]{3,2,1,0:T(8,128)} %copy-done.5, f32[16,4,128]{2,1,0:T(4,128)} %fusion.98, f32[16,4,128]{2,1,0:T(4,128)} %get-tuple-element.20, f32[16,4]{1,0:T(8,128)} %copy.273, f32[16,4]{1,0:T(8,128)} %copy.253, ...), kind=kOutput, calls=%fused_computation.49 | convolution fusion | flops 30408704 | bytes 8651824 | tf_op jit(solution)/shard_map/rhd,rhde->rhe/dot_general | solution.py:183
  405.6 11.0 %all-gather.2.cloned.1.call-done = bf16[512,1024]{1,0:T(8,128)(2,1)} async-done(((bf16[256,1024]{1,0:T(8,128)(2,1)}), bf16[512,1024]{1,0:T(8,128)(2,1)}) %all-gather.2.cloned.1.call-update) | async-done | bytes 1048592 | tf_op jit(solution)/shard_map/all_gather | solution.py:165
  416.6 5.5 %fusion.14 = f32[512,1408]{1,0:T(8,128)} fusion(bf16[512,1024]{1,0:T(8,128)(2,1)} %all-gather.2.cloned.1.call-done, bf16[2,1024,1408]{2,1,0:T(8,128)(2,1)} %param.42), kind=kOutput, calls=%fused_computation.37 | convolution fusion | flops 1476395008 | bytes 6815744 | tf_op jit(solution)/shard_map/dot_general | solution.py:166
  422.1 7.4 %convolution_convert_fusion = bf16[512,1024]{1,0:T(8,128)(2,1)} fusion(bf16[1408,1024]{1,0:T(8,128)(2,1)S(1)} %copy-done, bf16[512,1024]{1,0:T(8,128)(2,1)} %all-gather.2.cloned.1.call-done, bf16[2,1024,1408]{2,1,0:T(8,128)(2,1)} %param.42, f32[512,1408]{1,0:T(8,128)} %fusion.14), kind=kOutput, calls=%fused_computation.84 | convolution fusion | flops 2957639680 | bytes 10747904 | tf_op jit(solution)/shard_map/dot_general | solution.py:170
  429.6 15.2 %fusion.2 = f32[16,4,128,128]{3,2,1,0:T(8,128)} fusion(f32[16,4,128]{2,1,0:T(4,128)} %fusion.97, f32[16,4,128]{2,1,0:T(4,128)} %get-tuple-element.13, f32[16,4]{1,0:T(8,128)} %copy.275, f32[16,4,128]{2,1,0:T(4,128)} %fusion.98, f32[16,4,128]{2,1,0:T(4,128)} %get-tuple-element.20, f32[16,4]{1,0:T(8,128)} %copy.273, pred[16]{0:T(512)(128)(4,1)} %get-tuple-element.50, ...), kind=kLoop, calls=%fused_computation.7 | loop fusion | flops 41943040 | bytes 8915072 | tf_op jit(solution)/shard_map/jit(_where)/select_n | solution.py:190
  446.1 15.8 %add_select_fusion = f32[16,4,128,128]{3,2,1,0:T(8,128)} fusion(f32[16,4,128]{2,1,0:T(4,128)} %fusion.97, f32[16,4,128]{2,1,0:T(4,128)} %get-tuple-element.13, f32[16,4]{1,0:T(8,128)} %copy.275, f32[16,4,128]{2,1,0:T(4,128)} %fusion.98, f32[16,4,128,128]{3,2,1,0:T(8,128)} %copy-done.5, f32[16,4,128]{2,1,0:T(4,128)} %get-tuple-element.20, f32[16,4]{1,0:T(8,128)} %copy.273, ...), kind=kLoop, calls=%fused_computation.5 | loop fusion | flops 47185920 | bytes 13109888 | tf_op jit(solution)/shard_map/jit(_where)/select_n | solution.py:191
  461.9 2.0 fusion.80
  (218 shorter events, 57.5 us)
Async XLA Ops:
  7.2 414.9 %copy-start = (bf16[1408,1024]{1,0:T(8,128)(2,1)S(1)}, bf16[1408,1024]{1,0:T(8,128)(2,1)}, u32[]{:S(2)}) copy-start(bf16[1408,1024]{1,0:T(8,128)(2,1)} %param.43) | copy-start | bytes 8650756
  8.7 13.7 %all-to-all-start = ((s32[16,3,1]{1,2,0:T(1,128)}), s32[16,3,1]{1,2,0:T(1,128)S(1)}, u32[]{:S(2)}, u32[]{:S(2)}) async-start(s32[16,3,1]{1,2,0:T(1,128)} %bitcast.6), calls=%async_computation | async-start | bytes 16384 | tf_op jit(solution)/shard_map/all_to_all | solution.py:125
  22.4 20.1 %copy-start.48 = (s32[16,3,1]{1,2,0:T(1,128)}, s32[16,3,1]{1,2,0:T(1,128)S(1)}, u32[]{:S(2)}) copy-start(s32[16,3,1]{1,2,0:T(1,128)S(1)} %all-to-all-done) | copy-start | bytes 580
  22.4 20.2 %all-to-all-start.1 = ((s32[16,3,1]{1,2,0:T(1,128)}), s32[16,3,1]{1,2,0:T(1,128)S(1)}, u32[]{:S(2)}, u32[]{:S(2)}) async-start(s32[16,3,1]{1,2,0:T(1,128)} %bitcast.7), calls=%async_computation.1 | async-start | bytes 16384 | tf_op jit(solution)/shard_map/all_to_all | solution.py:126
  42.5 6.7 %copy-start.58 = (bf16[16,512]{1,0:T(8,128)(2,1)S(1)}, bf16[16,512]{1,0:T(8,128)(2,1)}, u32[]{:S(2)}) copy-start(bf16[16,512]{1,0:T(8,128)(2,1)} %param.29) | copy-start | bytes 49156
  42.5 7.3 %copy-start.59 = (bf16[16,512]{1,0:T(8,128)(2,1)S(1)}, bf16[16,512]{1,0:T(8,128)(2,1)}, u32[]{:S(2)}) copy-start(bf16[16,512]{1,0:T(8,128)(2,1)} %param.28) | copy-start | bytes 49156
  42.6 8.8 %copy-start.70 = (f32[1024]{0:T(1024)S(1)}, f32[1024]{0:T(1024)}, u32[]{:S(2)}) copy-start(f32[1024]{0:T(1024)} %param.23) | copy-start | bytes 12292
  43.2 229.8 %all-to-all-start.2 = ((bf16[48,2,128,512]{2,3,1,0:T(8,128)(2,1)}), bf16[48,2,128,512]{2,3,1,0:T(8,128)(2,1)}, u32[]{:S(2)}, u32[]{:S(2)}) async-start(bf16[48,2,128,512]{2,3,1,0:T(8,128)(2,1)} %copy.234), calls=%async_computation.2 | async-start | bytes 25165824 | tf_op jit(solution)/shard_map/all_to_all | solution.py:124
  49.2 342.6 %reduce-scatter.3.cloned.1.call-start = ((), (), s32[]{:S(2)}) async-start(), calls=%async_computation.5 | async-start | bytes 1572864 | tf_op jit(solution)/shard_map/reduce_scatter | solution.py:156
  58.8 11.6 %copy-start.68 = (s32[16,8]{0,1:T(8,128)S(1)}, s32[16,8]{0,1:T(8,128)}, u32[]{:S(2)}) copy-start(s32[16,8]{0,1:T(8,128)} %param.35) | copy-start | bytes 1540
  90.8 9.5 %copy-start.18 = (f32[16,8,4,128]{3,2,1,0:T(4,128)S(1)}, f32[16,8,4,128]{3,2,1,0:T(4,128)}, u32[]{:S(2)}) copy-start(f32[16,8,4,128]{3,2,1,0:T(4,128)} %convert.1) | copy-start | bytes 786436
  90.8 9.5 %copy-start.1 = (f32[16,4,128,128]{3,2,1,0:T(8,128)S(1)}, f32[16,4,128,128]{3,2,1,0:T(8,128)}, u32[]{:S(2)}) copy-start(f32[16,4,128,128]{3,2,1,0:T(8,128)} %param.38) | copy-start | bytes 12582916
  90.8 9.6 %copy-start.44 = (f32[16,4]{1,0:T(8,128)S(1)}, f32[16,4]{1,0:T(8,128)}, u32[]{:S(2)}) copy-start(f32[16,4]{1,0:T(8,128)} %copy.259) | copy-start | bytes 772
  92.9 41.6 %copy-start.52 = (pred[16]{0:T(512)(128)(4,1)}, pred[16]{0:T(512)(128)(4,1)S(1)}, u32[]{:S(2)}) copy-start(pred[16]{0:T(512)(128)(4,1)S(1)} %get-tuple-element.52) | copy-start | bytes 52
  92.9 41.6 %copy-start.54 = (pred[16]{0:T(512)(128)(4,1)}, pred[16]{0:T(512)(128)(4,1)S(1)}, u32[]{:S(2)}) copy-start(pred[16]{0:T(512)(128)(4,1)S(1)} %get-tuple-element.46) | copy-start | bytes 52
  92.9 41.6 %copy-start.56 = (pred[16]{0:T(512)(128)(4,1)}, pred[16]{0:T(512)(128)(4,1)S(1)}, u32[]{:S(2)}) copy-start(pred[16]{0:T(512)(128)(4,1)S(1)} %get-tuple-element.47) | copy-start | bytes 52
  92.9 47.4 %copy-start.60 = (pred[16]{0:T(512)(128)(4,1)}, pred[16]{0:T(512)(128)(4,1)S(1)}, u32[]{:S(2)}) copy-start(pred[16]{0:T(512)(128)(4,1)S(1)} %get-tuple-element.48) | copy-start | bytes 52
  94.5 40.0 %copy-start.9 = (f32[16,4,128]{2,1,0:T(4,128)}, f32[16,4,128]{2,1,0:T(4,128)S(1)}, u32[]{:S(2)}) copy-start(f32[16,4,128]{2,1,0:T(4,128)S(1)} %get-tuple-element.16) | copy-start | bytes 98308
  94.5 40.0 %copy-start.11 = (f32[16,4,128]{2,1,0:T(4,128)}, f32[16,4,128]{2,1,0:T(4,128)S(1)}, u32[]{:S(2)}) copy-start(f32[16,4,128]{2,1,0:T(4,128)S(1)} %get-tuple-element.17) | copy-start | bytes 98308
  94.5 45.8 %copy-start.19 = (f32[16,4,128]{2,1,0:T(4,128)}, f32[16,4,128]{2,1,0:T(4,128)S(1)}, u32[]{:S(2)}) copy-start(f32[16,4,128]{2,1,0:T(4,128)S(1)} %get-tuple-element.18) | copy-start | bytes 98308
  100.3 6.7 %copy-start.2 = (f32[16,4,128,128]{3,2,1,0:T(8,128)S(1)}, f32[16,4,128,128]{3,2,1,0:T(8,128)}, u32[]{:S(2)}) copy-start(f32[16,4,128,128]{3,2,1,0:T(8,128)} %param.37) | copy-start | bytes 12582916
  100.3 6.7 %copy-start.28 = (f32[16,4]{1,0:T(8,128)S(1)}, f32[16,4]{1,0:T(8,128)}, u32[]{:S(2)}) copy-start(f32[16,4]{1,0:T(8,128)} %copy.263) | copy-start | bytes 772
  100.3 6.7 %copy-start.47 = (f32[16,4]{1,0:T(8,128)S(1)}, f32[16,4]{1,0:T(8,128)}, u32[]{:S(2)}) copy-start(f32[16,4]{1,0:T(8,128)} %copy.258) | copy-start | bytes 772
  114.3 20.2 %copy-start.13 = (f32[16,4,128]{2,1,0:T(4,128)}, f32[16,4,128]{2,1,0:T(4,128)S(1)}, u32[]{:S(2)}) copy-start(f32[16,4,128]{2,1,0:T(4,128)S(1)} %fusion.102) | copy-start | bytes 98308
  114.3 8.0 %copy-start.32 = (f32[16,4]{1,0:T(8,128)S(1)}, f32[16,4]{1,0:T(8,128)}, u32[]{:S(2)}) copy-start(f32[16,4]{1,0:T(8,128)} %copy.267) | copy-start | bytes 772
  114.3 8.0 %copy-start.51 = (f32[16,4]{1,0:T(8,128)S(1)}, f32[16,4]{1,0:T(8,128)}, u32[]{:S(2)}) copy-start(f32[16,4]{1,0:T(8,128)} %copy.256) | copy-start | bytes 772
  122.3 12.2 %copy-start.15 = (f32[16,4,128]{2,1,0:T(4,128)}, f32[16,4,128]{2,1,0:T(4,128)S(1)}, u32[]{:S(2)}) copy-start(f32[16,4,128]{2,1,0:T(4,128)S(1)} %fusion.101) | copy-start | bytes 98308
  128.7 11.6 %copy-start.4 = (f32[16,4,128,128]{3,2,1,0:T(8,128)}, f32[16,4,128,128]{3,2,1,0:T(8,128)S(1)}, u32[]{:S(2)}) copy-start(f32[16,4,128,128]{3,2,1,0:T(8,128)S(1)} %add_select_fusion.4) | copy-start | bytes 12582916
  132.4 7.9 %copy-start.21 = (f32[16,4,128]{2,1,0:T(4,128)}, f32[16,4,128]{2,1,0:T(4,128)S(1)}, u32[]{:S(2)}) copy-start(f32[16,4,128]{2,1,0:T(4,128)S(1)} %fusion.100) | copy-start | bytes 98308
  134.5 7.8 %copy-start.36 = (f32[16,4]{1,0:T(8,128)S(1)}, f32[16,4]{1,0:T(8,128)}, u32[]{:S(2)}) copy-start(f32[16,4]{1,0:T(8,128)} %copy.269) | copy-start | bytes 772
  134.5 7.8 %copy-start.45 = (f32[16,4]{1,0:T(8,128)S(1)}, f32[16,4]{1,0:T(8,128)}, u32[]{:S(2)}) copy-start(f32[16,4]{1,0:T(8,128)} %copy.255) | copy-start | bytes 772
  272.9 8.6 %copy-start.8 = (bf16[48,32,512]{2,1,0:T(8,128)(2,1)S(1)}, bf16[48,32,512]{2,1,0:T(8,128)(2,1)}, u32[]{:S(2)}) copy-start(bf16[48,32,512]{2,1,0:T(8,128)(2,1)} %gather_fusion) | copy-start | bytes 4718596
  272.9 8.6 %copy-start.43 = (pred[48,128]{1,0:T(8,128)(4,1)S(1)}, pred[48,128]{1,0:T(8,128)(4,1)}, u32[]{:S(2)}) copy-start(pred[48,128]{1,0:T(8,128)(4,1)} %add_compare_fusion) | copy-start | bytes 18436
  320.3 5.4 %copy-start.10 = (f32[16,4,128]{2,1,0:T(4,128)S(1)}, f32[16,4,128]{2,1,0:T(4,128)}, u32[]{:S(2)}) copy-start(f32[16,4,128]{2,1,0:T(4,128)} %copy-done.9) | copy-start | bytes 98308
  320.3 5.4 %copy-start.12 = (f32[16,4,128]{2,1,0:T(4,128)S(1)}, f32[16,4,128]{2,1,0:T(4,128)}, u32[]{:S(2)}) copy-start(f32[16,4,128]{2,1,0:T(4,128)} %copy-done.11) | copy-start | bytes 98308
  320.3 5.4 %copy-start.14 = (f32[16,4,128]{2,1,0:T(4,128)S(1)}, f32[16,4,128]{2,1,0:T(4,128)}, u32[]{:S(2)}) copy-start(f32[16,4,128]{2,1,0:T(4,128)} %copy-done.13) | copy-start | bytes 98308
  320.3 5.4 %copy-start.16 = (f32[16,4,128]{2,1,0:T(4,128)S(1)}, f32[16,4,128]{2,1,0:T(4,128)}, u32[]{:S(2)}) copy-start(f32[16,4,128]{2,1,0:T(4,128)} %copy-done.15) | copy-start | bytes 98308
  320.4 5.4 %copy-start.20 = (f32[16,4,128]{2,1,0:T(4,128)S(1)}, f32[16,4,128]{2,1,0:T(4,128)}, u32[]{:S(2)}) copy-start(f32[16,4,128]{2,1,0:T(4,128)} %copy-done.19) | copy-start | bytes 98308
  320.4 5.4 %copy-start.22 = (f32[16,4,128]{2,1,0:T(4,128)S(1)}, f32[16,4,128]{2,1,0:T(4,128)}, u32[]{:S(2)}) copy-start(f32[16,4,128]{2,1,0:T(4,128)} %copy-done.21) | copy-start | bytes 98308
  320.4 5.4 %copy-start.26 = (f32[16,4,128]{2,1,0:T(4,128)S(1)}, f32[16,4,128]{2,1,0:T(4,128)}, u32[]{:S(2)}) copy-start(f32[16,4,128]{2,1,0:T(4,128)} %get-tuple-element.19) | copy-start | bytes 98308
  320.4 5.4 %copy-start.29 = (f32[16,4]{1,0:T(8,128)S(1)}, f32[16,4]{1,0:T(8,128)}, u32[]{:S(2)}) copy-start(f32[16,4]{1,0:T(8,128)} %copy.263) | copy-start | bytes 772
  320.4 5.4 %copy-start.31 = (f32[16,4]{1,0:T(8,128)S(1)}, f32[16,4]{1,0:T(8,128)}, u32[]{:S(2)}) copy-start(f32[16,4]{1,0:T(8,128)} %copy.265) | copy-start | bytes 772
  320.4 5.4 %copy-start.33 = (f32[16,4]{1,0:T(8,128)S(1)}, f32[16,4]{1,0:T(8,128)}, u32[]{:S(2)}) copy-start(f32[16,4]{1,0:T(8,128)} %copy.267) | copy-start | bytes 772
  322.7 93.9 %all-gather.2.cloned.1.call-start = ((), (), s32[]{:S(2)}) async-start(), calls=%async_computation.6 | async-start | bytes 1572864 | tf_op jit(solution)/shard_map/all_gather | solution.py:165
  323.5 12.7 %copy-start.27 = (f32[16,4,128]{2,1,0:T(4,128)}, f32[16,4,128]{2,1,0:T(4,128)S(1)}, u32[]{:S(2)}) copy-start(f32[16,4,128]{2,1,0:T(4,128)S(1)} %fusion.99) | copy-start | bytes 98308
  323.6 12.6 %copy-start.42 = (f32[16,4]{1,0:T(8,128)}, f32[16,4]{1,0:T(8,128)S(1)}, u32[]{:S(2)}) copy-start(f32[16,4]{1,0:T(8,128)S(1)} %copy.271) | copy-start | bytes 772
  325.9 12.4 %copy-start.38 = (f32[16,1,4,128]{3,2,1,0:T(4,128)S(1)}, f32[16,1,4,128]{3,2,1,0:T(4,128)}, u32[]{:S(2)}) copy-start(f32[16,1,4,128]{3,2,1,0:T(4,128)} %get-tuple-element.22) | copy-start | bytes 98308
  394.9 66.9 %reduce-scatter.5.cloned.1.call-start = ((), (), s32[]{:S(2)}) async-start(), calls=%async_computation.7 | async-start | bytes 1572864 | tf_op jit(solution)/shard_map/reduce_scatter | solution.py:169
  (29 other events, 113.6 us)
Sparse Core Ops, SparseCore 0:
  322.8 68.9 reduce-scatter.2
  395.1 21.4 all-gather.1
  429.7 20.3 reduce-scatter.4
where the time goes:
time: 478 us; the launch traced here: 471 us
  waiting for transfers between devices  176 us (37%)
  matrix products  97.1 us (20%)
  other arithmetic  91.1 us (19%)
  local copies, waits for them, and re-layouts  74.8 us (16%)
  starting transfers between devices  17 us (4%)
  between operations  15 us (3%)
    all_to_all x1, waiting for transfers between devices, on_device(): lax.all_to_all(kv_cache, 'req', split_axis=0, concat_axis=0, tiled=True)  111 us
    reduce_scatter x1, waiting for transfers between devices, on_device(): lax.psum_scatter(jnp.dot(mixed, w_out, preferred_element_type=jnp.float32...  48.5 us
    dot_general x8, matrix products, on_device(): jnp.einsum('rhd,rhde->rhe', unit, memory, precision=lax.Precision.HIGHEST)  45.4 us
    select_n x4, other arithmetic, on_device(): memory = jnp.where(live, new_mem, memory)  36 us
    unnamed x143, local copies, waits for them, and re-layouts  21.6 us
    select_n x2, other arithmetic, on_device(): momentum = jnp.where(live, new_mom, momentum)  20.9 us
    all_gather x1, waiting for transfers between devices, on_device(): piece = lax.all_gather(ffn_in, 'grp', axis=0, tiled=True)  11 us
  transfers between devices with their start and end apart: 6, of which 4 were waited for; matrix products, arithmetic and copies ran while one was open for 40% of the time, Pallas kernels for 0%

commit v1 on v0

v1 whole, which is shorter than its diff:
```python
import functools
import math

import jax
import jax.numpy as jnp
from jax import lax
from jax.experimental import pallas as pl
from jax.experimental.pallas import tpu as pltpu
from jax.sharding import PartitionSpec as P

HD = 128
LANES = 128
EXTRA = 16
PARTS = 3

EPS = 1e-06
THETA = 0.5
NEG = -1e30
TINY = 1e-30

VMEM = pltpu.VMEM
SMEM = pltpu.SMEM
F32 = jnp.float32
BF16 = jnp.bfloat16


def whole(space=VMEM):
    return pl.BlockSpec(memory_space=space)


def cost(flops, moved, special=0):
    return pl.CostEstimate(flops=flops, bytes_accessed=moved, transcendentals=special)


def params(mib=40):
    return pltpu.CompilerParams(vmem_limit_bytes=mib << 20)


def rms_norm(rows, gain):
    values = rows.astype(F32)
    factor = lax.rsqrt(jnp.mean(values * values, axis=-1, keepdims=True) + EPS)
    return (values * factor * gain).astype(BF16)


def nt_dot(left, right):
    return lax.dot_general(left, right, (((1,), (1,)), ((), ())), preferred_element_type=F32)


def column_to_row(column, count):
    row_id = lax.broadcasted_iota(jnp.int32, (count, LANES), 0)
    lane_id = lax.broadcasted_iota(jnp.int32, (count, LANES), 1)
    spread = jnp.where(row_id == lane_id, jnp.broadcast_to(column, (count, LANES)), 0.0)
    return jnp.sum(spread, axis=0, keepdims=True)


def pack_queries(codes, lengths, q_ref, out_ref, *, n, cap, reqs, draft, heads, page_len):
    block = cap * heads * draft + EXTRA
    row_id = lax.broadcasted_iota(jnp.int32, (EXTRA, LANES), 0)

    def one(d, carry):
        base = pl.multiple_of(d * block, 16)
        tail = jnp.zeros((EXTRA, LANES), F32)
        for c in range(cap):
            code = codes[d * cap + c]
            r = lax.rem(code, reqs)
            page = lax.div(code, reqs)
            live = jnp.clip(lengths[r] - page * page_len, 0, page_len)
            tail = jnp.where(row_id == c, live.astype(F32), tail)
            rows = pl.ds(pl.multiple_of(r * draft, draft), draft)
            for h in range(heads):
                out_ref[pl.ds(base + (c * heads + h) * draft, draft), :] = q_ref[
                    rows, h * HD : (h + 1) * HD
                ]
        out_ref[pl.ds(base + cap * heads * draft, EXTRA), :] = tail.astype(BF16)
        return carry

    lax.fori_loop(0, n, one, 0)


def page_attention(q_ref, kv_ref, out_ref, *, cap, draft, heads, page_len, scale):
    span = heads * draft
    tail_at = cap * span
    limits = q_ref[tail_at : tail_at + EXTRA, :].astype(F32)
    lane = lax.broadcasted_iota(jnp.int32, (draft, page_len), 1).astype(F32)
    row_id = lax.broadcasted_iota(jnp.int32, (EXTRA, LANES), 0)
    tail = jnp.zeros((EXTRA, LANES), F32)
    for c in range(cap):
        valid = lane < limits[c : c + 1, :]
        columns = []
        for h in range(heads):
            at = c * span + h * draft
            cols = slice(h * HD, (h + 1) * HD)
            scores = nt_dot(q_ref[at : at + draft, :], kv_ref[c, 0, :, cols]) * scale
            scores = jnp.where(valid, scores, NEG)
            top = jnp.max(scores, axis=1, keepdims=True)
            weight = jnp.where(valid, jnp.exp(scores - top), 0.0)
            total = jnp.sum(weight, axis=1, keepdims=True)
            numer = jnp.dot(weight.astype(BF16), kv_ref[c, 1, :, cols], preferred_element_type=F32)
            kept = jnp.maximum(total, TINY)
            out_ref[at : at + draft, :] = (numer / kept).astype(BF16)
            columns.append(jnp.where(total > 0.0, top + jnp.log(kept), NEG))
        row = column_to_row(jnp.concatenate(columns, axis=0), span)
        for p in range(PARTS):
            part = row.astype(BF16).astype(F32)
            tail = jnp.where(row_id == p * cap + c, part, tail)
            row = row - part
    out_ref[tail_at : tail_at + EXTRA, :] = tail.astype(BF16)


def local_attention(
    q_ref, k_ref, v_ref, pk_ref, pv_ref, mask_ref, mem_ref, o_ref, ret_ref, lse_ref,
    *, heads, draft, scale,
):
    r = pl.program_id(0)
    seen = mask_ref[0] == 1
    columns = []
    for h in range(heads):
        cols = slice(h * HD, (h + 1) * HD)
        rows = slice(h * draft, (h + 1) * draft)
        query = q_ref[:, cols]
        tree = jnp.where(seen, nt_dot(query, k_ref[:, cols]) * scale, NEG)
        fixed = nt_dot(query, pk_ref[:, cols]) * scale
        top = jnp.maximum(
            jnp.max(tree, axis=1, keepdims=True), jnp.max(fixed, axis=1, keepdims=True)
        )
        tree_w = jnp.exp(tree - top)
        fixed_w = jnp.exp(fixed - top)
        total = jnp.sum(tree_w, axis=1, keepdims=True) + jnp.sum(fixed_w, axis=1, keepdims=True)
        numer = jnp.dot(tree_w.astype(BF16), v_ref[:, cols], preferred_element_type=F32)
        numer = numer + jnp.dot(fixed_w.astype(BF16), pv_ref[:, cols], preferred_element_type=F32)
        o_ref[rows, :] = numer / total
        columns.append(top + jnp.log(total))
        wide = query.astype(F32)
        unit = wide * lax.rsqrt(jnp.sum(wide * wide, axis=1, keepdims=True) + EPS)
        ret_ref[rows, :] = jnp.dot(
            unit, mem_ref[0, h], preferred_element_type=F32, precision=lax.Precision.HIGHEST
        )
    lse_ref[pl.ds(r, 1), :] = column_to_row(jnp.concatenate(columns, axis=0), heads * draft)


def update_memory(
    path, count, mom_code, forget_code, k_ref, v_ref, mem_ref, mom_ref, mem_out, mom_out,
    wide_k, wide_v, unit_ref, value_ref, turned_ref, *, heads, steps,
):
    r = pl.program_id(0)
    wide_k[...] = k_ref[...].astype(F32)
    wide_v[...] = v_ref[...].astype(F32)
    unit_ref[...] = jnp.zeros_like(unit_ref)
    for n in range(steps):
        node = path[r * steps + n]
        k_row = wide_k[pl.ds(node, 1), :]
        v_row = wide_v[pl.ds(node, 1), :]
        for h in range(heads):
            unit_ref[h * steps + n : h * steps + n + 1, :] = k_row[:, h * HD : (h + 1) * HD]
            value_ref[h * steps + n : h * steps + n + 1, :] = v_row[:, h * HD : (h + 1) * HD]
    keys = unit_ref[...]
    unit = keys * lax.rsqrt(jnp.sum(keys * keys, axis=1, keepdims=True) + EPS)
    turned_ref[...] = jnp.transpose(unit)

    def advance(n, mem_src, mom_src):
        for h in range(heads):
            at = (r * steps + n) * heads + h
            eta = 0.97 - 0.06 * mom_code[at].astype(F32)
            keep = 1.0 - (0.01 + 0.02 * forget_code[at].astype(F32))
            row = h * steps + n
            column = turned_ref[:, row : row + 1]
            matrix = mem_src[0, h]
            predicted = jnp.sum(column * matrix, axis=0, keepdims=True)
            error = THETA * (predicted - value_ref[row : row + 1, :])
            moved = eta * mom_src[0, h] - column * error
            mom_out[0, h] = moved
            mem_out[0, h] = keep * matrix + moved

    advance(0, mem_ref, mom_ref)
    for n in range(1, steps):
        pl.when(n < count[r])(functools.partial(advance, n, mem_out, mom_out))


def combine(
    codes, msg_ref, o_ref, ret_ref, lse_ref, w_ref, out_ref,
    part_lse, best, total, weight, own_weight, acc, mixed,
    *, n, cap, reqs, draft, heads,
):
    span = heads * draft
    block = cap * span + EXTRA
    slots = n * cap
    for d in range(n):
        at = d * block + cap * span
        tail = msg_ref[at : at + EXTRA, :].astype(F32)
        part_lse[d * cap : (d + 1) * cap, :] = (
            tail[0:cap] + tail[cap : 2 * cap] + tail[2 * cap : 3 * cap]
        )
    best[...] = lse_ref[...]
    owners = [lax.rem(codes[s], reqs) for s in range(slots)]
    for s in range(slots):
        r = owners[s]
        best[pl.ds(r, 1), :] = jnp.maximum(best[pl.ds(r, 1), :], part_lse[s : s + 1, :])
    own_weight[...] = jnp.zeros_like(own_weight)
    weight[...] = jnp.zeros_like(weight)
    start = jnp.exp(lse_ref[...] - best[...])
    total[...] = start
    for s in range(slots):
        r = owners[s]
        term = jnp.exp(part_lse[s : s + 1, :] - best[pl.ds(r, 1), :])
        weight[s : s + 1, :] = term
        total[pl.ds(r, 1), :] = total[pl.ds(r, 1), :] + term
    inverse = 1.0 / total[...]
    own_weight[0:reqs, :] = start * inverse
    total[...] = inverse
    for s in range(slots):
        weight[s : s + 1, :] = weight[s : s + 1, :] * total[pl.ds(owners[s], 1), :]
    turned = jnp.transpose(weight[...])
    own_turned = jnp.transpose(own_weight[...])
    for r in range(reqs):
        rows = slice(r * span, (r + 1) * span)
        acc[rows, :] = o_ref[rows, :] * own_turned[0:span, r : r + 1] + ret_ref[rows, :]
    for s in range(slots):
        at = (s // cap) * block + (s % cap) * span
        rows = pl.ds(pl.multiple_of(owners[s] * span, span), span)
        acc[rows, :] = acc[rows, :] + msg_ref[at : at + span, :].astype(F32) * turned[
            0:span, s : s + 1
        ]
    for r in range(reqs):
        for h in range(heads):
            at = r * span + h * draft
            mixed[r * draft : (r + 1) * draft, h * HD : (h + 1) * HD] = acc[
                at : at + draft, :
            ].astype(BF16)
    out_ref[...] = jnp.dot(mixed[...], w_ref[...], preferred_element_type=F32).astype(BF16)


def on_device(
    tokens,
    norm_attn,
    w_query,
    w_key,
    w_value,
    w_out,
    persist_keys,
    persist_values,
    kv_cache,
    slot_request,
    slot_page,
    cache_len,
    tree_mask,
    accept_path,
    accept_len,
    memory,
    momentum,
    momentum_code,
    forget_code,
    norm_ffn,
    w_gate_up,
    w_down,
):
    n = lax.axis_size("req")
    group_rows, model = tokens.shape
    reqs = cache_len.shape[0]
    draft = tree_mask.shape[1]
    steps = accept_path.shape[1]
    width = w_query.shape[1]
    heads = width // HD
    span = heads * draft
    slots = kv_cache.shape[0]
    cap = slots // n
    fixed_count = persist_keys.shape[0]
    page_len = kv_cache.shape[2]
    block = cap * span + EXTRA
    scale = 1.0 / math.sqrt(HD)

    label = slot_page * reqs + lax.rem(slot_request, reqs)
    codes = lax.all_to_all(label, "req", split_axis=0, concat_axis=0, tiled=True)

    normed = rms_norm(tokens, norm_attn)
    queries = jnp.dot(normed, w_query, preferred_element_type=F32).astype(BF16)

    packed = pl.pallas_call(
        functools.partial(
            pack_queries, n=n, cap=cap, reqs=reqs, draft=draft, heads=heads, page_len=page_len
        ),
        out_shape=jax.ShapeDtypeStruct((n * block, LANES), BF16),
        in_specs=[whole(SMEM), whole(SMEM), whole()],
        out_specs=whole(),
        compiler_params=params(),
        cost_estimate=cost(0, 4 * n * block * LANES),
        name="pack_queries",
    )(codes, cache_len, queries)
    asked = lax.all_to_all(packed, "req", split_axis=0, concat_axis=0, tiled=True)

    keys = jnp.dot(normed, w_key, preferred_element_type=F32).astype(BF16)
    values = jnp.dot(normed, w_value, preferred_element_type=F32).astype(BF16)

    row_block = pl.BlockSpec((draft, width), lambda r, *_: (r, 0))
    fixed_block = pl.BlockSpec((fixed_count, width), lambda r, *_: (0, 0))
    matrix_block = pl.BlockSpec((1, heads, HD, HD), lambda r, *_: (r, 0, 0, 0))
    span_block = pl.BlockSpec((span, HD), lambda r, *_: (r, 0))
    own, retrieved, own_lse = pl.pallas_call(
        functools.partial(local_attention, heads=heads, draft=draft, scale=scale),
        grid=(reqs,),
        out_shape=(
            jax.ShapeDtypeStruct((reqs * span, HD), F32),
            jax.ShapeDtypeStruct((reqs * span, HD), F32),
            jax.ShapeDtypeStruct((reqs, LANES), F32),
        ),
        in_specs=[
            row_block,
            row_block,
            row_block,
            fixed_block,
            fixed_block,
            pl.BlockSpec((1, draft, draft), lambda r: (r, 0, 0)),
            matrix_block,
        ],
        out_specs=(span_block, span_block, pl.BlockSpec((reqs, LANES), lambda r: (0, 0))),
        compiler_params=params(),
        cost_estimate=cost(
            2 * reqs * span * HD * (2 * (draft + fixed_count) + 6 * HD),
            4 * reqs * (heads * HD * HD + 2 * span * HD),
            reqs * span * (draft + fixed_count),
        ),
        name="local_attention",
    )(queries, keys, values, persist_keys, persist_values, tree_mask, memory)

    matrices = jax.ShapeDtypeStruct(memory.shape, F32)
    memory_out, momentum_out = pl.pallas_call(
        functools.partial(update_memory, heads=heads, steps=steps),
        grid_spec=pltpu.PrefetchScalarGridSpec(
            num_scalar_prefetch=4,
            grid=(reqs,),
            in_specs=[row_block, row_block, matrix_block, matrix_block],
            out_specs=(matrix_block, matrix_block),
            scratch_shapes=[
                pltpu.VMEM((draft, width), F32),
                pltpu.VMEM((draft, width), F32),
                pltpu.VMEM((LANES, HD), F32),
                pltpu.VMEM((heads * steps, HD), F32),
                pltpu.VMEM((HD, LANES), F32),
            ],
        ),
        out_shape=(matrices, matrices),
        compiler_params=params(),
        cost_estimate=cost(
            14 * reqs * heads * HD * HD * steps * 8, 16 * reqs * heads * HD * HD
        ),
        name="update_memory",
    )(
        accept_path.reshape(-1),
        accept_len,
        momentum_code.reshape(-1),
        forget_code.reshape(-1),
        keys,
        values,
        memory,
        momentum,
    )

    message_block = pl.BlockSpec((block, LANES), lambda d: (d, 0))
    answers = pl.pallas_call(
        functools.partial(
            page_attention, cap=cap, draft=draft, heads=heads, page_len=page_len, scale=scale
        ),
        grid=(n,),
        out_shape=jax.ShapeDtypeStruct((n * block, LANES), BF16),
        in_specs=[
            message_block,
            pl.BlockSpec((cap, 2, page_len, width), lambda d: (d, 0, 0, 0)),
        ],
        out_specs=message_block,
        compiler_params=params(),
        cost_estimate=cost(
            4 * slots * span * page_len * HD,
            4 * slots * page_len * width + 4 * n * block * LANES,
            slots * span * page_len,
        ),
        name="page_attention",
    )(asked, kv_cache)
    returned = lax.all_to_all(answers, "req", split_axis=0, concat_axis=0, tiled=True)

    partial_out = pl.pallas_call(
        functools.partial(combine, n=n, cap=cap, reqs=reqs, draft=draft, heads=heads),
        out_shape=jax.ShapeDtypeStruct((group_rows, model), BF16),
        in_specs=[whole(SMEM)] + [whole()] * 5,
        out_specs=whole(),
        scratch_shapes=[
            pltpu.VMEM((slots, LANES), F32),
            pltpu.VMEM((reqs, LANES), F32),
            pltpu.VMEM((reqs, LANES), F32),
            pltpu.VMEM((LANES, LANES), F32),
            pltpu.VMEM((LANES, LANES), F32),
            pltpu.VMEM((reqs * span, HD), F32),
            pltpu.VMEM((group_rows, width), BF16),
        ],
        compiler_params=params(),
        cost_estimate=cost(
            2 * group_rows * width * model, 2 * n * block * LANES + 8 * reqs * span * HD
        ),
        name="combine",
    )(codes, returned, own, retrieved, own_lse, w_out)

    rows = group_rows // lax.axis_size("grp")
    head_sum = lax.psum_scatter(partial_out, "grp", scatter_dimension=0, tiled=True).astype(F32)
    own_rows = lax.dynamic_slice_in_dim(tokens, lax.axis_index("grp") * rows, rows, 0)
    residual = (own_rows.astype(F32) + head_sum).astype(BF16)
    ffn_in = rms_norm(residual, norm_ffn)
    piece = lax.all_gather(ffn_in, "grp", axis=0, tiled=True)
    gate = jnp.dot(piece, w_gate_up[0], preferred_element_type=F32)
    up = jnp.dot(piece, w_gate_up[1], preferred_element_type=F32)
    hidden = (jax.nn.silu(gate) * up).astype(BF16)
    ffn_out = lax.psum_scatter(
        jnp.dot(hidden, w_down, preferred_element_type=F32).astype(BF16),
        "grp",
        scatter_dimension=0,
        tiled=True,
    ).astype(F32)
    layer_out = (residual.astype(F32) + ffn_out).astype(BF16)
    return (layer_out, memory_out, momentum_out)


def solution(mesh):
    return jax.shard_map(
        on_device,
        mesh=mesh,
        in_specs=(
            P("req", None),
            P(),
            P(None, "grp"),
            P(None, "grp"),
            P(None, "grp"),
            P("grp", None),
            P(None, "grp"),
            P(None, "grp"),
            P("req", None, None, "grp"),
            P("req"),
            P("req"),
            P("req"),
            P("req", None, None),
            P("req", None),
            P("req"),
            P("req", "grp", None, None),
            P("req", "grp", None, None),
            P("req", None, "grp"),
            P("req", None, "grp"),
            P(),
            P(None, None, "grp"),
            P("grp", None),
        ),
        out_specs=(
            P(("req", "grp"), None),
            P("req", "grp", None, None),
            P("req", "grp", None, None),
        ),
        check_vma=False,
    )
```

time: 478 us -> 266 us (0.56); the launches traced: 471 us -> 265 us
  waiting for transfers between devices: 176 us -> 57.9 us
  Pallas kernels: 0 us -> 92.4 us
  other arithmetic: 91.1 us -> 9.42 us
  matrix products: 97.1 us -> 20.1 us
  local copies, waits for them, and re-layouts: 74.8 us -> 16 us
  blocking collectives: 0 us -> 43.2 us
  starting transfers between devices: 17 us -> 12.2 us
    all_to_all x3 -> x2, waiting for transfers between devices: 116 us -> 11.5 us  [the longest x1 9.04 us: on_device(): lax.all_to_all(answers, 'req', split_axis=0, concat_axis=0, tiled=True)]
    pallas_call x0 -> x5, Pallas kernels: none -> 92.4 us  [the longest x1 49.8 us: on_device(): pl.pallas_call(functools.partial(page_attention, cap=cap, draft=draft, he...]
    dot_general x24 -> x5, matrix products: 97.1 us -> 20.1 us  [the longest x1 7.5 us: on_device(): jnp.dot(hidden, w_down, preferred_element_type=F32).astype(BF16)]
    select_n x7 -> x0, other arithmetic: 57.6 us -> none  [the longest x4 36 us: on_device(): memory = jnp.where(live, new_mem, memory)]
    all_to_all x0 -> x1, blocking collectives: none -> 43.2 us  [on_device(): lax.all_to_all(packed, 'req', split_axis=0, concat_axis=0, tiled=True)]
    reduce_scatter x2, waiting for transfers between devices: 48.5 us -> 25.1 us  [the longest x1 25.1 us: on_device(): lax.psum_scatter(partial_out, 'grp', scatter_dimension=0, tiled=True)]
    sub x11 -> x0, local copies, waits for them, and re-layouts: 11.3 us -> none  [the longest x8 8.68 us: on_device(): new_mem = (1.0 - forget[:, step, :, None, None]) * memory + new_mom]
    mul x11 -> x0, local copies, waits for them, and re-layouts: 10.5 us -> none  [the longest x9 6.78 us: on_device(): new_mom = eta[:, step, :, None, None] * momentum - THETA * grad]
  transfers between devices with their start and end apart: 6 -> 5, of which waited for: 4 -> 4; matrix products, arithmetic and copies ran while one was open for 40% -> 3% of each run, Pallas kernels for 0% -> 14%
where the time goes in v1:
time: 266 us; the launch traced here: 265 us
  Pallas kernels  92.4 us (35%)
  waiting for transfers between devices  57.9 us (22%)
  blocking collectives  43.2 us (16%)
  matrix products  20.1 us (8%)
  local copies, waits for them, and re-layouts  16 us (6%)
  between operations  14 us (5%)
  starting transfers between devices  12.2 us (5%)
  other arithmetic  9.42 us (4%)
    pallas_call x1, Pallas kernels, on_device(): pl.pallas_call(functools.partial(page_attention, cap=cap, draft=draft, he...  49.8 us
    all_to_all x1, blocking collectives, on_device(): lax.all_to_all(packed, 'req', split_axis=0, concat_axis=0, tiled=True)  43.2 us
    reduce_scatter x1, waiting for transfers between devices, on_device(): lax.psum_scatter(partial_out, 'grp', scatter_dimension=0, tiled=True)  25.1 us
    all_gather x1, waiting for transfers between devices, on_device(): piece = lax.all_gather(ffn_in, 'grp', axis=0, tiled=True)  21.2 us
    pallas_call x1, Pallas kernels, on_device(): pl.pallas_call(functools.partial(update_memory, heads=heads, steps=steps)...  21 us
    pallas_call x1, Pallas kernels, on_device(): pl.pallas_call(functools.partial(local_attention, heads=heads, draft=draf...  16.3 us
    unnamed x53, local copies, waits for them, and re-layouts  14.4 us
    all_to_all x1, waiting for transfers between devices, on_device(): lax.all_to_all(answers, 'req', split_axis=0, concat_axis=0, tiled=True)  9.04 us
  transfers between devices with their start and end apart: 5, of which 4 were waited for; matrix products, arithmetic and copies ran while one was open for 3% of the time, Pallas kernels for 14%

profile of v1, /device:TPU:0, one launch (start us, length us, event | category | flops | bytes accessed | tf_op | source)
XLA Modules:
  0.0 265.3 jit_solution(12861578528304715610)
XLA Ops:
  7.2 0.8 fusion.16
  8.0 0.7 all_to_all.21
  8.7 7.4 %all-to-all-start = ((s32[16,3,1]{1,2,0:T(1,128)}), s32[16,3,1]{1,2,0:T(1,128)S(1)}, u32[]{:S(2)}, u32[]{:S(2)}) async-start(s32[16,3,1]{1,2,0:T(1,128)} %bitcast), calls=%async_computation | async-start | bytes 16384 | tf_op jit(solution)/shard_map/all_to_all | solution.py:272
  16.1 1.5 fusion.6
  17.6 2.3 convolution_convert_fusion.3.q_ref
  20.0 2.5 all-to-all-done
  22.4 0.5 broadcast.40
  23.0 0.7 reduce.3
  23.6 0.1 all_to_all.23.codes
  23.7 1.2 pack_queries.1
  24.9 43.2 %all_to_all.33 = bf16[16,400,128]{2,1,0:T(8,128)(2,1)S(1)} all-to-all(bf16[16,400,128]{2,1,0:T(8,128)(2,1)S(1)} %bitcast.20), channel_id=1, replica_groups=mesh['req'=16,'grp'=2] {'req'}, dimensions={0} | all-to-all | bytes 3276800 | tf_op jit(solution)/shard_map/all_to_all | solution.py:288
  68.1 49.8 %page_attention.1 = bf16[6400,128]{1,0:T(8,128)(2,1)S(1)} custom-call(bf16[6400,128]{1,0:T(8,128)(2,1)S(1)} %bitcast.22, bf16[48,2,128,512]{3,2,1,0:T(8,128)(2,1)} %kv_ref.1), custom_call_target="tpu_custom_call" | custom-call | flops 402653184 | bytes 15859712 | tf_op jit(solution)/shard_map/page_attention/pallas_call | solution.py:358
  117.9 1.2 copy-done.3
  119.0 4.5 %all-to-all-start.2 = ((bf16[16,400,128]{2,1,0:T(8,128)(2,1)}), bf16[16,400,128]{2,1,0:T(8,128)(2,1)}, u32[]{:S(2)}, u32[]{:S(2)}) async-start(bf16[16,400,128]{2,1,0:T(8,128)(2,1)} %bitcast.21), calls=%async_computation.2 | async-start | bytes 3276800 | tf_op jit(solution)/shard_map/all_to_all | solution.py:377
  123.6 0.0 reduce-scatter.3.cloned.1.call-start
  123.7 2.4 convolution_convert_fusion.2.k_ref
  126.2 2.4 convolution_convert_fusion.1.v_ref
  128.6 16.3 %local_attention.1 = (f32[2048,128]{1,0:T(8,128)S(1)}, f32[2048,128]{1,0:T(8,128)S(1)}, f32[16,128]{1,0:T(8,128)S(1)}) custom-call(bf16[512,512]{1,0:T(8,128)(2,1)S(1)} %copy-done.9, bf16[512,512]{1,0:T(8,128)(2,1)S(1)} %convolution_convert_fusion.2.k_ref, bf16[512,512]{1,0:T(8,128)(2,1)S(1)} %convolution_convert_fusion.1.v_ref, ...), custom_call_target="tpu_custom_call" | custom-call | flops 452984832 | bytes 6291456 | tf_op jit(solution)/shard_map/local_attention/pallas_call | solution.py:297
  144.9 0.8 copy-done.6
  145.7 1.0 copy-done.11
  146.7 1.0 copy-done.13
  147.6 9.0 %all-to-all-done.2 = bf16[16,400,128]{2,1,0:T(8,128)(2,1)} async-done(((bf16[16,400,128]{2,1,0:T(8,128)(2,1)}), bf16[16,400,128]{2,1,0:T(8,128)(2,1)}, u32[]{:S(2)}, u32[]{:S(2)}) %all-to-all-start.2) | async-done | bytes 1638432 | tf_op jit(solution)/shard_map/all_to_all | solution.py:377
  156.7 1.2 copy-done.10
  157.9 1.2 copy-done.12
  159.1 1.2 copy-done.14
  160.4 4.1 %combine.1 = bf16[512,1024]{1,0:T(8,128)(2,1)S(1)} custom-call(s32[48]{0:T(128)S(1)} %all_to_all.23.codes, bf16[6400,128]{1,0:T(8,128)(2,1)} %bitcast.4.msg_ref, f32[2048,128]{1,0:T(8,128)S(1)} %copy-done.12, f32[2048,128]{1,0:T(8,128)S(1)} %copy-done.14, f32[16,128]{1,0:T(8,128)S(1)} %get-tuple-element.10.lse_ref, bf16[512,1024]{1,0:T(8,128)(2,1)S(1)} %copy-done.10), custom_call_target="tpu_custom_call" | custom-call | flops 536870912 | bytes 3735552 | tf_op jit(solution)/shard_map/combine/pallas_call | solution.py:379
  164.5 1.0 copy-done.5
  165.5 0.0 reduce-scatter.3.cloned.1.call-update
  165.5 0.0 all-gather.2.cloned.1.call-start
  165.6 25.1 %reduce-scatter.3.cloned.1.call-done = bf16[256,1024]{1,0:T(8,128)(2,1)} async-done(((bf16[512,1024]{1,0:T(8,128)(2,1)}), bf16[256,1024]{1,0:T(8,128)(2,1)}) %reduce-scatter.3.cloned.1.call-update) | async-done | bytes 524304 | tf_op jit(solution)/shard_map/reduce_scatter | solution.py:401
  190.6 2.2 fusion.11
  192.8 2.0 fusion.13
  194.9 0.2 reduce-scatter.5.cloned.1.call-start
  195.1 21.2 %all-gather.2.cloned.1.call-done = bf16[512,1024]{1,0:T(8,128)(2,1)} async-done(((bf16[256,1024]{1,0:T(8,128)(2,1)}), bf16[512,1024]{1,0:T(8,128)(2,1)}) %all-gather.2.cloned.1.call-update) | async-done | bytes 1048592 | tf_op jit(solution)/shard_map/all_gather | solution.py:405
  216.3 5.5 %fusion.2 = f32[512,1408]{1,0:T(8,128)} fusion(bf16[512,1024]{1,0:T(8,128)(2,1)} %all-gather.2.cloned.1.call-done, bf16[2,1024,1408]{2,1,0:T(8,128)(2,1)} %param.42), kind=kOutput, calls=%fused_computation.3 | convolution fusion | flops 1476395008 | bytes 6815744 | tf_op jit(solution)/shard_map/dot_general | solution.py:406
  221.9 7.5 %convolution_convert_fusion = bf16[512,1024]{1,0:T(8,128)(2,1)} fusion(bf16[1408,1024]{1,0:T(8,128)(2,1)S(1)} %copy-done, bf16[512,1024]{1,0:T(8,128)(2,1)} %all-gather.2.cloned.1.call-done, bf16[2,1024,1408]{2,1,0:T(8,128)(2,1)} %param.42, f32[512,1408]{1,0:T(8,128)} %fusion.2), kind=kOutput, calls=%fused_computation.15 | convolution fusion | flops 2957639680 | bytes 10747904 | tf_op jit(solution)/shard_map/dot_general | solution.py:410
  229.4 0.0 reduce-scatter.5.cloned.1.call-update
  229.4 0.1 copy.30
  229.5 0.1 reshape.39.path
  229.6 0.1 copy.31
  229.7 0.1 reshape.40.mom_code
  229.8 0.1 copy.32
  230.0 0.1 reshape.41.forget_code
  230.1 2.2 copy-done.2
  232.3 2.2 copy-done.4
  234.5 1.1 copy-done.7
  235.5 21.0 %update_memory.1 = (f32[16,4,128,128]{3,2,1,0:T(8,128)}, f32[16,4,128,128]{3,2,1,0:T(8,128)}) custom-call(s32[128]{0:T(128)S(1)} %reshape.39.path, s32[16]{0:T(128)S(1)} %copy-done.18, s32[512]{0:T(512)S(1)} %reshape.40.mom_code, s32[512]{0:T(512)S(1)} %reshape.41.forget_code, bf16[512,512]{1,0:T(8,128)(2,1)S(1)} %convolution_convert_fusion.2.k_ref, ...), custom_call_target="tpu_custom_call" | custom-call | flops 939524096 | bytes 16777216 | tf_op jit(solution)/shard_map/update_memory/pallas_call | solution.py:325
  256.6 2.2 fusion.14
  (43 shorter events, 0.1 us)
Async XLA Ops:
  7.2 214.7 %copy-start = (bf16[1408,1024]{1,0:T(8,128)(2,1)S(1)}, bf16[1408,1024]{1,0:T(8,128)(2,1)}, u32[]{:S(2)}) copy-start(bf16[1408,1024]{1,0:T(8,128)(2,1)} %param.43) | copy-start | bytes 8650756
  7.2 16.5 %copy-start.19 = (s32[16]{0:T(128)S(1)}, s32[16]{0:T(128)}, u32[]{:S(2)}) copy-start(s32[16]{0:T(128)} %lengths.1) | copy-start | bytes 196
  8.7 13.7 %all-to-all-start = ((s32[16,3,1]{1,2,0:T(1,128)}), s32[16,3,1]{1,2,0:T(1,128)S(1)}, u32[]{:S(2)}, u32[]{:S(2)}) async-start(s32[16,3,1]{1,2,0:T(1,128)} %bitcast), calls=%async_computation | async-start | bytes 16384 | tf_op jit(solution)/shard_map/all_to_all | solution.py:272
  19.9 97.9 %copy-start.8 = (bf16[512,512]{1,0:T(8,128)(2,1)}, bf16[512,512]{1,0:T(8,128)(2,1)S(1)}, u32[]{:S(2)}) copy-start(bf16[512,512]{1,0:T(8,128)(2,1)S(1)} %convolution_convert_fusion.3.q_ref) | copy-start | bytes 1572868
  117.9 1.2 copy-start.3
  119.0 4.6 %copy-start.24 = (f32[1024]{0:T(1024)S(1)}, f32[1024]{0:T(1024)}, u32[]{:S(2)}) copy-start(f32[1024]{0:T(1024)} %param.23) | copy-start | bytes 12292
  119.0 37.6 %all-to-all-start.2 = ((bf16[16,400,128]{2,1,0:T(8,128)(2,1)}), bf16[16,400,128]{2,1,0:T(8,128)(2,1)}, u32[]{:S(2)}, u32[]{:S(2)}) async-start(bf16[16,400,128]{2,1,0:T(8,128)(2,1)} %bitcast.21), calls=%async_computation.2 | async-start | bytes 3276800 | tf_op jit(solution)/shard_map/all_to_all | solution.py:377
  123.6 67.0 %reduce-scatter.3.cloned.1.call-start = ((), (), s32[]{:S(2)}) async-start(), calls=%async_computation.5 | async-start | bytes 1572864 | tf_op jit(solution)/shard_map/reduce_scatter | solution.py:401
  123.6 4.9 %copy-start.1 = (f32[16,4,128,128]{3,2,1,0:T(8,128)S(1)}, f32[16,4,128,128]{3,2,1,0:T(8,128)}, u32[]{:S(2)}) copy-start(f32[16,4,128,128]{3,2,1,0:T(8,128)} %mem_ref.3) | copy-start | bytes 12582916
  126.1 2.4 copy-start.9
  126.1 2.4 copy-start.15
  126.1 2.4 copy-start.16
  126.1 2.4 copy-start.17
  144.9 0.8 copy-start.6
  145.7 1.0 copy-start.11
  146.6 1.0 copy-start.13
  156.7 1.2 copy-start.10
  157.9 1.2 copy-start.12
  159.1 1.2 copy-start.14
  160.4 32.5 %copy-start.22 = (f32[1024]{0:T(1024)S(1)}, f32[1024]{0:T(1024)}, u32[]{:S(2)}) copy-start(f32[1024]{0:T(1024)} %param.41) | copy-start | bytes 12292
  164.5 1.0 copy-start.5
  165.5 50.8 %all-gather.2.cloned.1.call-start = ((), (), s32[]{:S(2)}) async-start(), calls=%async_computation.6 | async-start | bytes 1572864 | tf_op jit(solution)/shard_map/all_gather | solution.py:405
  194.9 61.7 %reduce-scatter.5.cloned.1.call-start = ((), (), s32[]{:S(2)}) async-start(), calls=%async_computation.7 | async-start | bytes 1572864 | tf_op jit(solution)/shard_map/reduce_scatter | solution.py:409
  221.9 7.6 %copy-start.23 = (s32[16,8]{0,1:T(8,128)S(1)}, s32[16,8]{0,1:T(8,128)}, u32[]{:S(2)}) copy-start(s32[16,8]{0,1:T(8,128)} %param.35) | copy-start | bytes 1540
  221.9 7.7 %copy-start.20 = (s32[16,8,4]{0,2,1:T(4,128)S(1)}, s32[16,8,4]{0,2,1:T(4,128)}, u32[]{:S(2)}) copy-start(s32[16,8,4]{0,2,1:T(4,128)} %param.39) | copy-start | bytes 6148
  221.9 8.0 %copy-start.21 = (s32[16,8,4]{0,2,1:T(4,128)S(1)}, s32[16,8,4]{0,2,1:T(4,128)}, u32[]{:S(2)}) copy-start(s32[16,8,4]{0,2,1:T(4,128)} %param.40) | copy-start | bytes 6148
  221.9 8.2 %copy-start.18 = (s32[16]{0:T(128)S(1)}, s32[16]{0:T(128)}, u32[]{:S(2)}) copy-start(s32[16]{0:T(128)} %count.1) | copy-start | bytes 196
  230.1 2.2 copy-start.2
  232.3 2.2 copy-start.4
  234.5 1.1 copy-start.7
Sparse Core Ops, SparseCore 0:
  165.6 24.9 reduce-scatter.2
  195.0 21.3 all-gather.1
  229.5 20.3 reduce-scatter.4

commit v2 on v1

--- a/solution.py
+++ b/solution.py
@@ -11,12 +11,12 @@
 HD = 128
 LANES = 128
 EXTRA = 16
-PARTS = 3
+TOP_PARTS = 3
+SUM_PARTS = 2
 
 EPS = 1e-06
 THETA = 0.5
 NEG = -1e30
-TINY = 1e-30
 
 VMEM = pltpu.VMEM
 SMEM = pltpu.SMEM
@@ -53,12 +53,34 @@
     return jnp.sum(spread, axis=0, keepdims=True)
 
 
-def pack_queries(codes, lengths, q_ref, out_ref, *, n, cap, reqs, draft, heads, page_len):
-    block = cap * heads * draft + EXTRA
+def split_parts(row, count):
+    parts = []
+    for _ in range(count):
+        part = row.astype(BF16).astype(F32)
+        parts.append(part)
+        row = row - part
+    return parts
+
+
+def project_queries(tok_ref, gain_ref, w_ref, normed_ref, q_ref, turned_ref, *, reqs, draft, heads):
+    normed_ref[...] = rms_norm(tok_ref[...], gain_ref[...])
+    q_ref[...] = jnp.dot(normed_ref[...], w_ref[...], preferred_element_type=F32).astype(BF16)
+    span = heads * draft
+    for r in range(reqs):
+        rows = slice(r * draft, (r + 1) * draft)
+        pieces = [q_ref[rows, h * HD : (h + 1) * HD].astype(F32) for h in range(heads)]
+        if span < LANES:
+            pieces.append(jnp.zeros((LANES - span, HD), F32))
+        tile = jnp.concatenate(pieces, axis=0)
+        turned_ref[r * HD : (r + 1) * HD, :] = jnp.transpose(tile).astype(BF16)
+
+
+def pack_queries(codes, lengths, turned_ref, out_ref, *, n, cap, reqs, page_len):
+    block = cap * HD + EXTRA
     row_id = lax.broadcasted_iota(jnp.int32, (EXTRA, LANES), 0)
 
     def one(d, carry):
-        base = pl.multiple_of(d * block, 16)
+        base = pl.multiple_of(d * block, EXTRA)
         tail = jnp.zeros((EXTRA, LANES), F32)
         for c in range(cap):
             code = codes[d * cap + c]
@@ -66,12 +88,9 @@
             page = lax.div(code, reqs)
             live = jnp.clip(lengths[r] - page * page_len, 0, page_len)
             tail = jnp.where(row_id == c, live.astype(F32), tail)
-            rows = pl.ds(pl.multiple_of(r * draft, draft), draft)
-            for h in range(heads):
-                out_ref[pl.ds(base + (c * heads + h) * draft, draft), :] = q_ref[
-                    rows, h * HD : (h + 1) * HD
-                ]
-        out_ref[pl.ds(base + cap * heads * draft, EXTRA), :] = tail.astype(BF16)
+            rows = pl.ds(pl.multiple_of(r * HD, HD), HD)
+            out_ref[pl.ds(base + c * HD, HD), :] = turned_ref[rows, :]
+        out_ref[pl.ds(base + cap * HD, EXTRA), :] = tail.astype(BF16)
         return carry
 
     lax.fori_loop(0, n, one, 0)
@@ -79,41 +98,47 @@
 
 def page_attention(q_ref, kv_ref, out_ref, *, cap, draft, heads, page_len, scale):
     span = heads * draft
-    tail_at = cap * span
-    limits = q_ref[tail_at : tail_at + EXTRA, :].astype(F32)
-    lane = lax.broadcasted_iota(jnp.int32, (draft, page_len), 1).astype(F32)
+    limits = q_ref[cap * HD : cap * HD + EXTRA, :].astype(F32)
+    token = lax.broadcasted_iota(jnp.int32, (page_len, LANES), 0).astype(F32)
     row_id = lax.broadcasted_iota(jnp.int32, (EXTRA, LANES), 0)
+    head_of = lax.broadcasted_iota(jnp.int32, (HD, LANES), 1) // draft
     tail = jnp.zeros((EXTRA, LANES), F32)
+    all_scores = []
     for c in range(cap):
-        valid = lane < limits[c : c + 1, :]
-        columns = []
+        turned = q_ref[c * HD : (c + 1) * HD, :]
+        blocks = [jnp.where(head_of == h, turned, jnp.zeros_like(turned)) for h in range(heads)]
+        all_scores.append(
+            jnp.dot(kv_ref[c, 0], jnp.concatenate(blocks, axis=0), preferred_element_type=F32)
+        )
+    all_weights = []
+    for c in range(cap):
+        scores = jnp.where(token < limits[c : c + 1, :], all_scores[c] * scale, NEG)
+        top = jnp.max(scores, axis=0, keepdims=True)
+        weight = jnp.exp(scores - top)
+        total = jnp.sum(weight, axis=0, keepdims=True)
+        all_weights.append(jnp.transpose(weight).astype(BF16))
+        parts = split_parts(top, TOP_PARTS) + split_parts(total, SUM_PARTS)
+        for p, part in enumerate(parts):
+            tail = jnp.where(row_id == p * cap + c, part, tail)
+    for c in range(cap):
         for h in range(heads):
-            at = c * span + h * draft
-            cols = slice(h * HD, (h + 1) * HD)
-            scores = nt_dot(q_ref[at : at + draft, :], kv_ref[c, 0, :, cols]) * scale
-            scores = jnp.where(valid, scores, NEG)
-            top = jnp.max(scores, axis=1, keepdims=True)
-            weight = jnp.where(valid, jnp.exp(scores - top), 0.0)
-            total = jnp.sum(weight, axis=1, keepdims=True)
-            numer = jnp.dot(weight.astype(BF16), kv_ref[c, 1, :, cols], preferred_element_type=F32)
-            kept = jnp.maximum(total, TINY)
-            out_ref[at : at + draft, :] = (numer / kept).astype(BF16)
-            columns.append(jnp.where(total > 0.0, top + jnp.log(kept), NEG))
-        row = column_to_row(jnp.concatenate(columns, axis=0), span)
-        for p in range(PARTS):
-            part = row.astype(BF16).astype(F32)
-            tail = jnp.where(row_id == p * cap + c, part, tail)
-            row = row - part
-    out_ref[tail_at : tail_at + EXTRA, :] = tail.astype(BF16)
+            rows = slice(h * draft, (h + 1) * draft)
+            numer = jnp.dot(
+                all_weights[c][rows, :],
+                kv_ref[c, 1, :, h * HD : (h + 1) * HD],
+                preferred_element_type=F32,
+            )
+            out_ref[c * span + h * draft : c * span + (h + 1) * draft, :] = numer.astype(BF16)
+    out_ref[cap * span : cap * span + EXTRA, :] = tail.astype(BF16)
 
 
 def local_attention(
-    q_ref, k_ref, v_ref, pk_ref, pv_ref, mask_ref, mem_ref, o_ref, ret_ref, lse_ref,
-    *, heads, draft, scale,
+    q_ref, k_ref, v_ref, pk_ref, pv_ref, mask_ref, mem_ref,
+    o_ref, ret_ref, top_ref, sum_ref, *, heads, draft, scale,
 ):
     r = pl.program_id(0)
     seen = mask_ref[0] == 1
-    columns = []
+    tops, totals = [], []
     for h in range(heads):
         cols = slice(h * HD, (h + 1) * HD)
         rows = slice(h * draft, (h + 1) * draft)
@@ -128,14 +153,17 @@
         total = jnp.sum(tree_w, axis=1, keepdims=True) + jnp.sum(fixed_w, axis=1, keepdims=True)
         numer = jnp.dot(tree_w.astype(BF16), v_ref[:, cols], preferred_element_type=F32)
         numer = numer + jnp.dot(fixed_w.astype(BF16), pv_ref[:, cols], preferred_element_type=F32)
-        o_ref[rows, :] = numer / total
-        columns.append(top + jnp.log(total))
+        o_ref[rows, :] = numer
+        tops.append(top)
+        totals.append(total)
         wide = query.astype(F32)
         unit = wide * lax.rsqrt(jnp.sum(wide * wide, axis=1, keepdims=True) + EPS)
         ret_ref[rows, :] = jnp.dot(
             unit, mem_ref[0, h], preferred_element_type=F32, precision=lax.Precision.HIGHEST
         )
-    lse_ref[pl.ds(r, 1), :] = column_to_row(jnp.concatenate(columns, axis=0), heads * draft)
+    span = heads * draft
+    top_ref[pl.ds(r, 1), :] = column_to_row(jnp.concatenate(tops, axis=0), span)
+    sum_ref[pl.ds(r, 1), :] = column_to_row(jnp.concatenate(totals, axis=0), span)
 
 
 def update_memory(
@@ -177,33 +205,34 @@
 
 
 def combine(
-    codes, msg_ref, o_ref, ret_ref, lse_ref, w_ref, out_ref,
-    part_lse, best, total, weight, own_weight, acc, mixed,
-    *, n, cap, reqs, draft, heads,
+    codes, side, msg_ref, o_ref, ret_ref, own_top_ref, own_sum_ref, w_ref, *rest,
+    n, cap, reqs, draft, heads, pieces,
 ):
+    outs = rest[:pieces]
+    part_top, part_sum, best, total, weight, own_weight, acc, mixed = rest[pieces:]
     span = heads * draft
     block = cap * span + EXTRA
     slots = n * cap
     for d in range(n):
         at = d * block + cap * span
         tail = msg_ref[at : at + EXTRA, :].astype(F32)
-        part_lse[d * cap : (d + 1) * cap, :] = (
-            tail[0:cap] + tail[cap : 2 * cap] + tail[2 * cap : 3 * cap]
-        )
-    best[...] = lse_ref[...]
+        rows = [tail[p * cap : (p + 1) * cap] for p in range(TOP_PARTS + SUM_PARTS)]
+        part_top[d * cap : (d + 1) * cap, :] = rows[0] + rows[1] + rows[2]
+        part_sum[d * cap : (d + 1) * cap, :] = rows[3] + rows[4]
+    best[...] = own_top_ref[...]
     owners = [lax.rem(codes[s], reqs) for s in range(slots)]
     for s in range(slots):
         r = owners[s]
-        best[pl.ds(r, 1), :] = jnp.maximum(best[pl.ds(r, 1), :], part_lse[s : s + 1, :])
+        best[pl.ds(r, 1), :] = jnp.maximum(best[pl.ds(r, 1), :], part_top[s : s + 1, :])
     own_weight[...] = jnp.zeros_like(own_weight)
     weight[...] = jnp.zeros_like(weight)
-    start = jnp.exp(lse_ref[...] - best[...])
-    total[...] = start
+    start = jnp.exp(own_top_ref[...] - best[...])
+    total[...] = start * own_sum_ref[...]
     for s in range(slots):
         r = owners[s]
-        term = jnp.exp(part_lse[s : s + 1, :] - best[pl.ds(r, 1), :])
+        term = jnp.exp(part_top[s : s + 1, :] - best[pl.ds(r, 1), :])
         weight[s : s + 1, :] = term
-        total[pl.ds(r, 1), :] = total[pl.ds(r, 1), :] + term
+        total[pl.ds(r, 1), :] = total[pl.ds(r, 1), :] + term * part_sum[s : s + 1, :]
     inverse = 1.0 / total[...]
     own_weight[0:reqs, :] = start * inverse
     total[...] = inverse
@@ -226,7 +255,38 @@
             mixed[r * draft : (r + 1) * draft, h * HD : (h + 1) * HD] = acc[
                 at : at + draft, :
             ].astype(BF16)
-    out_ref[...] = jnp.dot(mixed[...], w_ref[...], preferred_element_type=F32).astype(BF16)
+    rows = reqs * draft // pieces
+    for p, out_ref in enumerate(outs):
+        first = lax.rem(side[0] + p, pieces) * rows
+        out_ref[...] = jnp.dot(
+            mixed[pl.ds(pl.multiple_of(first, rows), rows), :],
+            w_ref[...],
+            preferred_element_type=F32,
+        ).astype(BF16)
+
+
+def feed_forward(
+    side, tok_ref, mine_ref, theirs_ref, gain_ref, up_ref, down_ref, out_ref, hidden, *, own
+):
+    rows = mine_ref.shape[0]
+    units = down_ref.shape[0]
+    at = side[0] if own else 1 - side[0]
+    tokens = tok_ref[pl.ds(pl.multiple_of(at * rows, rows), rows), :].astype(F32)
+    summed = tokens + mine_ref[...].astype(F32) + theirs_ref[...].astype(F32)
+    residual = summed.astype(BF16)
+    ffn_in = rms_norm(residual, gain_ref[...])
+    step = 256
+    for first in range(0, units, step):
+        cols = slice(first, min(first + step, units))
+        gate = jnp.dot(ffn_in, up_ref[0, :, cols], preferred_element_type=F32)
+        up = jnp.dot(ffn_in, up_ref[1, :, cols], preferred_element_type=F32)
+        hidden[:, cols] = (gate / (1.0 + jnp.exp(-gate)) * up).astype(BF16)
+    for first in range(0, out_ref.shape[1], step):
+        cols = slice(first, first + step)
+        part = jnp.dot(hidden[...], down_ref[:, cols], preferred_element_type=F32)
+        if own:
+            part = part + residual[:, cols].astype(F32)
+        out_ref[:, cols] = part.astype(out_ref.dtype)
 
 
 def on_device(
@@ -265,26 +325,38 @@
     cap = slots // n
     fixed_count = persist_keys.shape[0]
     page_len = kv_cache.shape[2]
+    ask_block = cap * HD + EXTRA
     block = cap * span + EXTRA
     scale = 1.0 / math.sqrt(HD)
 
     label = slot_page * reqs + lax.rem(slot_request, reqs)
     codes = lax.all_to_all(label, "req", split_axis=0, concat_axis=0, tiled=True)
 
-    normed = rms_norm(tokens, norm_attn)
-    queries = jnp.dot(normed, w_query, preferred_element_type=F32).astype(BF16)
+    normed, queries, turned = pl.pallas_call(
+        functools.partial(project_queries, reqs=reqs, draft=draft, heads=heads),
+        out_shape=(
+            jax.ShapeDtypeStruct((group_rows, model), BF16),
+            jax.ShapeDtypeStruct((group_rows, width), BF16),
+            jax.ShapeDtypeStruct((reqs * HD, LANES), BF16),
+        ),
+        in_specs=[whole()] * 3,
+        out_specs=(whole(),) * 3,
+        compiler_params=params(12),
+        cost_estimate=cost(
+            2 * group_rows * model * width, 2 * model * (2 * group_rows + width)
+        ),
+        name="project_queries",
+    )(tokens, norm_attn.reshape(1, -1), w_query)
 
     packed = pl.pallas_call(
-        functools.partial(
-            pack_queries, n=n, cap=cap, reqs=reqs, draft=draft, heads=heads, page_len=page_len
-        ),
-        out_shape=jax.ShapeDtypeStruct((n * block, LANES), BF16),
+        functools.partial(pack_queries, n=n, cap=cap, reqs=reqs, page_len=page_len),
+        out_shape=jax.ShapeDtypeStruct((n * ask_block, LANES), BF16),
         in_specs=[whole(SMEM), whole(SMEM), whole()],
         out_specs=whole(),
-        compiler_params=params(),
-        cost_estimate=cost(0, 4 * n * block * LANES),
+        compiler_params=params(8),
+        cost_estimate=cost(0, 4 * n * ask_block * LANES),
         name="pack_queries",
-    )(codes, cache_len, queries)
+    )(codes, cache_len, turned)
     asked = lax.all_to_all(packed, "req", split_axis=0, concat_axis=0, tiled=True)
 
     keys = jnp.dot(normed, w_key, preferred_element_type=F32).astype(BF16)
@@ -294,12 +366,13 @@
     fixed_block = pl.BlockSpec((fixed_count, width), lambda r, *_: (0, 0))
     matrix_block = pl.BlockSpec((1, heads, HD, HD), lambda r, *_: (r, 0, 0, 0))
     span_block = pl.BlockSpec((span, HD), lambda r, *_: (r, 0))
-    own, retrieved, own_lse = pl.pallas_call(
+    own, retrieved, own_top, own_sum = pl.pallas_call(
         functools.partial(local_attention, heads=heads, draft=draft, scale=scale),
         grid=(reqs,),
         out_shape=(
             jax.ShapeDtypeStruct((reqs * span, HD), F32),
             jax.ShapeDtypeStruct((reqs * span, HD), F32),
+            jax.ShapeDtypeStruct((reqs, LANES), F32),
             jax.ShapeDtypeStruct((reqs, LANES), F32),
         ),
         in_specs=[
@@ -311,8 +384,8 @@
             pl.BlockSpec((1, draft, draft), lambda r: (r, 0, 0)),
             matrix_block,
         ],
-        out_specs=(span_block, span_block, pl.BlockSpec((reqs, LANES), lambda r: (0, 0))),
-        compiler_params=params(),
+        out_specs=(span_block, span_block) + (pl.BlockSpec((reqs, LANES), lambda r: (0, 0)),) * 2,
+        compiler_params=params(10),
         cost_estimate=cost(
             2 * reqs * span * HD * (2 * (draft + fixed_count) + 6 * HD),
             4 * reqs * (heads * HD * HD + 2 * span * HD),
@@ -338,7 +411,7 @@
             ],
         ),
         out_shape=(matrices, matrices),
-        compiler_params=params(),
+        compiler_params=params(10),
         cost_estimate=cost(
             14 * reqs * heads * HD * HD * steps * 8, 16 * reqs * heads * HD * HD
         ),
@@ -354,7 +427,9 @@
         momentum,
     )
 
-    message_block = pl.BlockSpec((block, LANES), lambda d: (d, 0))
+    asked, memory_out, momentum_out, keys, values = lax.optimization_barrier(
+        (asked, memory_out, momentum_out, keys, values)
+    )
     answers = pl.pallas_call(
         functools.partial(
             page_attention, cap=cap, draft=draft, heads=heads, page_len=page_len, scale=scale
@@ -362,11 +437,11 @@
         grid=(n,),
         out_shape=jax.ShapeDtypeStruct((n * block, LANES), BF16),
         in_specs=[
-            message_block,
+            pl.BlockSpec((ask_block, LANES), lambda d: (d, 0)),
             pl.BlockSpec((cap, 2, page_len, width), lambda d: (d, 0, 0, 0)),
         ],
-        out_specs=message_block,
-        compiler_params=params(),
+        out_specs=pl.BlockSpec((block, LANES), lambda d: (d, 0)),
+        compiler_params=params(12),
         cost_estimate=cost(
             4 * slots * span * page_len * HD,
             4 * slots * page_len * width + 4 * n * block * LANES,
@@ -376,12 +451,19 @@
     )(asked, kv_cache)
     returned = lax.all_to_all(answers, "req", split_axis=0, concat_axis=0, tiled=True)
 
-    partial_out = pl.pallas_call(
-        functools.partial(combine, n=n, cap=cap, reqs=reqs, draft=draft, heads=heads),
-        out_shape=jax.ShapeDtypeStruct((group_rows, model), BF16),
-        in_specs=[whole(SMEM)] + [whole()] * 5,
-        out_specs=whole(),
+    side = lax.axis_index("grp").astype(jnp.int32).reshape(1)
+    grp = lax.axis_size("grp")
+    pieces = 2 if grp == 2 and w_down.shape[0] % LANES == 0 else 1
+    rows = group_rows // grp
+    partials = pl.pallas_call(
+        functools.partial(
+            combine, n=n, cap=cap, reqs=reqs, draft=draft, heads=heads, pieces=pieces
+        ),
+        out_shape=(jax.ShapeDtypeStruct((group_rows // pieces, model), BF16),) * pieces,
+        in_specs=[whole(SMEM)] * 2 + [whole()] * 6,
+        out_specs=(whole(),) * pieces,
         scratch_shapes=[
+            pltpu.VMEM((slots, LANES), F32),
             pltpu.VMEM((slots, LANES), F32),
             pltpu.VMEM((reqs, LANES), F32),
             pltpu.VMEM((reqs, LANES), F32),
@@ -390,15 +472,39 @@
             pltpu.VMEM((reqs * span, HD), F32),
             pltpu.VMEM((group_rows, width), BF16),
         ],
-        compiler_params=params(),
+        compiler_params=params(16),
         cost_estimate=cost(
             2 * group_rows * width * model, 2 * n * block * LANES + 8 * reqs * span * HD
         ),
         name="combine",
-    )(codes, returned, own, retrieved, own_lse, w_out)
-
-    rows = group_rows // lax.axis_size("grp")
-    head_sum = lax.psum_scatter(partial_out, "grp", scatter_dimension=0, tiled=True).astype(F32)
+    )(codes, side, returned, own, retrieved, own_top, own_sum, w_out)
+
+    if pieces == 2:
+        swap = [(0, 1), (1, 0)]
+        own_part, peer_part = partials
+        theirs_peer = lax.ppermute(own_part, "grp", swap)
+        theirs_own = lax.ppermute(peer_part, "grp", swap)
+        units = w_down.shape[0]
+
+        def forward(mine, theirs, own_rows, dtype):
+            return pl.pallas_call(
+                functools.partial(feed_forward, own=own_rows),
+                out_shape=jax.ShapeDtypeStruct((rows, model), dtype),
+                in_specs=[whole(SMEM)] + [whole()] * 6,
+                out_specs=whole(),
+                scratch_shapes=[pltpu.VMEM((rows, units), BF16)],
+                compiler_params=params(24),
+                cost_estimate=cost(6 * rows * model * units, 6 * model * units),
+                name="feed_forward_own" if own_rows else "feed_forward_peer",
+            )(side, tokens, mine, theirs, norm_ffn.reshape(1, -1), w_gate_up, w_down)
+
+        sent = forward(peer_part, theirs_peer, False, BF16)
+        received = lax.ppermute(sent, "grp", swap)
+        base = forward(own_part, theirs_own, True, F32)
+        layer_out = (base + received.astype(F32)).astype(BF16)
+        return (layer_out, memory_out, momentum_out)
+
+    head_sum = lax.psum_scatter(partials[0], "grp", scatter_dimension=0, tiled=True).astype(F32)
     own_rows = lax.dynamic_slice_in_dim(tokens, lax.axis_index("grp") * rows, rows, 0)
     residual = (own_rows.astype(F32) + head_sum).astype(BF16)
     ffn_in = rms_norm(residual, norm_ffn)

time: 266 us -> 165 us (0.62)
  the two profiles are of different devices: /device:TPU:0 before, /device:TPU:14 now
where the time goes in v2:
time: 165 us; the launch traced here: 164 us
  Pallas kernels  57.9 us (35%)
  waiting for transfers between devices  46.8 us (28%)
  local copies, waits for them, and re-layouts  31.6 us (19%)
  starting transfers between devices  20 us (12%)
  matrix products  4.33 us (3%)
  other arithmetic  2.37 us (1%)
    unnamed x67, local copies, waits for them, and re-layouts  30 us
    pallas_call x1, Pallas kernels, on_device(): pl.pallas_call(functools.partial(update_memory, heads=heads, steps=steps)...  20.5 us
    pallas_call x1, Pallas kernels, on_device(): pl.pallas_call(functools.partial(local_attention, heads=heads, draft=draf...  16.2 us
    all_to_all x1, waiting for transfers between devices, on_device(): lax.all_to_all(answers, 'req', split_axis=0, concat_axis=0, tiled=True)  15 us
    ppermute x1, waiting for transfers between devices, on_device(): theirs_peer = lax.ppermute(own_part, 'grp', swap)  12.7 us
    all_to_all x1, waiting for transfers between devices, on_device(): lax.all_to_all(packed, 'req', split_axis=0, concat_axis=0, tiled=True)  8.88 us
    pallas_call x1, Pallas kernels, on_device(): pl.pallas_call(functools.partial(page_attention, cap=cap, draft=draft, he...  8 us
    all_to_all x1, starting transfers between devices, on_device(): lax.all_to_all(label, 'req', split_axis=0, concat_axis=0, tiled=True)  6.24 us
  transfers between devices with their start and end apart: 6, of which 5 were waited for; matrix products, arithmetic and copies ran while one was open for 3% of the time, Pallas kernels for 27%

profile of v2, /device:TPU:14, one launch (start us, length us, event | category | flops | bytes accessed | tf_op | source)
XLA Modules:
  0.0 163.9 jit_solution(3596704145891815906)
XLA Ops:
  0.7 0.8 fusion.1
  1.4 0.7 all_to_all.22
  2.1 6.2 %all-to-all-start = ((s32[16,3,1]{1,2,0:T(1,128)}), s32[16,3,1]{1,2,0:T(1,128)S(1)}, u32[]{:S(2)}, u32[]{:S(2)}) async-start(s32[16,3,1]{1,2,0:T(1,128)} %bitcast.1), calls=%async_computation | async-start | bytes 16384 | tf_op jit(solution)/shard_map/all_to_all | solution.py:333
  8.4 1.2 copy-done.7
  9.6 1.2 copy-done.13
  10.8 0.7 copy-done.25
  11.5 1.0 project_queries.1
  12.5 0.8 copy-done.19
  13.3 1.0 copy-done.28
  14.3 0.5 broadcast.14
  14.8 0.7 reduce.3
  15.6 0.6 copy-done.27
  16.2 2.2 %pack_queries.1 = bf16[6400,128]{1,0:T(8,128)(2,1)} custom-call(s32[48]{0:T(128)S(1)} %all_to_all.24.codes, s32[16]{0:T(128)S(1)} %copy-done.27, bf16[2048,128]{1,0:T(8,128)(2,1)S(1)} %get-tuple-element.17.turned_ref), custom_call_target="tpu_custom_call" | custom-call | bytes 3276800 | tf_op jit(solution)/shard_map/pack_queries/pallas_call | solution.py:351
  18.4 6.0 %all-to-all-start.1 = ((bf16[16,400,128]{2,1,0:T(8,128)(2,1)}), bf16[16,400,128]{2,1,0:T(8,128)(2,1)S(1)}, u32[]{:S(2)}, u32[]{:S(2)}) async-start(bf16[16,400,128]{2,1,0:T(8,128)(2,1)} %bitcast.3), calls=%async_computation.1 | async-start | bytes 3276800 | tf_op jit(solution)/shard_map/all_to_all | solution.py:360
  24.5 0.1 copy.31
  24.7 0.1 copy.32
  25.2 2.1 %convolution_convert_fusion.v_ref = bf16[512,512]{1,0:T(8,128)(2,1)S(1)} fusion(bf16[512,1024]{1,0:T(8,128)(2,1)} %copy-done.28, bf16[1024,512]{1,0:T(8,128)(2,1)S(1)} %copy-done), kind=kOutput, calls=%fused_computation | convolution fusion | flops 537133056 | bytes 2621440 | tf_op jit(solution)/shard_map/dot_general | solution.py:363
  27.3 2.2 %convolution_convert_fusion.1.k_ref = bf16[512,512]{1,0:T(8,128)(2,1)S(1)} fusion(bf16[512,1024]{1,0:T(8,128)(2,1)} %copy-done.28, bf16[1024,512]{1,0:T(8,128)(2,1)} %param.25), kind=kOutput, calls=%fused_computation.1 | convolution fusion | flops 537133056 | bytes 2621440 | tf_op jit(solution)/shard_map/dot_general | solution.py:362
  29.6 2.2 %copy-done.10 = f32[16,4,128,128]{3,2,1,0:T(8,128)S(1)} copy-done((f32[16,4,128,128]{3,2,1,0:T(8,128)S(1)}, f32[16,4,128,128]{3,2,1,0:T(8,128)}, u32[]{:S(2)}) %copy-start.10) | copy-done | bytes 4194328
  31.7 20.5 %update_memory.1 = (f32[16,4,128,128]{3,2,1,0:T(8,128)}, f32[16,4,128,128]{3,2,1,0:T(8,128)}) custom-call(s32[128]{0:T(128)S(1)} %reshape.33.path, s32[16]{0:T(128)S(1)} %copy-done.26, s32[512]{0:T(512)S(1)} %reshape.34.mom_code, s32[512]{0:T(512)S(1)} %reshape.35.forget_code, bf16[512,512]{1,0:T(8,128)(2,1)S(1)} %convolution_convert_fusion.1.k_ref, ...), custom_call_target="tpu_custom_call" | custom-call | flops 939524096 | bytes 16777216 | tf_op jit(solution)/shard_map/update_memory/pallas_call | solution.py:398
  52.2 0.8 copy-done.11
  53.0 8.9 %all-to-all-done.1 = bf16[16,400,128]{2,1,0:T(8,128)(2,1)S(1)} async-done(((bf16[16,400,128]{2,1,0:T(8,128)(2,1)}), bf16[16,400,128]{2,1,0:T(8,128)(2,1)S(1)}, u32[]{:S(2)}, u32[]{:S(2)}) %all-to-all-start.1) | async-done | bytes 1638432 | tf_op jit(solution)/shard_map/all_to_all | solution.py:360
  61.9 4.6 %copy-done.5 = bf16[48,2,128,512]{3,2,1,0:T(8,128)(2,1)S(1)} copy-done((bf16[48,2,128,512]{3,2,1,0:T(8,128)(2,1)S(1)}, bf16[48,2,128,512]{3,2,1,0:T(8,128)(2,1)}, u32[]{:S(2)}) %copy-start.5) | copy-done | bytes 12582936
  66.5 8.0 %page_attention.1 = bf16[6400,128]{1,0:T(8,128)(2,1)S(1)} custom-call(bf16[6400,128]{1,0:T(8,128)(2,1)S(1)} %bitcast.13, bf16[48,2,128,512]{3,2,1,0:T(8,128)(2,1)S(1)} %copy-done.5), custom_call_target="tpu_custom_call" | custom-call | flops 402653184 | bytes 15859712 | tf_op jit(solution)/shard_map/page_attention/pallas_call | solution.py:433
  74.5 1.2 copy-done.9
  75.7 5.1 %all-to-all-start.2 = ((bf16[16,400,128]{2,1,0:T(8,128)(2,1)}), bf16[16,400,128]{2,1,0:T(8,128)(2,1)}, u32[]{:S(2)}, u32[]{:S(2)}) async-start(bf16[16,400,128]{2,1,0:T(8,128)(2,1)} %bitcast.14), calls=%async_computation.2 | async-start | bytes 3276800 | tf_op jit(solution)/shard_map/all_to_all | solution.py:452
  80.8 2.2 %copy-done.4 = f32[16,4,128,128]{3,2,1,0:T(8,128)S(1)} copy-done((f32[16,4,128,128]{3,2,1,0:T(8,128)S(1)}, f32[16,4,128,128]{3,2,1,0:T(8,128)}, u32[]{:S(2)}) %copy-start.4) | copy-done | bytes 4194328
  82.9 1.0 copy-done.12
  84.0 1.0 copy-done.20
  85.0 16.2 %local_attention.1 = (f32[2048,128]{1,0:T(8,128)S(1)}, f32[2048,128]{1,0:T(8,128)S(1)}, f32[16,128]{1,0:T(8,128)S(1)}, f32[16,128]{1,0:T(8,128)S(1)}) custom-call(bf16[512,512]{1,0:T(8,128)(2,1)S(1)} %copy-done.20, bf16[512,512]{1,0:T(8,128)(2,1)S(1)} %copy-done.12, bf16[512,512]{1,0:T(8,128)(2,1)S(1)} %convolution_convert_fusion.v_ref, ...), custom_call_target="tpu_custom_call" | custom-call | flops 452984832 | bytes 6291456 | tf_op jit(solution)/shard_map/local_attention/pallas_call | solution.py:369
  101.3 1.0 copy-done.15
  102.2 1.0 copy-done.17
  103.2 15.0 %all-to-all-done.2 = bf16[16,400,128]{2,1,0:T(8,128)(2,1)} async-done(((bf16[16,400,128]{2,1,0:T(8,128)(2,1)}), bf16[16,400,128]{2,1,0:T(8,128)(2,1)}, u32[]{:S(2)}, u32[]{:S(2)}) %all-to-all-start.2) | async-done | bytes 1638432 | tf_op jit(solution)/shard_map/all_to_all | solution.py:452
  118.3 1.4 copy-done.14
  119.7 1.2 copy-done.16
  120.9 1.2 copy-done.18
  122.1 4.1 %combine.1 = (bf16[256,1024]{1,0:T(8,128)(2,1)S(1)}, bf16[256,1024]{1,0:T(8,128)(2,1)S(1)}) custom-call(s32[48]{0:T(128)S(1)} %all_to_all.24.codes, s32[1]{0:T(128)} %bitcast.side, bf16[6400,128]{1,0:T(8,128)(2,1)} %bitcast.6.msg_ref, f32[2048,128]{1,0:T(8,128)S(1)} %copy-done.16, f32[2048,128]{1,0:T(8,128)S(1)} %copy-done.18, ...), custom_call_target="tpu_custom_call" | custom-call | flops 536870912 | bytes 3735552 | tf_op jit(solution)/shard_map/combine/pallas_call | solution.py:458
  126.3 0.6 collective-permute-start.1
  126.8 1.5 collective-permute-start
  128.3 12.7 %collective-permute-done.1.theirs_ref = bf16[256,1024]{1,0:T(8,128)(2,1)S(1)} collective-permute-done((bf16[256,1024]{1,0:T(8,128)(2,1)S(1)}, bf16[256,1024]{1,0:T(8,128)(2,1)S(1)}, u32[]{:S(2)}, u32[]{:S(2)}) %collective-permute-start.1) | collective-permute-done | bytes 524320 | tf_op jit(solution)/shard_map/ppermute | solution.py:485
  141.1 2.6 %copy-done.1 = bf16[2,1024,1408]{2,1,0:T(8,128)(2,1)S(1)} copy-done((bf16[2,1024,1408]{2,1,0:T(8,128)(2,1)S(1)}, bf16[2,1024,1408]{2,1,0:T(8,128)(2,1)}, u32[]{:S(2)}) %copy-start.1) | copy-done | bytes 5767192
  143.7 2.9 %feed_forward_peer.1 = bf16[256,1024]{1,0:T(8,128)(2,1)S(1)} custom-call(s32[1]{0:T(128)} %bitcast.side, bf16[512,1024]{1,0:T(8,128)(2,1)S(1)} %copy-done.8, bf16[256,1024]{1,0:T(8,128)(2,1)S(1)} %get-tuple-element.28.mine_ref, bf16[256,1024]{1,0:T(8,128)(2,1)S(1)} %collective-permute-done.1.theirs_ref, f32[1,1024]{1,0:T(1,128)S(1)} %bitcast.15, ...), custom_call_target="tpu_custom_call" | custom-call | flops 2214592512 | bytes 8650752 | tf_op jit(solution)/shard_map/feed_forward_peer/pallas_call | solution.py:490
  146.6 0.6 collective-permute-start.2
  147.2 5.1 %collective-permute-done.theirs_ref = bf16[256,1024]{1,0:T(8,128)(2,1)S(1)} collective-permute-done((bf16[256,1024]{1,0:T(8,128)(2,1)S(1)}, bf16[256,1024]{1,0:T(8,128)(2,1)S(1)}, u32[]{:S(2)}, u32[]{:S(2)}) %collective-permute-start) | collective-permute-done | bytes 524320 | tf_op jit(solution)/shard_map/ppermute | solution.py:486
  152.3 2.6 %copy-done.2 = bf16[2,1024,1408]{2,1,0:T(8,128)(2,1)S(1)} copy-done((bf16[2,1024,1408]{2,1,0:T(8,128)(2,1)S(1)}, bf16[2,1024,1408]{2,1,0:T(8,128)(2,1)}, u32[]{:S(2)}) %copy-start.2) | copy-done | bytes 5767192
  154.9 2.9 %feed_forward_own.1 = f32[256,1024]{1,0:T(8,128)S(1)} custom-call(s32[1]{0:T(128)} %bitcast.side, bf16[512,1024]{1,0:T(8,128)(2,1)S(1)} %copy-done.8, bf16[256,1024]{1,0:T(8,128)(2,1)S(1)} %get-tuple-element.27.mine_ref, bf16[256,1024]{1,0:T(8,128)(2,1)S(1)} %collective-permute-done.theirs_ref, f32[1,1024]{1,0:T(1,128)S(1)} %bitcast.16, ...), custom_call_target="tpu_custom_call" | custom-call | flops 2214592512 | bytes 8650752 | tf_op jit(solution)/shard_map/feed_forward_own/pallas_call | solution.py:490
  157.9 5.1 %collective-permute-done.2 = bf16[256,1024]{1,0:T(8,128)(2,1)S(1)} collective-permute-done((bf16[256,1024]{1,0:T(8,128)(2,1)S(1)}, bf16[256,1024]{1,0:T(8,128)(2,1)S(1)}, u32[]{:S(2)}, u32[]{:S(2)}) %collective-permute-start.2) | collective-permute-done | bytes 524320 | tf_op jit(solution)/shard_map/ppermute | solution.py:502
  162.9 0.9 add_convert_fusion
  (50 shorter events, 0.6 us)
Async XLA Ops:
  0.6 24.5 %copy-start = (bf16[1024,512]{1,0:T(8,128)(2,1)S(1)}, bf16[1024,512]{1,0:T(8,128)(2,1)}, u32[]{:S(2)}) copy-start(bf16[1024,512]{1,0:T(8,128)(2,1)} %param.26) | copy-start | bytes 3145732
  0.6 23.8 %copy-start.29 = (s32[16,8,4]{0,2,1:T(4,128)S(1)}, s32[16,8,4]{0,2,1:T(4,128)}, u32[]{:S(2)}) copy-start(s32[16,8,4]{0,2,1:T(4,128)} %param.39) | copy-start | bytes 6148
  0.7 24.3 %copy-start.31 = (s32[16,8]{0,1:T(8,128)S(1)}, s32[16,8]{0,1:T(8,128)}, u32[]{:S(2)}) copy-start(s32[16,8]{0,1:T(8,128)} %param.35) | copy-start | bytes 1540
  2.1 12.2 %all-to-all-start = ((s32[16,3,1]{1,2,0:T(1,128)}), s32[16,3,1]{1,2,0:T(1,128)S(1)}, u32[]{:S(2)}, u32[]{:S(2)}) async-start(s32[16,3,1]{1,2,0:T(1,128)} %bitcast.1), calls=%async_computation | async-start | bytes 16384 | tf_op jit(solution)/shard_map/all_to_all | solution.py:333
  8.4 1.2 copy-start.7
  9.6 1.2 copy-start.13
  10.8 0.7 copy-start.25
  11.5 13.2 %copy-start.30 = (s32[16,8,4]{0,2,1:T(4,128)S(1)}, s32[16,8,4]{0,2,1:T(4,128)}, u32[]{:S(2)}) copy-start(s32[16,8,4]{0,2,1:T(4,128)} %param.40) | copy-start | bytes 6148
  12.5 0.8 copy-start.19
  13.3 1.0 copy-start.28
  15.6 0.7 copy-start.27
  18.4 43.5 %all-to-all-start.1 = ((bf16[16,400,128]{2,1,0:T(8,128)(2,1)}), bf16[16,400,128]{2,1,0:T(8,128)(2,1)S(1)}, u32[]{:S(2)}, u32[]{:S(2)}) async-start(bf16[16,400,128]{2,1,0:T(8,128)(2,1)} %bitcast.3), calls=%async_computation.1 | async-start | bytes 3276800 | tf_op jit(solution)/shard_map/all_to_all | solution.py:360
  24.5 5.0 %copy-start.26 = (s32[16]{0:T(128)S(1)}, s32[16]{0:T(128)}, u32[]{:S(2)}) copy-start(s32[16]{0:T(128)} %count.1) | copy-start | bytes 196
  25.2 4.4 %copy-start.3 = (f32[16,4,128,128]{3,2,1,0:T(8,128)S(1)}, f32[16,4,128,128]{3,2,1,0:T(8,128)}, u32[]{:S(2)}) copy-start(f32[16,4,128,128]{3,2,1,0:T(8,128)} %mem_ref.3) | copy-start | bytes 12582916
  29.5 2.2 %copy-start.10 = (f32[16,4,128,128]{3,2,1,0:T(8,128)S(1)}, f32[16,4,128,128]{3,2,1,0:T(8,128)}, u32[]{:S(2)}) copy-start(f32[16,4,128,128]{3,2,1,0:T(8,128)} %mom_ref.1) | copy-start | bytes 12582916
  52.2 0.8 copy-start.11
  61.9 4.6 %copy-start.5 = (bf16[48,2,128,512]{3,2,1,0:T(8,128)(2,1)S(1)}, bf16[48,2,128,512]{3,2,1,0:T(8,128)(2,1)}, u32[]{:S(2)}) copy-start(bf16[48,2,128,512]{3,2,1,0:T(8,128)(2,1)} %kv_ref.1) | copy-start | bytes 37748740
  66.5 14.2 %copy-start.21 = (s32[16,32,32]{2,1,0:T(8,128)S(1)}, s32[16,32,32]{2,1,0:T(8,128)}, u32[]{:S(2)}) copy-start(s32[16,32,32]{2,1,0:T(8,128)} %mask_ref.1) | copy-start | bytes 196612
  66.5 14.2 %copy-start.22 = (bf16[16,512]{1,0:T(8,128)(2,1)S(1)}, bf16[16,512]{1,0:T(8,128)(2,1)}, u32[]{:S(2)}) copy-start(bf16[16,512]{1,0:T(8,128)(2,1)} %pk_ref.1) | copy-start | bytes 49156
  66.5 14.3 %copy-start.23 = (bf16[16,512]{1,0:T(8,128)(2,1)S(1)}, bf16[16,512]{1,0:T(8,128)(2,1)}, u32[]{:S(2)}) copy-start(bf16[16,512]{1,0:T(8,128)(2,1)} %pv_ref.1) | copy-start | bytes 49156
  74.5 1.2 copy-start.9
  75.7 42.6 %all-to-all-start.2 = ((bf16[16,400,128]{2,1,0:T(8,128)(2,1)}), bf16[16,400,128]{2,1,0:T(8,128)(2,1)}, u32[]{:S(2)}, u32[]{:S(2)}) async-start(bf16[16,400,128]{2,1,0:T(8,128)(2,1)} %bitcast.14), calls=%async_computation.2 | async-start | bytes 3276800 | tf_op jit(solution)/shard_map/all_to_all | solution.py:452
  80.8 2.2 %copy-start.4 = (f32[16,4,128,128]{3,2,1,0:T(8,128)S(1)}, f32[16,4,128,128]{3,2,1,0:T(8,128)}, u32[]{:S(2)}) copy-start(f32[16,4,128,128]{3,2,1,0:T(8,128)} %mem_ref.3) | copy-start | bytes 12582916
  82.9 1.0 copy-start.12
  84.0 1.0 copy-start.20
  85.0 56.0 %copy-start.8 = (bf16[512,1024]{1,0:T(8,128)(2,1)S(1)}, bf16[512,1024]{1,0:T(8,128)(2,1)}, u32[]{:S(2)}) copy-start(bf16[512,1024]{1,0:T(8,128)(2,1)} %tok_ref.5) | copy-start | bytes 3145732
  85.0 56.0 %copy-start.24 = (f32[1024]{0:T(1024)S(1)}, f32[1024]{0:T(1024)}, u32[]{:S(2)}) copy-start(f32[1024]{0:T(1024)} %param.41) | copy-start | bytes 12292
  101.3 1.0 copy-start.15
  102.2 1.0 copy-start.17
  118.3 22.8 %copy-start.6 = (bf16[1408,1024]{1,0:T(8,128)(2,1)S(1)}, bf16[1408,1024]{1,0:T(8,128)(2,1)}, u32[]{:S(2)}) copy-start(bf16[1408,1024]{1,0:T(8,128)(2,1)} %down_ref.3) | copy-start | bytes 8650756
  118.3 1.4 copy-start.14
  119.7 1.2 copy-start.16
  120.9 1.2 copy-start.18
  126.3 14.8 %collective-permute-start.1 = (bf16[256,1024]{1,0:T(8,128)(2,1)S(1)}, bf16[256,1024]{1,0:T(8,128)(2,1)S(1)}, u32[]{:S(2)}, u32[]{:S(2)}) collective-permute-start(bf16[256,1024]{1,0:T(8,128)(2,1)S(1)} %get-tuple-element.27.mine_ref), channel_id=1, source_target_pairs={{0,1},{1,0},{2,3},{3,2},{4,5},{5,4},{6,7},{7,6},{8,9},{9,8},{10,11... | collective-permute-start | bytes 1572872 | tf_op jit(solution)/shard_map/ppermute | solution.py:485
  126.8 25.5 %collective-permute-start = (bf16[256,1024]{1,0:T(8,128)(2,1)S(1)}, bf16[256,1024]{1,0:T(8,128)(2,1)S(1)}, u32[]{:S(2)}, u32[]{:S(2)}) collective-permute-start(bf16[256,1024]{1,0:T(8,128)(2,1)S(1)} %get-tuple-element.28.mine_ref), channel_id=1, source_target_pairs={{0,1},{1,0},{2,3},{3,2},{4,5},{5,4},{6,7},{7,6},{8,9},{9,8},{10,11... | collective-permute-start | bytes 1572872 | tf_op jit(solution)/shard_map/ppermute | solution.py:486
  141.1 2.6 %copy-start.1 = (bf16[2,1024,1408]{2,1,0:T(8,128)(2,1)S(1)}, bf16[2,1024,1408]{2,1,0:T(8,128)(2,1)}, u32[]{:S(2)}) copy-start(bf16[2,1024,1408]{2,1,0:T(8,128)(2,1)} %up_ref.3) | copy-start | bytes 17301508
  146.6 16.3 %collective-permute-start.2 = (bf16[256,1024]{1,0:T(8,128)(2,1)S(1)}, bf16[256,1024]{1,0:T(8,128)(2,1)S(1)}, u32[]{:S(2)}, u32[]{:S(2)}) collective-permute-start(bf16[256,1024]{1,0:T(8,128)(2,1)S(1)} %feed_forward_peer.1), channel_id=1, source_target_pairs={{0,1},{1,0},{2,3},{3,2},{4,5},{5,4},{6,7},{7,6},{8,9},{9,8},{10,11... | collective-permute-start | bytes 1572872 | tf_op jit(solution)/shard_map/ppermute | solution.py:502
  152.3 2.6 %copy-start.2 = (bf16[2,1024,1408]{2,1,0:T(8,128)(2,1)S(1)}, bf16[2,1024,1408]{2,1,0:T(8,128)(2,1)}, u32[]{:S(2)}) copy-start(bf16[2,1024,1408]{2,1,0:T(8,128)(2,1)} %up_ref.3) | copy-start | bytes 17301508

commit v3 on v2

--- a/solution.py
+++ b/solution.py
@@ -20,6 +20,7 @@
 
 VMEM = pltpu.VMEM
 SMEM = pltpu.SMEM
+HBM = pltpu.HBM
 F32 = jnp.float32
 BF16 = jnp.bfloat16
 
@@ -30,6 +31,10 @@
 
 def cost(flops, moved, special=0):
     return pl.CostEstimate(flops=flops, bytes_accessed=moved, transcendentals=special)
+
+
+def keep_in(space, *arrays):
+    return tuple(pltpu.with_memory_space_constraint(array, space) for array in arrays)
 
 
 def params(mib=40):
@@ -75,6 +80,12 @@
         turned_ref[r * HD : (r + 1) * HD, :] = jnp.transpose(tile).astype(BF16)
 
 
+def project_keys(normed_ref, wk_ref, wv_ref, k_ref, v_ref):
+    normed = normed_ref[...]
+    k_ref[...] = jnp.dot(normed, wk_ref[...], preferred_element_type=F32).astype(BF16)
+    v_ref[...] = jnp.dot(normed, wv_ref[...], preferred_element_type=F32).astype(BF16)
+
+
 def pack_queries(codes, lengths, turned_ref, out_ref, *, n, cap, reqs, page_len):
     block = cap * HD + EXTRA
     row_id = lax.broadcasted_iota(jnp.int32, (EXTRA, LANES), 0)
@@ -83,7 +94,7 @@
         base = pl.multiple_of(d * block, EXTRA)
         tail = jnp.zeros((EXTRA, LANES), F32)
         for c in range(cap):
-            code = codes[d * cap + c]
+            code = codes[d, 0, c]
             r = lax.rem(code, reqs)
             page = lax.div(code, reqs)
             live = jnp.clip(lengths[r] - page * page_len, 0, page_len)
@@ -205,11 +216,18 @@
 
 
 def combine(
-    codes, side, msg_ref, o_ref, ret_ref, own_top_ref, own_sum_ref, w_ref, *rest,
+    codes, side, msg_ref, o_ref, ret_ref, own_top_ref, own_sum_ref, w_ref, up_hbm, down_hbm, *rest,
     n, cap, reqs, draft, heads, pieces,
 ):
     outs = rest[:pieces]
-    part_top, part_sum, best, total, weight, own_weight, acc, mixed = rest[pieces:]
+    staged = rest[pieces:-9]
+    part_top, part_sum, best, total, weight, own_weight, acc, mixed, sems = rest[-9:]
+    copies = [
+        pltpu.make_async_copy(source, target, sems.at[i])
+        for i, (source, target) in enumerate(zip((up_hbm, down_hbm), staged))
+    ]
+    for copy in copies:
+        copy.start()
     span = heads * draft
     block = cap * span + EXTRA
     slots = n * cap
@@ -220,7 +238,7 @@
         part_top[d * cap : (d + 1) * cap, :] = rows[0] + rows[1] + rows[2]
         part_sum[d * cap : (d + 1) * cap, :] = rows[3] + rows[4]
     best[...] = own_top_ref[...]
-    owners = [lax.rem(codes[s], reqs) for s in range(slots)]
+    owners = [lax.rem(codes[s // cap, 0, s % cap], reqs) for s in range(slots)]
     for s in range(slots):
         r = owners[s]
         best[pl.ds(r, 1), :] = jnp.maximum(best[pl.ds(r, 1), :], part_top[s : s + 1, :])
@@ -263,6 +281,8 @@
             w_ref[...],
             preferred_element_type=F32,
         ).astype(BF16)
+    for copy in copies:
+        copy.wait()
 
 
 def feed_forward(
@@ -329,14 +349,14 @@
     block = cap * span + EXTRA
     scale = 1.0 / math.sqrt(HD)
 
-    label = slot_page * reqs + lax.rem(slot_request, reqs)
+    label = (slot_page * reqs + lax.rem(slot_request, reqs)).reshape(n, 1, cap)
     codes = lax.all_to_all(label, "req", split_axis=0, concat_axis=0, tiled=True)
 
     normed, queries, turned = pl.pallas_call(
         functools.partial(project_queries, reqs=reqs, draft=draft, heads=heads),
         out_shape=(
-            jax.ShapeDtypeStruct((group_rows, model), BF16),
-            jax.ShapeDtypeStruct((group_rows, width), BF16),
+            HBM((group_rows, model), BF16),
+            HBM((group_rows, width), BF16),
             jax.ShapeDtypeStruct((reqs * HD, LANES), BF16),
         ),
         in_specs=[whole()] * 3,
@@ -346,21 +366,30 @@
             2 * group_rows * model * width, 2 * model * (2 * group_rows + width)
         ),
         name="project_queries",
-    )(tokens, norm_attn.reshape(1, -1), w_query)
+    )(*keep_in(HBM, tokens, norm_attn.reshape(1, -1), w_query))
 
     packed = pl.pallas_call(
         functools.partial(pack_queries, n=n, cap=cap, reqs=reqs, page_len=page_len),
-        out_shape=jax.ShapeDtypeStruct((n * ask_block, LANES), BF16),
+        out_shape=HBM((n * ask_block, LANES), BF16),
         in_specs=[whole(SMEM), whole(SMEM), whole()],
         out_specs=whole(),
         compiler_params=params(8),
         cost_estimate=cost(0, 4 * n * ask_block * LANES),
         name="pack_queries",
-    )(codes, cache_len, turned)
+    )(codes, *keep_in(HBM, cache_len), turned)
     asked = lax.all_to_all(packed, "req", split_axis=0, concat_axis=0, tiled=True)
 
-    keys = jnp.dot(normed, w_key, preferred_element_type=F32).astype(BF16)
-    values = jnp.dot(normed, w_value, preferred_element_type=F32).astype(BF16)
+    keys, values = pl.pallas_call(
+        project_keys,
+        out_shape=(HBM((group_rows, width), BF16),) * 2,
+        in_specs=[whole()] * 3,
+        out_specs=(whole(),) * 2,
+        compiler_params=params(12),
+        cost_estimate=cost(
+            4 * group_rows * model * width, 2 * model * (group_rows + 2 * width)
+        ),
+        name="project_keys",
+    )(*keep_in(HBM, normed, w_key, w_value))
 
     row_block = pl.BlockSpec((draft, width), lambda r, *_: (r, 0))
     fixed_block = pl.BlockSpec((fixed_count, width), lambda r, *_: (0, 0))
@@ -370,8 +399,8 @@
         functools.partial(local_attention, heads=heads, draft=draft, scale=scale),
         grid=(reqs,),
         out_shape=(
-            jax.ShapeDtypeStruct((reqs * span, HD), F32),
-            jax.ShapeDtypeStruct((reqs * span, HD), F32),
+            HBM((reqs * span, HD), F32),
+            HBM((reqs * span, HD), F32),
             jax.ShapeDtypeStruct((reqs, LANES), F32),
             jax.ShapeDtypeStruct((reqs, LANES), F32),
         ),
@@ -392,7 +421,7 @@
             reqs * span * (draft + fixed_count),
         ),
         name="local_attention",
-    )(queries, keys, values, persist_keys, persist_values, tree_mask, memory)
+    )(*keep_in(HBM, queries, keys, values, persist_keys, persist_values, tree_mask, memory))
 
     matrices = jax.ShapeDtypeStruct(memory.shape, F32)
     memory_out, momentum_out = pl.pallas_call(
@@ -421,10 +450,7 @@
         accept_len,
         momentum_code.reshape(-1),
         forget_code.reshape(-1),
-        keys,
-        values,
-        memory,
-        momentum,
+        *keep_in(HBM, keys, values, memory, momentum),
     )
 
     asked, memory_out, momentum_out, keys, values = lax.optimization_barrier(
@@ -435,7 +461,7 @@
             page_attention, cap=cap, draft=draft, heads=heads, page_len=page_len, scale=scale
         ),
         grid=(n,),
-        out_shape=jax.ShapeDtypeStruct((n * block, LANES), BF16),
+        out_shape=HBM((n * block, LANES), BF16),
         in_specs=[
             pl.BlockSpec((ask_block, LANES), lambda d: (d, 0)),
             pl.BlockSpec((cap, 2, page_len, width), lambda d: (d, 0, 0, 0)),
@@ -448,20 +474,20 @@
             slots * span * page_len,
         ),
         name="page_attention",
-    )(asked, kv_cache)
-    returned = lax.all_to_all(answers, "req", split_axis=0, concat_axis=0, tiled=True)
-
+    )(asked, *keep_in(HBM, kv_cache))
     side = lax.axis_index("grp").astype(jnp.int32).reshape(1)
     grp = lax.axis_size("grp")
     pieces = 2 if grp == 2 and w_down.shape[0] % LANES == 0 else 1
+    returned = lax.all_to_all(answers, "req", split_axis=0, concat_axis=0, tiled=True)
     rows = group_rows // grp
+    near = (VMEM(w_gate_up.shape, BF16), VMEM(w_down.shape, BF16)) if pieces == 2 else ()
     partials = pl.pallas_call(
         functools.partial(
             combine, n=n, cap=cap, reqs=reqs, draft=draft, heads=heads, pieces=pieces
         ),
-        out_shape=(jax.ShapeDtypeStruct((group_rows // pieces, model), BF16),) * pieces,
-        in_specs=[whole(SMEM)] * 2 + [whole()] * 6,
-        out_specs=(whole(),) * pieces,
+        out_shape=(jax.ShapeDtypeStruct((group_rows // pieces, model), BF16),) * pieces + near,
+        in_specs=[whole(SMEM)] * 2 + [whole()] * 6 + [whole(HBM)] * 2,
+        out_specs=(whole(),) * (pieces + len(near)),
         scratch_shapes=[
             pltpu.VMEM((slots, LANES), F32),
             pltpu.VMEM((slots, LANES), F32),
@@ -471,18 +497,20 @@
             pltpu.VMEM((LANES, LANES), F32),
             pltpu.VMEM((reqs * span, HD), F32),
             pltpu.VMEM((group_rows, width), BF16),
+            pltpu.SemaphoreType.DMA((2,)),
         ],
         compiler_params=params(16),
         cost_estimate=cost(
             2 * group_rows * width * model, 2 * n * block * LANES + 8 * reqs * span * HD
         ),
         name="combine",
-    )(codes, side, returned, own, retrieved, own_top, own_sum, w_out)
+    )(codes, side, *keep_in(HBM, returned, own, retrieved), own_top, own_sum, *keep_in(HBM, w_out, w_gate_up, w_down))
 
     if pieces == 2:
         swap = [(0, 1), (1, 0)]
-        own_part, peer_part = partials
+        own_part, peer_part, up_near, down_near = partials
         theirs_peer = lax.ppermute(own_part, "grp", swap)
+        peer_part, theirs_peer = lax.optimization_barrier((peer_part, theirs_peer))
         theirs_own = lax.ppermute(peer_part, "grp", swap)
         units = w_down.shape[0]
 
@@ -496,7 +524,7 @@
                 compiler_params=params(24),
                 cost_estimate=cost(6 * rows * model * units, 6 * model * units),
                 name="feed_forward_own" if own_rows else "feed_forward_peer",
-            )(side, tokens, mine, theirs, norm_ffn.reshape(1, -1), w_gate_up, w_down)
+            )(side, tokens, mine, theirs, norm_ffn.reshape(1, -1), *keep_in(VMEM, up_near, down_near))
 
         sent = forward(peer_part, theirs_peer, False, BF16)
         received = lax.ppermute(sent, "grp", swap)

time: 165 us -> 166 us (level)
  local copies, waits for them, and re-layouts: 31.6 us -> 2.52 us
  Pallas kernels: 57.9 us -> 78.7 us
  waiting for transfers between devices: 46.8 us -> 60.8 us
  matrix products: 4.33 us -> 0 us
    unnamed x67 -> x17, local copies, waits for them, and re-layouts: 30 us -> 1.53 us
    pallas_call x1, Pallas kernels: 8 us -> 15 us  [on_device(): pl.pallas_call(functools.partial(page_attention, cap=cap, draft=draft, he...]
    ppermute x1, waiting for transfers between devices: 5.09 us -> 9.8 us  [on_device(): theirs_own = lax.ppermute(peer_part, 'grp', swap)]
    dot_general x2 -> x0, matrix products: 4.33 us -> none  [the longest x1 2.25 us: on_device(): keys = jnp.dot(normed, w_key, preferred_element_type=F32).astype(BF16)]
    all_to_all x1, waiting for transfers between devices: 15 us -> 19.3 us  [on_device(): lax.all_to_all(answers, 'req', split_axis=0, concat_axis=0, tiled=True)]
    pallas_call x0 -> x1, Pallas kernels: none -> 3.91 us  [on_device(): pl.pallas_call(project_keys, out_shape=(HBM((group_rows, width), BF16),)...]
    pallas_call x1, Pallas kernels: 4.15 us -> 7.88 us  [on_device(): pl.pallas_call(functools.partial(combine, n=n, cap=cap, reqs=reqs, draft=...]
    pallas_call x1, Pallas kernels: 1.03 us -> 3.27 us  [on_device(): pl.pallas_call(functools.partial(project_queries, reqs=reqs, draft=draft,...]
  transfers between devices with their start and end apart: 6 -> 6, of which waited for: 5 -> 6; matrix products, arithmetic and copies ran while one was open for 3% -> 0% of each run, Pallas kernels for 27% -> 32%
where the time goes in v3:
time: 166 us; the launch traced here: 164 us
  Pallas kernels  78.7 us (47%)
  waiting for transfers between devices  60.8 us (37%)
  starting transfers between devices  20 us (12%)
  local copies, waits for them, and re-layouts  2.52 us (2%)
    pallas_call x1, Pallas kernels, on_device(): pl.pallas_call(functools.partial(update_memory, heads=heads, steps=steps)...  22.1 us
    all_to_all x1, waiting for transfers between devices, on_device(): lax.all_to_all(answers, 'req', split_axis=0, concat_axis=0, tiled=True)  19.3 us
    pallas_call x1, Pallas kernels, on_device(): pl.pallas_call(functools.partial(local_attention, heads=heads, draft=draf...  18.2 us
    pallas_call x1, Pallas kernels, on_device(): pl.pallas_call(functools.partial(page_attention, cap=cap, draft=draft, he...  15 us
    ppermute x1, waiting for transfers between devices, on_device(): theirs_peer = lax.ppermute(own_part, 'grp', swap)  13.6 us
    all_to_all x1, waiting for transfers between devices, on_device(): lax.all_to_all(packed, 'req', split_axis=0, concat_axis=0, tiled=True)  10.7 us
    ppermute x1, waiting for transfers between devices, on_device(): theirs_own = lax.ppermute(peer_part, 'grp', swap)  9.8 us
    pallas_call x1, Pallas kernels, on_device(): pl.pallas_call(functools.partial(combine, n=n, cap=cap, reqs=reqs, draft=...  7.88 us
  transfers between devices with their start and end apart: 6, of which 6 were waited for; matrix products, arithmetic and copies ran while one was open for 0% of the time, Pallas kernels for 32%

profile of v3, /device:TPU:14, one launch (start us, length us, event | category | flops | bytes accessed | tf_op | source)
XLA Modules:
  0.0 164.5 jit_solution(7462697081349260784)
XLA Ops:
  0.6 0.0 copy-start.6
  0.6 0.0 copy-start.4
  0.7 0.0 copy-start.5
  0.7 0.7 fusion.1
  1.4 0.7 reshape.33
  2.0 6.2 %all-to-all-start = ((s32[16,1,3]{2,1,0:T(1,128)}), s32[16,1,3]{2,1,0:T(1,128)S(1)}, u32[]{:S(2)}, u32[]{:S(2)}) async-start(s32[16,1,3]{2,1,0:T(1,128)} %bitcast.1), calls=%async_computation | async-start | bytes 16384 | tf_op jit(solution)/shard_map/all_to_all | solution.py:353
  8.3 3.3 %project_queries.1 = (bf16[512,1024]{1,0:T(8,128)(2,1)}, bf16[512,512]{1,0:T(8,128)(2,1)}, bf16[2048,128]{1,0:T(8,128)(2,1)S(1)}) custom-call(bf16[512,1024]{1,0:T(8,128)(2,1)} %tok_ref.5, f32[1,1024]{1,0:T(1,128)} %bitcast.14, bf16[1024,512]{1,0:T(8,128)(2,1)} %w_ref.2), custom_call_target="tpu_custom_call" | custom-call | flops 536870912 | bytes 3145728 | tf_op jit(solution)/shard_map/project_queries/pallas_call | solution.py:355
  11.6 0.7 all-to-all-done.codes
  12.3 2.4 %pack_queries.1 = bf16[6400,128]{1,0:T(8,128)(2,1)} custom-call(s32[16,1,3]{2,1,0:T(1,128)S(1)} %all-to-all-done.codes, s32[16]{0:T(128)} %lengths.1, bf16[2048,128]{1,0:T(8,128)(2,1)S(1)} %get-tuple-element.23.turned_ref), custom_call_target="tpu_custom_call" | custom-call | bytes 3276800 | tf_op jit(solution)/shard_map/pack_queries/pallas_call | solution.py:371
  14.7 0.0 copy-start.2
  14.7 6.1 %all-to-all-start.1 = ((bf16[16,400,128]{2,1,0:T(8,128)(2,1)}), bf16[16,400,128]{2,1,0:T(8,128)(2,1)S(1)}, u32[]{:S(2)}, u32[]{:S(2)}) async-start(bf16[16,400,128]{2,1,0:T(8,128)(2,1)} %bitcast.12), calls=%async_computation.1 | async-start | bytes 3276800 | tf_op jit(solution)/shard_map/all_to_all | solution.py:380
  20.8 0.0 copy-done.6
  20.8 0.1 copy.28
  20.9 0.1 reshape.35.path
  21.0 0.0 copy-done.4
  21.0 0.1 copy.29
  21.1 0.1 reshape.36.mom_code
  21.2 0.0 copy-done.5
  21.2 0.1 copy.30
  21.4 0.1 reshape.37.forget_code
  21.5 3.9 %project_keys.1 = (bf16[512,512]{1,0:T(8,128)(2,1)}, bf16[512,512]{1,0:T(8,128)(2,1)}) custom-call(bf16[512,1024]{1,0:T(8,128)(2,1)} %get-tuple-element.24.normed_ref, bf16[1024,512]{1,0:T(8,128)(2,1)} %wk_ref.1, bf16[1024,512]{1,0:T(8,128)(2,1)} %wv_ref.1), custom_call_target="tpu_custom_call" | custom-call | flops 1073741824 | bytes 3145728 | tf_op jit(solution)/shard_map/project_keys/pallas_call | solution.py:382
  25.4 0.0 copy-done.2
  25.4 22.1 %update_memory.1 = (f32[16,4,128,128]{3,2,1,0:T(8,128)}, f32[16,4,128,128]{3,2,1,0:T(8,128)}) custom-call(s32[128]{0:T(128)S(1)} %reshape.35.path, s32[16]{0:T(128)S(1)} %copy-done.2, s32[512]{0:T(512)S(1)} %reshape.36.mom_code, s32[512]{0:T(512)S(1)} %reshape.37.forget_code, bf16[512,512]{1,0:T(8,128)(2,1)} %get-tuple-element.25.k_ref, ...), custom_call_target="tpu_custom_call" | custom-call | flops 939524096 | bytes 16777216 | tf_op jit(solution)/shard_map/update_memory/pallas_call | solution.py:427
  47.5 10.7 %all-to-all-done.1 = bf16[16,400,128]{2,1,0:T(8,128)(2,1)S(1)} async-done(((bf16[16,400,128]{2,1,0:T(8,128)(2,1)}), bf16[16,400,128]{2,1,0:T(8,128)(2,1)S(1)}, u32[]{:S(2)}, u32[]{:S(2)}) %all-to-all-start.1) | async-done | bytes 1638432 | tf_op jit(solution)/shard_map/all_to_all | solution.py:380
  58.3 15.0 %page_attention.1 = bf16[6400,128]{1,0:T(8,128)(2,1)} custom-call(bf16[6400,128]{1,0:T(8,128)(2,1)S(1)} %bitcast.8, bf16[48,2,128,512]{3,2,1,0:T(8,128)(2,1)} %kv_ref.1), custom_call_target="tpu_custom_call" | custom-call | flops 402653184 | bytes 15859712 | tf_op jit(solution)/shard_map/page_attention/pallas_call | solution.py:459
  73.3 5.0 %all-to-all-start.2 = ((bf16[16,400,128]{2,1,0:T(8,128)(2,1)}), bf16[16,400,128]{2,1,0:T(8,128)(2,1)S(1)}, u32[]{:S(2)}, u32[]{:S(2)}) async-start(bf16[16,400,128]{2,1,0:T(8,128)(2,1)} %bitcast.13), calls=%async_computation.2 | async-start | bytes 3276800 | tf_op jit(solution)/shard_map/all_to_all | solution.py:481
  78.3 18.2 %local_attention.1 = (f32[2048,128]{1,0:T(8,128)}, f32[2048,128]{1,0:T(8,128)}, f32[16,128]{1,0:T(8,128)S(1)}, f32[16,128]{1,0:T(8,128)S(1)}) custom-call(bf16[512,512]{1,0:T(8,128)(2,1)} %get-tuple-element.30.q_ref, bf16[512,512]{1,0:T(8,128)(2,1)} %get-tuple-element.25.k_ref, bf16[512,512]{1,0:T(8,128)(2,1)} %get-tuple-element.26.v_ref, ...), custom_call_target="tpu_custom_call" | custom-call | flops 452984832 | bytes 6291456 | tf_op jit(solution)/shard_map/local_attention/pallas_call | solution.py:398
  96.5 19.3 %all-to-all-done.2 = bf16[16,400,128]{2,1,0:T(8,128)(2,1)S(1)} async-done(((bf16[16,400,128]{2,1,0:T(8,128)(2,1)}), bf16[16,400,128]{2,1,0:T(8,128)(2,1)S(1)}, u32[]{:S(2)}, u32[]{:S(2)}) %all-to-all-start.2) | async-done | bytes 1638432 | tf_op jit(solution)/shard_map/all_to_all | solution.py:481
  115.7 0.0 copy-start.3
  115.7 1.2 copy-done.3
  116.9 0.0 copy-start
  116.9 0.0 copy-start.1
  116.9 7.9 %combine.1 = (bf16[256,1024]{1,0:T(8,128)(2,1)S(1)}, bf16[256,1024]{1,0:T(8,128)(2,1)S(1)}, bf16[2,1024,1408]{2,1,0:T(8,128)(2,1)S(1)}, bf16[1408,1024]{1,0:T(8,128)(2,1)S(1)}) custom-call(s32[16,1,3]{2,1,0:T(1,128)S(1)} %all-to-all-done.codes, s32[1]{0:T(128)} %bitcast.side, bf16[6400,128]{1,0:T(8,128)(2,1)} %bitcast.11, ...), custom_call_target="tpu_custom_call" | custom-call | flops 536870912 | bytes 3735552 | tf_op jit(solution)/shard_map/combine/pallas_call | solution.py:484
  124.8 0.6 collective-permute-start
  125.4 13.6 %collective-permute-done.theirs_ref = bf16[256,1024]{1,0:T(8,128)(2,1)S(1)} collective-permute-done((bf16[256,1024]{1,0:T(8,128)(2,1)S(1)}, bf16[256,1024]{1,0:T(8,128)(2,1)S(1)}, u32[]{:S(2)}, u32[]{:S(2)}) %collective-permute-start) | collective-permute-done | bytes 524320 | tf_op jit(solution)/shard_map/ppermute | solution.py:512
  139.0 0.5 collective-permute-start.1
  139.5 0.0 copy-done
  139.5 0.0 copy-done.1
  139.5 3.0 %feed_forward_peer.1 = bf16[256,1024]{1,0:T(8,128)(2,1)S(1)} custom-call(s32[1]{0:T(128)} %bitcast.side, bf16[512,1024]{1,0:T(8,128)(2,1)S(1)} %copy-done, bf16[256,1024]{1,0:T(8,128)(2,1)S(1)} %get-tuple-element.37.mine_ref, bf16[256,1024]{1,0:T(8,128)(2,1)S(1)} %collective-permute-done.theirs_ref, f32[1,1024]{1,0:T(1,128)S(1)} %bitcast.9, ...), custom_call_target="tpu_custom_call" | custom-call | flops 2214592512 | bytes 8650752 | tf_op jit(solution)/shard_map/feed_forward_peer/pallas_call | solution.py:518
  142.5 1.6 collective-permute-start.2
  144.0 9.8 %collective-permute-done.1.theirs_ref = bf16[256,1024]{1,0:T(8,128)(2,1)S(1)} collective-permute-done((bf16[256,1024]{1,0:T(8,128)(2,1)S(1)}, bf16[256,1024]{1,0:T(8,128)(2,1)S(1)}, u32[]{:S(2)}, u32[]{:S(2)}) %collective-permute-start.1) | collective-permute-done | bytes 524320 | tf_op jit(solution)/shard_map/ppermute | solution.py:514
  153.8 3.0 %feed_forward_own.1 = f32[256,1024]{1,0:T(8,128)S(1)} custom-call(s32[1]{0:T(128)} %bitcast.side, bf16[512,1024]{1,0:T(8,128)(2,1)S(1)} %copy-done, bf16[256,1024]{1,0:T(8,128)(2,1)S(1)} %get-tuple-element.35.mine_ref, bf16[256,1024]{1,0:T(8,128)(2,1)S(1)} %collective-permute-done.1.theirs_ref, f32[1,1024]{1,0:T(1,128)S(1)} %bitcast.10, ...), custom_call_target="tpu_custom_call" | custom-call | flops 2214592512 | bytes 8650752 | tf_op jit(solution)/shard_map/feed_forward_own/pallas_call | solution.py:518
  156.8 6.7 %collective-permute-done.2 = bf16[256,1024]{1,0:T(8,128)(2,1)S(1)} collective-permute-done((bf16[256,1024]{1,0:T(8,128)(2,1)S(1)}, bf16[256,1024]{1,0:T(8,128)(2,1)S(1)}, u32[]{:S(2)}, u32[]{:S(2)}) %collective-permute-start.2) | collective-permute-done | bytes 524320 | tf_op jit(solution)/shard_map/ppermute | solution.py:530
  163.5 0.9 add_convert_fusion
Async XLA Ops:
  0.6 20.2 %copy-start.6 = (s32[16,8]{0,1:T(8,128)S(1)}, s32[16,8]{0,1:T(8,128)}, u32[]{:S(2)}) copy-start(s32[16,8]{0,1:T(8,128)} %param.35) | copy-start | bytes 1540
  0.6 20.3 %copy-start.4 = (s32[16,8,4]{0,2,1:T(4,128)S(1)}, s32[16,8,4]{0,2,1:T(4,128)}, u32[]{:S(2)}) copy-start(s32[16,8,4]{0,2,1:T(4,128)} %param.39) | copy-start | bytes 6148
  0.7 20.6 %copy-start.5 = (s32[16,8,4]{0,2,1:T(4,128)S(1)}, s32[16,8,4]{0,2,1:T(4,128)}, u32[]{:S(2)}) copy-start(s32[16,8,4]{0,2,1:T(4,128)} %param.40) | copy-start | bytes 6148
  2.0 10.3 %all-to-all-start = ((s32[16,1,3]{2,1,0:T(1,128)}), s32[16,1,3]{2,1,0:T(1,128)S(1)}, u32[]{:S(2)}, u32[]{:S(2)}) async-start(s32[16,1,3]{2,1,0:T(1,128)} %bitcast.1), calls=%async_computation | async-start | bytes 16384 | tf_op jit(solution)/shard_map/all_to_all | solution.py:353
  14.7 10.7 %copy-start.2 = (s32[16]{0:T(128)S(1)}, s32[16]{0:T(128)}, u32[]{:S(2)}) copy-start(s32[16]{0:T(128)} %count.1) | copy-start | bytes 196
  14.7 43.5 %all-to-all-start.1 = ((bf16[16,400,128]{2,1,0:T(8,128)(2,1)}), bf16[16,400,128]{2,1,0:T(8,128)(2,1)S(1)}, u32[]{:S(2)}, u32[]{:S(2)}) async-start(bf16[16,400,128]{2,1,0:T(8,128)(2,1)} %bitcast.12), calls=%async_computation.1 | async-start | bytes 3276800 | tf_op jit(solution)/shard_map/all_to_all | solution.py:380
  73.3 42.5 %all-to-all-start.2 = ((bf16[16,400,128]{2,1,0:T(8,128)(2,1)}), bf16[16,400,128]{2,1,0:T(8,128)(2,1)S(1)}, u32[]{:S(2)}, u32[]{:S(2)}) async-start(bf16[16,400,128]{2,1,0:T(8,128)(2,1)} %bitcast.13), calls=%async_computation.2 | async-start | bytes 3276800 | tf_op jit(solution)/shard_map/all_to_all | solution.py:481
  115.7 1.2 copy-start.3
  116.9 22.6 %copy-start = (bf16[512,1024]{1,0:T(8,128)(2,1)S(1)}, bf16[512,1024]{1,0:T(8,128)(2,1)}, u32[]{:S(2)}) copy-start(bf16[512,1024]{1,0:T(8,128)(2,1)} %tok_ref.5) | copy-start | bytes 3145732
  116.9 22.6 %copy-start.1 = (f32[1024]{0:T(1024)S(1)}, f32[1024]{0:T(1024)}, u32[]{:S(2)}) copy-start(f32[1024]{0:T(1024)} %param.41) | copy-start | bytes 12292
  124.8 14.2 %collective-permute-start = (bf16[256,1024]{1,0:T(8,128)(2,1)S(1)}, bf16[256,1024]{1,0:T(8,128)(2,1)S(1)}, u32[]{:S(2)}, u32[]{:S(2)}) collective-permute-start(bf16[256,1024]{1,0:T(8,128)(2,1)S(1)} %get-tuple-element.35.mine_ref), channel_id=1, source_target_pairs={{0,1},{1,0},{2,3},{3,2},{4,5},{5,4},{6,7},{7,6},{8,9},{9,8},{10,11... | collective-permute-start | bytes 1572872 | tf_op jit(solution)/shard_map/ppermute | solution.py:512
  139.0 14.9 %collective-permute-start.1 = (bf16[256,1024]{1,0:T(8,128)(2,1)S(1)}, bf16[256,1024]{1,0:T(8,128)(2,1)S(1)}, u32[]{:S(2)}, u32[]{:S(2)}) collective-permute-start(bf16[256,1024]{1,0:T(8,128)(2,1)S(1)} %get-tuple-element.37.mine_ref), channel_id=1, source_target_pairs={{0,1},{1,0},{2,3},{3,2},{4,5},{5,4},{6,7},{7,6},{8,9},{9,8},{10,11... | collective-permute-start | bytes 1572872 | tf_op jit(solution)/shard_map/ppermute | solution.py:514
  142.5 21.0 %collective-permute-start.2 = (bf16[256,1024]{1,0:T(8,128)(2,1)S(1)}, bf16[256,1024]{1,0:T(8,128)(2,1)S(1)}, u32[]{:S(2)}, u32[]{:S(2)}) collective-permute-start(bf16[256,1024]{1,0:T(8,128)(2,1)S(1)} %feed_forward_peer.1), channel_id=1, source_target_pairs={{0,1},{1,0},{2,3},{3,2},{4,5},{5,4},{6,7},{7,6},{8,9},{9,8},{10,11... | collective-permute-start | bytes 1572872 | tf_op jit(solution)/shard_map/ppermute | solution.py:530

commit v4 on v3

--- a/solution.py
+++ b/solution.py
@@ -107,40 +107,78 @@
     lax.fori_loop(0, n, one, 0)
 
 
-def page_attention(q_ref, kv_ref, out_ref, *, cap, draft, heads, page_len, scale):
+def page_attention(
+    q_ref, kv_hbm, out_hbm, kv_buf, out_buf, in_sems, out_sems,
+    *, n, cap, draft, heads, page_len, scale, group,
+):
     span = heads * draft
-    limits = q_ref[cap * HD : cap * HD + EXTRA, :].astype(F32)
+    ask_block = cap * HD + EXTRA
+    block = cap * span + EXTRA
     token = lax.broadcasted_iota(jnp.int32, (page_len, LANES), 0).astype(F32)
     row_id = lax.broadcasted_iota(jnp.int32, (EXTRA, LANES), 0)
     head_of = lax.broadcasted_iota(jnp.int32, (HD, LANES), 1) // draft
-    tail = jnp.zeros((EXTRA, LANES), F32)
-    all_scores = []
-    for c in range(cap):
-        turned = q_ref[c * HD : (c + 1) * HD, :]
-        blocks = [jnp.where(head_of == h, turned, jnp.zeros_like(turned)) for h in range(heads)]
-        all_scores.append(
-            jnp.dot(kv_ref[c, 0], jnp.concatenate(blocks, axis=0), preferred_element_type=F32)
+
+    def arrival(d):
+        return pltpu.make_async_copy(
+            kv_hbm.at[pl.ds(d * cap, cap)], kv_buf.at[d], in_sems.at[d]
         )
-    all_weights = []
-    for c in range(cap):
-        scores = jnp.where(token < limits[c : c + 1, :], all_scores[c] * scale, NEG)
-        top = jnp.max(scores, axis=0, keepdims=True)
-        weight = jnp.exp(scores - top)
-        total = jnp.sum(weight, axis=0, keepdims=True)
-        all_weights.append(jnp.transpose(weight).astype(BF16))
-        parts = split_parts(top, TOP_PARTS) + split_parts(total, SUM_PARTS)
-        for p, part in enumerate(parts):
-            tail = jnp.where(row_id == p * cap + c, part, tail)
-    for c in range(cap):
-        for h in range(heads):
-            rows = slice(h * draft, (h + 1) * draft)
-            numer = jnp.dot(
-                all_weights[c][rows, :],
-                kv_ref[c, 1, :, h * HD : (h + 1) * HD],
-                preferred_element_type=F32,
+
+    def departure(d):
+        rows = pl.ds(pl.multiple_of(d * block, EXTRA), block)
+        return pltpu.make_async_copy(out_buf.at[rows], out_hbm.at[rows], out_sems.at[d])
+
+    for d in range(n):
+        arrival(d).start()
+
+    def one(i, carry):
+        pairs = [(i * group + g, c) for g in range(group) for c in range(cap)]
+        limits = []
+        for g in range(group):
+            d = i * group + g
+            arrival(d).wait()
+            at = pl.multiple_of(d * ask_block + cap * HD, EXTRA)
+            limits.append(q_ref[pl.ds(at, EXTRA), :].astype(F32))
+        all_scores = []
+        for d, c in pairs:
+            at = pl.multiple_of(d * ask_block + c * HD, EXTRA)
+            turned = q_ref[pl.ds(at, HD), :]
+            blocks = [jnp.where(head_of == h, turned, jnp.zeros_like(turned)) for h in range(heads)]
+            all_scores.append(
+                jnp.dot(
+                    kv_buf[d, c, 0], jnp.concatenate(blocks, axis=0), preferred_element_type=F32
+                )
             )
-            out_ref[c * span + h * draft : c * span + (h + 1) * draft, :] = numer.astype(BF16)
-    out_ref[cap * span : cap * span + EXTRA, :] = tail.astype(BF16)
+        all_weights = []
+        tails = [jnp.zeros((EXTRA, LANES), F32) for _ in range(group)]
+        for j, (d, c) in enumerate(pairs):
+            g = j // cap
+            scores = jnp.where(token < limits[g][c : c + 1, :], all_scores[j] * scale, NEG)
+            top = jnp.max(scores, axis=0, keepdims=True)
+            weight = jnp.exp(scores - top)
+            total = jnp.sum(weight, axis=0, keepdims=True)
+            all_weights.append(jnp.transpose(weight).astype(BF16))
+            parts = split_parts(top, TOP_PARTS) + split_parts(total, SUM_PARTS)
+            for p, part in enumerate(parts):
+                tails[g] = jnp.where(row_id == p * cap + c, part, tails[g])
+        for j, (d, c) in enumerate(pairs):
+            for h in range(heads):
+                numer = jnp.dot(
+                    all_weights[j][h * draft : (h + 1) * draft, :],
+                    kv_buf[d, c, 1, :, h * HD : (h + 1) * HD],
+                    preferred_element_type=F32,
+                )
+                at = pl.multiple_of(d * block + c * span + h * draft, EXTRA)
+                out_buf[pl.ds(at, draft), :] = numer.astype(BF16)
+        for g in range(group):
+            d = i * group + g
+            at = pl.multiple_of(d * block + cap * span, EXTRA)
+            out_buf[pl.ds(at, EXTRA), :] = tails[g].astype(BF16)
+            departure(d).start()
+        return carry
+
+    lax.fori_loop(0, n // group, one, 0)
+    for d in range(n):
+        departure(d).wait()
 
 
 def local_attention(
@@ -216,15 +254,16 @@
 
 
 def combine(
-    codes, side, msg_ref, o_ref, ret_ref, own_top_ref, own_sum_ref, w_ref, up_hbm, down_hbm, *rest,
+    codes, side, msg_ref, o_hbm, ret_hbm, own_top_ref, own_sum_ref, *rest,
     n, cap, reqs, draft, heads, pieces,
 ):
     outs = rest[:pieces]
-    staged = rest[pieces:-9]
-    part_top, part_sum, best, total, weight, own_weight, acc, mixed, sems = rest[-9:]
+    part_top, part_sum, best, total, weight, own_weight, acc, mixed, o_ref, ret_ref, sems = rest[
+        pieces:
+    ]
     copies = [
-        pltpu.make_async_copy(source, target, sems.at[i])
-        for i, (source, target) in enumerate(zip((up_hbm, down_hbm), staged))
+        pltpu.make_async_copy(o_hbm, o_ref, sems.at[0]),
+        pltpu.make_async_copy(ret_hbm, ret_ref, sems.at[1]),
     ]
     for copy in copies:
         copy.start()
@@ -258,6 +297,8 @@
         weight[s : s + 1, :] = weight[s : s + 1, :] * total[pl.ds(owners[s], 1), :]
     turned = jnp.transpose(weight[...])
     own_turned = jnp.transpose(own_weight[...])
+    for copy in copies:
+        copy.wait()
     for r in range(reqs):
         rows = slice(r * span, (r + 1) * span)
         acc[rows, :] = o_ref[rows, :] * own_turned[0:span, r : r + 1] + ret_ref[rows, :]
@@ -276,37 +317,67 @@
     rows = reqs * draft // pieces
     for p, out_ref in enumerate(outs):
         first = lax.rem(side[0] + p, pieces) * rows
-        out_ref[...] = jnp.dot(
-            mixed[pl.ds(pl.multiple_of(first, rows), rows), :],
-            w_ref[...],
-            preferred_element_type=F32,
-        ).astype(BF16)
+        out_ref[...] = mixed[pl.ds(pl.multiple_of(first, rows), rows), :]
+
+
+def run_copies(pairs, sems):
+    copies = [
+        pltpu.make_async_copy(source, target, sems.at[i])
+        for i, (source, target) in enumerate(pairs)
+    ]
+    for copy in copies:
+        copy.start()
+    return copies
+
+
+def stage_weights(
+    side, out_w, gate_up_w, down_w, one_a, one_o, two_a, two_o, out_all, gate_up_all, down_own, sems
+):
+    width = out_w.shape[0] // 2
+    pairs = [(out_w, out_all.at[0]), (gate_up_w, gate_up_all.at[0]), (down_w, down_own)]
+    for half, a, o in ((side[1], one_a, one_o), (1 - side[1], two_a, two_o)):
+        rows = pl.ds(pl.multiple_of(half * width, EXTRA), width)
+        pairs.append((o, out_all.at[1, rows]))
+        pairs.append((a, gate_up_all.at[1, half]))
+    for copy in run_copies(pairs, sems):
+        copy.wait()
+
+
+def feed_up(
+    side, tok_ref, mine_ref, theirs_ref, gain_ref, out_w, gate_up_w, residual_ref, hidden_ref
+):
+    rows = mine_ref.shape[0]
+    units = gate_up_w.shape[3]
+    tokens = tok_ref[pl.ds(pl.multiple_of(side[0] * rows, rows), rows), :].astype(F32)
+    summed = tokens + jnp.dot(mine_ref[...], out_w[0], preferred_element_type=F32)
+    summed = summed + jnp.dot(theirs_ref[...], out_w[1], preferred_element_type=F32)
+    residual_ref[...] = summed.astype(BF16)
+    ffn_in = rms_norm(residual_ref[...], gain_ref[...])
+    step = 256
+    for half in range(2):
+        for first in range(0, units, step):
+            cols = slice(first, min(first + step, units))
+            gate = jnp.dot(ffn_in, gate_up_w[half, 0, :, cols], preferred_element_type=F32)
+            up = jnp.dot(ffn_in, gate_up_w[half, 1, :, cols], preferred_element_type=F32)
+            hidden_ref[half, :, cols] = (gate / (1.0 + jnp.exp(-gate)) * up).astype(BF16)
+
+
+def feed_down(
+    side, residual_ref, hidden_ref, down_own, one_d, two_d, out_ref, down_peer, total, sems
+):
+    depth = one_d.shape[0]
+    pairs = []
+    for half, d in ((side[1], one_d), (1 - side[1], two_d)):
+        pairs.append((d, down_peer.at[pl.ds(pl.multiple_of(half * depth, EXTRA), depth)]))
+    copies = run_copies(pairs, sems)
+    total[...] = residual_ref[...].astype(F32) + jnp.dot(
+        hidden_ref[0], down_own[...], preferred_element_type=F32
+    )
     for copy in copies:
         copy.wait()
-
-
-def feed_forward(
-    side, tok_ref, mine_ref, theirs_ref, gain_ref, up_ref, down_ref, out_ref, hidden, *, own
-):
-    rows = mine_ref.shape[0]
-    units = down_ref.shape[0]
-    at = side[0] if own else 1 - side[0]
-    tokens = tok_ref[pl.ds(pl.multiple_of(at * rows, rows), rows), :].astype(F32)
-    summed = tokens + mine_ref[...].astype(F32) + theirs_ref[...].astype(F32)
-    residual = summed.astype(BF16)
-    ffn_in = rms_norm(residual, gain_ref[...])
-    step = 256
-    for first in range(0, units, step):
-        cols = slice(first, min(first + step, units))
-        gate = jnp.dot(ffn_in, up_ref[0, :, cols], preferred_element_type=F32)
-        up = jnp.dot(ffn_in, up_ref[1, :, cols], preferred_element_type=F32)
-        hidden[:, cols] = (gate / (1.0 + jnp.exp(-gate)) * up).astype(BF16)
-    for first in range(0, out_ref.shape[1], step):
-        cols = slice(first, first + step)
-        part = jnp.dot(hidden[...], down_ref[:, cols], preferred_element_type=F32)
-        if own:
-            part = part + residual[:, cols].astype(F32)
-        out_ref[:, cols] = part.astype(out_ref.dtype)
+    out_ref[...] = (
+        total[...] + jnp.dot(hidden_ref[1], down_peer[...], preferred_element_type=F32)
+    ).astype(BF16)
 
 
 def on_device(
@@ -352,6 +423,19 @@
     label = (slot_page * reqs + lax.rem(slot_request, reqs)).reshape(n, 1, cap)
     codes = lax.all_to_all(label, "req", split_axis=0, concat_axis=0, tiled=True)
 
+    grp = lax.axis_size("grp")
+    pieces = 2 if grp == 2 and w_down.shape[0] % (2 * EXTRA) == 0 and n % 2 == 0 else 1
+    core = lax.rem(lax.axis_index("req"), 2)
+    side = jnp.stack([lax.axis_index("grp"), core]).astype(jnp.int32)
+    if pieces == 2:
+        swap = [(0, 1), (1, 0)]
+        half_down, half_out = w_down.shape[0] // 2, width // 2
+        one_a = lax.ppermute(
+            lax.dynamic_index_in_dim(w_gate_up, core, 0, keepdims=False), "grp", swap
+        )
+        out_half = lax.dynamic_slice_in_dim(w_out, core * half_out, half_out, 0)
+        down_half = lax.dynamic_slice_in_dim(w_down, core * half_down, half_down, 0)
+
     normed, queries, turned = pl.pallas_call(
         functools.partial(project_queries, reqs=reqs, draft=draft, heads=heads),
         out_shape=(
@@ -458,16 +542,19 @@
     )
     answers = pl.pallas_call(
         functools.partial(
-            page_attention, cap=cap, draft=draft, heads=heads, page_len=page_len, scale=scale
-        ),
-        grid=(n,),
+            page_attention, n=n, cap=cap, draft=draft, heads=heads, page_len=page_len,
+            scale=scale, group=2,
+        ),
         out_shape=HBM((n * block, LANES), BF16),
-        in_specs=[
-            pl.BlockSpec((ask_block, LANES), lambda d: (d, 0)),
-            pl.BlockSpec((cap, 2, page_len, width), lambda d: (d, 0, 0, 0)),
+        in_specs=[whole(), whole(HBM)],
+        out_specs=whole(HBM),
+        scratch_shapes=[
+            pltpu.VMEM((n, cap) + kv_cache.shape[1:], BF16),
+            pltpu.VMEM((n * block, LANES), BF16),
+            pltpu.SemaphoreType.DMA((n,)),
+            pltpu.SemaphoreType.DMA((n,)),
         ],
-        out_specs=pl.BlockSpec((block, LANES), lambda d: (d, 0)),
-        compiler_params=params(12),
+        compiler_params=params(24),
         cost_estimate=cost(
             4 * slots * span * page_len * HD,
             4 * slots * page_len * width + 4 * n * block * LANES,
@@ -475,19 +562,29 @@
         ),
         name="page_attention",
     )(asked, *keep_in(HBM, kv_cache))
-    side = lax.axis_index("grp").astype(jnp.int32).reshape(1)
-    grp = lax.axis_size("grp")
-    pieces = 2 if grp == 2 and w_down.shape[0] % LANES == 0 else 1
+    if pieces == 2:
+        down_half, out_half, one_a, _ = lax.optimization_barrier(
+            (down_half, out_half, one_a, answers)
+        )
     returned = lax.all_to_all(answers, "req", split_axis=0, concat_axis=0, tiled=True)
+    if pieces == 2:
+        cores = [(i, i ^ 1) for i in range(n)]
+        one_d = lax.ppermute(down_half, "grp", swap)
+        one_o = lax.ppermute(out_half, "grp", swap)
+        two_a = lax.ppermute(one_a, "req", cores)
+        returned, one_d, one_o, two_a, own, retrieved, own_top, own_sum = lax.optimization_barrier(
+            (returned, one_d, one_o, two_a, own, retrieved, own_top, own_sum)
+        )
+        two_o = lax.ppermute(one_o, "req", cores)
+        two_d = lax.ppermute(one_d, "req", cores)
     rows = group_rows // grp
-    near = (VMEM(w_gate_up.shape, BF16), VMEM(w_down.shape, BF16)) if pieces == 2 else ()
-    partials = pl.pallas_call(
+    mixed = pl.pallas_call(
         functools.partial(
             combine, n=n, cap=cap, reqs=reqs, draft=draft, heads=heads, pieces=pieces
         ),
-        out_shape=(jax.ShapeDtypeStruct((group_rows // pieces, model), BF16),) * pieces + near,
-        in_specs=[whole(SMEM)] * 2 + [whole()] * 6 + [whole(HBM)] * 2,
-        out_specs=(whole(),) * (pieces + len(near)),
+        out_shape=(jax.ShapeDtypeStruct((group_rows // pieces, width), BF16),) * pieces,
+        in_specs=[whole(SMEM)] * 2 + [whole()] + [whole(HBM)] * 2 + [whole()] * 2,
+        out_specs=(whole(),) * pieces,
         scratch_shapes=[
             pltpu.VMEM((slots, LANES), F32),
             pltpu.VMEM((slots, LANES), F32),
@@ -497,42 +594,70 @@
             pltpu.VMEM((LANES, LANES), F32),
             pltpu.VMEM((reqs * span, HD), F32),
             pltpu.VMEM((group_rows, width), BF16),
+            pltpu.VMEM((reqs * span, HD), F32),
+            pltpu.VMEM((reqs * span, HD), F32),
             pltpu.SemaphoreType.DMA((2,)),
         ],
-        compiler_params=params(16),
+        compiler_params=params(12),
         cost_estimate=cost(
-            2 * group_rows * width * model, 2 * n * block * LANES + 8 * reqs * span * HD
+            8 * slots * span * HD, 2 * n * block * LANES + 8 * reqs * span * HD
         ),
         name="combine",
-    )(codes, side, *keep_in(HBM, returned, own, retrieved), own_top, own_sum, *keep_in(HBM, w_out, w_gate_up, w_down))
+    )(codes, side, returned, *keep_in(HBM, own, retrieved), own_top, own_sum)
 
     if pieces == 2:
-        swap = [(0, 1), (1, 0)]
-        own_part, peer_part, up_near, down_near = partials
-        theirs_peer = lax.ppermute(own_part, "grp", swap)
-        peer_part, theirs_peer = lax.optimization_barrier((peer_part, theirs_peer))
-        theirs_own = lax.ppermute(peer_part, "grp", swap)
+        mine, asked_for = mixed
+        theirs = lax.ppermute(asked_for, "grp", swap)
+        mine, one_a, one_o, two_a, two_o = lax.optimization_barrier(
+            (mine, one_a, one_o, two_a, two_o)
+        )
         units = w_down.shape[0]
-
-        def forward(mine, theirs, own_rows, dtype):
-            return pl.pallas_call(
-                functools.partial(feed_forward, own=own_rows),
-                out_shape=jax.ShapeDtypeStruct((rows, model), dtype),
-                in_specs=[whole(SMEM)] + [whole()] * 6,
-                out_specs=whole(),
-                scratch_shapes=[pltpu.VMEM((rows, units), BF16)],
-                compiler_params=params(24),
-                cost_estimate=cost(6 * rows * model * units, 6 * model * units),
-                name="feed_forward_own" if own_rows else "feed_forward_peer",
-            )(side, tokens, mine, theirs, norm_ffn.reshape(1, -1), *keep_in(VMEM, up_near, down_near))
-
-        sent = forward(peer_part, theirs_peer, False, BF16)
-        received = lax.ppermute(sent, "grp", swap)
-        base = forward(own_part, theirs_own, True, F32)
-        layer_out = (base + received.astype(F32)).astype(BF16)
+        out_near, gate_up_near, down_near = pl.pallas_call(
+            stage_weights,
+            out_shape=(
+                VMEM((2,) + w_out.shape, BF16),
+                VMEM((2,) + w_gate_up.shape, BF16),
+                VMEM(w_down.shape, BF16),
+            ),
+            in_specs=[whole(SMEM)] + [whole(HBM)] * 3 + [whole(pl.ANY)] * 4,
+            out_specs=(whole(),) * 3,
+            scratch_shapes=[pltpu.SemaphoreType.DMA((7,))],
+            compiler_params=params(2),
+            cost_estimate=cost(0, 2 * model * (2 * width + 5 * units)),
+            name="stage_weights",
+        )(side, *keep_in(HBM, w_out, w_gate_up, w_down), one_a, one_o, two_a, two_o)
+        residual, hidden = pl.pallas_call(
+            feed_up,
+            out_shape=(VMEM((rows, model), BF16), VMEM((2, rows, units), BF16)),
+            in_specs=[whole(SMEM)] + [whole()] * 6,
+            out_specs=(whole(),) * 2,
+            compiler_params=params(12),
+            cost_estimate=cost(
+                4 * rows * model * (width + 2 * units), 4 * model * (width + 2 * units)
+            ),
+            name="feed_up",
+        )(
+            side, tokens, mine, theirs, norm_ffn.reshape(1, -1),
+            *keep_in(VMEM, out_near, gate_up_near),
+        )
+        layer_out = pl.pallas_call(
+            feed_down,
+            out_shape=jax.ShapeDtypeStruct((rows, model), BF16),
+            in_specs=[whole(SMEM)] + [whole()] * 3 + [whole(pl.ANY)] * 2,
+            out_specs=whole(),
+            scratch_shapes=[
+                pltpu.VMEM(w_down.shape, BF16),
+                pltpu.VMEM((rows, model), F32),
+                pltpu.SemaphoreType.DMA((2,)),
+            ],
+            compiler_params=params(12),
+            cost_estimate=cost(4 * rows * model * units, 4 * model * units),
+            name="feed_down",
+        )(side, *keep_in(VMEM, residual, hidden, down_near), one_d, two_d)
         return (layer_out, memory_out, momentum_out)
 
-    head_sum = lax.psum_scatter(partials[0], "grp", scatter_dimension=0, tiled=True).astype(F32)
+    partial_out = jnp.dot(mixed[0], w_out, preferred_element_type=F32).astype(BF16)
+    head_sum = lax.psum_scatter(partial_out, "grp", scatter_dimension=0, tiled=True).astype(F32)
     own_rows = lax.dynamic_slice_in_dim(tokens, lax.axis_index("grp") * rows, rows, 0)
     residual = (own_rows.astype(F32) + head_sum).astype(BF16)
     ffn_in = rms_norm(residual, norm_ffn)

time: 166 us -> 161 us (0.970)
  the two profiles are of different devices: /device:TPU:14 before, /device:TPU:0 now
where the time goes in v4:
time: 161 us; the launch traced here: 160 us
  Pallas kernels  76.9 us (48%)
  waiting for transfers between devices  45.9 us (29%)
  starting transfers between devices  25.9 us (16%)
  local copies, waits for them, and re-layouts  9.81 us (6%)
    ppermute x1, waiting for transfers between devices, on_device(): one_o = lax.ppermute(out_half, 'grp', swap)  25 us
    pallas_call x1, Pallas kernels, on_device(): pl.pallas_call(functools.partial(update_memory, heads=heads, steps=steps)...  23.5 us
    pallas_call x1, Pallas kernels, on_device(): pl.pallas_call(functools.partial(local_attention, heads=heads, draft=draf...  18.2 us
    ppermute x1, waiting for transfers between devices, on_device(): lax.ppermute(lax.dynamic_index_in_dim(w_gate_up, core, 0, keepdims=False)...  16.5 us
    all_to_all x1, starting transfers between devices, on_device(): lax.all_to_all(answers, 'req', split_axis=0, concat_axis=0, tiled=True)  9.27 us
    all_to_all x1, starting transfers between devices, on_device(): lax.all_to_all(label, 'req', split_axis=0, concat_axis=0, tiled=True)  7.39 us
    pallas_call x1, Pallas kernels, on_device(): pl.pallas_call(functools.partial(page_attention, n=n, cap=cap, draft=draf...  7.19 us
    pallas_call x1, Pallas kernels, on_device(): pl.pallas_call(stage_weights, out_shape=(VMEM((2,) + w_out.shape, BF16),...  5.37 us
  transfers between devices with their start and end apart: 10, of which 4 were waited for; matrix products, arithmetic and copies ran while one was open for 4% of the time, Pallas kernels for 44%

profile of v4, /device:TPU:0, one launch (start us, length us, event | category | flops | bytes accessed | tf_op | source)
XLA Modules:
  0.0 160.3 jit_solution(14357009615800858862)
XLA Ops:
  0.6 0.7 fusion.1
  1.3 0.7 reshape.28
  2.0 7.4 %all-to-all-start = ((s32[16,1,3]{2,1,0:T(1,128)}), s32[16,1,3]{2,1,0:T(1,128)S(1)}, u32[]{:S(2)}, u32[]{:S(2)}) async-start(s32[16,1,3]{2,1,0:T(1,128)} %bitcast.2), calls=%async_computation | async-start | bytes 16384 | tf_op jit(solution)/shard_map/all_to_all | solution.py:424
  9.4 3.3 %project_queries.1 = (bf16[512,1024]{1,0:T(8,128)(2,1)}, bf16[512,512]{1,0:T(8,128)(2,1)}, bf16[2048,128]{1,0:T(8,128)(2,1)S(1)}) custom-call(bf16[512,1024]{1,0:T(8,128)(2,1)} %tok_ref.3, f32[1,1024]{1,0:T(1,128)} %bitcast.16, bf16[1024,512]{1,0:T(8,128)(2,1)} %w_ref.1), custom_call_target="tpu_custom_call" | custom-call | flops 536870912 | bytes 3145728 | tf_op jit(solution)/shard_map/project_queries/pallas_call | solution.py:439
  12.7 3.1 %all-to-all-done.codes = s32[16,1,3]{2,1,0:T(1,128)S(1)} async-done(((s32[16,1,3]{2,1,0:T(1,128)}), s32[16,1,3]{2,1,0:T(1,128)S(1)}, u32[]{:S(2)}, u32[]{:S(2)}) %all-to-all-start) | async-done | bytes 224 | tf_op jit(solution)/shard_map/all_to_all | solution.py:424
  15.7 2.4 %pack_queries.1 = bf16[6400,128]{1,0:T(8,128)(2,1)} custom-call(s32[16,1,3]{2,1,0:T(1,128)S(1)} %all-to-all-done.codes, s32[16]{0:T(128)} %lengths.1, bf16[2048,128]{1,0:T(8,128)(2,1)S(1)} %get-tuple-element.40.turned_ref), custom_call_target="tpu_custom_call" | custom-call | bytes 3276800 | tf_op jit(solution)/shard_map/pack_queries/pallas_call | solution.py:455
  18.1 3.7 %all-to-all-start.1 = ((bf16[16,400,128]{2,1,0:T(8,128)(2,1)}), bf16[16,400,128]{2,1,0:T(8,128)(2,1)S(1)}, u32[]{:S(2)}, u32[]{:S(2)}) async-start(bf16[16,400,128]{2,1,0:T(8,128)(2,1)} %bitcast.14), calls=%async_computation.1 | async-start | bytes 3276800 | tf_op jit(solution)/shard_map/all_to_all | solution.py:464
  21.9 0.0 copy-start.11
  21.9 0.0 copy-start.9
  21.9 0.0 copy-start.10
  21.9 3.6 %dynamic-slice_bitcast_fusion = bf16[1024,1408]{1,0:T(8,128)(2,1)} fusion(bf16[2,1024,1408]{2,1,0:T(8,128)(2,1)} %gate_up_w.1, s32[]{:T(128)S(6)} %select_n.12), kind=kLoop, calls=%fused_computation | loop fusion | bytes 5767172 | tf_op jit(solution)/shard_map/jit(dynamic_index_in_dim)/squeeze | solution.py:434
  25.6 1.5 collective-permute-start
  27.0 0.1 copy.28
  27.1 0.1 reshape.30.path
  27.2 0.1 copy.29
  27.3 0.1 reshape.31.mom_code
  27.5 0.1 copy.30
  27.6 0.1 reshape.32.forget_code
  27.7 3.9 %project_keys.1 = (bf16[512,512]{1,0:T(8,128)(2,1)}, bf16[512,512]{1,0:T(8,128)(2,1)}) custom-call(bf16[512,1024]{1,0:T(8,128)(2,1)} %get-tuple-element.41.normed_ref, bf16[1024,512]{1,0:T(8,128)(2,1)} %wk_ref.1, bf16[1024,512]{1,0:T(8,128)(2,1)} %wv_ref.1), custom_call_target="tpu_custom_call" | custom-call | flops 1073741824 | bytes 3145728 | tf_op jit(solution)/shard_map/project_keys/pallas_call | solution.py:466
  31.6 23.5 %update_memory.1 = (f32[16,4,128,128]{3,2,1,0:T(8,128)}, f32[16,4,128,128]{3,2,1,0:T(8,128)}) custom-call(s32[128]{0:T(128)S(1)} %reshape.30.path, s32[16]{0:T(128)S(1)} %copy-done.6, s32[512]{0:T(512)S(1)} %reshape.31.mom_code, s32[512]{0:T(512)S(1)} %reshape.32.forget_code, bf16[512,512]{1,0:T(8,128)(2,1)} %get-tuple-element.42.k_ref, ...), custom_call_target="tpu_custom_call" | custom-call | flops 939524096 | bytes 16777216 | tf_op jit(solution)/shard_map/update_memory/pallas_call | solution.py:511
  55.1 0.0 all-to-all-done.1
  55.1 7.2 %page_attention.1 = bf16[6400,128]{1,0:T(8,128)(2,1)} custom-call(bf16[6400,128]{1,0:T(8,128)(2,1)S(1)} %bitcast.12, bf16[48,2,128,512]{3,2,1,0:T(8,128)(2,1)} %kv_hbm.1), custom_call_target="tpu_custom_call" | custom-call | flops 402653184 | bytes 15859712 | tf_op jit(solution)/shard_map/page_attention/pallas_call | solution.py:543
  62.3 0.0 copy-start.7
  62.4 9.3 %all-to-all-start.2 = ((bf16[16,400,128]{2,1,0:T(8,128)(2,1)}), bf16[16,400,128]{2,1,0:T(8,128)(2,1)S(1)}, u32[]{:S(2)}, u32[]{:S(2)}) async-start(bf16[16,400,128]{2,1,0:T(8,128)(2,1)} %bitcast.15), calls=%async_computation.2 | async-start | bytes 3276800 | tf_op jit(solution)/shard_map/all_to_all | solution.py:569
  71.6 0.9 constant_dynamic-slice_fusion
  72.5 1.5 constant_dynamic-slice_fusion.1
  74.0 16.5 %collective-permute-done.one_a = bf16[1024,1408]{1,0:T(8,128)(2,1)} collective-permute-done((bf16[1024,1408]{1,0:T(8,128)(2,1)}, bf16[1024,1408]{1,0:T(8,128)(2,1)}, u32[]{:S(2)}, u32[]{:S(2)}) %collective-permute-start) | collective-permute-done | bytes 2883616 | tf_op jit(solution)/shard_map/ppermute | solution.py:433
  90.5 0.0 collective-permute-start.3
  90.5 1.5 collective-permute-start.1
  92.0 0.5 collective-permute-start.2
  92.6 18.2 %local_attention.1 = (f32[2048,128]{1,0:T(8,128)}, f32[2048,128]{1,0:T(8,128)}, f32[16,128]{1,0:T(8,128)S(1)}, f32[16,128]{1,0:T(8,128)S(1)}) custom-call(bf16[512,512]{1,0:T(8,128)(2,1)} %get-tuple-element.50.q_ref, bf16[512,512]{1,0:T(8,128)(2,1)} %get-tuple-element.42.k_ref, bf16[512,512]{1,0:T(8,128)(2,1)} %get-tuple-element.43.v_ref, ...), custom_call_target="tpu_custom_call" | custom-call | flops 452984832 | bytes 6291456 | tf_op jit(solution)/shard_map/local_attention/pallas_call | solution.py:482
  110.7 25.0 %collective-permute-done.2.one_o = bf16[256,1024]{1,0:T(8,128)(2,1)S(1)} collective-permute-done((bf16[256,1024]{1,0:T(8,128)(2,1)S(1)}, bf16[256,1024]{1,0:T(8,128)(2,1)S(1)}, u32[]{:S(2)}, u32[]{:S(2)}) %collective-permute-start.2) | collective-permute-done | bytes 524320 | tf_op jit(solution)/shard_map/ppermute | solution.py:573
  135.8 0.0 collective-permute-done.1.one_d
  135.8 0.8 copy-done.3
  136.6 1.6 copy-done.1
  138.2 0.0 all-to-all-done.2
  138.2 0.0 collective-permute-start.6
  138.2 0.5 collective-permute-start.4
  138.7 0.1 pad_add_fusion.side
  138.8 4.1 %combine.1 = (bf16[256,512]{1,0:T(8,128)(2,1)S(1)}, bf16[256,512]{1,0:T(8,128)(2,1)S(1)}) custom-call(s32[16,1,3]{2,1,0:T(1,128)S(1)} %all-to-all-done.codes, s32[2]{0:T(128)S(1)} %pad_add_fusion.side, bf16[6400,128]{1,0:T(8,128)(2,1)S(1)} %bitcast.11, f32[2048,128]{1,0:T(8,128)} %get-tuple-element.56.o_hbm, f32[2048,128]{1,0:T(8,128)} %get-tuple-element.57.ret_hbm, ...), custom_call_target="tpu_custom_call" | custom-call | flops 6291456 | bytes 3735552 | tf_op jit(solution)/shard_map/combine/pallas_call | solution.py:581
  142.9 1.6 collective-permute-start.5
  144.5 0.0 collective-permute-done.4.two_o
  144.5 0.0 copy-start
  144.5 0.0 copy-start.5
  144.5 5.4 %stage_weights.1 = (bf16[2,512,1024]{2,1,0:T(8,128)(2,1)S(1)}, bf16[2,2,1024,1408]{3,2,1,0:T(8,128)(2,1)S(1)}, bf16[1408,1024]{1,0:T(8,128)(2,1)S(1)}) custom-call(s32[2]{0:T(128)S(1)} %pad_add_fusion.side, bf16[512,1024]{1,0:T(8,128)(2,1)} %out_w.1, bf16[2,1024,1408]{2,1,0:T(8,128)(2,1)} %gate_up_w.1, bf16[1408,1024]{1,0:T(8,128)(2,1)} %down_w.1, ...), custom_call_target="tpu_custom_call" | custom-call | bytes 16515072 | tf_op jit(solution)/shard_map/stage_weights/pallas_call | solution.py:615
  149.9 1.3 collective-permute-done.5.theirs_ref
  151.2 4.9 %feed_up.1 = (bf16[256,1024]{1,0:T(8,128)(2,1)S(1)}, bf16[2,256,1408]{2,1,0:T(8,128)(2,1)S(1)}) custom-call(s32[2]{0:T(128)S(1)} %pad_add_fusion.side, bf16[512,1024]{1,0:T(8,128)(2,1)S(1)} %copy-done, bf16[256,512]{1,0:T(8,128)(2,1)S(1)} %get-tuple-element.63.mine_ref, bf16[256,512]{1,0:T(8,128)(2,1)S(1)} %collective-permute-done.5.theirs_ref, ...), custom_call_target="tpu_custom_call" | custom-call | flops 3489660928 | bytes 13631488 | tf_op jit(solution)/shard_map/feed_up/pallas_call | solution.py:629
  156.0 4.1 %feed_down.1 = bf16[256,1024]{1,0:T(8,128)(2,1)} custom-call(s32[2]{0:T(128)S(1)} %pad_add_fusion.side, bf16[256,1024]{1,0:T(8,128)(2,1)S(1)} %get-tuple-element.71.residual_ref, bf16[2,256,1408]{2,1,0:T(8,128)(2,1)S(1)} %get-tuple-element.72.hidden_ref, bf16[1408,1024]{1,0:T(8,128)(2,1)S(1)} %get-tuple-element.73.down_own, ...), custom_call_target="tpu_custom_call" | custom-call | flops 1476395008 | bytes 5767168 | tf_op jit(solution)/shard_map/feed_down/pallas_call | solution.py:643
  (18 shorter events, 0.0 us)
Async XLA Ops:
  2.0 13.7 %all-to-all-start = ((s32[16,1,3]{2,1,0:T(1,128)}), s32[16,1,3]{2,1,0:T(1,128)S(1)}, u32[]{:S(2)}, u32[]{:S(2)}) async-start(s32[16,1,3]{2,1,0:T(1,128)} %bitcast.2), calls=%async_computation | async-start | bytes 16384 | tf_op jit(solution)/shard_map/all_to_all | solution.py:424
  18.1 37.0 %all-to-all-start.1 = ((bf16[16,400,128]{2,1,0:T(8,128)(2,1)}), bf16[16,400,128]{2,1,0:T(8,128)(2,1)S(1)}, u32[]{:S(2)}, u32[]{:S(2)}) async-start(bf16[16,400,128]{2,1,0:T(8,128)(2,1)} %bitcast.14), calls=%async_computation.1 | async-start | bytes 3276800 | tf_op jit(solution)/shard_map/all_to_all | solution.py:464
  21.9 5.2 %copy-start.11 = (s32[16,8]{0,1:T(8,128)S(1)}, s32[16,8]{0,1:T(8,128)}, u32[]{:S(2)}) copy-start(s32[16,8]{0,1:T(8,128)} %param.35) | copy-start | bytes 1540
  21.9 5.3 %copy-start.9 = (s32[16,8,4]{0,2,1:T(4,128)S(1)}, s32[16,8,4]{0,2,1:T(4,128)}, u32[]{:S(2)}) copy-start(s32[16,8,4]{0,2,1:T(4,128)} %param.39) | copy-start | bytes 6148
  21.9 5.6 %copy-start.10 = (s32[16,8,4]{0,2,1:T(4,128)S(1)}, s32[16,8,4]{0,2,1:T(4,128)}, u32[]{:S(2)}) copy-start(s32[16,8,4]{0,2,1:T(4,128)} %param.40) | copy-start | bytes 6148
  25.5 6.1 %copy-start.6 = (s32[16]{0:T(128)S(1)}, s32[16]{0:T(128)}, u32[]{:S(2)}) copy-start(s32[16]{0:T(128)} %count.1) | copy-start | bytes 196
  25.6 65.0 %collective-permute-start = (bf16[1024,1408]{1,0:T(8,128)(2,1)}, bf16[1024,1408]{1,0:T(8,128)(2,1)}, u32[]{:S(2)}, u32[]{:S(2)}) collective-permute-start(bf16[1024,1408]{1,0:T(8,128)(2,1)} %dynamic-slice_bitcast_fusion), channel_id=1, source_target_pairs={{0,1},{1,0},{2,3},{3,2},{4,5},{5,4},{6,7},{7,6},{8,9},{9,8},{10,11... | collective-permute-start | bytes 8650760 | tf_op jit(solution)/shard_map/ppermute | solution.py:433
  62.3 9.3 %copy-start.7 = (bf16[512,1024]{1,0:T(8,128)(2,1)S(1)}, bf16[512,1024]{1,0:T(8,128)(2,1)}, u32[]{:S(2)}) copy-start(bf16[512,1024]{1,0:T(8,128)(2,1)} %out_w.1) | copy-start | bytes 3145732
  62.4 75.8 %all-to-all-start.2 = ((bf16[16,400,128]{2,1,0:T(8,128)(2,1)}), bf16[16,400,128]{2,1,0:T(8,128)(2,1)S(1)}, u32[]{:S(2)}, u32[]{:S(2)}) async-start(bf16[16,400,128]{2,1,0:T(8,128)(2,1)} %bitcast.15), calls=%async_computation.2 | async-start | bytes 3276800 | tf_op jit(solution)/shard_map/all_to_all | solution.py:569
  72.5 19.5 %copy-start.8 = (bf16[256,1024]{1,0:T(8,128)(2,1)S(1)}, bf16[256,1024]{1,0:T(8,128)(2,1)}, u32[]{:S(2)}) copy-start(bf16[256,1024]{1,0:T(8,128)(2,1)} %constant_dynamic-slice_fusion) | copy-start | bytes 1572868
  90.5 46.0 %collective-permute-start.3 = (bf16[1024,1408]{1,0:T(8,128)(2,1)}, bf16[1024,1408]{1,0:T(8,128)(2,1)S(1)}, u32[]{:S(2)}, u32[]{:S(2)}) collective-permute-start(bf16[1024,1408]{1,0:T(8,128)(2,1)} %collective-permute-done.one_a), channel_id=1, source_target_pairs={{0,2},{2,0},{4,6},{6,4},{8,10},{10,8},{12,14},{14,12},{16,18},{18,... | collective-permute-start | bytes 8650760 | tf_op jit(solution)/shard_map/ppermute | solution.py:574
  90.5 45.2 %collective-permute-start.1 = (bf16[704,1024]{1,0:T(8,128)(2,1)S(1)}, bf16[704,1024]{1,0:T(8,128)(2,1)S(1)}, u32[]{:S(2)}, u32[]{:S(2)}) collective-permute-start(bf16[704,1024]{1,0:T(8,128)(2,1)S(1)} %constant_dynamic-slice_fusion.1), channel_id=1, source_target_pairs={{0,1},{1,0},{2,3},{3,2},{4,5},{5,4},{6,7},{7,6},{8,9},{9,8},{10,11... | collective-permute-start | bytes 4325384 | tf_op jit(solution)/shard_map/ppermute | solution.py:572
  92.0 43.7 %collective-permute-start.2 = (bf16[256,1024]{1,0:T(8,128)(2,1)S(1)}, bf16[256,1024]{1,0:T(8,128)(2,1)S(1)}, u32[]{:S(2)}, u32[]{:S(2)}) collective-permute-start(bf16[256,1024]{1,0:T(8,128)(2,1)S(1)} %copy-done.8), channel_id=1, source_target_pairs={{0,1},{1,0},{2,3},{3,2},{4,5},{5,4},{6,7},{7,6},{8,9},{9,8},{10,11... | collective-permute-start | bytes 1572872 | tf_op jit(solution)/shard_map/ppermute | solution.py:573
  135.8 0.8 copy-start.3
  136.6 1.6 %copy-start.1 = (bf16[1024,1408]{1,0:T(8,128)(2,1)}, bf16[1024,1408]{1,0:T(8,128)(2,1)S(1)}, u32[]{:S(2)}) copy-start(bf16[1024,1408]{1,0:T(8,128)(2,1)S(1)} %collective-permute-done.3.two_a) | copy-start | bytes 8650756
  138.2 17.9 %collective-permute-start.6 = (bf16[704,1024]{1,0:T(8,128)(2,1)S(1)}, bf16[704,1024]{1,0:T(8,128)(2,1)}, u32[]{:S(2)}, u32[]{:S(2)}) collective-permute-start(bf16[704,1024]{1,0:T(8,128)(2,1)S(1)} %collective-permute-done.1.one_d), channel_id=1, source_target_pairs={{0,2},{2,0},{4,6},{6,4},{8,10},{10,8},{12,14},{14,12},{16,18},{18,... | collective-permute-start | bytes 4325384 | tf_op jit(solution)/shard_map/ppermute | solution.py:579
  138.2 6.3 %collective-permute-start.4 = (bf16[256,1024]{1,0:T(8,128)(2,1)}, bf16[256,1024]{1,0:T(8,128)(2,1)}, u32[]{:S(2)}, u32[]{:S(2)}) collective-permute-start(bf16[256,1024]{1,0:T(8,128)(2,1)} %copy-done.3), channel_id=1, source_target_pairs={{0,2},{2,0},{4,6},{6,4},{8,10},{10,8},{12,14},{14,12},{16,18},{18,... | collective-permute-start | bytes 1572872 | tf_op jit(solution)/shard_map/ppermute | solution.py:578
  138.7 5.8 %copy-start.2 = (bf16[1024,1408]{1,0:T(8,128)(2,1)S(1)}, bf16[1024,1408]{1,0:T(8,128)(2,1)}, u32[]{:S(2)}) copy-start(bf16[1024,1408]{1,0:T(8,128)(2,1)} %copy-done.1) | copy-start | bytes 8650756
  138.7 5.8 %copy-start.4 = (bf16[256,1024]{1,0:T(8,128)(2,1)S(1)}, bf16[256,1024]{1,0:T(8,128)(2,1)}, u32[]{:S(2)}) copy-start(bf16[256,1024]{1,0:T(8,128)(2,1)} %copy-done.3) | copy-start | bytes 1572868
  142.9 8.2 %collective-permute-start.5 = (bf16[256,512]{1,0:T(8,128)(2,1)S(1)}, bf16[256,512]{1,0:T(8,128)(2,1)S(1)}, u32[]{:S(2)}, u32[]{:S(2)}) collective-permute-start(bf16[256,512]{1,0:T(8,128)(2,1)S(1)} %get-tuple-element.64), channel_id=1, source_target_pairs={{0,1},{1,0},{2,3},{3,2},{4,5},{5,4},{6,7},{7,6},{8,9},{9,8},{10,11... | collective-permute-start | bytes 786440 | tf_op jit(solution)/shard_map/ppermute | solution.py:610
  144.5 6.7 %copy-start = (bf16[512,1024]{1,0:T(8,128)(2,1)S(1)}, bf16[512,1024]{1,0:T(8,128)(2,1)}, u32[]{:S(2)}) copy-start(bf16[512,1024]{1,0:T(8,128)(2,1)} %tok_ref.3) | copy-start | bytes 3145732
  144.5 6.7 %copy-start.5 = (f32[1024]{0:T(1024)S(1)}, f32[1024]{0:T(1024)}, u32[]{:S(2)}) copy-start(f32[1024]{0:T(1024)} %param.41) | copy-start | bytes 12292

commit v5 on v4

--- a/solution.py
+++ b/solution.py
@@ -330,15 +330,46 @@
     return copies
 
 
+def cut_weights(side, gate_up_w, down_w, out_w, first_ref, last_ref, quarter_ref, sems, *, first):
+    last = gate_up_w.shape[1] - first
+    depth, width = down_w.shape[0] // 4, out_w.shape[0] // 4
+    half = gate_up_w.at[side[1]]
+    pairs = [
+        (half.at[pl.ds(0, first)], first_ref),
+        (half.at[pl.ds(first, last)], last_ref),
+        (
+            down_w.at[pl.ds(pl.multiple_of(side[2] * depth, EXTRA), depth)],
+            quarter_ref.at[pl.ds(0, depth)],
+        ),
+        (
+            out_w.at[pl.ds(pl.multiple_of(side[2] * width, EXTRA), width)],
+            quarter_ref.at[pl.ds(depth, width)],
+        ),
+    ]
+    for copy in run_copies(pairs, sems):
+        copy.wait()
+
+
 def stage_weights(
-    side, out_w, gate_up_w, down_w, one_a, one_o, two_a, two_o, out_all, gate_up_all, down_own, sems
+    side, out_w, gate_up_w, down_w, one_a, one_b, one_q, two_a, two_b, two_q, three_q, four_q,
+    out_all, gate_up_all, down_all, sems,
 ):
-    width = out_w.shape[0] // 2
-    pairs = [(out_w, out_all.at[0]), (gate_up_w, gate_up_all.at[0]), (down_w, down_own)]
-    for half, a, o in ((side[1], one_a, one_o), (1 - side[1], two_a, two_o)):
-        rows = pl.ds(pl.multiple_of(half * width, EXTRA), width)
-        pairs.append((o, out_all.at[1, rows]))
-        pairs.append((a, gate_up_all.at[1, half]))
+    width, depth = out_w.shape[0] // 4, down_w.shape[0] // 4
+    first, last = one_a.shape[0], one_b.shape[0]
+    pairs = [(gate_up_w, gate_up_all.at[0]), (down_w, down_all.at[0]), (out_w, out_all.at[0])]
+    for half, a, b in ((side[1], one_a, one_b), (1 - side[1], two_a, two_b)):
+        target = gate_up_all.at[1, half]
+        pairs.append((a, target.at[pl.ds(0, first)]))
+        pairs.append((b, target.at[pl.ds(first, last)]))
+    core, chip = side[1], side[2] // 2
+    for x, y, q in ((core, chip, one_q), (1 - core, chip, two_q), (core, 1 - chip, three_q), (
+        1 - core, 1 - chip, four_q,
+    )):
+        part = 2 * y + x
+        units = pl.ds(pl.multiple_of(part * depth, EXTRA), depth)
+        rows = pl.ds(pl.multiple_of(part * width, EXTRA), width)
+        pairs.append((q.at[pl.ds(0, depth)], down_all.at[1, units]))
+        pairs.append((q.at[pl.ds(depth, width)], out_all.at[1, rows]))
     for copy in run_copies(pairs, sems):
         copy.wait()
 
@@ -362,22 +393,16 @@
             hidden_ref[half, :, cols] = (gate / (1.0 + jnp.exp(-gate)) * up).astype(BF16)
 
 
-def feed_down(
-    side, residual_ref, hidden_ref, down_own, one_d, two_d, out_ref, down_peer, total, sems
-):
-    depth = one_d.shape[0]
-    pairs = []
-    for half, d in ((side[1], one_d), (1 - side[1], two_d)):
-        pairs.append((d, down_peer.at[pl.ds(pl.multiple_of(half * depth, EXTRA), depth)]))
-    copies = run_copies(pairs, sems)
-    total[...] = residual_ref[...].astype(F32) + jnp.dot(
-        hidden_ref[0], down_own[...], preferred_element_type=F32
-    )
-    for copy in copies:
-        copy.wait()
-    out_ref[...] = (
-        total[...] + jnp.dot(hidden_ref[1], down_peer[...], preferred_element_type=F32)
-    ).astype(BF16)
+def feed_down(residual_ref, hidden_ref, down_w, out_ref):
+    step = 256
+    for at in range(0, out_ref.shape[1], step):
+        cols = slice(at, at + step)
+        total = residual_ref[:, cols].astype(F32)
+        for half in range(2):
+            total = total + jnp.dot(
+                hidden_ref[half], down_w[half, :, cols], preferred_element_type=F32
+            )
+        out_ref[:, cols] = total.astype(BF16)
 
 
 def on_device(
@@ -424,17 +449,28 @@
     codes = lax.all_to_all(label, "req", split_axis=0, concat_axis=0, tiled=True)
 
     grp = lax.axis_size("grp")
-    pieces = 2 if grp == 2 and w_down.shape[0] % (2 * EXTRA) == 0 and n % 2 == 0 else 1
-    core = lax.rem(lax.axis_index("req"), 2)
-    side = jnp.stack([lax.axis_index("grp"), core]).astype(jnp.int32)
+    depth, out_depth = w_down.shape[0] // 4, width // 4
+    first = model * 10 // 32
+    split = (depth, out_depth, first)
+    pieces = 2 if grp == 2 and n % 4 == 0 and not any(size % EXTRA for size in split) else 1
+    quarter = lax.rem(lax.axis_index("req"), 4)
+    core = lax.rem(quarter, 2)
+    side = jnp.stack([lax.axis_index("grp"), core, quarter]).astype(jnp.int32)
     if pieces == 2:
-        swap = [(0, 1), (1, 0)]
-        half_down, half_out = w_down.shape[0] // 2, width // 2
-        one_a = lax.ppermute(
-            lax.dynamic_index_in_dim(w_gate_up, core, 0, keepdims=False), "grp", swap
-        )
-        out_half = lax.dynamic_slice_in_dim(w_out, core * half_out, half_out, 0)
-        down_half = lax.dynamic_slice_in_dim(w_down, core * half_down, half_down, 0)
+        half_first, half_last, quarters = pl.pallas_call(
+            functools.partial(cut_weights, first=first),
+            out_shape=(
+                HBM((first, w_down.shape[0]), BF16),
+                HBM((model - first, w_down.shape[0]), BF16),
+                HBM((depth + out_depth, model), BF16),
+            ),
+            in_specs=[whole(SMEM)] + [whole(HBM)] * 3,
+            out_specs=(whole(HBM),) * 3,
+            scratch_shapes=[pltpu.SemaphoreType.DMA((4,))],
+            compiler_params=params(2),
+            cost_estimate=cost(0, 4 * model * (w_down.shape[0] + depth + out_depth)),
+            name="cut_weights",
+        )(side, *keep_in(HBM, w_gate_up, w_down, w_out))
 
     normed, queries, turned = pl.pallas_call(
         functools.partial(project_queries, reqs=reqs, draft=draft, heads=heads),
@@ -451,6 +487,14 @@
         ),
         name="project_queries",
     )(*keep_in(HBM, tokens, norm_attn.reshape(1, -1), w_query))
+
+    if pieces == 2:
+        turned, half_first, half_last, quarters = lax.optimization_barrier(
+            (turned, half_first, half_last, quarters)
+        )
+        swap = [(0, 1), (1, 0)]
+        one_a = lax.ppermute(half_first, "grp", swap)
+        one_q = lax.ppermute(quarters, "grp", swap)
 
     packed = pl.pallas_call(
         functools.partial(pack_queries, n=n, cap=cap, reqs=reqs, page_len=page_len),
@@ -563,20 +607,24 @@
         name="page_attention",
     )(asked, *keep_in(HBM, kv_cache))
     if pieces == 2:
-        down_half, out_half, one_a, _ = lax.optimization_barrier(
-            (down_half, out_half, one_a, answers)
+        answers, half_last, one_a, one_q = lax.optimization_barrier(
+            (answers, half_last, one_a, one_q)
         )
     returned = lax.all_to_all(answers, "req", split_axis=0, concat_axis=0, tiled=True)
     if pieces == 2:
-        cores = [(i, i ^ 1) for i in range(n)]
-        one_d = lax.ppermute(down_half, "grp", swap)
-        one_o = lax.ppermute(out_half, "grp", swap)
-        two_a = lax.ppermute(one_a, "req", cores)
-        returned, one_d, one_o, two_a, own, retrieved, own_top, own_sum = lax.optimization_barrier(
-            (returned, one_d, one_o, two_a, own, retrieved, own_top, own_sum)
-        )
-        two_o = lax.ppermute(one_o, "req", cores)
-        two_d = lax.ppermute(one_d, "req", cores)
+        other_core = [(i, i ^ 1) for i in range(n)]
+        other_chip = [(i, i ^ 2) for i in range(n)]
+        one_b = lax.ppermute(half_last, "grp", swap)
+        three_q = lax.ppermute(one_q, "req", other_chip)
+        two_a = lax.ppermute(one_a, "req", other_core)
+        two_q = lax.ppermute(one_q, "req", other_core)
+        returned, one_b, two_a, two_q, three_q, own, retrieved, own_top, own_sum = (
+            lax.optimization_barrier(
+                (returned, one_b, two_a, two_q, three_q, own, retrieved, own_top, own_sum)
+            )
+        )
+        two_b = lax.ppermute(one_b, "req", other_core)
+        four_q = lax.ppermute(three_q, "req", other_core)
     rows = group_rows // grp
     mixed = pl.pallas_call(
         functools.partial(
@@ -608,8 +656,8 @@
     if pieces == 2:
         mine, asked_for = mixed
         theirs = lax.ppermute(asked_for, "grp", swap)
-        mine, one_a, one_o, two_a, two_o = lax.optimization_barrier(
-            (mine, one_a, one_o, two_a, two_o)
+        mine, two_a, two_b, two_q, four_q = lax.optimization_barrier(
+            (mine, two_a, two_b, two_q, four_q)
         )
         units = w_down.shape[0]
         out_near, gate_up_near, down_near = pl.pallas_call(
@@ -617,15 +665,21 @@
             out_shape=(
                 VMEM((2,) + w_out.shape, BF16),
                 VMEM((2,) + w_gate_up.shape, BF16),
-                VMEM(w_down.shape, BF16),
+                VMEM((2,) + w_down.shape, BF16),
             ),
-            in_specs=[whole(SMEM)] + [whole(HBM)] * 3 + [whole(pl.ANY)] * 4,
+            in_specs=[whole(SMEM)] + [whole(pl.ANY)] * 11,
             out_specs=(whole(),) * 3,
-            scratch_shapes=[pltpu.SemaphoreType.DMA((7,))],
+            scratch_shapes=[pltpu.SemaphoreType.DMA((15,))],
             compiler_params=params(2),
-            cost_estimate=cost(0, 2 * model * (2 * width + 5 * units)),
+            cost_estimate=cost(0, 2 * model * (2 * width + 6 * units)),
             name="stage_weights",
-        )(side, *keep_in(HBM, w_out, w_gate_up, w_down), one_a, one_o, two_a, two_o)
+        )(
+            side,
+            *keep_in(HBM, w_out, w_gate_up, w_down, one_a, one_b, one_q, two_a),
+            two_b,
+            *keep_in(HBM, two_q, three_q),
+            four_q,
+        )
         residual, hidden = pl.pallas_call(
             feed_up,
             out_shape=(VMEM((rows, model), BF16), VMEM((2, rows, units), BF16)),
@@ -643,17 +697,12 @@
         layer_out = pl.pallas_call(
             feed_down,
             out_shape=jax.ShapeDtypeStruct((rows, model), BF16),
-            in_specs=[whole(SMEM)] + [whole()] * 3 + [whole(pl.ANY)] * 2,
+            in_specs=[whole()] * 3,
             out_specs=whole(),
-            scratch_shapes=[
-                pltpu.VMEM(w_down.shape, BF16),
-                pltpu.VMEM((rows, model), F32),
-                pltpu.SemaphoreType.DMA((2,)),
-            ],
-            compiler_params=params(12),
+            compiler_params=params(6),
             cost_estimate=cost(4 * rows * model * units, 4 * model * units),
             name="feed_down",
-        )(side, *keep_in(VMEM, residual, hidden, down_near), one_d, two_d)
+        )(*keep_in(VMEM, residual, hidden, down_near))
         return (layer_out, memory_out, momentum_out)
 
     partial_out = jnp.dot(mixed[0], w_out, preferred_element_type=F32).astype(BF16)

time: 161 us -> 257 us (1.60)
  Pallas kernels: 76.9 us -> 195 us
  waiting for transfers between devices: 45.9 us -> 24.6 us
    pallas_call x0 -> x1, Pallas kernels: none -> 119 us  [on_device(): pl.pallas_call(functools.partial(cut_weights, first=first), out_shape=(HB...]
    ppermute x6 -> x8, waiting for transfers between devices: 41.5 us -> 24.2 us  [the longest x1 19.6 us: on_device(): three_q = lax.ppermute(one_q, 'req', other_chip)]
    squeeze x1 -> x0, local copies, waits for them, and re-layouts: 3.64 us -> none  [on_device(): lax.dynamic_index_in_dim(w_gate_up, core, 0, keepdims=False)]
    all_to_all x1, starting transfers between devices: 9.27 us -> 6.08 us  [on_device(): lax.all_to_all(answers, 'req', split_axis=0, concat_axis=0, tiled=True)]
    all_to_all x1, waiting for transfers between devices: 3.05 us -> 0.01 us  [on_device(): lax.all_to_all(label, 'req', split_axis=0, concat_axis=0, tiled=True)]
    ppermute x6 -> x8, starting transfers between devices: 4.03 us -> 6.58 us  [the longest x1 1.91 us: on_device(): three_q = lax.ppermute(one_q, 'req', other_chip)]
  transfers between devices with their start and end apart: 10 -> 12, of which waited for: 4 -> 4; matrix products, arithmetic and copies ran while one was open for 4% -> 2% of each run, Pallas kernels for 44% -> 72%
where the time goes in v5:
time: 257 us; the launch traced here: 256 us
  Pallas kernels  195 us (76%)
  starting transfers between devices  27.6 us (11%)
  waiting for transfers between devices  24.6 us (10%)
  local copies, waits for them, and re-layouts  7.61 us (3%)
    pallas_call x1, Pallas kernels, on_device(): pl.pallas_call(functools.partial(cut_weights, first=first), out_shape=(HB...  119 us
    pallas_call x1, Pallas kernels, on_device(): pl.pallas_call(functools.partial(update_memory, heads=heads, steps=steps)...  23 us
    ppermute x1, waiting for transfers between devices, on_device(): three_q = lax.ppermute(one_q, 'req', other_chip)  19.6 us
    pallas_call x1, Pallas kernels, on_device(): pl.pallas_call(functools.partial(local_attention, heads=heads, draft=draf...  18.2 us
    all_to_all x1, starting transfers between devices, on_device(): lax.all_to_all(label, 'req', split_axis=0, concat_axis=0, tiled=True)  7.39 us
    pallas_call x1, Pallas kernels, on_device(): pl.pallas_call(functools.partial(page_attention, n=n, cap=cap, draft=draf...  7.22 us
    pallas_call x1, Pallas kernels, on_device(): pl.pallas_call(stage_weights, out_shape=(VMEM((2,) + w_out.shape, BF16),...  6.34 us
    all_to_all x1, starting transfers between devices, on_device(): lax.all_to_all(answers, 'req', split_axis=0, concat_axis=0, tiled=True)  6.08 us
  transfers between devices with their start and end apart: 12, of which 4 were waited for; matrix products, arithmetic and copies ran while one was open for 2% of the time, Pallas kernels for 72%

profile of v5, /device:TPU:0, one launch (start us, length us, event | category | flops | bytes accessed | tf_op | source)
XLA Modules:
  0.0 256.1 jit_solution(3708970222296805512)
XLA Ops:
  0.6 0.7 fusion.1
  1.3 0.7 reshape.28
  2.0 7.4 %all-to-all-start = ((s32[16,1,3]{2,1,0:T(1,128)}), s32[16,1,3]{2,1,0:T(1,128)S(1)}, u32[]{:S(2)}, u32[]{:S(2)}) async-start(s32[16,1,3]{2,1,0:T(1,128)} %bitcast.3), calls=%async_computation | async-start | bytes 16384 | tf_op jit(solution)/shard_map/all_to_all | solution.py:449
  9.4 0.1 pad_add_fusion.side
  9.5 3.3 %project_queries.1 = (bf16[512,1024]{1,0:T(8,128)(2,1)}, bf16[512,512]{1,0:T(8,128)(2,1)}, bf16[2048,128]{1,0:T(8,128)(2,1)S(1)}) custom-call(bf16[512,1024]{1,0:T(8,128)(2,1)} %tok_ref.3, f32[1,1024]{1,0:T(1,128)} %bitcast.15, bf16[1024,512]{1,0:T(8,128)(2,1)} %w_ref.1), custom_call_target="tpu_custom_call" | custom-call | flops 536870912 | bytes 3145728 | tf_op jit(solution)/shard_map/project_queries/pallas_call | solution.py:475
  12.8 118.8 %cut_weights.1 = (bf16[320,1408]{1,0:T(8,128)(2,1)}, bf16[704,1408]{1,0:T(8,128)(2,1)}, bf16[480,1024]{1,0:T(8,128)(2,1)}) custom-call(s32[3]{0:T(128)S(1)} %pad_add_fusion.side, bf16[2,1024,1408]{2,1,0:T(8,128)(2,1)} %gate_up_w.3, bf16[1408,1024]{1,0:T(8,128)(2,1)} %down_w.3, bf16[512,1024]{1,0:T(8,128)(2,1)} %out_w.3), custom_call_target="tpu_custom_call" | custom-call | bytes 7733248 | tf_op jit(solution)/shard_map/cut_weights/pallas_call | solution.py:460
  131.6 0.0 copy-start.8
  131.6 0.0 all-to-all-done.codes
  131.6 2.4 pack_queries.1
  134.0 6.0 %all-to-all-start.1 = ((bf16[16,400,128]{2,1,0:T(8,128)(2,1)}), bf16[16,400,128]{2,1,0:T(8,128)(2,1)S(1)}, u32[]{:S(2)}, u32[]{:S(2)}) async-start(bf16[16,400,128]{2,1,0:T(8,128)(2,1)} %bitcast.13), calls=%async_computation.1 | async-start | bytes 3276800 | tf_op jit(solution)/shard_map/all_to_all | solution.py:508
  140.0 0.0 copy-start.2
  140.0 1.6 collective-permute-start.1
  141.6 0.5 collective-permute-start
  142.1 0.1 copy.28
  142.2 0.1 reshape.30.path
  142.3 1.5 copy.29
  143.7 0.9 reshape.31.mom_code
  144.7 1.5 copy.30
  146.2 0.9 reshape.32.forget_code
  147.1 3.9 %project_keys.1 = (bf16[512,512]{1,0:T(8,128)(2,1)}, bf16[512,512]{1,0:T(8,128)(2,1)}) custom-call(bf16[512,1024]{1,0:T(8,128)(2,1)} %get-tuple-element.54.normed_ref, bf16[1024,512]{1,0:T(8,128)(2,1)} %wk_ref.1, bf16[1024,512]{1,0:T(8,128)(2,1)} %wv_ref.1), custom_call_target="tpu_custom_call" | custom-call | flops 1073741824 | bytes 3145728 | tf_op jit(solution)/shard_map/project_keys/pallas_call | solution.py:510
  151.0 23.0 %update_memory.1 = (f32[16,4,128,128]{3,2,1,0:T(8,128)}, f32[16,4,128,128]{3,2,1,0:T(8,128)}) custom-call(s32[128]{0:T(128)S(1)} %reshape.30.path, s32[16]{0:T(128)S(1)} %copy-done.2, s32[512]{0:T(512)S(1)} %reshape.31.mom_code, s32[512]{0:T(512)S(1)} %reshape.32.forget_code, bf16[512,512]{1,0:T(8,128)(2,1)} %get-tuple-element.55.k_ref, ...), custom_call_target="tpu_custom_call" | custom-call | flops 939524096 | bytes 16777216 | tf_op jit(solution)/shard_map/update_memory/pallas_call | solution.py:555
  174.0 0.0 all-to-all-done.1
  174.1 7.2 %page_attention.1 = bf16[6400,128]{1,0:T(8,128)(2,1)} custom-call(bf16[6400,128]{1,0:T(8,128)(2,1)S(1)} %bitcast.11, bf16[48,2,128,512]{3,2,1,0:T(8,128)(2,1)} %kv_hbm.1), custom_call_target="tpu_custom_call" | custom-call | flops 402653184 | bytes 15859712 | tf_op jit(solution)/shard_map/page_attention/pallas_call | solution.py:587
  181.3 2.4 collective-permute-done.one_a
  183.7 0.0 collective-permute-done.1.one_q
  183.7 6.1 %all-to-all-start.2 = ((bf16[16,400,128]{2,1,0:T(8,128)(2,1)}), bf16[16,400,128]{2,1,0:T(8,128)(2,1)S(1)}, u32[]{:S(2)}, u32[]{:S(2)}) async-start(bf16[16,400,128]{2,1,0:T(8,128)(2,1)} %bitcast.14), calls=%async_computation.2 | async-start | bytes 3276800 | tf_op jit(solution)/shard_map/all_to_all | solution.py:613
  189.8 1.6 collective-permute-start.2
  191.3 1.9 collective-permute-start.5
  193.3 0.0 collective-permute-start.4
  193.3 0.5 collective-permute-start.3
  193.8 18.2 %local_attention.1 = (f32[2048,128]{1,0:T(8,128)}, f32[2048,128]{1,0:T(8,128)}, f32[16,128]{1,0:T(8,128)S(1)}, f32[16,128]{1,0:T(8,128)S(1)}) custom-call(bf16[512,512]{1,0:T(8,128)(2,1)} %get-tuple-element.67.q_ref, bf16[512,512]{1,0:T(8,128)(2,1)} %get-tuple-element.55.k_ref, bf16[512,512]{1,0:T(8,128)(2,1)} %get-tuple-element.56.v_ref, ...), custom_call_target="tpu_custom_call" | custom-call | flops 452984832 | bytes 6291456 | tf_op jit(solution)/shard_map/local_attention/pallas_call | solution.py:526
  211.9 0.0 collective-permute-done.3.two_a
  212.0 19.6 %collective-permute-done.5.three_q = bf16[480,1024]{1,0:T(8,128)(2,1)S(1)} collective-permute-done((bf16[480,1024]{1,0:T(8,128)(2,1)S(1)}, bf16[480,1024]{1,0:T(8,128)(2,1)S(1)}, u32[]{:S(2)}, u32[]{:S(2)}) %collective-permute-start.5) | collective-permute-done | bytes 983072 | tf_op jit(solution)/shard_map/ppermute | solution.py:618
  231.5 0.0 collective-permute-done.4.two_q
  231.5 1.0 copy-done.4
  232.5 1.0 copy-done.5
  233.5 2.2 collective-permute-done.2.one_b
  235.7 0.0 all-to-all-done.2
  235.7 0.0 collective-permute-start.6
  235.7 0.5 collective-permute-start.7
  236.2 4.1 %combine.1 = (bf16[256,512]{1,0:T(8,128)(2,1)S(1)}, bf16[256,512]{1,0:T(8,128)(2,1)S(1)}) custom-call(s32[16,1,3]{2,1,0:T(1,128)S(1)} %all-to-all-done.codes, s32[3]{0:T(128)S(1)} %pad_add_fusion.side, bf16[6400,128]{1,0:T(8,128)(2,1)S(1)} %bitcast.10, f32[2048,128]{1,0:T(8,128)} %get-tuple-element.73.o_hbm, f32[2048,128]{1,0:T(8,128)} %get-tuple-element.74.ret_hbm, ...), custom_call_target="tpu_custom_call" | custom-call | flops 6291456 | bytes 3735552 | tf_op jit(solution)/shard_map/combine/pallas_call | solution.py:629
  240.3 1.6 collective-permute-start.8
  241.9 0.0 collective-permute-done.7.four_q
  241.9 0.0 copy-start.1
  241.9 6.3 %stage_weights.1 = (bf16[2,512,1024]{2,1,0:T(8,128)(2,1)S(1)}, bf16[2,2,1024,1408]{3,2,1,0:T(8,128)(2,1)S(1)}, bf16[2,1408,1024]{2,1,0:T(8,128)(2,1)S(1)}) custom-call(s32[3]{0:T(128)S(1)} %pad_add_fusion.side, bf16[512,1024]{1,0:T(8,128)(2,1)} %out_w.3, bf16[2,1024,1408]{2,1,0:T(8,128)(2,1)} %gate_up_w.3, bf16[1408,1024]{1,0:T(8,128)(2,1)} %down_w.3, ...), custom_call_target="tpu_custom_call" | custom-call | bytes 19398656 | tf_op jit(solution)/shard_map/stage_weights/pallas_call | solution.py:663
  248.2 0.4 collective-permute-done.8.theirs_ref
  248.6 4.9 %feed_up.1 = (bf16[256,1024]{1,0:T(8,128)(2,1)S(1)}, bf16[2,256,1408]{2,1,0:T(8,128)(2,1)S(1)}) custom-call(s32[3]{0:T(128)S(1)} %pad_add_fusion.side, bf16[512,1024]{1,0:T(8,128)(2,1)S(1)} %copy-done, bf16[256,512]{1,0:T(8,128)(2,1)S(1)} %get-tuple-element.82.mine_ref, bf16[256,512]{1,0:T(8,128)(2,1)S(1)} %collective-permute-done.8.theirs_ref, ...), custom_call_target="tpu_custom_call" | custom-call | flops 3489660928 | bytes 13631488 | tf_op jit(solution)/shard_map/feed_up/pallas_call | solution.py:683
  253.5 2.6 %feed_down.1 = bf16[256,1024]{1,0:T(8,128)(2,1)} custom-call(bf16[256,1024]{1,0:T(8,128)(2,1)S(1)} %get-tuple-element.90.residual_ref, bf16[2,256,1408]{2,1,0:T(8,128)(2,1)S(1)} %get-tuple-element.91.hidden_ref, bf16[2,1408,1024]{2,1,0:T(8,128)(2,1)S(1)} %get-tuple-element.92.down_w), custom_call_target="tpu_custom_call" | custom-call | flops 1476395008 | bytes 5767168 | tf_op jit(solution)/shard_map/feed_down/pallas_call | solution.py:697
  (14 shorter events, 0.0 us)
Async XLA Ops:
  2.0 129.6 %all-to-all-start = ((s32[16,1,3]{2,1,0:T(1,128)}), s32[16,1,3]{2,1,0:T(1,128)S(1)}, u32[]{:S(2)}, u32[]{:S(2)}) async-start(s32[16,1,3]{2,1,0:T(1,128)} %bitcast.3), calls=%async_computation | async-start | bytes 16384 | tf_op jit(solution)/shard_map/all_to_all | solution.py:449
  131.6 10.5 %copy-start.8 = (s32[16,8]{0,1:T(8,128)S(1)}, s32[16,8]{0,1:T(8,128)}, u32[]{:S(2)}) copy-start(s32[16,8]{0,1:T(8,128)} %param.35) | copy-start | bytes 1540
  134.0 40.0 %all-to-all-start.1 = ((bf16[16,400,128]{2,1,0:T(8,128)(2,1)}), bf16[16,400,128]{2,1,0:T(8,128)(2,1)S(1)}, u32[]{:S(2)}, u32[]{:S(2)}) async-start(bf16[16,400,128]{2,1,0:T(8,128)(2,1)} %bitcast.13), calls=%async_computation.1 | async-start | bytes 3276800 | tf_op jit(solution)/shard_map/all_to_all | solution.py:508
  140.0 11.0 %copy-start.2 = (s32[16]{0:T(128)S(1)}, s32[16]{0:T(128)}, u32[]{:S(2)}) copy-start(s32[16]{0:T(128)} %count.1) | copy-start | bytes 196
  140.0 43.7 %collective-permute-start.1 = (bf16[480,1024]{1,0:T(8,128)(2,1)}, bf16[480,1024]{1,0:T(8,128)(2,1)S(1)}, u32[]{:S(2)}, u32[]{:S(2)}) collective-permute-start(bf16[480,1024]{1,0:T(8,128)(2,1)} %get-tuple-element.62), channel_id=1, source_target_pairs={{0,1},{1,0},{2,3},{3,2},{4,5},{5,4},{6,7},{7,6},{8,9},{9,8},{10,11... | collective-permute-start | bytes 2949128 | tf_op jit(solution)/shard_map/ppermute | solution.py:497
  141.6 42.1 %collective-permute-start = (bf16[320,1408]{1,0:T(8,128)(2,1)}, bf16[320,1408]{1,0:T(8,128)(2,1)S(1)}, u32[]{:S(2)}, u32[]{:S(2)}) collective-permute-start(bf16[320,1408]{1,0:T(8,128)(2,1)} %get-tuple-element.61), channel_id=1, source_target_pairs={{0,1},{1,0},{2,3},{3,2},{4,5},{5,4},{6,7},{7,6},{8,9},{9,8},{10,11... | collective-permute-start | bytes 2703368 | tf_op jit(solution)/shard_map/ppermute | solution.py:496
  183.7 28.2 %copy-start.6 = (bf16[320,1408]{1,0:T(8,128)(2,1)}, bf16[320,1408]{1,0:T(8,128)(2,1)S(1)}, u32[]{:S(2)}) copy-start(bf16[320,1408]{1,0:T(8,128)(2,1)S(1)} %collective-permute-done.one_a) | copy-start | bytes 2703364
  183.7 28.2 %copy-start.3 = (bf16[480,1024]{1,0:T(8,128)(2,1)}, bf16[480,1024]{1,0:T(8,128)(2,1)S(1)}, u32[]{:S(2)}) copy-start(bf16[480,1024]{1,0:T(8,128)(2,1)S(1)} %collective-permute-done.1.one_q) | copy-start | bytes 2949124
  183.7 52.0 %all-to-all-start.2 = ((bf16[16,400,128]{2,1,0:T(8,128)(2,1)}), bf16[16,400,128]{2,1,0:T(8,128)(2,1)S(1)}, u32[]{:S(2)}, u32[]{:S(2)}) async-start(bf16[16,400,128]{2,1,0:T(8,128)(2,1)} %bitcast.14), calls=%async_computation.2 | async-start | bytes 3276800 | tf_op jit(solution)/shard_map/all_to_all | solution.py:613
  189.8 45.9 %collective-permute-start.2 = (bf16[704,1408]{1,0:T(8,128)(2,1)}, bf16[704,1408]{1,0:T(8,128)(2,1)}, u32[]{:S(2)}, u32[]{:S(2)}) collective-permute-start(bf16[704,1408]{1,0:T(8,128)(2,1)} %get-tuple-element.64), channel_id=1, source_target_pairs={{0,1},{1,0},{2,3},{3,2},{4,5},{5,4},{6,7},{7,6},{8,9},{9,8},{10,11... | collective-permute-start | bytes 5947400 | tf_op jit(solution)/shard_map/ppermute | solution.py:617
  191.3 40.2 %collective-permute-start.5 = (bf16[480,1024]{1,0:T(8,128)(2,1)S(1)}, bf16[480,1024]{1,0:T(8,128)(2,1)S(1)}, u32[]{:S(2)}, u32[]{:S(2)}) collective-permute-start(bf16[480,1024]{1,0:T(8,128)(2,1)S(1)} %collective-permute-done.1.one_q), channel_id=1, source_target_pairs={{0,4},{2,6},{4,0},{6,2},{8,12},{10,14},{12,8},{14,10},{16,20},{18,... | collective-permute-start | bytes 2949128 | tf_op jit(solution)/shard_map/ppermute | solution.py:618
  193.3 38.3 %collective-permute-start.4 = (bf16[480,1024]{1,0:T(8,128)(2,1)S(1)}, bf16[480,1024]{1,0:T(8,128)(2,1)S(1)}, u32[]{:S(2)}, u32[]{:S(2)}) collective-permute-start(bf16[480,1024]{1,0:T(8,128)(2,1)S(1)} %collective-permute-done.1.one_q), channel_id=1, source_target_pairs={{0,2},{2,0},{4,6},{6,4},{8,10},{10,8},{12,14},{14,12},{16,18},{18,... | collective-permute-start | bytes 2949128 | tf_op jit(solution)/shard_map/ppermute | solution.py:620
  193.3 18.7 %collective-permute-start.3 = (bf16[320,1408]{1,0:T(8,128)(2,1)S(1)}, bf16[320,1408]{1,0:T(8,128)(2,1)S(1)}, u32[]{:S(2)}, u32[]{:S(2)}) collective-permute-start(bf16[320,1408]{1,0:T(8,128)(2,1)S(1)} %collective-permute-done.one_a), channel_id=1, source_target_pairs={{0,2},{2,0},{4,6},{6,4},{8,10},{10,8},{12,14},{14,12},{16,18},{18,... | collective-permute-start | bytes 2703368 | tf_op jit(solution)/shard_map/ppermute | solution.py:619
  212.0 19.6 %copy-start.7 = (bf16[320,1408]{1,0:T(8,128)(2,1)}, bf16[320,1408]{1,0:T(8,128)(2,1)S(1)}, u32[]{:S(2)}) copy-start(bf16[320,1408]{1,0:T(8,128)(2,1)S(1)} %collective-permute-done.3.two_a) | copy-start | bytes 2703364
  231.5 1.0 copy-start.4
  232.5 1.0 copy-start.5
  235.7 6.2 %collective-permute-start.6 = (bf16[704,1408]{1,0:T(8,128)(2,1)}, bf16[704,1408]{1,0:T(8,128)(2,1)S(1)}, u32[]{:S(2)}, u32[]{:S(2)}) collective-permute-start(bf16[704,1408]{1,0:T(8,128)(2,1)} %collective-permute-done.2.one_b), channel_id=1, source_target_pairs={{0,2},{2,0},{4,6},{6,4},{8,10},{10,8},{12,14},{14,12},{16,18},{18,... | collective-permute-start | bytes 5947400 | tf_op jit(solution)/shard_map/ppermute | solution.py:626
  235.7 6.2 %collective-permute-start.7 = (bf16[480,1024]{1,0:T(8,128)(2,1)}, bf16[480,1024]{1,0:T(8,128)(2,1)S(1)}, u32[]{:S(2)}, u32[]{:S(2)}) collective-permute-start(bf16[480,1024]{1,0:T(8,128)(2,1)} %copy-done.4), channel_id=1, source_target_pairs={{0,2},{2,0},{4,6},{6,4},{8,10},{10,8},{12,14},{14,12},{16,18},{18,... | collective-permute-start | bytes 2949128 | tf_op jit(solution)/shard_map/ppermute | solution.py:627
  240.3 8.3 %collective-permute-start.8 = (bf16[256,512]{1,0:T(8,128)(2,1)S(1)}, bf16[256,512]{1,0:T(8,128)(2,1)S(1)}, u32[]{:S(2)}, u32[]{:S(2)}) collective-permute-start(bf16[256,512]{1,0:T(8,128)(2,1)S(1)} %get-tuple-element.83), channel_id=1, source_target_pairs={{0,1},{1,0},{2,3},{3,2},{4,5},{5,4},{6,7},{7,6},{8,9},{9,8},{10,11... | collective-permute-start | bytes 786440 | tf_op jit(solution)/shard_map/ppermute | solution.py:658
  241.9 6.8 %copy-start = (bf16[512,1024]{1,0:T(8,128)(2,1)S(1)}, bf16[512,1024]{1,0:T(8,128)(2,1)}, u32[]{:S(2)}) copy-start(bf16[512,1024]{1,0:T(8,128)(2,1)} %tok_ref.3) | copy-start | bytes 3145732
  241.9 6.8 %copy-start.1 = (f32[1024]{0:T(1024)S(1)}, f32[1024]{0:T(1024)}, u32[]{:S(2)}) copy-start(f32[1024]{0:T(1024)} %param.41) | copy-start | bytes 12292

commit v6 on v5

--- a/solution.py
+++ b/solution.py
@@ -330,23 +330,23 @@
     return copies
 
 
-def cut_weights(side, gate_up_w, down_w, out_w, first_ref, last_ref, quarter_ref, sems, *, first):
-    last = gate_up_w.shape[1] - first
+def cut_first(side, gate_up_w, down_w, out_w, first_ref, quarter_ref, sems):
     depth, width = down_w.shape[0] // 4, out_w.shape[0] // 4
-    half = gate_up_w.at[side[1]]
+    down_rows = pl.ds(pl.multiple_of(side[2] * depth, EXTRA), depth)
+    out_rows = pl.ds(pl.multiple_of(side[2] * width, EXTRA), width)
     pairs = [
-        (half.at[pl.ds(0, first)], first_ref),
-        (half.at[pl.ds(first, last)], last_ref),
-        (
-            down_w.at[pl.ds(pl.multiple_of(side[2] * depth, EXTRA), depth)],
-            quarter_ref.at[pl.ds(0, depth)],
-        ),
-        (
-            out_w.at[pl.ds(pl.multiple_of(side[2] * width, EXTRA), width)],
-            quarter_ref.at[pl.ds(depth, width)],
-        ),
+        (gate_up_w.at[side[1], pl.ds(0, first_ref.shape[0])], first_ref),
+        (down_w.at[down_rows], quarter_ref.at[pl.ds(0, depth)]),
+        (out_w.at[out_rows], quarter_ref.at[pl.ds(depth, width)]),
     ]
     for copy in run_copies(pairs, sems):
+        copy.wait()
+
+
+def cut_last(side, gate_up_w, last_ref, sems):
+    last = last_ref.shape[0]
+    rows = pl.ds(gate_up_w.shape[1] - last, last)
+    for copy in run_copies([(gate_up_w.at[side[1], rows], last_ref)], sems):
         copy.wait()
 
 
@@ -457,20 +457,27 @@
     core = lax.rem(quarter, 2)
     side = jnp.stack([lax.axis_index("grp"), core, quarter]).astype(jnp.int32)
     if pieces == 2:
-        half_first, half_last, quarters = pl.pallas_call(
-            functools.partial(cut_weights, first=first),
-            out_shape=(
-                HBM((first, w_down.shape[0]), BF16),
-                HBM((model - first, w_down.shape[0]), BF16),
-                HBM((depth + out_depth, model), BF16),
-            ),
+        units = w_down.shape[0]
+        half_first, quarters = pl.pallas_call(
+            cut_first,
+            out_shape=(HBM((first, units), BF16), HBM((depth + out_depth, model), BF16)),
             in_specs=[whole(SMEM)] + [whole(HBM)] * 3,
-            out_specs=(whole(HBM),) * 3,
-            scratch_shapes=[pltpu.SemaphoreType.DMA((4,))],
-            compiler_params=params(2),
-            cost_estimate=cost(0, 4 * model * (w_down.shape[0] + depth + out_depth)),
-            name="cut_weights",
+            out_specs=(whole(),) * 2,
+            scratch_shapes=[pltpu.SemaphoreType.DMA((3,))],
+            compiler_params=params(4),
+            cost_estimate=cost(0, 4 * (first * units + (depth + out_depth) * model)),
+            name="cut_first",
         )(side, *keep_in(HBM, w_gate_up, w_down, w_out))
+        half_last = pl.pallas_call(
+            cut_last,
+            out_shape=HBM((model - first, units), BF16),
+            in_specs=[whole(SMEM), whole(HBM)],
+            out_specs=whole(),
+            scratch_shapes=[pltpu.SemaphoreType.DMA((1,))],
+            compiler_params=params(4),
+            cost_estimate=cost(0, 4 * (model - first) * units),
+            name="cut_last",
+        )(side, *keep_in(HBM, w_gate_up))
 
     normed, queries, turned = pl.pallas_call(
         functools.partial(project_queries, reqs=reqs, draft=draft, heads=heads),
@@ -489,9 +496,7 @@
     )(*keep_in(HBM, tokens, norm_attn.reshape(1, -1), w_query))
 
     if pieces == 2:
-        turned, half_first, half_last, quarters = lax.optimization_barrier(
-            (turned, half_first, half_last, quarters)
-        )
+        turned, half_first, quarters = lax.optimization_barrier((turned, half_first, quarters))
         swap = [(0, 1), (1, 0)]
         one_a = lax.ppermute(half_first, "grp", swap)
         one_q = lax.ppermute(quarters, "grp", swap)
@@ -584,6 +589,8 @@
     asked, memory_out, momentum_out, keys, values = lax.optimization_barrier(
         (asked, memory_out, momentum_out, keys, values)
     )
+    if pieces == 2:
+        asked, half_last = lax.optimization_barrier((asked, half_last))
     answers = pl.pallas_call(
         functools.partial(
             page_attention, n=n, cap=cap, draft=draft, heads=heads, page_len=page_len,
@@ -659,7 +666,6 @@
         mine, two_a, two_b, two_q, four_q = lax.optimization_barrier(
             (mine, two_a, two_b, two_q, four_q)
         )
-        units = w_down.shape[0]
         out_near, gate_up_near, down_near = pl.pallas_call(
             stage_weights,
             out_shape=(

time: 257 us -> 143 us (0.56)
  Pallas kernels: 195 us -> 82.4 us
    pallas_call x1 -> x2, Pallas kernels: 119 us -> 6.63 us  [the longest x1 3.41 us: on_device(): pl.pallas_call(cut_last, out_shape=HBM((model - first, units), BF16), in_...]
  transfers between devices with their start and end apart: 12 -> 12, of which waited for: 4 -> 3; matrix products, arithmetic and copies ran while one was open for 2% -> 4% of each run, Pallas kernels for 72% -> 51%
where the time goes in v6:
time: 143 us; the launch traced here: 141 us
  Pallas kernels  82.4 us (58%)
  starting transfers between devices  27.3 us (19%)
  waiting for transfers between devices  22.2 us (16%)
  local copies, waits for them, and re-layouts  7.61 us (5%)
    pallas_call x1, Pallas kernels, on_device(): pl.pallas_call(functools.partial(update_memory, heads=heads, steps=steps)...  23 us
    ppermute x1, waiting for transfers between devices, on_device(): three_q = lax.ppermute(one_q, 'req', other_chip)  19.6 us
    pallas_call x1, Pallas kernels, on_device(): pl.pallas_call(functools.partial(local_attention, heads=heads, draft=draf...  18.2 us
    all_to_all x1, starting transfers between devices, on_device(): lax.all_to_all(label, 'req', split_axis=0, concat_axis=0, tiled=True)  7.39 us
    pallas_call x1, Pallas kernels, on_device(): pl.pallas_call(functools.partial(page_attention, n=n, cap=cap, draft=draf...  7.21 us
    pallas_call x1, Pallas kernels, on_device(): pl.pallas_call(stage_weights, out_shape=(VMEM((2,) + w_out.shape, BF16),...  6.34 us
    all_to_all x1, starting transfers between devices, on_device(): lax.all_to_all(packed, 'req', split_axis=0, concat_axis=0, tiled=True)  6 us
    all_to_all x1, starting transfers between devices, on_device(): lax.all_to_all(answers, 'req', split_axis=0, concat_axis=0, tiled=True)  5.75 us
  transfers between devices with their start and end apart: 12, of which 3 were waited for; matrix products, arithmetic and copies ran while one was open for 4% of the time, Pallas kernels for 51%

profile of v6, /device:TPU:0, one launch (start us, length us, event | category | flops | bytes accessed | tf_op | source)
XLA Modules:
  0.0 141.1 jit_solution(4898569054571778723)
XLA Ops:
  0.6 0.7 fusion.1
  1.3 0.7 reshape.28
  2.0 7.4 %all-to-all-start = ((s32[16,1,3]{2,1,0:T(1,128)}), s32[16,1,3]{2,1,0:T(1,128)S(1)}, u32[]{:S(2)}, u32[]{:S(2)}) async-start(s32[16,1,3]{2,1,0:T(1,128)} %bitcast.3), calls=%async_computation | async-start | bytes 16384 | tf_op jit(solution)/shard_map/all_to_all | solution.py:449
  9.4 0.1 pad_add_fusion.side
  9.5 3.3 %project_queries.1 = (bf16[512,1024]{1,0:T(8,128)(2,1)}, bf16[512,512]{1,0:T(8,128)(2,1)}, bf16[2048,128]{1,0:T(8,128)(2,1)S(1)}) custom-call(bf16[512,1024]{1,0:T(8,128)(2,1)} %tok_ref.3, f32[1,1024]{1,0:T(1,128)} %bitcast.15, bf16[1024,512]{1,0:T(8,128)(2,1)} %w_ref.1), custom_call_target="tpu_custom_call" | custom-call | flops 536870912 | bytes 3145728 | tf_op jit(solution)/shard_map/project_queries/pallas_call | solution.py:482
  12.8 3.2 %cut_first.1 = (bf16[320,1408]{1,0:T(8,128)(2,1)}, bf16[480,1024]{1,0:T(8,128)(2,1)}) custom-call(s32[3]{0:T(128)S(1)} %pad_add_fusion.side, bf16[2,1024,1408]{2,1,0:T(8,128)(2,1)} %gate_up_w.5, bf16[1408,1024]{1,0:T(8,128)(2,1)} %down_w.3, bf16[512,1024]{1,0:T(8,128)(2,1)} %out_w.3), custom_call_target="tpu_custom_call" | custom-call | bytes 3768320 | tf_op jit(solution)/shard_map/cut_first/pallas_call | solution.py:461
  16.0 0.0 all-to-all-done.codes
  16.0 2.4 %pack_queries.1 = bf16[6400,128]{1,0:T(8,128)(2,1)} custom-call(s32[16,1,3]{2,1,0:T(1,128)S(1)} %all-to-all-done.codes, s32[16]{0:T(128)} %lengths.1, bf16[2048,128]{1,0:T(8,128)(2,1)S(1)} %get-tuple-element.52.turned_ref), custom_call_target="tpu_custom_call" | custom-call | bytes 3276800 | tf_op jit(solution)/shard_map/pack_queries/pallas_call | solution.py:504
  18.4 6.0 %all-to-all-start.1 = ((bf16[16,400,128]{2,1,0:T(8,128)(2,1)}), bf16[16,400,128]{2,1,0:T(8,128)(2,1)S(1)}, u32[]{:S(2)}, u32[]{:S(2)}) async-start(bf16[16,400,128]{2,1,0:T(8,128)(2,1)} %bitcast.13), calls=%async_computation.1 | async-start | bytes 3276800 | tf_op jit(solution)/shard_map/all_to_all | solution.py:513
  24.4 0.0 copy-start.8
  24.4 1.6 %collective-permute-start.1 = (bf16[480,1024]{1,0:T(8,128)(2,1)}, bf16[480,1024]{1,0:T(8,128)(2,1)S(1)}, u32[]{:S(2)}, u32[]{:S(2)}) collective-permute-start(bf16[480,1024]{1,0:T(8,128)(2,1)} %get-tuple-element.62), channel_id=1, source_target_pairs={{0,1},{1,0},{2,3},{3,2},{4,5},{5,4},{6,7},{7,6},{8,9},{9,8},{10,11... | collective-permute-start | bytes 2949128 | tf_op jit(solution)/shard_map/ppermute | solution.py:502
  26.0 0.5 collective-permute-start
  26.5 3.4 %cut_last.1 = bf16[704,1408]{1,0:T(8,128)(2,1)} custom-call(s32[3]{0:T(128)S(1)} %pad_add_fusion.side, bf16[2,1024,1408]{2,1,0:T(8,128)(2,1)} %gate_up_w.5), custom_call_target="tpu_custom_call" | custom-call | bytes 3964928 | tf_op jit(solution)/shard_map/cut_last/pallas_call | solution.py:471
  29.9 0.0 copy-start.2
  30.0 0.1 copy.28
  30.0 0.1 reshape.30.path
  30.1 1.5 %copy.29 = s32[16,8,4]{2,1,0:T(8,128)} copy(s32[16,8,4]{0,2,1:T(4,128)} %param.39) | data formatting | bytes 4096 | tf_op args[17]
  31.6 0.9 reshape.31.mom_code
  32.5 1.5 %copy.30 = s32[16,8,4]{2,1,0:T(8,128)} copy(s32[16,8,4]{0,2,1:T(4,128)} %param.40) | data formatting | bytes 4096 | tf_op args[18]
  34.0 0.9 reshape.32.forget_code
  34.9 3.9 %project_keys.1 = (bf16[512,512]{1,0:T(8,128)(2,1)}, bf16[512,512]{1,0:T(8,128)(2,1)}) custom-call(bf16[512,1024]{1,0:T(8,128)(2,1)} %get-tuple-element.53.normed_ref, bf16[1024,512]{1,0:T(8,128)(2,1)} %wk_ref.1, bf16[1024,512]{1,0:T(8,128)(2,1)} %wv_ref.1), custom_call_target="tpu_custom_call" | custom-call | flops 1073741824 | bytes 3145728 | tf_op jit(solution)/shard_map/project_keys/pallas_call | solution.py:515
  38.9 23.0 %update_memory.1 = (f32[16,4,128,128]{3,2,1,0:T(8,128)}, f32[16,4,128,128]{3,2,1,0:T(8,128)}) custom-call(s32[128]{0:T(128)S(1)} %reshape.30.path, s32[16]{0:T(128)S(1)} %copy-done.2, s32[512]{0:T(512)S(1)} %reshape.31.mom_code, s32[512]{0:T(512)S(1)} %reshape.32.forget_code, bf16[512,512]{1,0:T(8,128)(2,1)} %get-tuple-element.54.k_ref, ...), custom_call_target="tpu_custom_call" | custom-call | flops 939524096 | bytes 16777216 | tf_op jit(solution)/shard_map/update_memory/pallas_call | solution.py:560
  61.9 0.0 all-to-all-done.1
  61.9 7.2 %page_attention.1 = bf16[6400,128]{1,0:T(8,128)(2,1)} custom-call(bf16[6400,128]{1,0:T(8,128)(2,1)S(1)} %bitcast.11, bf16[48,2,128,512]{3,2,1,0:T(8,128)(2,1)} %kv_hbm.1), custom_call_target="tpu_custom_call" | custom-call | flops 402653184 | bytes 15859712 | tf_op jit(solution)/shard_map/page_attention/pallas_call | solution.py:594
  69.1 0.0 collective-permute-done.one_a
  69.1 0.0 collective-permute-done.1.one_q
  69.1 5.8 %all-to-all-start.2 = ((bf16[16,400,128]{2,1,0:T(8,128)(2,1)}), bf16[16,400,128]{2,1,0:T(8,128)(2,1)S(1)}, u32[]{:S(2)}, u32[]{:S(2)}) async-start(bf16[16,400,128]{2,1,0:T(8,128)(2,1)} %bitcast.14), calls=%async_computation.2 | async-start | bytes 3276800 | tf_op jit(solution)/shard_map/all_to_all | solution.py:620
  74.9 1.6 %collective-permute-start.2 = (bf16[704,1408]{1,0:T(8,128)(2,1)}, bf16[704,1408]{1,0:T(8,128)(2,1)}, u32[]{:S(2)}, u32[]{:S(2)}) collective-permute-start(bf16[704,1408]{1,0:T(8,128)(2,1)} %cut_last.1), channel_id=1, source_target_pairs={{0,1},{1,0},{2,3},{3,2},{4,5},{5,4},{6,7},{7,6},{8,9},{9,8},{10,11... | collective-permute-start | bytes 5947400 | tf_op jit(solution)/shard_map/ppermute | solution.py:624
  76.4 1.9 %collective-permute-start.5 = (bf16[480,1024]{1,0:T(8,128)(2,1)S(1)}, bf16[480,1024]{1,0:T(8,128)(2,1)S(1)}, u32[]{:S(2)}, u32[]{:S(2)}) collective-permute-start(bf16[480,1024]{1,0:T(8,128)(2,1)S(1)} %collective-permute-done.1.one_q), channel_id=1, source_target_pairs={{0,4},{2,6},{4,0},{6,2},{8,12},{10,14},{12,8},{14,10},{16,20},{18,... | collective-permute-start | bytes 2949128 | tf_op jit(solution)/shard_map/ppermute | solution.py:625
  78.4 0.0 collective-permute-start.4
  78.4 0.5 collective-permute-start.3
  78.9 18.2 %local_attention.1 = (f32[2048,128]{1,0:T(8,128)}, f32[2048,128]{1,0:T(8,128)}, f32[16,128]{1,0:T(8,128)S(1)}, f32[16,128]{1,0:T(8,128)S(1)}) custom-call(bf16[512,512]{1,0:T(8,128)(2,1)} %get-tuple-element.67.q_ref, bf16[512,512]{1,0:T(8,128)(2,1)} %get-tuple-element.54.k_ref, bf16[512,512]{1,0:T(8,128)(2,1)} %get-tuple-element.55.v_ref, ...), custom_call_target="tpu_custom_call" | custom-call | flops 452984832 | bytes 6291456 | tf_op jit(solution)/shard_map/local_attention/pallas_call | solution.py:531
  97.0 0.0 collective-permute-done.3.two_a
  97.1 19.6 %collective-permute-done.5.three_q = bf16[480,1024]{1,0:T(8,128)(2,1)S(1)} collective-permute-done((bf16[480,1024]{1,0:T(8,128)(2,1)S(1)}, bf16[480,1024]{1,0:T(8,128)(2,1)S(1)}, u32[]{:S(2)}, u32[]{:S(2)}) %collective-permute-start.5) | collective-permute-done | bytes 983072 | tf_op jit(solution)/shard_map/ppermute | solution.py:625
  116.6 1.0 copy-done.4
  117.6 1.0 copy-done.5
  118.6 2.2 %collective-permute-done.2.one_b = bf16[704,1408]{1,0:T(8,128)(2,1)} collective-permute-done((bf16[704,1408]{1,0:T(8,128)(2,1)}, bf16[704,1408]{1,0:T(8,128)(2,1)}, u32[]{:S(2)}, u32[]{:S(2)}) %collective-permute-start.2) | collective-permute-done | bytes 1982496 | tf_op jit(solution)/shard_map/ppermute | solution.py:624
  120.8 0.0 all-to-all-done.2
  120.8 0.0 collective-permute-start.6
  120.8 0.5 collective-permute-start.7
  121.3 4.1 %combine.1 = (bf16[256,512]{1,0:T(8,128)(2,1)S(1)}, bf16[256,512]{1,0:T(8,128)(2,1)S(1)}) custom-call(s32[16,1,3]{2,1,0:T(1,128)S(1)} %all-to-all-done.codes, s32[3]{0:T(128)S(1)} %pad_add_fusion.side, bf16[6400,128]{1,0:T(8,128)(2,1)S(1)} %bitcast.10, f32[2048,128]{1,0:T(8,128)} %get-tuple-element.73.o_hbm, f32[2048,128]{1,0:T(8,128)} %get-tuple-element.74.ret_hbm, ...), custom_call_target="tpu_custom_call" | custom-call | flops 6291456 | bytes 3735552 | tf_op jit(solution)/shard_map/combine/pallas_call | solution.py:636
  125.4 1.6 %collective-permute-start.8 = (bf16[256,512]{1,0:T(8,128)(2,1)S(1)}, bf16[256,512]{1,0:T(8,128)(2,1)S(1)}, u32[]{:S(2)}, u32[]{:S(2)}) collective-permute-start(bf16[256,512]{1,0:T(8,128)(2,1)S(1)} %get-tuple-element.83), channel_id=1, source_target_pairs={{0,1},{1,0},{2,3},{3,2},{4,5},{5,4},{6,7},{7,6},{8,9},{9,8},{10,11... | collective-permute-start | bytes 786440 | tf_op jit(solution)/shard_map/ppermute | solution.py:665
  127.0 0.0 collective-permute-done.7.four_q
  127.0 0.0 copy-start.1
  127.0 6.3 %stage_weights.1 = (bf16[2,512,1024]{2,1,0:T(8,128)(2,1)S(1)}, bf16[2,2,1024,1408]{3,2,1,0:T(8,128)(2,1)S(1)}, bf16[2,1408,1024]{2,1,0:T(8,128)(2,1)S(1)}) custom-call(s32[3]{0:T(128)S(1)} %pad_add_fusion.side, bf16[512,1024]{1,0:T(8,128)(2,1)} %out_w.3, bf16[2,1024,1408]{2,1,0:T(8,128)(2,1)} %gate_up_w.5, bf16[1408,1024]{1,0:T(8,128)(2,1)} %down_w.3, ...), custom_call_target="tpu_custom_call" | custom-call | bytes 19398656 | tf_op jit(solution)/shard_map/stage_weights/pallas_call | solution.py:669
  133.4 0.3 collective-permute-done.8.theirs_ref
  133.7 4.8 %feed_up.1 = (bf16[256,1024]{1,0:T(8,128)(2,1)S(1)}, bf16[2,256,1408]{2,1,0:T(8,128)(2,1)S(1)}) custom-call(s32[3]{0:T(128)S(1)} %pad_add_fusion.side, bf16[512,1024]{1,0:T(8,128)(2,1)S(1)} %copy-done, bf16[256,512]{1,0:T(8,128)(2,1)S(1)} %get-tuple-element.82.mine_ref, bf16[256,512]{1,0:T(8,128)(2,1)S(1)} %collective-permute-done.8.theirs_ref, ...), custom_call_target="tpu_custom_call" | custom-call | flops 3489660928 | bytes 13631488 | tf_op jit(solution)/shard_map/feed_up/pallas_call | solution.py:689
  138.5 2.6 %feed_down.1 = bf16[256,1024]{1,0:T(8,128)(2,1)} custom-call(bf16[256,1024]{1,0:T(8,128)(2,1)S(1)} %get-tuple-element.90.residual_ref, bf16[2,256,1408]{2,1,0:T(8,128)(2,1)S(1)} %get-tuple-element.91.hidden_ref, bf16[2,1408,1024]{2,1,0:T(8,128)(2,1)S(1)} %get-tuple-element.92.down_w), custom_call_target="tpu_custom_call" | custom-call | flops 1476395008 | bytes 5767168 | tf_op jit(solution)/shard_map/feed_down/pallas_call | solution.py:703
  (15 shorter events, 0.0 us)
Async XLA Ops:
  2.0 14.0 %all-to-all-start = ((s32[16,1,3]{2,1,0:T(1,128)}), s32[16,1,3]{2,1,0:T(1,128)S(1)}, u32[]{:S(2)}, u32[]{:S(2)}) async-start(s32[16,1,3]{2,1,0:T(1,128)} %bitcast.3), calls=%async_computation | async-start | bytes 16384 | tf_op jit(solution)/shard_map/all_to_all | solution.py:449
  18.4 43.5 %all-to-all-start.1 = ((bf16[16,400,128]{2,1,0:T(8,128)(2,1)}), bf16[16,400,128]{2,1,0:T(8,128)(2,1)S(1)}, u32[]{:S(2)}, u32[]{:S(2)}) async-start(bf16[16,400,128]{2,1,0:T(8,128)(2,1)} %bitcast.13), calls=%async_computation.1 | async-start | bytes 3276800 | tf_op jit(solution)/shard_map/all_to_all | solution.py:513
  24.4 5.5 %copy-start.8 = (s32[16,8]{0,1:T(8,128)S(1)}, s32[16,8]{0,1:T(8,128)}, u32[]{:S(2)}) copy-start(s32[16,8]{0,1:T(8,128)} %param.35) | copy-start | bytes 1540
  24.4 44.7 %collective-permute-start.1 = (bf16[480,1024]{1,0:T(8,128)(2,1)}, bf16[480,1024]{1,0:T(8,128)(2,1)S(1)}, u32[]{:S(2)}, u32[]{:S(2)}) collective-permute-start(bf16[480,1024]{1,0:T(8,128)(2,1)} %get-tuple-element.62), channel_id=1, source_target_pairs={{0,1},{1,0},{2,3},{3,2},{4,5},{5,4},{6,7},{7,6},{8,9},{9,8},{10,11... | collective-permute-start | bytes 2949128 | tf_op jit(solution)/shard_map/ppermute | solution.py:502
  26.0 43.1 %collective-permute-start = (bf16[320,1408]{1,0:T(8,128)(2,1)}, bf16[320,1408]{1,0:T(8,128)(2,1)S(1)}, u32[]{:S(2)}, u32[]{:S(2)}) collective-permute-start(bf16[320,1408]{1,0:T(8,128)(2,1)} %get-tuple-element.61), channel_id=1, source_target_pairs={{0,1},{1,0},{2,3},{3,2},{4,5},{5,4},{6,7},{7,6},{8,9},{9,8},{10,11... | collective-permute-start | bytes 2703368 | tf_op jit(solution)/shard_map/ppermute | solution.py:501
  29.9 8.9 %copy-start.2 = (s32[16]{0:T(128)S(1)}, s32[16]{0:T(128)}, u32[]{:S(2)}) copy-start(s32[16]{0:T(128)} %count.1) | copy-start | bytes 196
  69.1 27.9 %copy-start.6 = (bf16[320,1408]{1,0:T(8,128)(2,1)}, bf16[320,1408]{1,0:T(8,128)(2,1)S(1)}, u32[]{:S(2)}) copy-start(bf16[320,1408]{1,0:T(8,128)(2,1)S(1)} %collective-permute-done.one_a) | copy-start | bytes 2703364
  69.1 27.9 %copy-start.3 = (bf16[480,1024]{1,0:T(8,128)(2,1)}, bf16[480,1024]{1,0:T(8,128)(2,1)S(1)}, u32[]{:S(2)}) copy-start(bf16[480,1024]{1,0:T(8,128)(2,1)S(1)} %collective-permute-done.1.one_q) | copy-start | bytes 2949124
  69.1 51.6 %all-to-all-start.2 = ((bf16[16,400,128]{2,1,0:T(8,128)(2,1)}), bf16[16,400,128]{2,1,0:T(8,128)(2,1)S(1)}, u32[]{:S(2)}, u32[]{:S(2)}) async-start(bf16[16,400,128]{2,1,0:T(8,128)(2,1)} %bitcast.14), calls=%async_computation.2 | async-start | bytes 3276800 | tf_op jit(solution)/shard_map/all_to_all | solution.py:620
  74.9 45.9 %collective-permute-start.2 = (bf16[704,1408]{1,0:T(8,128)(2,1)}, bf16[704,1408]{1,0:T(8,128)(2,1)}, u32[]{:S(2)}, u32[]{:S(2)}) collective-permute-start(bf16[704,1408]{1,0:T(8,128)(2,1)} %cut_last.1), channel_id=1, source_target_pairs={{0,1},{1,0},{2,3},{3,2},{4,5},{5,4},{6,7},{7,6},{8,9},{9,8},{10,11... | collective-permute-start | bytes 5947400 | tf_op jit(solution)/shard_map/ppermute | solution.py:624
  76.4 40.2 %collective-permute-start.5 = (bf16[480,1024]{1,0:T(8,128)(2,1)S(1)}, bf16[480,1024]{1,0:T(8,128)(2,1)S(1)}, u32[]{:S(2)}, u32[]{:S(2)}) collective-permute-start(bf16[480,1024]{1,0:T(8,128)(2,1)S(1)} %collective-permute-done.1.one_q), channel_id=1, source_target_pairs={{0,4},{2,6},{4,0},{6,2},{8,12},{10,14},{12,8},{14,10},{16,20},{18,... | collective-permute-start | bytes 2949128 | tf_op jit(solution)/shard_map/ppermute | solution.py:625
  78.4 38.3 %collective-permute-start.4 = (bf16[480,1024]{1,0:T(8,128)(2,1)S(1)}, bf16[480,1024]{1,0:T(8,128)(2,1)S(1)}, u32[]{:S(2)}, u32[]{:S(2)}) collective-permute-start(bf16[480,1024]{1,0:T(8,128)(2,1)S(1)} %collective-permute-done.1.one_q), channel_id=1, source_target_pairs={{0,2},{2,0},{4,6},{6,4},{8,10},{10,8},{12,14},{14,12},{16,18},{18,... | collective-permute-start | bytes 2949128 | tf_op jit(solution)/shard_map/ppermute | solution.py:627
  78.4 18.7 %collective-permute-start.3 = (bf16[320,1408]{1,0:T(8,128)(2,1)S(1)}, bf16[320,1408]{1,0:T(8,128)(2,1)S(1)}, u32[]{:S(2)}, u32[]{:S(2)}) collective-permute-start(bf16[320,1408]{1,0:T(8,128)(2,1)S(1)} %collective-permute-done.one_a), channel_id=1, source_target_pairs={{0,2},{2,0},{4,6},{6,4},{8,10},{10,8},{12,14},{14,12},{16,18},{18,... | collective-permute-start | bytes 2703368 | tf_op jit(solution)/shard_map/ppermute | solution.py:626
  97.1 19.6 %copy-start.7 = (bf16[320,1408]{1,0:T(8,128)(2,1)}, bf16[320,1408]{1,0:T(8,128)(2,1)S(1)}, u32[]{:S(2)}) copy-start(bf16[320,1408]{1,0:T(8,128)(2,1)S(1)} %collective-permute-done.3.two_a) | copy-start | bytes 2703364
  116.6 1.0 copy-start.4
  117.6 1.0 copy-start.5
  120.8 6.2 %collective-permute-start.6 = (bf16[704,1408]{1,0:T(8,128)(2,1)}, bf16[704,1408]{1,0:T(8,128)(2,1)S(1)}, u32[]{:S(2)}, u32[]{:S(2)}) collective-permute-start(bf16[704,1408]{1,0:T(8,128)(2,1)} %collective-permute-done.2.one_b), channel_id=1, source_target_pairs={{0,2},{2,0},{4,6},{6,4},{8,10},{10,8},{12,14},{14,12},{16,18},{18,... | collective-permute-start | bytes 5947400 | tf_op jit(solution)/shard_map/ppermute | solution.py:633
  120.8 6.2 %collective-permute-start.7 = (bf16[480,1024]{1,0:T(8,128)(2,1)}, bf16[480,1024]{1,0:T(8,128)(2,1)S(1)}, u32[]{:S(2)}, u32[]{:S(2)}) collective-permute-start(bf16[480,1024]{1,0:T(8,128)(2,1)} %copy-done.4), channel_id=1, source_target_pairs={{0,2},{2,0},{4,6},{6,4},{8,10},{10,8},{12,14},{14,12},{16,18},{18,... | collective-permute-start | bytes 2949128 | tf_op jit(solution)/shard_map/ppermute | solution.py:634
  125.4 8.3 %collective-permute-start.8 = (bf16[256,512]{1,0:T(8,128)(2,1)S(1)}, bf16[256,512]{1,0:T(8,128)(2,1)S(1)}, u32[]{:S(2)}, u32[]{:S(2)}) collective-permute-start(bf16[256,512]{1,0:T(8,128)(2,1)S(1)} %get-tuple-element.83), channel_id=1, source_target_pairs={{0,1},{1,0},{2,3},{3,2},{4,5},{5,4},{6,7},{7,6},{8,9},{9,8},{10,11... | collective-permute-start | bytes 786440 | tf_op jit(solution)/shard_map/ppermute | solution.py:665
  127.0 6.7 %copy-start = (bf16[512,1024]{1,0:T(8,128)(2,1)S(1)}, bf16[512,1024]{1,0:T(8,128)(2,1)}, u32[]{:S(2)}) copy-start(bf16[512,1024]{1,0:T(8,128)(2,1)} %tok_ref.3) | copy-start | bytes 3145732
  127.0 6.7 %copy-start.1 = (f32[1024]{0:T(1024)S(1)}, f32[1024]{0:T(1024)}, u32[]{:S(2)}) copy-start(f32[1024]{0:T(1024)} %param.41) | copy-start | bytes 12292

commit v7 on v6

--- a/solution.py
+++ b/solution.py
@@ -12,6 +12,7 @@
 LANES = 128
 EXTRA = 16
 TOP_PARTS = 3
+WEIGHT = 20
 SUM_PARTS = 2
 
 EPS = 1e-06
@@ -30,7 +31,9 @@
 
 
 def cost(flops, moved, special=0):
-    return pl.CostEstimate(flops=flops, bytes_accessed=moved, transcendentals=special)
+    return pl.CostEstimate(
+        flops=WEIGHT * flops, bytes_accessed=WEIGHT * moved, transcendentals=special
+    )
 
 
 def keep_in(space, *arrays):
@@ -216,41 +219,67 @@
 
 
 def update_memory(
-    path, count, mom_code, forget_code, k_ref, v_ref, mem_ref, mom_ref, mem_out, mom_out,
-    wide_k, wide_v, unit_ref, value_ref, turned_ref, *, heads, steps,
+    path, count, mom_code, forget_code, k_ref, v_ref, mem_hbm, mom_hbm, mem_out, mom_out,
+    mem_buf, mom_buf, wide_k, wide_v, unit_ref, value_ref, turned_ref, in_sems, out_sems,
+    *, reqs, draft, heads, steps,
 ):
-    r = pl.program_id(0)
-    wide_k[...] = k_ref[...].astype(F32)
-    wide_v[...] = v_ref[...].astype(F32)
+    def arrivals(r):
+        return (
+            pltpu.make_async_copy(mem_hbm.at[r], mem_buf.at[r], in_sems.at[0, r]),
+            pltpu.make_async_copy(mom_hbm.at[r], mom_buf.at[r], in_sems.at[1, r]),
+        )
+
+    def departures(r):
+        return (
+            pltpu.make_async_copy(mem_buf.at[r], mem_out.at[r], out_sems.at[0, r]),
+            pltpu.make_async_copy(mom_buf.at[r], mom_out.at[r], out_sems.at[1, r]),
+        )
+
+    for r in range(reqs):
+        for copy in arrivals(r):
+            copy.start()
     unit_ref[...] = jnp.zeros_like(unit_ref)
-    for n in range(steps):
-        node = path[r * steps + n]
-        k_row = wide_k[pl.ds(node, 1), :]
-        v_row = wide_v[pl.ds(node, 1), :]
-        for h in range(heads):
-            unit_ref[h * steps + n : h * steps + n + 1, :] = k_row[:, h * HD : (h + 1) * HD]
-            value_ref[h * steps + n : h * steps + n + 1, :] = v_row[:, h * HD : (h + 1) * HD]
-    keys = unit_ref[...]
-    unit = keys * lax.rsqrt(jnp.sum(keys * keys, axis=1, keepdims=True) + EPS)
-    turned_ref[...] = jnp.transpose(unit)
-
-    def advance(n, mem_src, mom_src):
-        for h in range(heads):
-            at = (r * steps + n) * heads + h
-            eta = 0.97 - 0.06 * mom_code[at].astype(F32)
-            keep = 1.0 - (0.01 + 0.02 * forget_code[at].astype(F32))
-            row = h * steps + n
-            column = turned_ref[:, row : row + 1]
-            matrix = mem_src[0, h]
-            predicted = jnp.sum(column * matrix, axis=0, keepdims=True)
-            error = THETA * (predicted - value_ref[row : row + 1, :])
-            moved = eta * mom_src[0, h] - column * error
-            mom_out[0, h] = moved
-            mem_out[0, h] = keep * matrix + moved
-
-    advance(0, mem_ref, mom_ref)
-    for n in range(1, steps):
-        pl.when(n < count[r])(functools.partial(advance, n, mem_out, mom_out))
+
+    def one(r, carry):
+        rows = pl.ds(pl.multiple_of(r * draft, draft), draft)
+        wide_k[...] = k_ref[rows, :].astype(F32)
+        wide_v[...] = v_ref[rows, :].astype(F32)
+        for n in range(steps):
+            node = path[n, r]
+            k_row = wide_k[pl.ds(node, 1), :]
+            v_row = wide_v[pl.ds(node, 1), :]
+            for h in range(heads):
+                unit_ref[h * steps + n : h * steps + n + 1, :] = k_row[:, h * HD : (h + 1) * HD]
+                value_ref[h * steps + n : h * steps + n + 1, :] = v_row[:, h * HD : (h + 1) * HD]
+        keys = unit_ref[...]
+        unit = keys * lax.rsqrt(jnp.sum(keys * keys, axis=1, keepdims=True) + EPS)
+        turned_ref[...] = jnp.transpose(unit)
+        for copy in arrivals(r):
+            copy.wait()
+
+        def advance(n):
+            for h in range(heads):
+                eta = 0.97 - 0.06 * mom_code[n, h, r].astype(F32)
+                keep = 1.0 - (0.01 + 0.02 * forget_code[n, h, r].astype(F32))
+                row = h * steps + n
+                column = turned_ref[:, row : row + 1]
+                matrix = mem_buf[r, h]
+                predicted = jnp.sum(column * matrix, axis=0, keepdims=True)
+                error = THETA * (predicted - value_ref[row : row + 1, :])
+                moved = eta * mom_buf[r, h] - column * error
+                mom_buf[r, h] = moved
+                mem_buf[r, h] = keep * matrix + moved
+
+        for n in range(steps):
+            pl.when(n < count[r])(functools.partial(advance, n))
+        for copy in departures(r):
+            copy.start()
+        return carry
+
+    lax.fori_loop(0, reqs, one, 0)
+    for r in range(reqs):
+        for copy in departures(r):
+            copy.wait()
 
 
 def combine(
@@ -343,24 +372,29 @@
         copy.wait()
 
 
-def cut_last(side, gate_up_w, last_ref, sems):
-    last = last_ref.shape[0]
-    rows = pl.ds(gate_up_w.shape[1] - last, last)
-    for copy in run_copies([(gate_up_w.at[side[1], rows], last_ref)], sems):
+def cut_last(side, gate_up_w, mid_ref, last_ref, sems, *, pieces):
+    step = last_ref.shape[0] // pieces
+    start = gate_up_w.shape[1] - last_ref.shape[0]
+    half = gate_up_w.at[side[1]]
+    middle = mid_ref.shape[0]
+    pairs = [(half.at[pl.ds(start - middle, middle)], mid_ref)]
+    for i in range(pieces):
+        pairs.append((half.at[pl.ds(start + i * step, step)], last_ref.at[pl.ds(i * step, step)]))
+    for copy in run_copies(pairs, sems):
         copy.wait()
 
 
 def stage_weights(
-    side, out_w, gate_up_w, down_w, one_a, one_b, one_q, two_a, two_b, two_q, three_q, four_q,
-    out_all, gate_up_all, down_all, sems,
+    side, out_w, gate_up_w, down_w, one_a, one_m, one_b, one_q, two_a, two_m, two_b, two_q, three_q,
+    four_q, out_all, gate_up_all, down_all, sems,
 ):
     width, depth = out_w.shape[0] // 4, down_w.shape[0] // 4
-    first, last = one_a.shape[0], one_b.shape[0]
     pairs = [(gate_up_w, gate_up_all.at[0]), (down_w, down_all.at[0]), (out_w, out_all.at[0])]
-    for half, a, b in ((side[1], one_a, one_b), (1 - side[1], two_a, two_b)):
-        target = gate_up_all.at[1, half]
-        pairs.append((a, target.at[pl.ds(0, first)]))
-        pairs.append((b, target.at[pl.ds(first, last)]))
+    for half, parts in ((side[1], (one_a, one_m, one_b)), (1 - side[1], (two_a, two_m, two_b))):
+        at = 0
+        for part in parts:
+            pairs.append((part, gate_up_all.at[1, half, pl.ds(at, part.shape[0])]))
+            at += part.shape[0]
     core, chip = side[1], side[2] // 2
     for x, y, q in ((core, chip, one_q), (1 - core, chip, two_q), (core, 1 - chip, three_q), (
         1 - core, 1 - chip, four_q,
@@ -374,34 +408,29 @@
         copy.wait()
 
 
-def feed_up(
-    side, tok_ref, mine_ref, theirs_ref, gain_ref, out_w, gate_up_w, residual_ref, hidden_ref
+def feed_forward(
+    side, tok_ref, mine_ref, theirs_ref, gain_ref, out_w, gate_up_w, down_w, out_ref,
+    residual, hidden,
 ):
     rows = mine_ref.shape[0]
     units = gate_up_w.shape[3]
     tokens = tok_ref[pl.ds(pl.multiple_of(side[0] * rows, rows), rows), :].astype(F32)
     summed = tokens + jnp.dot(mine_ref[...], out_w[0], preferred_element_type=F32)
     summed = summed + jnp.dot(theirs_ref[...], out_w[1], preferred_element_type=F32)
-    residual_ref[...] = summed.astype(BF16)
-    ffn_in = rms_norm(residual_ref[...], gain_ref[...])
+    residual[...] = summed.astype(BF16)
+    ffn_in = rms_norm(residual[...], gain_ref[...])
     step = 256
     for half in range(2):
         for first in range(0, units, step):
             cols = slice(first, min(first + step, units))
             gate = jnp.dot(ffn_in, gate_up_w[half, 0, :, cols], preferred_element_type=F32)
             up = jnp.dot(ffn_in, gate_up_w[half, 1, :, cols], preferred_element_type=F32)
-            hidden_ref[half, :, cols] = (gate / (1.0 + jnp.exp(-gate)) * up).astype(BF16)
-
-
-def feed_down(residual_ref, hidden_ref, down_w, out_ref):
-    step = 256
+            hidden[half, :, cols] = (gate / (1.0 + jnp.exp(-gate)) * up).astype(BF16)
     for at in range(0, out_ref.shape[1], step):
         cols = slice(at, at + step)
-        total = residual_ref[:, cols].astype(F32)
+        total = residual[:, cols].astype(F32)
         for half in range(2):
-            total = total + jnp.dot(
-                hidden_ref[half], down_w[half, :, cols], preferred_element_type=F32
-            )
+            total = total + jnp.dot(hidden[half], down_w[half, :, cols], preferred_element_type=F32)
         out_ref[:, cols] = total.astype(BF16)
 
 
@@ -450,8 +479,8 @@
 
     grp = lax.axis_size("grp")
     depth, out_depth = w_down.shape[0] // 4, width // 4
-    first = model * 10 // 32
-    split = (depth, out_depth, first)
+    first, middle = model // 4, model * 3 // 16
+    split = (depth, out_depth, first, middle, (model - first - middle) // 3)
     pieces = 2 if grp == 2 and n % 4 == 0 and not any(size % EXTRA for size in split) else 1
     quarter = lax.rem(lax.axis_index("req"), 4)
     core = lax.rem(quarter, 2)
@@ -460,7 +489,7 @@
         units = w_down.shape[0]
         half_first, quarters = pl.pallas_call(
             cut_first,
-            out_shape=(HBM((first, units), BF16), HBM((depth + out_depth, model), BF16)),
+            out_shape=(VMEM((first, units), BF16), VMEM((depth + out_depth, model), BF16)),
             in_specs=[whole(SMEM)] + [whole(HBM)] * 3,
             out_specs=(whole(),) * 2,
             scratch_shapes=[pltpu.SemaphoreType.DMA((3,))],
@@ -468,16 +497,6 @@
             cost_estimate=cost(0, 4 * (first * units + (depth + out_depth) * model)),
             name="cut_first",
         )(side, *keep_in(HBM, w_gate_up, w_down, w_out))
-        half_last = pl.pallas_call(
-            cut_last,
-            out_shape=HBM((model - first, units), BF16),
-            in_specs=[whole(SMEM), whole(HBM)],
-            out_specs=whole(),
-            scratch_shapes=[pltpu.SemaphoreType.DMA((1,))],
-            compiler_params=params(4),
-            cost_estimate=cost(0, 4 * (model - first) * units),
-            name="cut_last",
-        )(side, *keep_in(HBM, w_gate_up))
 
     normed, queries, turned = pl.pallas_call(
         functools.partial(project_queries, reqs=reqs, draft=draft, heads=heads),
@@ -510,7 +529,20 @@
         cost_estimate=cost(0, 4 * n * ask_block * LANES),
         name="pack_queries",
     )(codes, *keep_in(HBM, cache_len), turned)
+    packed, normed, late = lax.optimization_barrier((packed, normed, w_gate_up))
     asked = lax.all_to_all(packed, "req", split_axis=0, concat_axis=0, tiled=True)
+
+    if pieces == 2:
+        half_mid, half_last = pl.pallas_call(
+            functools.partial(cut_last, pieces=3),
+            out_shape=(VMEM((middle, units), BF16), VMEM((model - first - middle, units), BF16)),
+            in_specs=[whole(SMEM), whole(HBM)],
+            out_specs=(whole(),) * 2,
+            scratch_shapes=[pltpu.SemaphoreType.DMA((4,))],
+            compiler_params=params(4),
+            cost_estimate=cost(0, 4 * (model - first) * units),
+            name="cut_last",
+        )(side, *keep_in(HBM, late))
 
     keys, values = pl.pallas_call(
         project_keys,
@@ -548,49 +580,53 @@
         ],
         out_specs=(span_block, span_block) + (pl.BlockSpec((reqs, LANES), lambda r: (0, 0)),) * 2,
         compiler_params=params(10),
-        cost_estimate=cost(
-            2 * reqs * span * HD * (2 * (draft + fixed_count) + 6 * HD),
-            4 * reqs * (heads * HD * HD + 2 * span * HD),
-            reqs * span * (draft + fixed_count),
-        ),
+        cost_estimate=cost(1, 1),
         name="local_attention",
     )(*keep_in(HBM, queries, keys, values, persist_keys, persist_values, tree_mask, memory))
 
-    matrices = jax.ShapeDtypeStruct(memory.shape, F32)
     memory_out, momentum_out = pl.pallas_call(
-        functools.partial(update_memory, heads=heads, steps=steps),
-        grid_spec=pltpu.PrefetchScalarGridSpec(
-            num_scalar_prefetch=4,
-            grid=(reqs,),
-            in_specs=[row_block, row_block, matrix_block, matrix_block],
-            out_specs=(matrix_block, matrix_block),
-            scratch_shapes=[
-                pltpu.VMEM((draft, width), F32),
-                pltpu.VMEM((draft, width), F32),
-                pltpu.VMEM((LANES, HD), F32),
-                pltpu.VMEM((heads * steps, HD), F32),
-                pltpu.VMEM((HD, LANES), F32),
-            ],
-        ),
-        out_shape=(matrices, matrices),
-        compiler_params=params(10),
+        functools.partial(update_memory, reqs=reqs, draft=draft, heads=heads, steps=steps),
+        out_shape=(HBM(memory.shape, F32),) * 2,
+        in_specs=[whole(SMEM)] * 4 + [whole()] * 2 + [whole(HBM)] * 2,
+        out_specs=(whole(HBM),) * 2,
+        scratch_shapes=[
+            pltpu.VMEM(memory.shape, F32),
+            pltpu.VMEM(memory.shape, F32),
+            pltpu.VMEM((draft, width), F32),
+            pltpu.VMEM((draft, width), F32),
+            pltpu.VMEM((LANES, HD), F32),
+            pltpu.VMEM((heads * steps, HD), F32),
+            pltpu.VMEM((HD, LANES), F32),
+            pltpu.SemaphoreType.DMA((2, reqs)),
+            pltpu.SemaphoreType.DMA((2, reqs)),
+        ],
+        compiler_params=params(16),
         cost_estimate=cost(
             14 * reqs * heads * HD * HD * steps * 8, 16 * reqs * heads * HD * HD
         ),
         name="update_memory",
     )(
-        accept_path.reshape(-1),
+        jnp.transpose(accept_path),
         accept_len,
-        momentum_code.reshape(-1),
-        forget_code.reshape(-1),
+        jnp.transpose(momentum_code, (1, 2, 0)),
+        jnp.transpose(forget_code, (1, 2, 0)),
         *keep_in(HBM, keys, values, memory, momentum),
     )
 
+    if pieces == 2:
+        memory_out, momentum_out, half_mid, half_last, one_a, one_q = lax.optimization_barrier(
+            (memory_out, momentum_out, half_mid, half_last, one_a, one_q)
+        )
+        other_core = [(i, i ^ 1) for i in range(n)]
+        other_chip = [(i, i ^ 2) for i in range(n)]
+        one_m = lax.ppermute(half_mid, "grp", swap)
+        one_b = lax.ppermute(half_last, "grp", swap)
+        three_q = lax.ppermute(one_q, "req", other_chip)
+        two_a = lax.ppermute(one_a, "req", other_core)
+        two_q = lax.ppermute(one_q, "req", other_core)
     asked, memory_out, momentum_out, keys, values = lax.optimization_barrier(
         (asked, memory_out, momentum_out, keys, values)
     )
-    if pieces == 2:
-        asked, half_last = lax.optimization_barrier((asked, half_last))
     answers = pl.pallas_call(
         functools.partial(
             page_attention, n=n, cap=cap, draft=draft, heads=heads, page_len=page_len,
@@ -614,20 +650,13 @@
         name="page_attention",
     )(asked, *keep_in(HBM, kv_cache))
     if pieces == 2:
-        answers, half_last, one_a, one_q = lax.optimization_barrier(
-            (answers, half_last, one_a, one_q)
-        )
+        answers, one_m = lax.optimization_barrier((answers, one_m))
+        two_m = lax.ppermute(one_m, "req", other_core)
     returned = lax.all_to_all(answers, "req", split_axis=0, concat_axis=0, tiled=True)
     if pieces == 2:
-        other_core = [(i, i ^ 1) for i in range(n)]
-        other_chip = [(i, i ^ 2) for i in range(n)]
-        one_b = lax.ppermute(half_last, "grp", swap)
-        three_q = lax.ppermute(one_q, "req", other_chip)
-        two_a = lax.ppermute(one_a, "req", other_core)
-        two_q = lax.ppermute(one_q, "req", other_core)
-        returned, one_b, two_a, two_q, three_q, own, retrieved, own_top, own_sum = (
+        returned, one_b, two_a, two_m, two_q, three_q, own, retrieved, own_top, own_sum = (
             lax.optimization_barrier(
-                (returned, one_b, two_a, two_q, three_q, own, retrieved, own_top, own_sum)
+                (returned, one_b, two_a, two_m, two_q, three_q, own, retrieved, own_top, own_sum)
             )
         )
         two_b = lax.ppermute(one_b, "req", other_core)
@@ -673,42 +702,37 @@
                 VMEM((2,) + w_gate_up.shape, BF16),
                 VMEM((2,) + w_down.shape, BF16),
             ),
-            in_specs=[whole(SMEM)] + [whole(pl.ANY)] * 11,
+            in_specs=[whole(SMEM)] + [whole(pl.ANY)] * 13,
             out_specs=(whole(),) * 3,
-            scratch_shapes=[pltpu.SemaphoreType.DMA((15,))],
+            scratch_shapes=[pltpu.SemaphoreType.DMA((17,))],
             compiler_params=params(2),
             cost_estimate=cost(0, 2 * model * (2 * width + 6 * units)),
             name="stage_weights",
         )(
             side,
-            *keep_in(HBM, w_out, w_gate_up, w_down, one_a, one_b, one_q, two_a),
+            *keep_in(HBM, w_out, w_gate_up, w_down, one_a, one_m, one_b, one_q, two_a, two_m),
             two_b,
             *keep_in(HBM, two_q, three_q),
             four_q,
         )
-        residual, hidden = pl.pallas_call(
-            feed_up,
-            out_shape=(VMEM((rows, model), BF16), VMEM((2, rows, units), BF16)),
-            in_specs=[whole(SMEM)] + [whole()] * 6,
-            out_specs=(whole(),) * 2,
-            compiler_params=params(12),
+        layer_out = pl.pallas_call(
+            feed_forward,
+            out_shape=jax.ShapeDtypeStruct((rows, model), BF16),
+            in_specs=[whole(SMEM)] + [whole()] * 7,
+            out_specs=whole(),
+            scratch_shapes=[
+                pltpu.VMEM((rows, model), BF16),
+                pltpu.VMEM((2, rows, units), BF16),
+            ],
+            compiler_params=params(14),
             cost_estimate=cost(
-                4 * rows * model * (width + 2 * units), 4 * model * (width + 2 * units)
+                4 * rows * model * (width + 3 * units), 4 * model * (width + 3 * units)
             ),
-            name="feed_up",
+            name="feed_forward",
         )(
             side, tokens, mine, theirs, norm_ffn.reshape(1, -1),
-            *keep_in(VMEM, out_near, gate_up_near),
-        )
-        layer_out = pl.pallas_call(
-            feed_down,
-            out_shape=jax.ShapeDtypeStruct((rows, model), BF16),
-            in_specs=[whole()] * 3,
-            out_specs=whole(),
-            compiler_params=params(6),
-            cost_estimate=cost(4 * rows * model * units, 4 * model * units),
-            name="feed_down",
-        )(*keep_in(VMEM, residual, hidden, down_near))
+            *keep_in(VMEM, out_near, gate_up_near, down_near),
+        )
         return (layer_out, memory_out, momentum_out)
 
     partial_out = jnp.dot(mixed[0], w_out, preferred_element_type=F32).astype(BF16)

time: 143 us -> 142 us (level)
  local copies, waits for them, and re-layouts: 7.61 us -> 3.15 us
  waiting for transfers between devices: 22.2 us -> 25 us
    ppermute x0 -> x2, waiting for transfers between devices: none -> 3.81 us  [the longest x1 3.8 us: on_device(): one_m = lax.ppermute(half_mid, 'grp', swap)]
    unnamed x21 -> x20, local copies, waits for them, and re-layouts: 4.95 us -> 2.46 us
    ppermute x1, waiting for transfers between devices: 2.22 us -> 0.01 us  [on_device(): one_b = lax.ppermute(half_last, 'grp', swap)]
    reshape x3 -> x0, local copies, waits for them, and re-layouts: 1.97 us -> none  [the longest x1 0.94 us: on_device(): forget_code.reshape(-1)]
    ppermute x0 -> x2, starting transfers between devices: none -> 1.56 us  [the longest x1 1.55 us: on_device(): one_m = lax.ppermute(half_mid, 'grp', swap)]
    pallas_call x5 -> x4, Pallas kernels: 37 us -> 36.7 us  [the longest x1 23.3 us: on_device(): pl.pallas_call(functools.partial(update_memory, reqs=reqs, draft=draft, h...]
  transfers between devices with their start and end apart: 12 -> 14, of which waited for: 3 -> 4; matrix products, arithmetic and copies ran while one was open for 4% -> 0% of each run, Pallas kernels for 51% -> 53%
where the time goes in v7:
time: 142 us; the launch traced here: 141 us
  Pallas kernels  82.3 us (58%)
  starting transfers between devices  28.7 us (20%)
  waiting for transfers between devices  25 us (18%)
  local copies, waits for them, and re-layouts  3.15 us (2%)
    pallas_call x1, Pallas kernels, on_device(): pl.pallas_call(functools.partial(update_memory, reqs=reqs, draft=draft, h...  23.3 us
    ppermute x1, waiting for transfers between devices, on_device(): three_q = lax.ppermute(one_q, 'req', other_chip)  19.6 us
    pallas_call x1, Pallas kernels, on_device(): pl.pallas_call(functools.partial(local_attention, heads=heads, draft=draf...  18.2 us
    all_to_all x1, starting transfers between devices, on_device(): lax.all_to_all(label, 'req', split_axis=0, concat_axis=0, tiled=True)  7.39 us
    pallas_call x1, Pallas kernels, on_device(): pl.pallas_call(feed_forward, out_shape=jax.ShapeDtypeStruct((rows, model)...  7.32 us
    pallas_call x1, Pallas kernels, on_device(): pl.pallas_call(functools.partial(page_attention, n=n, cap=cap, draft=draf...  7.22 us
    pallas_call x1, Pallas kernels, on_device(): pl.pallas_call(stage_weights, out_shape=(VMEM((2,) + w_out.shape, BF16),...  6.5 us
    all_to_all x1, starting transfers between devices, on_device(): lax.all_to_all(packed, 'req', split_axis=0, concat_axis=0, tiled=True)  6 us
  transfers between devices with their start and end apart: 14, of which 4 were waited for; matrix products, arithmetic and copies ran while one was open for 0% of the time, Pallas kernels for 53%

profile of v7, /device:TPU:0, one launch (start us, length us, event | category | flops | bytes accessed | tf_op | source)
XLA Modules:
  0.0 140.8 jit_solution(4397196061155577590)
XLA Ops:
  0.6 0.7 fusion.1
  1.3 0.7 reshape.19
  2.0 7.4 %all-to-all-start = ((s32[16,1,3]{2,1,0:T(1,128)}), s32[16,1,3]{2,1,0:T(1,128)S(1)}, u32[]{:S(2)}, u32[]{:S(2)}) async-start(s32[16,1,3]{2,1,0:T(1,128)} %bitcast.3), calls=%async_computation | async-start | bytes 16384 | tf_op jit(solution)/shard_map/all_to_all | solution.py:478
  9.4 0.1 pad_add_fusion.side
  9.5 3.3 %project_queries.1 = (bf16[512,1024]{1,0:T(8,128)(2,1)}, bf16[512,512]{1,0:T(8,128)(2,1)}, bf16[2048,128]{1,0:T(8,128)(2,1)S(1)}) custom-call(bf16[512,1024]{1,0:T(8,128)(2,1)} %tok_ref.3, f32[1,1024]{1,0:T(1,128)} %bitcast.21, bf16[1024,512]{1,0:T(8,128)(2,1)} %w_ref.1), custom_call_target="tpu_custom_call" | custom-call | flops 10737418240 | bytes 62914560 | tf_op jit(solution)/shard_map/project_queries/pallas_call | solution.py:501
  12.8 3.2 %cut_first.1 = (bf16[256,1408]{1,0:T(8,128)(2,1)}, bf16[480,1024]{1,0:T(8,128)(2,1)}) custom-call(s32[3]{0:T(128)S(1)} %pad_add_fusion.side, bf16[2,1024,1408]{2,1,0:T(8,128)(2,1)} %gate_up_w.4, bf16[1408,1024]{1,0:T(8,128)(2,1)} %down_w.3, bf16[512,1024]{1,0:T(8,128)(2,1)} %out_w.3), custom_call_target="tpu_custom_call" | custom-call | bytes 68157440 | tf_op jit(solution)/shard_map/cut_first/pallas_call | solution.py:490
  15.9 1.6 %collective-permute-start = (bf16[256,1408]{1,0:T(8,128)(2,1)}, bf16[256,1408]{1,0:T(8,128)(2,1)}, u32[]{:S(2)}, u32[]{:S(2)}) collective-permute-start(bf16[256,1408]{1,0:T(8,128)(2,1)} %get-tuple-element.69), channel_id=1, source_target_pairs={{0,1},{1,0},{2,3},{3,2},{4,5},{5,4},{6,7},{7,6},{8,9},{9,8},{10,11... | collective-permute-start | bytes 2162696 | tf_op jit(solution)/shard_map/ppermute | solution.py:520
  17.5 0.5 collective-permute-start.1
  18.0 0.0 all-to-all-done.codes
  18.0 2.5 %pack_queries.1 = bf16[6400,128]{1,0:T(8,128)(2,1)} custom-call(s32[16,1,3]{2,1,0:T(1,128)S(1)} %all-to-all-done.codes, s32[16]{0:T(128)} %lengths.1, bf16[2048,128]{1,0:T(8,128)(2,1)S(1)} %get-tuple-element.58.turned_ref), custom_call_target="tpu_custom_call" | custom-call | bytes 65536000 | tf_op jit(solution)/shard_map/pack_queries/pallas_call | solution.py:523
  20.5 6.0 %all-to-all-start.1 = ((bf16[16,400,128]{2,1,0:T(8,128)(2,1)}), bf16[16,400,128]{2,1,0:T(8,128)(2,1)S(1)}, u32[]{:S(2)}, u32[]{:S(2)}) async-start(bf16[16,400,128]{2,1,0:T(8,128)(2,1)} %bitcast.19), calls=%async_computation.1 | async-start | bytes 3276800 | tf_op jit(solution)/shard_map/all_to_all | solution.py:533
  26.5 0.0 copy-start.1
  26.5 0.0 copy-start.2
  26.5 0.0 copy-start.3
  26.5 0.0 copy-start.5
  26.6 3.9 %project_keys.1 = (bf16[512,512]{1,0:T(8,128)(2,1)}, bf16[512,512]{1,0:T(8,128)(2,1)}) custom-call(bf16[512,1024]{1,0:T(8,128)(2,1)} %get-tuple-element.61.normed_ref, bf16[1024,512]{1,0:T(8,128)(2,1)} %wk_ref.1, bf16[1024,512]{1,0:T(8,128)(2,1)} %wv_ref.1), custom_call_target="tpu_custom_call" | custom-call | flops 21474836480 | bytes 62914560 | tf_op jit(solution)/shard_map/project_keys/pallas_call | solution.py:547
  30.5 23.3 %update_memory.1 = (f32[16,4,128,128]{3,2,1,0:T(8,128)}, f32[16,4,128,128]{3,2,1,0:T(8,128)}) custom-call(s32[8,16]{1,0:T(8,128)S(1)} %bitcast.17, s32[16]{0:T(128)S(1)} %copy-done.5, s32[8,4,16]{2,1,0:T(4,128)S(1)} %bitcast.15, s32[8,4,16]{2,1,0:T(4,128)S(1)} %bitcast.16, bf16[512,512]{1,0:T(8,128)(2,1)} %get-tuple-element.62.k_ref, ...), custom_call_target="tpu_custom_call" | custom-call | flops 18790481920 | bytes 335544320 | tf_op jit(solution)/shard_map/update_memory/pallas_call | solution.py:587
  53.8 2.9 %cut_last.1 = (bf16[192,1408]{1,0:T(8,128)(2,1)}, bf16[576,1408]{1,0:T(8,128)(2,1)S(1)}) custom-call(s32[3]{0:T(128)S(1)} %pad_add_fusion.side, bf16[2,1024,1408]{2,1,0:T(8,128)(2,1)} %gate_up_w.4), custom_call_target="tpu_custom_call" | custom-call | bytes 86507520 | tf_op jit(solution)/shard_map/cut_last/pallas_call | solution.py:536
  56.7 0.0 collective-permute-done.one_a
  56.7 0.0 collective-permute-done.1.one_q
  56.7 1.6 %collective-permute-start.2 = (bf16[192,1408]{1,0:T(8,128)(2,1)}, bf16[192,1408]{1,0:T(8,128)(2,1)}, u32[]{:S(2)}, u32[]{:S(2)}) collective-permute-start(bf16[192,1408]{1,0:T(8,128)(2,1)} %get-tuple-element.74), channel_id=1, source_target_pairs={{0,1},{1,0},{2,3},{3,2},{4,5},{5,4},{6,7},{7,6},{8,9},{9,8},{10,11... | collective-permute-start | bytes 1622024 | tf_op jit(solution)/shard_map/ppermute | solution.py:622
  58.3 1.4 all-to-all-done.1
  59.6 7.2 %page_attention.1 = bf16[6400,128]{1,0:T(8,128)(2,1)} custom-call(bf16[6400,128]{1,0:T(8,128)(2,1)S(1)} %bitcast.14, bf16[48,2,128,512]{3,2,1,0:T(8,128)(2,1)} %kv_hbm.1), custom_call_target="tpu_custom_call" | custom-call | flops 8053063680 | bytes 317194240 | tf_op jit(solution)/shard_map/page_attention/pallas_call | solution.py:630
  66.9 3.8 %collective-permute-done.2.one_m = bf16[192,1408]{1,0:T(8,128)(2,1)} collective-permute-done((bf16[192,1408]{1,0:T(8,128)(2,1)}, bf16[192,1408]{1,0:T(8,128)(2,1)}, u32[]{:S(2)}, u32[]{:S(2)}) %collective-permute-start.2) | collective-permute-done | bytes 540704 | tf_op jit(solution)/shard_map/ppermute | solution.py:622
  70.7 5.6 %all-to-all-start.2 = ((bf16[16,400,128]{2,1,0:T(8,128)(2,1)}), bf16[16,400,128]{2,1,0:T(8,128)(2,1)S(1)}, u32[]{:S(2)}, u32[]{:S(2)}) async-start(bf16[16,400,128]{2,1,0:T(8,128)(2,1)} %bitcast.20), calls=%async_computation.2 | async-start | bytes 3276800 | tf_op jit(solution)/shard_map/all_to_all | solution.py:655
  76.3 1.6 %collective-permute-start.3 = (bf16[576,1408]{1,0:T(8,128)(2,1)S(1)}, bf16[576,1408]{1,0:T(8,128)(2,1)S(1)}, u32[]{:S(2)}, u32[]{:S(2)}) collective-permute-start(bf16[576,1408]{1,0:T(8,128)(2,1)S(1)} %get-tuple-element.76), channel_id=1, source_target_pairs={{0,1},{1,0},{2,3},{3,2},{4,5},{5,4},{6,7},{7,6},{8,9},{9,8},{10,11... | collective-permute-start | bytes 4866056 | tf_op jit(solution)/shard_map/ppermute | solution.py:623
  77.8 1.9 %collective-permute-start.7 = (bf16[480,1024]{1,0:T(8,128)(2,1)}, bf16[480,1024]{1,0:T(8,128)(2,1)S(1)}, u32[]{:S(2)}, u32[]{:S(2)}) collective-permute-start(bf16[480,1024]{1,0:T(8,128)(2,1)} %collective-permute-done.1.one_q), channel_id=1, source_target_pairs={{0,4},{2,6},{4,0},{6,2},{8,12},{10,14},{12,8},{14,10},{16,20},{18,... | collective-permute-start | bytes 2949128 | tf_op jit(solution)/shard_map/ppermute | solution.py:624
  79.7 0.0 collective-permute-start.6
  79.7 0.5 collective-permute-start.4
  80.2 0.0 collective-permute-start.5
  80.3 18.2 %local_attention.1 = (f32[2048,128]{1,0:T(8,128)}, f32[2048,128]{1,0:T(8,128)}, f32[16,128]{1,0:T(8,128)S(1)}, f32[16,128]{1,0:T(8,128)S(1)}) custom-call(bf16[512,512]{1,0:T(8,128)(2,1)} %get-tuple-element.80.q_ref, bf16[512,512]{1,0:T(8,128)(2,1)} %get-tuple-element.62.k_ref, bf16[512,512]{1,0:T(8,128)(2,1)} %get-tuple-element.63.v_ref, ...), custom_call_target="tpu_custom_call" | custom-call | flops 20 | bytes 20 | tf_op jit(solution)/shard_map/local_attention/pallas_call | solution.py:563
  98.4 0.0 collective-permute-done.4.two_a
  98.4 19.6 %collective-permute-done.7.three_q = bf16[480,1024]{1,0:T(8,128)(2,1)S(1)} collective-permute-done((bf16[480,1024]{1,0:T(8,128)(2,1)}, bf16[480,1024]{1,0:T(8,128)(2,1)S(1)}, u32[]{:S(2)}, u32[]{:S(2)}) %collective-permute-start.7) | collective-permute-done | bytes 983072 | tf_op jit(solution)/shard_map/ppermute | solution.py:624
  118.0 0.0 collective-permute-done.6.two_q
  118.0 0.0 collective-permute-done.3.one_b
  118.0 1.0 copy-done.7
  119.1 0.2 copy-done.8
  119.3 1.2 copy-done.6
  120.5 0.0 collective-permute-done.5.two_m
  120.5 0.0 all-to-all-done.2
  120.5 0.0 collective-permute-start.8
  120.5 0.5 collective-permute-start.9
  121.0 4.1 %combine.1 = (bf16[256,512]{1,0:T(8,128)(2,1)S(1)}, bf16[256,512]{1,0:T(8,128)(2,1)S(1)}) custom-call(s32[16,1,3]{2,1,0:T(1,128)S(1)} %all-to-all-done.codes, s32[3]{0:T(128)S(1)} %pad_add_fusion.side, bf16[6400,128]{1,0:T(8,128)(2,1)S(1)} %bitcast.13, f32[2048,128]{1,0:T(8,128)} %get-tuple-element.86.o_hbm, f32[2048,128]{1,0:T(8,128)} %get-tuple-element.87.ret_hbm, ...), custom_call_target="tpu_custom_call" | custom-call | flops 125829120 | bytes 74711040 | tf_op jit(solution)/shard_map/combine/pallas_call | solution.py:665
  125.1 1.6 %collective-permute-start.10 = (bf16[256,512]{1,0:T(8,128)(2,1)S(1)}, bf16[256,512]{1,0:T(8,128)(2,1)S(1)}, u32[]{:S(2)}, u32[]{:S(2)}) collective-permute-start(bf16[256,512]{1,0:T(8,128)(2,1)S(1)} %get-tuple-element.96), channel_id=1, source_target_pairs={{0,1},{1,0},{2,3},{3,2},{4,5},{5,4},{6,7},{7,6},{8,9},{9,8},{10,11... | collective-permute-start | bytes 786440 | tf_op jit(solution)/shard_map/ppermute | solution.py:694
  126.7 0.0 copy-start.4
  126.7 6.5 %stage_weights.1 = (bf16[2,512,1024]{2,1,0:T(8,128)(2,1)S(1)}, bf16[2,2,1024,1408]{3,2,1,0:T(8,128)(2,1)S(1)}, bf16[2,1408,1024]{2,1,0:T(8,128)(2,1)S(1)}) custom-call(s32[3]{0:T(128)S(1)} %pad_add_fusion.side, bf16[512,1024]{1,0:T(8,128)(2,1)} %out_w.3, bf16[2,1024,1408]{2,1,0:T(8,128)(2,1)} %gate_up_w.4, bf16[1408,1024]{1,0:T(8,128)(2,1)} %down_w.3, ...), custom_call_target="tpu_custom_call" | custom-call | bytes 387973120 | tf_op jit(solution)/shard_map/stage_weights/pallas_call | solution.py:698
  133.2 0.3 collective-permute-done.10.theirs_ref
  133.4 7.3 %feed_forward.1 = bf16[256,1024]{1,0:T(8,128)(2,1)} custom-call(s32[3]{0:T(128)S(1)} %pad_add_fusion.side, bf16[512,1024]{1,0:T(8,128)(2,1)S(1)} %copy-done, bf16[256,512]{1,0:T(8,128)(2,1)S(1)} %get-tuple-element.95.mine_ref, bf16[256,512]{1,0:T(8,128)(2,1)S(1)} %collective-permute-done.10.theirs_ref, f32[1,1024]{1,0:T(1,128)S(1)} %bitcast.18, ...), custom_call_target="tpu_custom_call" | custom-call | flops 99321118720 | bytes 387973120 | tf_op jit(solution)/shard_map/feed_forward/pallas_call | solution.py:718
  (14 shorter events, 0.0 us)
Async XLA Ops:
  2.0 16.0 %all-to-all-start = ((s32[16,1,3]{2,1,0:T(1,128)}), s32[16,1,3]{2,1,0:T(1,128)S(1)}, u32[]{:S(2)}, u32[]{:S(2)}) async-start(s32[16,1,3]{2,1,0:T(1,128)} %bitcast.3), calls=%async_computation | async-start | bytes 16384 | tf_op jit(solution)/shard_map/all_to_all | solution.py:478
  15.9 40.8 %collective-permute-start = (bf16[256,1408]{1,0:T(8,128)(2,1)}, bf16[256,1408]{1,0:T(8,128)(2,1)}, u32[]{:S(2)}, u32[]{:S(2)}) collective-permute-start(bf16[256,1408]{1,0:T(8,128)(2,1)} %get-tuple-element.69), channel_id=1, source_target_pairs={{0,1},{1,0},{2,3},{3,2},{4,5},{5,4},{6,7},{7,6},{8,9},{9,8},{10,11... | collective-permute-start | bytes 2162696 | tf_op jit(solution)/shard_map/ppermute | solution.py:520
  17.5 39.2 %collective-permute-start.1 = (bf16[480,1024]{1,0:T(8,128)(2,1)}, bf16[480,1024]{1,0:T(8,128)(2,1)}, u32[]{:S(2)}, u32[]{:S(2)}) collective-permute-start(bf16[480,1024]{1,0:T(8,128)(2,1)} %get-tuple-element.70), channel_id=1, source_target_pairs={{0,1},{1,0},{2,3},{3,2},{4,5},{5,4},{6,7},{7,6},{8,9},{9,8},{10,11... | collective-permute-start | bytes 2949128 | tf_op jit(solution)/shard_map/ppermute | solution.py:521
  20.5 39.1 %all-to-all-start.1 = ((bf16[16,400,128]{2,1,0:T(8,128)(2,1)}), bf16[16,400,128]{2,1,0:T(8,128)(2,1)S(1)}, u32[]{:S(2)}, u32[]{:S(2)}) async-start(bf16[16,400,128]{2,1,0:T(8,128)(2,1)} %bitcast.19), calls=%async_computation.1 | async-start | bytes 3276800 | tf_op jit(solution)/shard_map/all_to_all | solution.py:533
  26.5 4.0 %copy-start.1 = (s32[16,8,4]{0,2,1:T(4,128)S(1)}, s32[16,8,4]{0,2,1:T(4,128)}, u32[]{:S(2)}) copy-start(s32[16,8,4]{0,2,1:T(4,128)} %param.39) | copy-start | bytes 6148
  26.5 4.0 %copy-start.2 = (s32[16,8,4]{0,2,1:T(4,128)S(1)}, s32[16,8,4]{0,2,1:T(4,128)}, u32[]{:S(2)}) copy-start(s32[16,8,4]{0,2,1:T(4,128)} %param.40) | copy-start | bytes 6148
  26.5 3.9 %copy-start.3 = (s32[16,8]{0,1:T(8,128)S(1)}, s32[16,8]{0,1:T(8,128)}, u32[]{:S(2)}) copy-start(s32[16,8]{0,1:T(8,128)} %param.35) | copy-start | bytes 1540
  26.5 3.9 %copy-start.5 = (s32[16]{0:T(128)S(1)}, s32[16]{0:T(128)}, u32[]{:S(2)}) copy-start(s32[16]{0:T(128)} %count.1) | copy-start | bytes 196
  56.7 13.9 %collective-permute-start.2 = (bf16[192,1408]{1,0:T(8,128)(2,1)}, bf16[192,1408]{1,0:T(8,128)(2,1)}, u32[]{:S(2)}, u32[]{:S(2)}) collective-permute-start(bf16[192,1408]{1,0:T(8,128)(2,1)} %get-tuple-element.74), channel_id=1, source_target_pairs={{0,1},{1,0},{2,3},{3,2},{4,5},{5,4},{6,7},{7,6},{8,9},{9,8},{10,11... | collective-permute-start | bytes 1622024 | tf_op jit(solution)/shard_map/ppermute | solution.py:622
  70.7 49.8 %all-to-all-start.2 = ((bf16[16,400,128]{2,1,0:T(8,128)(2,1)}), bf16[16,400,128]{2,1,0:T(8,128)(2,1)S(1)}, u32[]{:S(2)}, u32[]{:S(2)}) async-start(bf16[16,400,128]{2,1,0:T(8,128)(2,1)} %bitcast.20), calls=%async_computation.2 | async-start | bytes 3276800 | tf_op jit(solution)/shard_map/all_to_all | solution.py:655
  76.3 41.8 %collective-permute-start.3 = (bf16[576,1408]{1,0:T(8,128)(2,1)S(1)}, bf16[576,1408]{1,0:T(8,128)(2,1)S(1)}, u32[]{:S(2)}, u32[]{:S(2)}) collective-permute-start(bf16[576,1408]{1,0:T(8,128)(2,1)S(1)} %get-tuple-element.76), channel_id=1, source_target_pairs={{0,1},{1,0},{2,3},{3,2},{4,5},{5,4},{6,7},{7,6},{8,9},{9,8},{10,11... | collective-permute-start | bytes 4866056 | tf_op jit(solution)/shard_map/ppermute | solution.py:623
  77.8 40.2 %collective-permute-start.7 = (bf16[480,1024]{1,0:T(8,128)(2,1)}, bf16[480,1024]{1,0:T(8,128)(2,1)S(1)}, u32[]{:S(2)}, u32[]{:S(2)}) collective-permute-start(bf16[480,1024]{1,0:T(8,128)(2,1)} %collective-permute-done.1.one_q), channel_id=1, source_target_pairs={{0,4},{2,6},{4,0},{6,2},{8,12},{10,14},{12,8},{14,10},{16,20},{18,... | collective-permute-start | bytes 2949128 | tf_op jit(solution)/shard_map/ppermute | solution.py:624
  79.7 38.3 %collective-permute-start.6 = (bf16[480,1024]{1,0:T(8,128)(2,1)}, bf16[480,1024]{1,0:T(8,128)(2,1)S(1)}, u32[]{:S(2)}, u32[]{:S(2)}) collective-permute-start(bf16[480,1024]{1,0:T(8,128)(2,1)} %collective-permute-done.1.one_q), channel_id=1, source_target_pairs={{0,2},{2,0},{4,6},{6,4},{8,10},{10,8},{12,14},{14,12},{16,18},{18,... | collective-permute-start | bytes 2949128 | tf_op jit(solution)/shard_map/ppermute | solution.py:626
  79.7 18.7 %collective-permute-start.4 = (bf16[256,1408]{1,0:T(8,128)(2,1)}, bf16[256,1408]{1,0:T(8,128)(2,1)S(1)}, u32[]{:S(2)}, u32[]{:S(2)}) collective-permute-start(bf16[256,1408]{1,0:T(8,128)(2,1)} %collective-permute-done.one_a), channel_id=1, source_target_pairs={{0,2},{2,0},{4,6},{6,4},{8,10},{10,8},{12,14},{14,12},{16,18},{18,... | collective-permute-start | bytes 2162696 | tf_op jit(solution)/shard_map/ppermute | solution.py:625
  80.2 40.2 %collective-permute-start.5 = (bf16[192,1408]{1,0:T(8,128)(2,1)}, bf16[192,1408]{1,0:T(8,128)(2,1)}, u32[]{:S(2)}, u32[]{:S(2)}) collective-permute-start(bf16[192,1408]{1,0:T(8,128)(2,1)} %collective-permute-done.2.one_m), channel_id=1, source_target_pairs={{0,2},{2,0},{4,6},{6,4},{8,10},{10,8},{12,14},{14,12},{16,18},{18,... | collective-permute-start | bytes 1622024 | tf_op jit(solution)/shard_map/ppermute | solution.py:654
  98.4 19.6 %copy-start.9 = (bf16[256,1408]{1,0:T(8,128)(2,1)}, bf16[256,1408]{1,0:T(8,128)(2,1)S(1)}, u32[]{:S(2)}) copy-start(bf16[256,1408]{1,0:T(8,128)(2,1)S(1)} %collective-permute-done.4.two_a) | copy-start | bytes 2162692
  118.0 1.1 copy-start.7
  118.0 1.3 copy-start.8
  119.3 1.2 copy-start.6
  120.5 6.2 %collective-permute-start.8 = (bf16[576,1408]{1,0:T(8,128)(2,1)}, bf16[576,1408]{1,0:T(8,128)(2,1)S(1)}, u32[]{:S(2)}, u32[]{:S(2)}) collective-permute-start(bf16[576,1408]{1,0:T(8,128)(2,1)} %copy-done.6), channel_id=1, source_target_pairs={{0,2},{2,0},{4,6},{6,4},{8,10},{10,8},{12,14},{14,12},{16,18},{18,... | collective-permute-start | bytes 4866056 | tf_op jit(solution)/shard_map/ppermute | solution.py:662
  120.5 6.2 %collective-permute-start.9 = (bf16[480,1024]{1,0:T(8,128)(2,1)}, bf16[480,1024]{1,0:T(8,128)(2,1)S(1)}, u32[]{:S(2)}, u32[]{:S(2)}) collective-permute-start(bf16[480,1024]{1,0:T(8,128)(2,1)} %copy-done.7), channel_id=1, source_target_pairs={{0,2},{2,0},{4,6},{6,4},{8,10},{10,8},{12,14},{14,12},{16,18},{18,... | collective-permute-start | bytes 2949128 | tf_op jit(solution)/shard_map/ppermute | solution.py:663
  125.1 8.3 %collective-permute-start.10 = (bf16[256,512]{1,0:T(8,128)(2,1)S(1)}, bf16[256,512]{1,0:T(8,128)(2,1)S(1)}, u32[]{:S(2)}, u32[]{:S(2)}) collective-permute-start(bf16[256,512]{1,0:T(8,128)(2,1)S(1)} %get-tuple-element.96), channel_id=1, source_target_pairs={{0,1},{1,0},{2,3},{3,2},{4,5},{5,4},{6,7},{7,6},{8,9},{9,8},{10,11... | collective-permute-start | bytes 786440 | tf_op jit(solution)/shard_map/ppermute | solution.py:694
  126.7 6.8 %copy-start = (bf16[512,1024]{1,0:T(8,128)(2,1)S(1)}, bf16[512,1024]{1,0:T(8,128)(2,1)}, u32[]{:S(2)}) copy-start(bf16[512,1024]{1,0:T(8,128)(2,1)} %tok_ref.3) | copy-start | bytes 3145732
  126.7 6.8 %copy-start.4 = (f32[1024]{0:T(1024)S(1)}, f32[1024]{0:T(1024)}, u32[]{:S(2)}) copy-start(f32[1024]{0:T(1024)} %param.41) | copy-start | bytes 12292

commit v8 on v7

--- a/solution.py
+++ b/solution.py
@@ -89,9 +89,13 @@
     v_ref[...] = jnp.dot(normed, wv_ref[...], preferred_element_type=F32).astype(BF16)
 
 
-def pack_queries(codes, lengths, turned_ref, out_ref, *, n, cap, reqs, page_len):
+def pack_queries(codes, lengths, turned_ref, out_hbm, out_ref, sems, *, n, cap, reqs, page_len):
     block = cap * HD + EXTRA
     row_id = lax.broadcasted_iota(jnp.int32, (EXTRA, LANES), 0)
+
+    def departure(d):
+        rows = pl.ds(pl.multiple_of(d * block, EXTRA), block)
+        return pltpu.make_async_copy(out_ref.at[rows], out_hbm.at[rows], sems.at[d])
 
     def one(d, carry):
         base = pl.multiple_of(d * block, EXTRA)
@@ -105,9 +109,12 @@
             rows = pl.ds(pl.multiple_of(r * HD, HD), HD)
             out_ref[pl.ds(base + c * HD, HD), :] = turned_ref[rows, :]
         out_ref[pl.ds(base + cap * HD, EXTRA), :] = tail.astype(BF16)
+        departure(d).start()
         return carry
 
     lax.fori_loop(0, n, one, 0)
+    for d in range(n):
+        departure(d).wait()
 
 
 def page_attention(
@@ -359,15 +366,22 @@
     return copies
 
 
-def cut_first(side, gate_up_w, down_w, out_w, first_ref, quarter_ref, sems):
+def cut_first(side, gate_up_w, down_w, out_w, first_ref, near_ref, far_ref, sems):
     depth, width = down_w.shape[0] // 4, out_w.shape[0] // 4
-    down_rows = pl.ds(pl.multiple_of(side[2] * depth, EXTRA), depth)
+    near = near_ref.shape[0]
+    base = pl.multiple_of(side[2] * depth, EXTRA)
     out_rows = pl.ds(pl.multiple_of(side[2] * width, EXTRA), width)
     pairs = [
-        (gate_up_w.at[side[1], pl.ds(0, first_ref.shape[0])], first_ref),
-        (down_w.at[down_rows], quarter_ref.at[pl.ds(0, depth)]),
-        (out_w.at[out_rows], quarter_ref.at[pl.ds(depth, width)]),
+        (out_w.at[out_rows], far_ref.at[pl.ds(depth - near, width)]),
+        (down_w.at[pl.ds(base + near, depth - near)], far_ref.at[pl.ds(0, depth - near)]),
     ]
+    step = near // 3
+    for i in range(3):
+        pairs.append((down_w.at[pl.ds(base + i * step, step)], near_ref.at[pl.ds(i * step, step)]))
+    step = first_ref.shape[0] // 4
+    for i in range(4):
+        rows = pl.ds(i * step, step)
+        pairs.append((gate_up_w.at[side[1], rows], first_ref.at[rows]))
     for copy in run_copies(pairs, sems):
         copy.wait()
 
@@ -385,8 +399,8 @@
 
 
 def stage_weights(
-    side, out_w, gate_up_w, down_w, one_a, one_m, one_b, one_q, two_a, two_m, two_b, two_q, three_q,
-    four_q, out_all, gate_up_all, down_all, sems,
+    side, out_w, gate_up_w, down_w, one_a, one_m, one_b, one_q, one_r, two_a, two_m, two_q, two_r,
+    three_q, three_r, four_q, two_b, four_r, out_all, gate_up_all, down_all, sems,
 ):
     width, depth = out_w.shape[0] // 4, down_w.shape[0] // 4
     pairs = [(gate_up_w, gate_up_all.at[0]), (down_w, down_all.at[0]), (out_w, out_all.at[0])]
@@ -396,14 +410,17 @@
             pairs.append((part, gate_up_all.at[1, half, pl.ds(at, part.shape[0])]))
             at += part.shape[0]
     core, chip = side[1], side[2] // 2
-    for x, y, q in ((core, chip, one_q), (1 - core, chip, two_q), (core, 1 - chip, three_q), (
-        1 - core, 1 - chip, four_q,
-    )):
-        part = 2 * y + x
-        units = pl.ds(pl.multiple_of(part * depth, EXTRA), depth)
-        rows = pl.ds(pl.multiple_of(part * width, EXTRA), width)
-        pairs.append((q.at[pl.ds(0, depth)], down_all.at[1, units]))
-        pairs.append((q.at[pl.ds(depth, width)], out_all.at[1, rows]))
+    near = one_q.shape[0]
+    places = ((core, chip), (1 - core, chip), (core, 1 - chip), (1 - core, 1 - chip))
+    got = ((one_q, one_r), (two_q, two_r), (three_q, three_r), (four_q, four_r))
+    for (x, y), (q, r) in zip(places, got):
+        base = pl.multiple_of((2 * y + x) * depth, EXTRA)
+        rows = pl.ds(pl.multiple_of((2 * y + x) * width, EXTRA), width)
+        pairs.append((q, down_all.at[1, pl.ds(base, near)]))
+        pairs.append(
+            (r.at[pl.ds(0, depth - near)], down_all.at[1, pl.ds(base + near, depth - near)])
+        )
+        pairs.append((r.at[pl.ds(depth - near, width)], out_all.at[1, rows]))
     for copy in run_copies(pairs, sems):
         copy.wait()
 
@@ -480,19 +497,24 @@
     grp = lax.axis_size("grp")
     depth, out_depth = w_down.shape[0] // 4, width // 4
     first, middle = model // 4, model * 3 // 16
-    split = (depth, out_depth, first, middle, (model - first - middle) // 3)
+    near = (depth + out_depth) // 2 // 48 * 48
+    split = (depth, out_depth, first // 4, middle, (model - first - middle) // 3)
     pieces = 2 if grp == 2 and n % 4 == 0 and not any(size % EXTRA for size in split) else 1
     quarter = lax.rem(lax.axis_index("req"), 4)
     core = lax.rem(quarter, 2)
     side = jnp.stack([lax.axis_index("grp"), core, quarter]).astype(jnp.int32)
     if pieces == 2:
         units = w_down.shape[0]
-        half_first, quarters = pl.pallas_call(
+        half_first, near_part, far_part = pl.pallas_call(
             cut_first,
-            out_shape=(VMEM((first, units), BF16), VMEM((depth + out_depth, model), BF16)),
+            out_shape=(
+                VMEM((first, units), BF16),
+                VMEM((near, model), BF16),
+                VMEM((depth + out_depth - near, model), BF16),
+            ),
             in_specs=[whole(SMEM)] + [whole(HBM)] * 3,
-            out_specs=(whole(),) * 2,
-            scratch_shapes=[pltpu.SemaphoreType.DMA((3,))],
+            out_specs=(whole(),) * 3,
+            scratch_shapes=[pltpu.SemaphoreType.DMA((9,))],
             compiler_params=params(4),
             cost_estimate=cost(0, 4 * (first * units + (depth + out_depth) * model)),
             name="cut_first",
@@ -515,16 +537,23 @@
     )(*keep_in(HBM, tokens, norm_attn.reshape(1, -1), w_query))
 
     if pieces == 2:
-        turned, half_first, quarters = lax.optimization_barrier((turned, half_first, quarters))
+        turned, half_first, near_part, far_part = lax.optimization_barrier(
+            (turned, half_first, near_part, far_part)
+        )
         swap = [(0, 1), (1, 0)]
         one_a = lax.ppermute(half_first, "grp", swap)
-        one_q = lax.ppermute(quarters, "grp", swap)
+        one_q = lax.ppermute(near_part, "grp", swap)
+        one_r = lax.ppermute(far_part, "grp", swap)
 
     packed = pl.pallas_call(
         functools.partial(pack_queries, n=n, cap=cap, reqs=reqs, page_len=page_len),
         out_shape=HBM((n * ask_block, LANES), BF16),
         in_specs=[whole(SMEM), whole(SMEM), whole()],
-        out_specs=whole(),
+        out_specs=whole(HBM),
+        scratch_shapes=[
+            pltpu.VMEM((n * ask_block, LANES), BF16),
+            pltpu.SemaphoreType.DMA((n,)),
+        ],
         compiler_params=params(8),
         cost_estimate=cost(0, 4 * n * ask_block * LANES),
         name="pack_queries",
@@ -614,16 +643,17 @@
     )
 
     if pieces == 2:
-        memory_out, momentum_out, half_mid, half_last, one_a, one_q = lax.optimization_barrier(
-            (memory_out, momentum_out, half_mid, half_last, one_a, one_q)
+        memory_out, momentum_out, half_mid, half_last, one_a, one_q, one_r = (
+            lax.optimization_barrier(
+                (memory_out, momentum_out, half_mid, half_last, one_a, one_q, one_r)
+            )
         )
         other_core = [(i, i ^ 1) for i in range(n)]
         other_chip = [(i, i ^ 2) for i in range(n)]
         one_m = lax.ppermute(half_mid, "grp", swap)
         one_b = lax.ppermute(half_last, "grp", swap)
         three_q = lax.ppermute(one_q, "req", other_chip)
-        two_a = lax.ppermute(one_a, "req", other_core)
-        two_q = lax.ppermute(one_q, "req", other_core)
+        three_r = lax.ppermute(one_r, "req", other_chip)
     asked, memory_out, momentum_out, keys, values = lax.optimization_barrier(
         (asked, memory_out, momentum_out, keys, values)
     )
@@ -650,17 +680,22 @@
         name="page_attention",
     )(asked, *keep_in(HBM, kv_cache))
     if pieces == 2:
-        answers, one_m = lax.optimization_barrier((answers, one_m))
-        two_m = lax.ppermute(one_m, "req", other_core)
+        answers, one_m, three_q = lax.optimization_barrier((answers, one_m, three_q))
+        own, one_a, one_m, one_q, one_r, three_q = lax.optimization_barrier(
+            (own, one_a, one_m, one_q, one_r, three_q)
+        )
+        two_a, two_m, two_q, two_r, four_q = (
+            lax.ppermute(part, "req", other_core) for part in (one_a, one_m, one_q, one_r, three_q)
+        )
     returned = lax.all_to_all(answers, "req", split_axis=0, concat_axis=0, tiled=True)
     if pieces == 2:
-        returned, one_b, two_a, two_m, two_q, three_q, own, retrieved, own_top, own_sum = (
+        returned, one_b, two_a, two_m, two_q, four_q, two_r, three_r, own, retrieved = (
             lax.optimization_barrier(
-                (returned, one_b, two_a, two_m, two_q, three_q, own, retrieved, own_top, own_sum)
+                (returned, one_b, two_a, two_m, two_q, four_q, two_r, three_r, own, retrieved)
             )
         )
         two_b = lax.ppermute(one_b, "req", other_core)
-        four_q = lax.ppermute(three_q, "req", other_core)
+        four_r = lax.ppermute(three_r, "req", other_core)
     rows = group_rows // grp
     mixed = pl.pallas_call(
         functools.partial(
@@ -692,9 +727,7 @@
     if pieces == 2:
         mine, asked_for = mixed
         theirs = lax.ppermute(asked_for, "grp", swap)
-        mine, two_a, two_b, two_q, four_q = lax.optimization_barrier(
-            (mine, two_a, two_b, two_q, four_q)
-        )
+        mine, two_b, four_r = lax.optimization_barrier((mine, two_b, four_r))
         out_near, gate_up_near, down_near = pl.pallas_call(
             stage_weights,
             out_shape=(
@@ -702,18 +735,20 @@
                 VMEM((2,) + w_gate_up.shape, BF16),
                 VMEM((2,) + w_down.shape, BF16),
             ),
-            in_specs=[whole(SMEM)] + [whole(pl.ANY)] * 13,
+            in_specs=[whole(SMEM)] + [whole(pl.ANY)] * 17,
             out_specs=(whole(),) * 3,
-            scratch_shapes=[pltpu.SemaphoreType.DMA((17,))],
+            scratch_shapes=[pltpu.SemaphoreType.DMA((21,))],
             compiler_params=params(2),
             cost_estimate=cost(0, 2 * model * (2 * width + 6 * units)),
             name="stage_weights",
         )(
             side,
-            *keep_in(HBM, w_out, w_gate_up, w_down, one_a, one_m, one_b, one_q, two_a, two_m),
+            *keep_in(
+                HBM, w_out, w_gate_up, w_down, one_a, one_m, one_b, one_q, one_r, two_a, two_m, two_q,
+                two_r, three_q, three_r, four_q,
+            ),
             two_b,
-            *keep_in(HBM, two_q, three_q),
-            four_q,
+            four_r,
         )
         layer_out = pl.pallas_call(
             feed_forward,

time: 142 us -> 140 us (0.986)
  Pallas kernels: 82.3 us -> 80.6 us
  local copies, waits for them, and re-layouts: 3.15 us -> 1.64 us
    ppermute x1, waiting for transfers between devices: 19.6 us -> 3.78 us  [on_device(): three_q = lax.ppermute(one_q, 'req', other_chip)]
    ppermute x1, waiting for transfers between devices: 0.01 us -> 10.8 us  [on_device(): one_b = lax.ppermute(half_last, 'grp', swap)]
    ppermute x5 -> x9, waiting for transfers between devices: 0.01 us -> 7.84 us  [the longest x1 5.79 us: on_device(): three_r = lax.ppermute(one_r, 'req', other_chip)]
    ppermute x1, waiting for transfers between devices: 3.8 us -> 0.01 us  [on_device(): one_m = lax.ppermute(half_mid, 'grp', swap)]
    ppermute x5 -> x9, starting transfers between devices: 1.55 us -> 4.98 us  [the longest x1 1.91 us: on_device(): three_r = lax.ppermute(one_r, 'req', other_chip)]
    pallas_call x1, Pallas kernels: 23.3 us -> 21.6 us  [on_device(): pl.pallas_call(functools.partial(update_memory, reqs=reqs, draft=draft, h...]
    unnamed x20 -> x24, local copies, waits for them, and re-layouts: 2.46 us -> 0.95 us
  transfers between devices with their start and end apart: 14 -> 18, of which waited for: 4 -> 6; matrix products, arithmetic and copies ran while one was open for 0% -> 0% of each run, Pallas kernels for 53% -> 53%
where the time goes in v8:
time: 140 us; the launch traced here: 139 us
  Pallas kernels  80.6 us (58%)
  starting transfers between devices  29.5 us (21%)
  waiting for transfers between devices  25.5 us (18%)
  local copies, waits for them, and re-layouts  1.64 us (1%)
    pallas_call x1, Pallas kernels, on_device(): pl.pallas_call(functools.partial(update_memory, reqs=reqs, draft=draft, h...  21.6 us
    pallas_call x1, Pallas kernels, on_device(): pl.pallas_call(functools.partial(local_attention, heads=heads, draft=draf...  18.2 us
    ppermute x1, waiting for transfers between devices, on_device(): one_b = lax.ppermute(half_last, 'grp', swap)  10.8 us
    all_to_all x1, starting transfers between devices, on_device(): lax.all_to_all(label, 'req', split_axis=0, concat_axis=0, tiled=True)  7.39 us
    pallas_call x1, Pallas kernels, on_device(): pl.pallas_call(functools.partial(page_attention, n=n, cap=cap, draft=draf...  7.23 us
    pallas_call x1, Pallas kernels, on_device(): pl.pallas_call(feed_forward, out_shape=jax.ShapeDtypeStruct((rows, model)...  7.19 us
    pallas_call x1, Pallas kernels, on_device(): pl.pallas_call(stage_weights, out_shape=(VMEM((2,) + w_out.shape, BF16),...  6.71 us
    all_to_all x1, starting transfers between devices, on_device(): lax.all_to_all(packed, 'req', split_axis=0, concat_axis=0, tiled=True)  6.01 us
  transfers between devices with their start and end apart: 18, of which 6 were waited for; matrix products, arithmetic and copies ran while one was open for 0% of the time, Pallas kernels for 53%

profile of v8, /device:TPU:0, one launch (start us, length us, event | category | flops | bytes accessed | tf_op | source)
XLA Modules:
  0.0 138.8 jit_solution(6625093031864425959)
XLA Ops:
  0.6 0.7 fusion.1
  1.3 0.7 reshape.19
  2.0 7.4 %all-to-all-start = ((s32[16,1,3]{2,1,0:T(1,128)}), s32[16,1,3]{2,1,0:T(1,128)S(1)}, u32[]{:S(2)}, u32[]{:S(2)}) async-start(s32[16,1,3]{2,1,0:T(1,128)} %bitcast.3), calls=%async_computation | async-start | bytes 16384 | tf_op jit(solution)/shard_map/all_to_all | solution.py:495
  9.4 0.1 pad_add_fusion.side
  9.5 3.3 %project_queries.1 = (bf16[512,1024]{1,0:T(8,128)(2,1)}, bf16[512,512]{1,0:T(8,128)(2,1)}, bf16[2048,128]{1,0:T(8,128)(2,1)S(1)}) custom-call(bf16[512,1024]{1,0:T(8,128)(2,1)} %tok_ref.3, f32[1,1024]{1,0:T(1,128)} %bitcast.21, bf16[1024,512]{1,0:T(8,128)(2,1)} %w_ref.1), custom_call_target="tpu_custom_call" | custom-call | flops 10737418240 | bytes 62914560 | tf_op jit(solution)/shard_map/project_queries/pallas_call | solution.py:523
  12.8 3.3 %cut_first.1 = (bf16[256,1408]{1,0:T(8,128)(2,1)}, bf16[240,1024]{1,0:T(8,128)(2,1)}, bf16[240,1024]{1,0:T(8,128)(2,1)}) custom-call(s32[3]{0:T(128)S(1)} %pad_add_fusion.side, bf16[2,1024,1408]{2,1,0:T(8,128)(2,1)} %gate_up_w.4, bf16[1408,1024]{1,0:T(8,128)(2,1)} %down_w.3, bf16[512,1024]{1,0:T(8,128)(2,1)} %out_w.3), custom_call_target="tpu_custom_call" | custom-call | bytes 68157440 | tf_op jit(solution)/shard_map/cut_first/pallas_call | solution.py:508
  16.0 1.6 %collective-permute-start.1 = (bf16[240,1024]{1,0:T(8,128)(2,1)}, bf16[240,1024]{1,0:T(8,128)(2,1)}, u32[]{:S(2)}, u32[]{:S(2)}) collective-permute-start(bf16[240,1024]{1,0:T(8,128)(2,1)} %get-tuple-element.79), channel_id=1, source_target_pairs={{0,1},{1,0},{2,3},{3,2},{4,5},{5,4},{6,7},{7,6},{8,9},{9,8},{10,11... | collective-permute-start | bytes 1474568 | tf_op jit(solution)/shard_map/ppermute | solution.py:545
  17.6 0.5 collective-permute-start.2
  18.1 1.5 %collective-permute-start = (bf16[256,1408]{1,0:T(8,128)(2,1)}, bf16[256,1408]{1,0:T(8,128)(2,1)}, u32[]{:S(2)}, u32[]{:S(2)}) collective-permute-start(bf16[256,1408]{1,0:T(8,128)(2,1)} %get-tuple-element.78), channel_id=1, source_target_pairs={{0,1},{1,0},{2,3},{3,2},{4,5},{5,4},{6,7},{7,6},{8,9},{9,8},{10,11... | collective-permute-start | bytes 2162696 | tf_op jit(solution)/shard_map/ppermute | solution.py:544
  19.6 2.2 %pack_queries.1 = bf16[6400,128]{1,0:T(8,128)(2,1)} custom-call(s32[16,1,3]{2,1,0:T(1,128)S(1)} %all-to-all-done.codes, s32[16]{0:T(128)} %lengths.1, bf16[2048,128]{1,0:T(8,128)(2,1)S(1)} %get-tuple-element.67.turned_ref), custom_call_target="tpu_custom_call" | custom-call | bytes 65536000 | tf_op jit(solution)/shard_map/pack_queries/pallas_call | solution.py:548
  21.8 6.0 %all-to-all-start.1 = ((bf16[16,400,128]{2,1,0:T(8,128)(2,1)}), bf16[16,400,128]{2,1,0:T(8,128)(2,1)S(1)}, u32[]{:S(2)}, u32[]{:S(2)}) async-start(bf16[16,400,128]{2,1,0:T(8,128)(2,1)} %bitcast.19), calls=%async_computation.1 | async-start | bytes 3276800 | tf_op jit(solution)/shard_map/all_to_all | solution.py:562
  27.8 0.0 copy-start.1
  27.8 0.0 copy-start.2
  27.8 0.0 copy-start.3
  27.8 0.0 copy-start.5
  27.9 4.0 %project_keys.1 = (bf16[512,512]{1,0:T(8,128)(2,1)}, bf16[512,512]{1,0:T(8,128)(2,1)}) custom-call(bf16[512,1024]{1,0:T(8,128)(2,1)} %get-tuple-element.70.normed_ref, bf16[1024,512]{1,0:T(8,128)(2,1)} %wk_ref.1, bf16[1024,512]{1,0:T(8,128)(2,1)} %wv_ref.1), custom_call_target="tpu_custom_call" | custom-call | flops 21474836480 | bytes 62914560 | tf_op jit(solution)/shard_map/project_keys/pallas_call | solution.py:576
  31.9 21.6 %update_memory.1 = (f32[16,4,128,128]{3,2,1,0:T(8,128)}, f32[16,4,128,128]{3,2,1,0:T(8,128)}) custom-call(s32[8,16]{1,0:T(8,128)S(1)} %bitcast.17, s32[16]{0:T(128)S(1)} %copy-done.5, s32[8,4,16]{2,1,0:T(4,128)S(1)} %bitcast.15, s32[8,4,16]{2,1,0:T(4,128)S(1)} %bitcast.16, bf16[512,512]{1,0:T(8,128)(2,1)} %get-tuple-element.71.k_ref, ...), custom_call_target="tpu_custom_call" | custom-call | flops 18790481920 | bytes 335544320 | tf_op jit(solution)/shard_map/update_memory/pallas_call | solution.py:616
  53.4 2.9 %cut_last.1 = (bf16[192,1408]{1,0:T(8,128)(2,1)}, bf16[576,1408]{1,0:T(8,128)(2,1)S(1)}) custom-call(s32[3]{0:T(128)S(1)} %pad_add_fusion.side, bf16[2,1024,1408]{2,1,0:T(8,128)(2,1)} %gate_up_w.4), custom_call_target="tpu_custom_call" | custom-call | bytes 86507520 | tf_op jit(solution)/shard_map/cut_last/pallas_call | solution.py:565
  56.4 0.0 collective-permute-done.one_a
  56.4 1.2 collective-permute-start.4
  57.6 1.5 %collective-permute-start.3 = (bf16[192,1408]{1,0:T(8,128)(2,1)}, bf16[192,1408]{1,0:T(8,128)(2,1)}, u32[]{:S(2)}, u32[]{:S(2)}) collective-permute-start(bf16[192,1408]{1,0:T(8,128)(2,1)} %get-tuple-element.84), channel_id=1, source_target_pairs={{0,1},{1,0},{2,3},{3,2},{4,5},{5,4},{6,7},{7,6},{8,9},{9,8},{10,11... | collective-permute-start | bytes 1622024 | tf_op jit(solution)/shard_map/ppermute | solution.py:653
  59.1 1.9 %all-to-all-done.1 = bf16[16,400,128]{2,1,0:T(8,128)(2,1)S(1)} async-done(((bf16[16,400,128]{2,1,0:T(8,128)(2,1)}), bf16[16,400,128]{2,1,0:T(8,128)(2,1)S(1)}, u32[]{:S(2)}, u32[]{:S(2)}) %all-to-all-start.1) | async-done | bytes 1638432 | tf_op jit(solution)/shard_map/all_to_all | solution.py:562
  61.0 7.2 %page_attention.1 = bf16[6400,128]{1,0:T(8,128)(2,1)} custom-call(bf16[6400,128]{1,0:T(8,128)(2,1)S(1)} %bitcast.14, bf16[48,2,128,512]{3,2,1,0:T(8,128)(2,1)} %kv_hbm.1), custom_call_target="tpu_custom_call" | custom-call | flops 8053063680 | bytes 317194240 | tf_op jit(solution)/shard_map/page_attention/pallas_call | solution.py:660
  68.3 3.8 %collective-permute-done.4.three_q = bf16[240,1024]{1,0:T(8,128)(2,1)} collective-permute-done((bf16[240,1024]{1,0:T(8,128)(2,1)}, bf16[240,1024]{1,0:T(8,128)(2,1)}, u32[]{:S(2)}, u32[]{:S(2)}) %collective-permute-start.4) | collective-permute-done | bytes 491552 | tf_op jit(solution)/shard_map/ppermute | solution.py:655
  72.0 0.0 collective-permute-done.3.one_m
  72.1 5.7 %all-to-all-start.2 = ((bf16[16,400,128]{2,1,0:T(8,128)(2,1)}), bf16[16,400,128]{2,1,0:T(8,128)(2,1)S(1)}, u32[]{:S(2)}, u32[]{:S(2)}) async-start(bf16[16,400,128]{2,1,0:T(8,128)(2,1)} %bitcast.20), calls=%async_computation.2 | async-start | bytes 3276800 | tf_op jit(solution)/shard_map/all_to_all | solution.py:690
  77.7 0.6 collective-permute-start.5
  78.3 1.9 %collective-permute-start.11 = (bf16[240,1024]{1,0:T(8,128)(2,1)}, bf16[240,1024]{1,0:T(8,128)(2,1)S(1)}, u32[]{:S(2)}, u32[]{:S(2)}) collective-permute-start(bf16[240,1024]{1,0:T(8,128)(2,1)} %collective-permute-done.2.one_r), channel_id=1, source_target_pairs={{0,4},{2,6},{4,0},{6,2},{8,12},{10,14},{12,8},{14,10},{16,20},{18,... | collective-permute-start | bytes 1474568 | tf_op jit(solution)/shard_map/ppermute | solution.py:656
  80.2 18.2 %local_attention.1 = (f32[2048,128]{1,0:T(8,128)}, f32[2048,128]{1,0:T(8,128)}, f32[16,128]{1,0:T(8,128)S(1)}, f32[16,128]{1,0:T(8,128)S(1)}) custom-call(bf16[512,512]{1,0:T(8,128)(2,1)} %get-tuple-element.88.q_ref, bf16[512,512]{1,0:T(8,128)(2,1)} %get-tuple-element.71.k_ref, bf16[512,512]{1,0:T(8,128)(2,1)} %get-tuple-element.72.v_ref, ...), custom_call_target="tpu_custom_call" | custom-call | flops 20 | bytes 20 | tf_op jit(solution)/shard_map/local_attention/pallas_call | solution.py:592
  98.4 0.5 collective-permute-start.7
  98.9 0.1 collective-permute-start.8
  98.9 5.8 %collective-permute-done.11.three_r = bf16[240,1024]{1,0:T(8,128)(2,1)S(1)} collective-permute-done((bf16[240,1024]{1,0:T(8,128)(2,1)}, bf16[240,1024]{1,0:T(8,128)(2,1)S(1)}, u32[]{:S(2)}, u32[]{:S(2)}) %collective-permute-start.11) | collective-permute-done | bytes 491552 | tf_op jit(solution)/shard_map/ppermute | solution.py:656
  104.7 0.0 collective-permute-start.9
  104.7 10.8 %collective-permute-done.5.one_b = bf16[576,1408]{1,0:T(8,128)(2,1)S(1)} collective-permute-done((bf16[576,1408]{1,0:T(8,128)(2,1)S(1)}, bf16[576,1408]{1,0:T(8,128)(2,1)S(1)}, u32[]{:S(2)}, u32[]{:S(2)}) %collective-permute-start.5) | collective-permute-done | bytes 1622048 | tf_op jit(solution)/shard_map/ppermute | solution.py:654
  115.6 0.0 copy-start.9
  115.6 2.0 %collective-permute-done.10.two_r = bf16[240,1024]{1,0:T(8,128)(2,1)S(1)} collective-permute-done((bf16[240,1024]{1,0:T(8,128)(2,1)}, bf16[240,1024]{1,0:T(8,128)(2,1)S(1)}, u32[]{:S(2)}, u32[]{:S(2)}) %collective-permute-start.10) | collective-permute-done | bytes 491552 | tf_op jit(solution)/shard_map/ppermute | solution.py:688
  117.7 0.0 collective-permute-done.7.two_m
  117.7 0.9 copy-done.7
  118.6 0.1 collective-permute-start.12
  118.7 0.4 collective-permute-start.13
  119.1 4.1 %combine.1 = (bf16[256,512]{1,0:T(8,128)(2,1)S(1)}, bf16[256,512]{1,0:T(8,128)(2,1)S(1)}) custom-call(s32[16,1,3]{2,1,0:T(1,128)S(1)} %all-to-all-done.codes, s32[3]{0:T(128)S(1)} %pad_add_fusion.side, bf16[6400,128]{1,0:T(8,128)(2,1)S(1)} %bitcast.13, f32[2048,128]{1,0:T(8,128)} %get-tuple-element.102.o_hbm, f32[2048,128]{1,0:T(8,128)} %get-tuple-element.103.ret_hbm, ...), custom_call_target="tpu_custom_call" | custom-call | flops 125829120 | bytes 74711040 | tf_op jit(solution)/shard_map/combine/pallas_call | solution.py:700
  123.2 0.6 collective-permute-start.14
  123.8 0.0 collective-permute-done.12.two_b
  123.8 0.0 copy-start
  123.8 0.0 copy-start.4
  123.8 6.7 %stage_weights.1 = (bf16[2,512,1024]{2,1,0:T(8,128)(2,1)S(1)}, bf16[2,2,1024,1408]{3,2,1,0:T(8,128)(2,1)S(1)}, bf16[2,1408,1024]{2,1,0:T(8,128)(2,1)S(1)}) custom-call(s32[3]{0:T(128)S(1)} %pad_add_fusion.side, bf16[512,1024]{1,0:T(8,128)(2,1)} %out_w.3, bf16[2,1024,1408]{2,1,0:T(8,128)(2,1)} %gate_up_w.4, bf16[1408,1024]{1,0:T(8,128)(2,1)} %down_w.3, ...), custom_call_target="tpu_custom_call" | custom-call | bytes 387973120 | tf_op jit(solution)/shard_map/stage_weights/pallas_call | solution.py:731
  130.6 1.1 collective-permute-done.14.theirs_ref
  131.6 7.2 %feed_forward.1 = bf16[256,1024]{1,0:T(8,128)(2,1)} custom-call(s32[3]{0:T(128)S(1)} %pad_add_fusion.side, bf16[512,1024]{1,0:T(8,128)(2,1)S(1)} %copy-done, bf16[256,512]{1,0:T(8,128)(2,1)S(1)} %get-tuple-element.109.mine_ref, bf16[256,512]{1,0:T(8,128)(2,1)S(1)} %collective-permute-done.14.theirs_ref, f32[1,1024]{1,0:T(1,128)S(1)} %bitcast.18, ...), custom_call_target="tpu_custom_call" | custom-call | flops 99321118720 | bytes 387973120 | tf_op jit(solution)/shard_map/feed_forward/pallas_call | solution.py:753
  (26 shorter events, 0.1 us)
Async XLA Ops:
  2.0 17.6 %all-to-all-start = ((s32[16,1,3]{2,1,0:T(1,128)}), s32[16,1,3]{2,1,0:T(1,128)S(1)}, u32[]{:S(2)}, u32[]{:S(2)}) async-start(s32[16,1,3]{2,1,0:T(1,128)} %bitcast.3), calls=%async_computation | async-start | bytes 16384 | tf_op jit(solution)/shard_map/all_to_all | solution.py:495
  16.0 40.3 %collective-permute-start.1 = (bf16[240,1024]{1,0:T(8,128)(2,1)}, bf16[240,1024]{1,0:T(8,128)(2,1)}, u32[]{:S(2)}, u32[]{:S(2)}) collective-permute-start(bf16[240,1024]{1,0:T(8,128)(2,1)} %get-tuple-element.79), channel_id=1, source_target_pairs={{0,1},{1,0},{2,3},{3,2},{4,5},{5,4},{6,7},{7,6},{8,9},{9,8},{10,11... | collective-permute-start | bytes 1474568 | tf_op jit(solution)/shard_map/ppermute | solution.py:545
  17.6 38.8 %collective-permute-start.2 = (bf16[240,1024]{1,0:T(8,128)(2,1)}, bf16[240,1024]{1,0:T(8,128)(2,1)}, u32[]{:S(2)}, u32[]{:S(2)}) collective-permute-start(bf16[240,1024]{1,0:T(8,128)(2,1)} %get-tuple-element.80), channel_id=1, source_target_pairs={{0,1},{1,0},{2,3},{3,2},{4,5},{5,4},{6,7},{7,6},{8,9},{9,8},{10,11... | collective-permute-start | bytes 1474568 | tf_op jit(solution)/shard_map/ppermute | solution.py:546
  18.1 38.3 %collective-permute-start = (bf16[256,1408]{1,0:T(8,128)(2,1)}, bf16[256,1408]{1,0:T(8,128)(2,1)}, u32[]{:S(2)}, u32[]{:S(2)}) collective-permute-start(bf16[256,1408]{1,0:T(8,128)(2,1)} %get-tuple-element.78), channel_id=1, source_target_pairs={{0,1},{1,0},{2,3},{3,2},{4,5},{5,4},{6,7},{7,6},{8,9},{9,8},{10,11... | collective-permute-start | bytes 2162696 | tf_op jit(solution)/shard_map/ppermute | solution.py:544
  21.8 39.2 %all-to-all-start.1 = ((bf16[16,400,128]{2,1,0:T(8,128)(2,1)}), bf16[16,400,128]{2,1,0:T(8,128)(2,1)S(1)}, u32[]{:S(2)}, u32[]{:S(2)}) async-start(bf16[16,400,128]{2,1,0:T(8,128)(2,1)} %bitcast.19), calls=%async_computation.1 | async-start | bytes 3276800 | tf_op jit(solution)/shard_map/all_to_all | solution.py:562
  27.8 4.0 %copy-start.1 = (s32[16,8,4]{0,2,1:T(4,128)S(1)}, s32[16,8,4]{0,2,1:T(4,128)}, u32[]{:S(2)}) copy-start(s32[16,8,4]{0,2,1:T(4,128)} %param.39) | copy-start | bytes 6148
  27.8 4.0 %copy-start.2 = (s32[16,8,4]{0,2,1:T(4,128)S(1)}, s32[16,8,4]{0,2,1:T(4,128)}, u32[]{:S(2)}) copy-start(s32[16,8,4]{0,2,1:T(4,128)} %param.40) | copy-start | bytes 6148
  27.8 4.0 %copy-start.3 = (s32[16,8]{0,1:T(8,128)S(1)}, s32[16,8]{0,1:T(8,128)}, u32[]{:S(2)}) copy-start(s32[16,8]{0,1:T(8,128)} %param.35) | copy-start | bytes 1540
  27.8 4.0 %copy-start.5 = (s32[16]{0:T(128)S(1)}, s32[16]{0:T(128)}, u32[]{:S(2)}) copy-start(s32[16]{0:T(128)} %count.1) | copy-start | bytes 196
  56.4 15.7 %collective-permute-start.4 = (bf16[240,1024]{1,0:T(8,128)(2,1)}, bf16[240,1024]{1,0:T(8,128)(2,1)}, u32[]{:S(2)}, u32[]{:S(2)}) collective-permute-start(bf16[240,1024]{1,0:T(8,128)(2,1)} %collective-permute-done.1.one_q), channel_id=1, source_target_pairs={{0,4},{2,6},{4,0},{6,2},{8,12},{10,14},{12,8},{14,10},{16,20},{18,... | collective-permute-start | bytes 1474568 | tf_op jit(solution)/shard_map/ppermute | solution.py:655
  57.6 14.5 %collective-permute-start.3 = (bf16[192,1408]{1,0:T(8,128)(2,1)}, bf16[192,1408]{1,0:T(8,128)(2,1)}, u32[]{:S(2)}, u32[]{:S(2)}) collective-permute-start(bf16[192,1408]{1,0:T(8,128)(2,1)} %get-tuple-element.84), channel_id=1, source_target_pairs={{0,1},{1,0},{2,3},{3,2},{4,5},{5,4},{6,7},{7,6},{8,9},{9,8},{10,11... | collective-permute-start | bytes 1622024 | tf_op jit(solution)/shard_map/ppermute | solution.py:653
  72.1 46.6 %all-to-all-start.2 = ((bf16[16,400,128]{2,1,0:T(8,128)(2,1)}), bf16[16,400,128]{2,1,0:T(8,128)(2,1)S(1)}, u32[]{:S(2)}, u32[]{:S(2)}) async-start(bf16[16,400,128]{2,1,0:T(8,128)(2,1)} %bitcast.20), calls=%async_computation.2 | async-start | bytes 3276800 | tf_op jit(solution)/shard_map/all_to_all | solution.py:690
  77.7 37.8 %collective-permute-start.5 = (bf16[576,1408]{1,0:T(8,128)(2,1)S(1)}, bf16[576,1408]{1,0:T(8,128)(2,1)S(1)}, u32[]{:S(2)}, u32[]{:S(2)}) collective-permute-start(bf16[576,1408]{1,0:T(8,128)(2,1)S(1)} %get-tuple-element.87), channel_id=1, source_target_pairs={{0,1},{1,0},{2,3},{3,2},{4,5},{5,4},{6,7},{7,6},{8,9},{9,8},{10,11... | collective-permute-start | bytes 4866056 | tf_op jit(solution)/shard_map/ppermute | solution.py:654
  78.3 26.4 %collective-permute-start.11 = (bf16[240,1024]{1,0:T(8,128)(2,1)}, bf16[240,1024]{1,0:T(8,128)(2,1)S(1)}, u32[]{:S(2)}, u32[]{:S(2)}) collective-permute-start(bf16[240,1024]{1,0:T(8,128)(2,1)} %collective-permute-done.2.one_r), channel_id=1, source_target_pairs={{0,4},{2,6},{4,0},{6,2},{8,12},{10,14},{12,8},{14,10},{16,20},{18,... | collective-permute-start | bytes 1474568 | tf_op jit(solution)/shard_map/ppermute | solution.py:656
  98.4 20.2 %collective-permute-start.6 = (bf16[256,1408]{1,0:T(8,128)(2,1)}, bf16[256,1408]{1,0:T(8,128)(2,1)}, u32[]{:S(2)}, u32[]{:S(2)}) collective-permute-start(bf16[256,1408]{1,0:T(8,128)(2,1)} %collective-permute-done.one_a), channel_id=1, source_target_pairs={{0,2},{2,0},{4,6},{6,4},{8,10},{10,8},{12,14},{14,12},{16,18},{18,... | collective-permute-start | bytes 2162696 | tf_op jit(solution)/shard_map/ppermute | solution.py:688
  98.4 19.3 %collective-permute-start.7 = (bf16[192,1408]{1,0:T(8,128)(2,1)}, bf16[192,1408]{1,0:T(8,128)(2,1)S(1)}, u32[]{:S(2)}, u32[]{:S(2)}) collective-permute-start(bf16[192,1408]{1,0:T(8,128)(2,1)} %collective-permute-done.3.one_m), channel_id=1, source_target_pairs={{0,2},{2,0},{4,6},{6,4},{8,10},{10,8},{12,14},{14,12},{16,18},{18,... | collective-permute-start | bytes 1622024 | tf_op jit(solution)/shard_map/ppermute | solution.py:688
  98.9 16.7 %collective-permute-start.8 = (bf16[240,1024]{1,0:T(8,128)(2,1)}, bf16[240,1024]{1,0:T(8,128)(2,1)S(1)}, u32[]{:S(2)}, u32[]{:S(2)}) collective-permute-start(bf16[240,1024]{1,0:T(8,128)(2,1)} %collective-permute-done.1.one_q), channel_id=1, source_target_pairs={{0,2},{2,0},{4,6},{6,4},{8,10},{10,8},{12,14},{14,12},{16,18},{18,... | collective-permute-start | bytes 1474568 | tf_op jit(solution)/shard_map/ppermute | solution.py:688
  104.7 12.9 %copy-start.8 = (bf16[240,1024]{1,0:T(8,128)(2,1)}, bf16[240,1024]{1,0:T(8,128)(2,1)S(1)}, u32[]{:S(2)}) copy-start(bf16[240,1024]{1,0:T(8,128)(2,1)S(1)} %collective-permute-done.11.three_r) | copy-start | bytes 1474564
  104.7 10.9 %collective-permute-start.9 = (bf16[240,1024]{1,0:T(8,128)(2,1)}, bf16[240,1024]{1,0:T(8,128)(2,1)S(1)}, u32[]{:S(2)}, u32[]{:S(2)}) collective-permute-start(bf16[240,1024]{1,0:T(8,128)(2,1)} %collective-permute-done.4.three_q), channel_id=1, source_target_pairs={{0,2},{2,0},{4,6},{6,4},{8,10},{10,8},{12,14},{14,12},{16,18},{18,... | collective-permute-start | bytes 1474568 | tf_op jit(solution)/shard_map/ppermute | solution.py:688
  115.6 2.1 %copy-start.6 = (bf16[576,1408]{1,0:T(8,128)(2,1)}, bf16[576,1408]{1,0:T(8,128)(2,1)S(1)}, u32[]{:S(2)}) copy-start(bf16[576,1408]{1,0:T(8,128)(2,1)S(1)} %collective-permute-done.5.one_b) | copy-start | bytes 4866052
  115.6 2.1 %collective-permute-start.10 = (bf16[240,1024]{1,0:T(8,128)(2,1)}, bf16[240,1024]{1,0:T(8,128)(2,1)S(1)}, u32[]{:S(2)}, u32[]{:S(2)}) collective-permute-start(bf16[240,1024]{1,0:T(8,128)(2,1)} %collective-permute-done.2.one_r), channel_id=1, source_target_pairs={{0,2},{2,0},{4,6},{6,4},{8,10},{10,8},{12,14},{14,12},{16,18},{18,... | collective-permute-start | bytes 1474568 | tf_op jit(solution)/shard_map/ppermute | solution.py:688
  115.6 2.1 %copy-start.9 = (bf16[240,1024]{1,0:T(8,128)(2,1)}, bf16[240,1024]{1,0:T(8,128)(2,1)S(1)}, u32[]{:S(2)}) copy-start(bf16[240,1024]{1,0:T(8,128)(2,1)S(1)} %collective-permute-done.8.two_q) | copy-start | bytes 1474564
  115.6 2.1 %copy-start.10 = (bf16[240,1024]{1,0:T(8,128)(2,1)}, bf16[240,1024]{1,0:T(8,128)(2,1)S(1)}, u32[]{:S(2)}) copy-start(bf16[240,1024]{1,0:T(8,128)(2,1)S(1)} %collective-permute-done.9.four_q) | copy-start | bytes 1474564
  117.7 6.2 %copy-start.11 = (bf16[240,1024]{1,0:T(8,128)(2,1)}, bf16[240,1024]{1,0:T(8,128)(2,1)S(1)}, u32[]{:S(2)}) copy-start(bf16[240,1024]{1,0:T(8,128)(2,1)S(1)} %collective-permute-done.10.two_r) | copy-start | bytes 1474564
  117.7 0.9 copy-start.7
  118.6 5.2 %collective-permute-start.12 = (bf16[576,1408]{1,0:T(8,128)(2,1)}, bf16[576,1408]{1,0:T(8,128)(2,1)S(1)}, u32[]{:S(2)}, u32[]{:S(2)}) collective-permute-start(bf16[576,1408]{1,0:T(8,128)(2,1)} %copy-done.6), channel_id=1, source_target_pairs={{0,2},{2,0},{4,6},{6,4},{8,10},{10,8},{12,14},{14,12},{16,18},{18,... | collective-permute-start | bytes 4866056 | tf_op jit(solution)/shard_map/ppermute | solution.py:697
  118.7 5.1 %collective-permute-start.13 = (bf16[240,1024]{1,0:T(8,128)(2,1)}, bf16[240,1024]{1,0:T(8,128)(2,1)S(1)}, u32[]{:S(2)}, u32[]{:S(2)}) collective-permute-start(bf16[240,1024]{1,0:T(8,128)(2,1)} %copy-done.8), channel_id=1, source_target_pairs={{0,2},{2,0},{4,6},{6,4},{8,10},{10,8},{12,14},{14,12},{16,18},{18,... | collective-permute-start | bytes 1474568 | tf_op jit(solution)/shard_map/ppermute | solution.py:698
  123.2 8.4 %collective-permute-start.14 = (bf16[256,512]{1,0:T(8,128)(2,1)S(1)}, bf16[256,512]{1,0:T(8,128)(2,1)S(1)}, u32[]{:S(2)}, u32[]{:S(2)}) collective-permute-start(bf16[256,512]{1,0:T(8,128)(2,1)S(1)} %get-tuple-element.110), channel_id=1, source_target_pairs={{0,1},{1,0},{2,3},{3,2},{4,5},{5,4},{6,7},{7,6},{8,9},{9,8},{10,11... | collective-permute-start | bytes 786440 | tf_op jit(solution)/shard_map/ppermute | solution.py:729
  123.8 7.8 %copy-start = (bf16[512,1024]{1,0:T(8,128)(2,1)S(1)}, bf16[512,1024]{1,0:T(8,128)(2,1)}, u32[]{:S(2)}) copy-start(bf16[512,1024]{1,0:T(8,128)(2,1)} %tok_ref.3) | copy-start | bytes 3145732
  123.8 7.8 %copy-start.4 = (f32[1024]{0:T(1024)S(1)}, f32[1024]{0:T(1024)}, u32[]{:S(2)}) copy-start(f32[1024]{0:T(1024)} %param.41) | copy-start | bytes 12292

commit v9 on v8

--- a/solution.py
+++ b/solution.py
@@ -70,7 +70,15 @@
     return parts
 
 
-def project_queries(tok_ref, gain_ref, w_ref, normed_ref, q_ref, turned_ref, *, reqs, draft, heads):
+def project_queries(*refs, reqs, draft, heads, cut):
+    copies = []
+    if cut:
+        side, gate_up_w, down_w, out_w, *refs, sems = refs
+        *refs, first_ref, quarter_ref = refs
+        copies = run_copies(
+            first_pairs(side, gate_up_w, down_w, out_w, first_ref, quarter_ref), sems
+        )
+    tok_ref, gain_ref, w_ref, normed_ref, q_ref, turned_ref = refs
     normed_ref[...] = rms_norm(tok_ref[...], gain_ref[...])
     q_ref[...] = jnp.dot(normed_ref[...], w_ref[...], preferred_element_type=F32).astype(BF16)
     span = heads * draft
@@ -81,6 +89,8 @@
             pieces.append(jnp.zeros((LANES - span, HD), F32))
         tile = jnp.concatenate(pieces, axis=0)
         turned_ref[r * HD : (r + 1) * HD, :] = jnp.transpose(tile).astype(BF16)
+    for copy in copies:
+        copy.wait()
 
 
 def project_keys(normed_ref, wk_ref, wv_ref, k_ref, v_ref):
@@ -366,24 +376,19 @@
     return copies
 
 
-def cut_first(side, gate_up_w, down_w, out_w, first_ref, near_ref, far_ref, sems):
+def first_pairs(side, gate_up_w, down_w, out_w, first_ref, quarter_ref):
     depth, width = down_w.shape[0] // 4, out_w.shape[0] // 4
-    near = near_ref.shape[0]
-    base = pl.multiple_of(side[2] * depth, EXTRA)
+    down_rows = pl.ds(pl.multiple_of(side[2] * depth, EXTRA), depth)
     out_rows = pl.ds(pl.multiple_of(side[2] * width, EXTRA), width)
     pairs = [
-        (out_w.at[out_rows], far_ref.at[pl.ds(depth - near, width)]),
-        (down_w.at[pl.ds(base + near, depth - near)], far_ref.at[pl.ds(0, depth - near)]),
+        (down_w.at[down_rows], quarter_ref.at[pl.ds(0, depth)]),
+        (out_w.at[out_rows], quarter_ref.at[pl.ds(depth, width)]),
     ]
-    step = near // 3
-    for i in range(3):
-        pairs.append((down_w.at[pl.ds(base + i * step, step)], near_ref.at[pl.ds(i * step, step)]))
-    step = first_ref.shape[0] // 4
-    for i in range(4):
+    step = first_ref.shape[0] // 2
+    for i in range(2):
         rows = pl.ds(i * step, step)
         pairs.append((gate_up_w.at[side[1], rows], first_ref.at[rows]))
-    for copy in run_copies(pairs, sems):
-        copy.wait()
+    return pairs
 
 
 def cut_last(side, gate_up_w, mid_ref, last_ref, sems, *, pieces):
@@ -399,8 +404,8 @@
 
 
 def stage_weights(
-    side, out_w, gate_up_w, down_w, one_a, one_m, one_b, one_q, one_r, two_a, two_m, two_q, two_r,
-    three_q, three_r, four_q, two_b, four_r, out_all, gate_up_all, down_all, sems,
+    side, out_w, gate_up_w, down_w, one_a, one_m, one_b, one_q, two_a, two_m, two_q, three_q,
+    three_r, four_q, two_b, four_r, out_all, gate_up_all, down_all, sems,
 ):
     width, depth = out_w.shape[0] // 4, down_w.shape[0] // 4
     pairs = [(gate_up_w, gate_up_all.at[0]), (down_w, down_all.at[0]), (out_w, out_all.at[0])]
@@ -410,17 +415,18 @@
             pairs.append((part, gate_up_all.at[1, half, pl.ds(at, part.shape[0])]))
             at += part.shape[0]
     core, chip = side[1], side[2] // 2
-    near = one_q.shape[0]
+    near = three_q.shape[0]
     places = ((core, chip), (1 - core, chip), (core, 1 - chip), (1 - core, 1 - chip))
-    got = ((one_q, one_r), (two_q, two_r), (three_q, three_r), (four_q, four_r))
-    for (x, y), (q, r) in zip(places, got):
+    got = ((one_q,), (two_q,), (three_q, three_r), (four_q, four_r))
+    for (x, y), parts in zip(places, got):
         base = pl.multiple_of((2 * y + x) * depth, EXTRA)
         rows = pl.ds(pl.multiple_of((2 * y + x) * width, EXTRA), width)
-        pairs.append((q, down_all.at[1, pl.ds(base, near)]))
-        pairs.append(
-            (r.at[pl.ds(0, depth - near)], down_all.at[1, pl.ds(base + near, depth - near)])
-        )
-        pairs.append((r.at[pl.ds(depth - near, width)], out_all.at[1, rows]))
+        if len(parts) == 2:
+            pairs.append((parts[0], down_all.at[1, pl.ds(base, near)]))
+        at = near if len(parts) == 2 else 0
+        rest = depth - at
+        pairs.append((parts[-1].at[pl.ds(0, rest)], down_all.at[1, pl.ds(base + at, rest)]))
+        pairs.append((parts[-1].at[pl.ds(rest, width)], out_all.at[1, rows]))
     for copy in run_copies(pairs, sems):
         copy.wait()
 
@@ -496,54 +502,44 @@
 
     grp = lax.axis_size("grp")
     depth, out_depth = w_down.shape[0] // 4, width // 4
-    first, middle = model // 4, model * 3 // 16
+    first, middle = model // 4, model * 7 // 32
     near = (depth + out_depth) // 2 // 48 * 48
-    split = (depth, out_depth, first // 4, middle, (model - first - middle) // 3)
+    split = (depth, out_depth, first // 2, middle, (model - first - middle) // 2)
     pieces = 2 if grp == 2 and n % 4 == 0 and not any(size % EXTRA for size in split) else 1
     quarter = lax.rem(lax.axis_index("req"), 4)
     core = lax.rem(quarter, 2)
     side = jnp.stack([lax.axis_index("grp"), core, quarter]).astype(jnp.int32)
-    if pieces == 2:
-        units = w_down.shape[0]
-        half_first, near_part, far_part = pl.pallas_call(
-            cut_first,
-            out_shape=(
-                VMEM((first, units), BF16),
-                VMEM((near, model), BF16),
-                VMEM((depth + out_depth - near, model), BF16),
-            ),
-            in_specs=[whole(SMEM)] + [whole(HBM)] * 3,
-            out_specs=(whole(),) * 3,
-            scratch_shapes=[pltpu.SemaphoreType.DMA((9,))],
-            compiler_params=params(4),
-            cost_estimate=cost(0, 4 * (first * units + (depth + out_depth) * model)),
-            name="cut_first",
-        )(side, *keep_in(HBM, w_gate_up, w_down, w_out))
-
-    normed, queries, turned = pl.pallas_call(
-        functools.partial(project_queries, reqs=reqs, draft=draft, heads=heads),
+
+    cut, units = pieces == 2, w_down.shape[0]
+    cuts = ((first, units), (depth + out_depth, model)) if cut else ()
+    normed, queries, turned, *shares = pl.pallas_call(
+        functools.partial(project_queries, reqs=reqs, draft=draft, heads=heads, cut=cut),
         out_shape=(
             HBM((group_rows, model), BF16),
             HBM((group_rows, width), BF16),
             jax.ShapeDtypeStruct((reqs * HD, LANES), BF16),
-        ),
-        in_specs=[whole()] * 3,
-        out_specs=(whole(),) * 3,
-        compiler_params=params(12),
+        )
+        + tuple(VMEM(shape, BF16) for shape in cuts),
+        in_specs=([whole(SMEM)] + [whole(HBM)] * 3) * cut + [whole()] * 3,
+        out_specs=(whole(),) * (3 + len(cuts)),
+        scratch_shapes=[pltpu.SemaphoreType.DMA((4,))] * cut,
+        compiler_params=params(14),
         cost_estimate=cost(
             2 * group_rows * model * width, 2 * model * (2 * group_rows + width)
         ),
         name="project_queries",
-    )(*keep_in(HBM, tokens, norm_attn.reshape(1, -1), w_query))
+    )(
+        *((side, *keep_in(HBM, w_gate_up, w_down, w_out)) if cut else ()),
+        *keep_in(HBM, tokens, norm_attn.reshape(1, -1), w_query),
+    )
+    if cut:
+        half_first, quarters = shares
 
     if pieces == 2:
-        turned, half_first, near_part, far_part = lax.optimization_barrier(
-            (turned, half_first, near_part, far_part)
-        )
+        turned, half_first, quarters = lax.optimization_barrier((turned, half_first, quarters))
         swap = [(0, 1), (1, 0)]
         one_a = lax.ppermute(half_first, "grp", swap)
-        one_q = lax.ppermute(near_part, "grp", swap)
-        one_r = lax.ppermute(far_part, "grp", swap)
+        one_q = lax.ppermute(quarters, "grp", swap)
 
     packed = pl.pallas_call(
         functools.partial(pack_queries, n=n, cap=cap, reqs=reqs, page_len=page_len),
@@ -563,11 +559,11 @@
 
     if pieces == 2:
         half_mid, half_last = pl.pallas_call(
-            functools.partial(cut_last, pieces=3),
+            functools.partial(cut_last, pieces=2),
             out_shape=(VMEM((middle, units), BF16), VMEM((model - first - middle, units), BF16)),
             in_specs=[whole(SMEM), whole(HBM)],
             out_specs=(whole(),) * 2,
-            scratch_shapes=[pltpu.SemaphoreType.DMA((4,))],
+            scratch_shapes=[pltpu.SemaphoreType.DMA((3,))],
             compiler_params=params(4),
             cost_estimate=cost(0, 4 * (model - first) * units),
             name="cut_last",
@@ -643,17 +639,15 @@
     )
 
     if pieces == 2:
-        memory_out, momentum_out, half_mid, half_last, one_a, one_q, one_r = (
-            lax.optimization_barrier(
-                (memory_out, momentum_out, half_mid, half_last, one_a, one_q, one_r)
-            )
+        memory_out, momentum_out, half_mid, half_last, one_a, one_q = lax.optimization_barrier(
+            (memory_out, momentum_out, half_mid, half_last, one_a, one_q)
         )
         other_core = [(i, i ^ 1) for i in range(n)]
         other_chip = [(i, i ^ 2) for i in range(n)]
         one_m = lax.ppermute(half_mid, "grp", swap)
         one_b = lax.ppermute(half_last, "grp", swap)
-        three_q = lax.ppermute(one_q, "req", other_chip)
-        three_r = lax.ppermute(one_r, "req", other_chip)
+        three_q = lax.ppermute(one_q[:near], "req", other_chip)
+        three_r = lax.ppermute(one_q[near:], "req", other_chip)
     asked, memory_out, momentum_out, keys, values = lax.optimization_barrier(
         (asked, memory_out, momentum_out, keys, values)
     )
@@ -681,17 +675,16 @@
     )(asked, *keep_in(HBM, kv_cache))
     if pieces == 2:
         answers, one_m, three_q = lax.optimization_barrier((answers, one_m, three_q))
-        own, one_a, one_m, one_q, one_r, three_q = lax.optimization_barrier(
-            (own, one_a, one_m, one_q, one_r, three_q)
-        )
-        two_a, two_m, two_q, two_r, four_q = (
-            lax.ppermute(part, "req", other_core) for part in (one_a, one_m, one_q, one_r, three_q)
+        _, one_a, one_q = lax.optimization_barrier((answers, one_a, one_q))
+        own, one_m, three_q = lax.optimization_barrier((own, one_m, three_q))
+        two_a, two_q, two_m, four_q = (
+            lax.ppermute(part, "req", other_core) for part in (one_a, one_q, one_m, three_q)
         )
     returned = lax.all_to_all(answers, "req", split_axis=0, concat_axis=0, tiled=True)
     if pieces == 2:
-        returned, one_b, two_a, two_m, two_q, four_q, two_r, three_r, own, retrieved = (
+        returned, one_b, two_a, two_m, two_q, four_q, three_r, own, retrieved = (
             lax.optimization_barrier(
-                (returned, one_b, two_a, two_m, two_q, four_q, two_r, three_r, own, retrieved)
+                (returned, one_b, two_a, two_m, two_q, four_q, three_r, own, retrieved)
             )
         )
         two_b = lax.ppermute(one_b, "req", other_core)
@@ -735,17 +728,17 @@
                 VMEM((2,) + w_gate_up.shape, BF16),
                 VMEM((2,) + w_down.shape, BF16),
             ),
-            in_specs=[whole(SMEM)] + [whole(pl.ANY)] * 17,
+            in_specs=[whole(SMEM)] + [whole(pl.ANY)] * 15,
             out_specs=(whole(),) * 3,
-            scratch_shapes=[pltpu.SemaphoreType.DMA((21,))],
+            scratch_shapes=[pltpu.SemaphoreType.DMA((19,))],
             compiler_params=params(2),
             cost_estimate=cost(0, 2 * model * (2 * width + 6 * units)),
             name="stage_weights",
         )(
             side,
             *keep_in(
-                HBM, w_out, w_gate_up, w_down, one_a, one_m, one_b, one_q, one_r, two_a, two_m, two_q,
-                two_r, three_q, three_r, four_q,
+                HBM, w_out, w_gate_up, w_down, one_a, one_m, one_b, one_q, two_a, two_m, two_q,
+                three_q, three_r, four_q,
             ),
             two_b,
             four_r,

time: 140 us -> 138 us (0.986)
  Pallas kernels: 80.6 us -> 75.3 us
  local copies, waits for them, and re-layouts: 1.64 us -> 5.3 us
  waiting for transfers between devices: 25.5 us -> 23.1 us
  starting transfers between devices: 29.5 us -> 31.5 us
    ppermute x4 -> x3, waiting for transfers between devices: 9.57 us -> 13.8 us  [the longest x1 5.19 us: on_device(): three_r = lax.ppermute(one_q[near:], 'req', other_chip)]
    pallas_call x1, Pallas kernels: 21.6 us -> 18 us  [on_device(): pl.pallas_call(functools.partial(update_memory, reqs=reqs, draft=draft, h...]
    pallas_call x2 -> x1, Pallas kernels: 6.21 us -> 2.99 us  [on_device(): pl.pallas_call(functools.partial(cut_last, pieces=2), out_shape=(VMEM((mi...]
    slice x0 -> x1, local copies, waits for them, and re-layouts: none -> 2.2 us  [on_device(): three_r = lax.ppermute(one_q[near:], 'req', other_chip)]
    ppermute x5 -> x4, waiting for transfers between devices: 2.04 us -> 0.01 us  [on_device(): lax.ppermute(part, 'req', other_core)]
    all_to_all x1, waiting for transfers between devices: 1.95 us -> 0.01 us  [on_device(): lax.all_to_all(packed, 'req', split_axis=0, concat_axis=0, tiled=True)]
    ppermute x1, waiting for transfers between devices: 10.8 us -> 8.91 us  [on_device(): one_b = lax.ppermute(half_last, 'grp', swap)]
    all_to_all x1, starting transfers between devices: 5.68 us -> 7.49 us  [on_device(): lax.all_to_all(answers, 'req', split_axis=0, concat_axis=0, tiled=True)]
  transfers between devices with their start and end apart: 18 -> 16, of which waited for: 6 -> 5; matrix products, arithmetic and copies ran while one was open for 0% -> 2% of each run, Pallas kernels for 53% -> 50%
where the time goes in v9:
time: 138 us; the launch traced here: 137 us
  Pallas kernels  75.3 us (55%)
  starting transfers between devices  31.5 us (23%)
  waiting for transfers between devices  23.1 us (17%)
  local copies, waits for them, and re-layouts  5.3 us (4%)
    pallas_call x1, Pallas kernels, on_device(): pl.pallas_call(functools.partial(local_attention, heads=heads, draft=draf...  18.2 us
    pallas_call x1, Pallas kernels, on_device(): pl.pallas_call(functools.partial(update_memory, reqs=reqs, draft=draft, h...  18 us
    ppermute x1, waiting for transfers between devices, on_device(): one_b = lax.ppermute(half_last, 'grp', swap)  8.91 us
    all_to_all x1, starting transfers between devices, on_device(): lax.all_to_all(answers, 'req', split_axis=0, concat_axis=0, tiled=True)  7.49 us
    all_to_all x1, starting transfers between devices, on_device(): lax.all_to_all(label, 'req', split_axis=0, concat_axis=0, tiled=True)  7.39 us
    pallas_call x1, Pallas kernels, on_device(): pl.pallas_call(feed_forward, out_shape=jax.ShapeDtypeStruct((rows, model)...  7.31 us
    pallas_call x1, Pallas kernels, on_device(): pl.pallas_call(functools.partial(page_attention, n=n, cap=cap, draft=draf...  7.23 us
    pallas_call x1, Pallas kernels, on_device(): pl.pallas_call(stage_weights, out_shape=(VMEM((2,) + w_out.shape, BF16),...  6.69 us
  transfers between devices with their start and end apart: 16, of which 5 were waited for; matrix products, arithmetic and copies ran while one was open for 2% of the time, Pallas kernels for 50%

profile of v9, /device:TPU:0, one launch (start us, length us, event | category | flops | bytes accessed | tf_op | source)
XLA Modules:
  0.0 136.7 jit_solution(17769234041780026687)
XLA Ops:
  0.6 0.7 fusion.1
  1.3 0.7 reshape.19
  2.0 7.4 %all-to-all-start = ((s32[16,1,3]{2,1,0:T(1,128)}), s32[16,1,3]{2,1,0:T(1,128)S(1)}, u32[]{:S(2)}, u32[]{:S(2)}) async-start(s32[16,1,3]{2,1,0:T(1,128)} %bitcast.3), calls=%async_computation | async-start | bytes 16384 | tf_op jit(solution)/shard_map/all_to_all | solution.py:501
  9.4 0.1 pad_add_fusion.refs_0_.side
  9.5 4.7 %project_queries.1 = (bf16[512,1024]{1,0:T(8,128)(2,1)}, bf16[512,512]{1,0:T(8,128)(2,1)}, bf16[2048,128]{1,0:T(8,128)(2,1)S(1)}, bf16[256,1408]{1,0:T(8,128)(2,1)}, bf16[480,1024]{1,0:T(8,128)(2,1)}) custom-call(s32[3]{0:T(128)S(1)} %pad_add_fusion.refs_0_.side, bf16[2,1024,1408]{2,1,0:T(8,128)(2,1)} %gate_up_w.2, bf16[1408,1024]{1,0:T(8,128)(2,1)} %down_w.1, ...), custom_call_target="tpu_custom_call" | custom-call | flops 10737418240 | bytes 62914560 | tf_op jit(solution)/shard_map/project_queries/pallas_call | solution.py:515
  14.2 1.6 %collective-permute-start = (bf16[256,1408]{1,0:T(8,128)(2,1)}, bf16[256,1408]{1,0:T(8,128)(2,1)}, u32[]{:S(2)}, u32[]{:S(2)}) collective-permute-start(bf16[256,1408]{1,0:T(8,128)(2,1)} %get-tuple-element.72), channel_id=1, source_target_pairs={{0,1},{1,0},{2,3},{3,2},{4,5},{5,4},{6,7},{7,6},{8,9},{9,8},{10,11... | collective-permute-start | bytes 2162696 | tf_op jit(solution)/shard_map/ppermute | solution.py:541
  15.8 0.5 collective-permute-start.1
  16.3 0.0 all-to-all-done.codes
  16.3 2.2 %pack_queries.1 = bf16[6400,128]{1,0:T(8,128)(2,1)} custom-call(s32[16,1,3]{2,1,0:T(1,128)S(1)} %all-to-all-done.codes, s32[16]{0:T(128)} %lengths.1, bf16[2048,128]{1,0:T(8,128)(2,1)S(1)} %get-tuple-element.61.turned_ref), custom_call_target="tpu_custom_call" | custom-call | bytes 65536000 | tf_op jit(solution)/shard_map/pack_queries/pallas_call | solution.py:544
  18.5 6.0 %all-to-all-start.1 = ((bf16[16,400,128]{2,1,0:T(8,128)(2,1)}), bf16[16,400,128]{2,1,0:T(8,128)(2,1)S(1)}, u32[]{:S(2)}, u32[]{:S(2)}) async-start(bf16[16,400,128]{2,1,0:T(8,128)(2,1)} %bitcast.19), calls=%async_computation.1 | async-start | bytes 3276800 | tf_op jit(solution)/shard_map/all_to_all | solution.py:558
  24.5 0.0 copy-start.1
  24.5 0.0 copy-start.2
  24.5 0.0 copy-start.3
  24.5 0.0 copy-start.5
  24.5 3.9 %project_keys.1 = (bf16[512,512]{1,0:T(8,128)(2,1)}, bf16[512,512]{1,0:T(8,128)(2,1)}) custom-call(bf16[512,1024]{1,0:T(8,128)(2,1)} %get-tuple-element.64.normed_ref, bf16[1024,512]{1,0:T(8,128)(2,1)} %wk_ref.1, bf16[1024,512]{1,0:T(8,128)(2,1)} %wv_ref.1), custom_call_target="tpu_custom_call" | custom-call | flops 21474836480 | bytes 62914560 | tf_op jit(solution)/shard_map/project_keys/pallas_call | solution.py:572
  28.5 18.0 %update_memory.1 = (f32[16,4,128,128]{3,2,1,0:T(8,128)}, f32[16,4,128,128]{3,2,1,0:T(8,128)}) custom-call(s32[8,16]{1,0:T(8,128)S(1)} %bitcast.17, s32[16]{0:T(128)S(1)} %copy-done.5, s32[8,4,16]{2,1,0:T(4,128)S(1)} %bitcast.15, s32[8,4,16]{2,1,0:T(4,128)S(1)} %bitcast.16, bf16[512,512]{1,0:T(8,128)(2,1)} %get-tuple-element.65.k_ref, ...), custom_call_target="tpu_custom_call" | custom-call | flops 18790481920 | bytes 335544320 | tf_op jit(solution)/shard_map/update_memory/pallas_call | solution.py:612
  46.5 3.0 %cut_last.1 = (bf16[224,1408]{1,0:T(8,128)(2,1)}, bf16[544,1408]{1,0:T(8,128)(2,1)S(1)}) custom-call(s32[3]{0:T(128)S(1)} %pad_add_fusion.refs_0_.side, bf16[2,1024,1408]{2,1,0:T(8,128)(2,1)} %gate_up_w.2), custom_call_target="tpu_custom_call" | custom-call | bytes 86507520 | tf_op jit(solution)/shard_map/cut_last/pallas_call | solution.py:561
  49.5 0.0 collective-permute-done.one_a
  49.5 4.6 %collective-permute-done.1.one_q = bf16[480,1024]{1,0:T(8,128)(2,1)} collective-permute-done((bf16[480,1024]{1,0:T(8,128)(2,1)}, bf16[480,1024]{1,0:T(8,128)(2,1)}, u32[]{:S(2)}, u32[]{:S(2)}) %collective-permute-start.1) | collective-permute-done | bytes 983072 | tf_op jit(solution)/shard_map/ppermute | solution.py:542
  54.1 1.5 %collective-permute-start.2 = (bf16[224,1408]{1,0:T(8,128)(2,1)}, bf16[224,1408]{1,0:T(8,128)(2,1)}, u32[]{:S(2)}, u32[]{:S(2)}) collective-permute-start(bf16[224,1408]{1,0:T(8,128)(2,1)} %get-tuple-element.77), channel_id=1, source_target_pairs={{0,1},{1,0},{2,3},{3,2},{4,5},{5,4},{6,7},{7,6},{8,9},{9,8},{10,11... | collective-permute-start | bytes 1892360 | tf_op jit(solution)/shard_map/ppermute | solution.py:647
  55.6 2.2 %fusion.2 = (bf16[240,1024]{1,0:T(8,128)(2,1)}, bf16[240,1024]{1,0:T(8,128)(2,1)}) fusion(bf16[480,1024]{1,0:T(8,128)(2,1)} %collective-permute-done.1.one_q), kind=kLoop, calls=%fused_computation.5 | loop fusion | bytes 1966080 | tf_op jit(solution)/shard_map/slice | solution.py:650
  57.8 1.6 %collective-permute-start.3 = (bf16[240,1024]{1,0:T(8,128)(2,1)}, bf16[240,1024]{1,0:T(8,128)(2,1)}, u32[]{:S(2)}, u32[]{:S(2)}) collective-permute-start(bf16[240,1024]{1,0:T(8,128)(2,1)} %get-tuple-element.114), channel_id=1, source_target_pairs={{0,4},{2,6},{4,0},{6,2},{8,12},{10,14},{12,8},{14,10},{16,20},{18,... | collective-permute-start | bytes 1474568 | tf_op jit(solution)/shard_map/ppermute | solution.py:649
  59.4 0.0 all-to-all-done.1
  59.4 7.2 %page_attention.1 = bf16[6400,128]{1,0:T(8,128)(2,1)} custom-call(bf16[6400,128]{1,0:T(8,128)(2,1)S(1)} %bitcast.14, bf16[48,2,128,512]{3,2,1,0:T(8,128)(2,1)} %kv_hbm.1), custom_call_target="tpu_custom_call" | custom-call | flops 8053063680 | bytes 317194240 | tf_op jit(solution)/shard_map/page_attention/pallas_call | solution.py:654
  66.7 3.9 %collective-permute-done.3.three_q = bf16[240,1024]{1,0:T(8,128)(2,1)} collective-permute-done((bf16[240,1024]{1,0:T(8,128)(2,1)}, bf16[240,1024]{1,0:T(8,128)(2,1)}, u32[]{:S(2)}, u32[]{:S(2)}) %collective-permute-start.3) | collective-permute-done | bytes 491552 | tf_op jit(solution)/shard_map/ppermute | solution.py:649
  70.6 0.0 collective-permute-done.2.one_m
  70.6 7.5 %all-to-all-start.2 = ((bf16[16,400,128]{2,1,0:T(8,128)(2,1)}), bf16[16,400,128]{2,1,0:T(8,128)(2,1)S(1)}, u32[]{:S(2)}, u32[]{:S(2)}) async-start(bf16[16,400,128]{2,1,0:T(8,128)(2,1)} %bitcast.20), calls=%async_computation.2 | async-start | bytes 3276800 | tf_op jit(solution)/shard_map/all_to_all | solution.py:683
  78.1 1.2 collective-permute-start.4
  79.3 1.9 %collective-permute-start.9 = (bf16[240,1024]{1,0:T(8,128)(2,1)}, bf16[240,1024]{1,0:T(8,128)(2,1)S(1)}, u32[]{:S(2)}, u32[]{:S(2)}) collective-permute-start(bf16[240,1024]{1,0:T(8,128)(2,1)} %get-tuple-element.113), channel_id=1, source_target_pairs={{0,4},{2,6},{4,0},{6,2},{8,12},{10,14},{12,8},{14,10},{16,20},{18,... | collective-permute-start | bytes 1474568 | tf_op jit(solution)/shard_map/ppermute | solution.py:650
  81.2 0.0 collective-permute-start.7
  81.2 0.5 collective-permute-start.5
  81.8 18.2 %local_attention.1 = (f32[2048,128]{1,0:T(8,128)}, f32[2048,128]{1,0:T(8,128)}, f32[16,128]{1,0:T(8,128)S(1)}, f32[16,128]{1,0:T(8,128)S(1)}) custom-call(bf16[512,512]{1,0:T(8,128)(2,1)} %get-tuple-element.83.q_ref, bf16[512,512]{1,0:T(8,128)(2,1)} %get-tuple-element.65.k_ref, bf16[512,512]{1,0:T(8,128)(2,1)} %get-tuple-element.66.v_ref, ...), custom_call_target="tpu_custom_call" | custom-call | flops 20 | bytes 20 | tf_op jit(solution)/shard_map/local_attention/pallas_call | solution.py:588
  99.9 0.0 collective-permute-start.6
  99.9 5.2 %collective-permute-done.9.three_r = bf16[240,1024]{1,0:T(8,128)(2,1)S(1)} collective-permute-done((bf16[240,1024]{1,0:T(8,128)(2,1)}, bf16[240,1024]{1,0:T(8,128)(2,1)S(1)}, u32[]{:S(2)}, u32[]{:S(2)}) %collective-permute-start.9) | collective-permute-done | bytes 491552 | tf_op jit(solution)/shard_map/ppermute | solution.py:650
  105.1 0.0 collective-permute-start.8
  105.1 8.9 %collective-permute-done.4.one_b = bf16[544,1408]{1,0:T(8,128)(2,1)S(1)} collective-permute-done((bf16[544,1408]{1,0:T(8,128)(2,1)S(1)}, bf16[544,1408]{1,0:T(8,128)(2,1)S(1)}, u32[]{:S(2)}, u32[]{:S(2)}) %collective-permute-start.4) | collective-permute-done | bytes 1531936 | tf_op jit(solution)/shard_map/ppermute | solution.py:648
  114.1 1.1 copy-done.6
  115.2 0.2 copy-done.10
  115.3 0.2 copy-done.8
  115.5 0.9 copy-done.7
  116.4 0.0 collective-permute-done.7.two_q
  116.5 0.5 collective-permute-start.11
  117.0 4.1 %combine.1 = (bf16[256,512]{1,0:T(8,128)(2,1)S(1)}, bf16[256,512]{1,0:T(8,128)(2,1)S(1)}) custom-call(s32[16,1,3]{2,1,0:T(1,128)S(1)} %all-to-all-done.codes, s32[3]{0:T(128)S(1)} %pad_add_fusion.refs_0_.side, bf16[6400,128]{1,0:T(8,128)(2,1)S(1)} %bitcast.13, f32[2048,128]{1,0:T(8,128)} %get-tuple-element.93.o_hbm, f32[2048,128]{1,0:T(8,128)} %get-tuple-element.94.ret_hbm, ...), custom_call_target="tpu_custom_call" | custom-call | flops 125829120 | bytes 74711040 | tf_op jit(solution)/shard_map/combine/pallas_call | solution.py:693
  121.1 1.2 collective-permute-start.12
  122.3 0.0 copy-start.4
  122.3 6.7 %stage_weights.1 = (bf16[2,512,1024]{2,1,0:T(8,128)(2,1)S(1)}, bf16[2,2,1024,1408]{3,2,1,0:T(8,128)(2,1)S(1)}, bf16[2,1408,1024]{2,1,0:T(8,128)(2,1)S(1)}) custom-call(s32[3]{0:T(128)S(1)} %pad_add_fusion.refs_0_.side, bf16[512,1024]{1,0:T(8,128)(2,1)} %out_w.1, bf16[2,1024,1408]{2,1,0:T(8,128)(2,1)} %gate_up_w.2, bf16[1408,1024]{1,0:T(8,128)(2,1)} %down_w.1, ...), custom_call_target="tpu_custom_call" | custom-call | bytes 387973120 | tf_op jit(solution)/shard_map/stage_weights/pallas_call | solution.py:724
  129.0 0.4 collective-permute-done.12.theirs_ref
  129.4 7.3 %feed_forward.1 = bf16[256,1024]{1,0:T(8,128)(2,1)} custom-call(s32[3]{0:T(128)S(1)} %pad_add_fusion.refs_0_.side, bf16[512,1024]{1,0:T(8,128)(2,1)S(1)} %copy-done, bf16[256,512]{1,0:T(8,128)(2,1)S(1)} %get-tuple-element.100.mine_ref, bf16[256,512]{1,0:T(8,128)(2,1)S(1)} %collective-permute-done.12.theirs_ref, f32[1,1024]{1,0:T(1,128)S(1)} %bitcast.18, ...), custom_call_target="tpu_custom_call" | custom-call | flops 99321118720 | bytes 387973120 | tf_op jit(solution)/shard_map/feed_forward/pallas_call | solution.py:746
  (20 shorter events, 0.0 us)
Async XLA Ops:
  2.0 14.3 %all-to-all-start = ((s32[16,1,3]{2,1,0:T(1,128)}), s32[16,1,3]{2,1,0:T(1,128)S(1)}, u32[]{:S(2)}, u32[]{:S(2)}) async-start(s32[16,1,3]{2,1,0:T(1,128)} %bitcast.3), calls=%async_computation | async-start | bytes 16384 | tf_op jit(solution)/shard_map/all_to_all | solution.py:501
  14.2 35.3 %collective-permute-start = (bf16[256,1408]{1,0:T(8,128)(2,1)}, bf16[256,1408]{1,0:T(8,128)(2,1)}, u32[]{:S(2)}, u32[]{:S(2)}) collective-permute-start(bf16[256,1408]{1,0:T(8,128)(2,1)} %get-tuple-element.72), channel_id=1, source_target_pairs={{0,1},{1,0},{2,3},{3,2},{4,5},{5,4},{6,7},{7,6},{8,9},{9,8},{10,11... | collective-permute-start | bytes 2162696 | tf_op jit(solution)/shard_map/ppermute | solution.py:541
  15.8 38.4 %collective-permute-start.1 = (bf16[480,1024]{1,0:T(8,128)(2,1)}, bf16[480,1024]{1,0:T(8,128)(2,1)}, u32[]{:S(2)}, u32[]{:S(2)}) collective-permute-start(bf16[480,1024]{1,0:T(8,128)(2,1)} %get-tuple-element.73), channel_id=1, source_target_pairs={{0,1},{1,0},{2,3},{3,2},{4,5},{5,4},{6,7},{7,6},{8,9},{9,8},{10,11... | collective-permute-start | bytes 2949128 | tf_op jit(solution)/shard_map/ppermute | solution.py:542
  18.5 41.0 %all-to-all-start.1 = ((bf16[16,400,128]{2,1,0:T(8,128)(2,1)}), bf16[16,400,128]{2,1,0:T(8,128)(2,1)S(1)}, u32[]{:S(2)}, u32[]{:S(2)}) async-start(bf16[16,400,128]{2,1,0:T(8,128)(2,1)} %bitcast.19), calls=%async_computation.1 | async-start | bytes 3276800 | tf_op jit(solution)/shard_map/all_to_all | solution.py:558
  24.5 4.0 %copy-start.1 = (s32[16,8,4]{0,2,1:T(4,128)S(1)}, s32[16,8,4]{0,2,1:T(4,128)}, u32[]{:S(2)}) copy-start(s32[16,8,4]{0,2,1:T(4,128)} %param.39) | copy-start | bytes 6148
  24.5 4.0 %copy-start.2 = (s32[16,8,4]{0,2,1:T(4,128)S(1)}, s32[16,8,4]{0,2,1:T(4,128)}, u32[]{:S(2)}) copy-start(s32[16,8,4]{0,2,1:T(4,128)} %param.40) | copy-start | bytes 6148
  24.5 4.0 %copy-start.3 = (s32[16,8]{0,1:T(8,128)S(1)}, s32[16,8]{0,1:T(8,128)}, u32[]{:S(2)}) copy-start(s32[16,8]{0,1:T(8,128)} %param.35) | copy-start | bytes 1540
  24.5 3.9 %copy-start.5 = (s32[16]{0:T(128)S(1)}, s32[16]{0:T(128)}, u32[]{:S(2)}) copy-start(s32[16]{0:T(128)} %count.1) | copy-start | bytes 196
  54.1 16.5 %collective-permute-start.2 = (bf16[224,1408]{1,0:T(8,128)(2,1)}, bf16[224,1408]{1,0:T(8,128)(2,1)}, u32[]{:S(2)}, u32[]{:S(2)}) collective-permute-start(bf16[224,1408]{1,0:T(8,128)(2,1)} %get-tuple-element.77), channel_id=1, source_target_pairs={{0,1},{1,0},{2,3},{3,2},{4,5},{5,4},{6,7},{7,6},{8,9},{9,8},{10,11... | collective-permute-start | bytes 1892360 | tf_op jit(solution)/shard_map/ppermute | solution.py:647
  57.8 12.8 %collective-permute-start.3 = (bf16[240,1024]{1,0:T(8,128)(2,1)}, bf16[240,1024]{1,0:T(8,128)(2,1)}, u32[]{:S(2)}, u32[]{:S(2)}) collective-permute-start(bf16[240,1024]{1,0:T(8,128)(2,1)} %get-tuple-element.114), channel_id=1, source_target_pairs={{0,4},{2,6},{4,0},{6,2},{8,12},{10,14},{12,8},{14,10},{16,20},{18,... | collective-permute-start | bytes 1474568 | tf_op jit(solution)/shard_map/ppermute | solution.py:649
  70.6 45.8 %all-to-all-start.2 = ((bf16[16,400,128]{2,1,0:T(8,128)(2,1)}), bf16[16,400,128]{2,1,0:T(8,128)(2,1)S(1)}, u32[]{:S(2)}, u32[]{:S(2)}) async-start(bf16[16,400,128]{2,1,0:T(8,128)(2,1)} %bitcast.20), calls=%async_computation.2 | async-start | bytes 3276800 | tf_op jit(solution)/shard_map/all_to_all | solution.py:683
  78.1 35.9 %collective-permute-start.4 = (bf16[544,1408]{1,0:T(8,128)(2,1)S(1)}, bf16[544,1408]{1,0:T(8,128)(2,1)S(1)}, u32[]{:S(2)}, u32[]{:S(2)}) collective-permute-start(bf16[544,1408]{1,0:T(8,128)(2,1)S(1)} %get-tuple-element.80), channel_id=1, source_target_pairs={{0,1},{1,0},{2,3},{3,2},{4,5},{5,4},{6,7},{7,6},{8,9},{9,8},{10,11... | collective-permute-start | bytes 4595720 | tf_op jit(solution)/shard_map/ppermute | solution.py:648
  79.3 25.8 %collective-permute-start.9 = (bf16[240,1024]{1,0:T(8,128)(2,1)}, bf16[240,1024]{1,0:T(8,128)(2,1)S(1)}, u32[]{:S(2)}, u32[]{:S(2)}) collective-permute-start(bf16[240,1024]{1,0:T(8,128)(2,1)} %get-tuple-element.113), channel_id=1, source_target_pairs={{0,4},{2,6},{4,0},{6,2},{8,12},{10,14},{12,8},{14,10},{16,20},{18,... | collective-permute-start | bytes 1474568 | tf_op jit(solution)/shard_map/ppermute | solution.py:650
  81.2 35.2 %collective-permute-start.7 = (bf16[480,1024]{1,0:T(8,128)(2,1)}, bf16[480,1024]{1,0:T(8,128)(2,1)}, u32[]{:S(2)}, u32[]{:S(2)}) collective-permute-start(bf16[480,1024]{1,0:T(8,128)(2,1)} %collective-permute-done.1.one_q), channel_id=1, source_target_pairs={{0,2},{2,0},{4,6},{6,4},{8,10},{10,8},{12,14},{14,12},{16,18},{18,... | collective-permute-start | bytes 2949128 | tf_op jit(solution)/shard_map/ppermute | solution.py:681
  81.2 32.8 %collective-permute-start.5 = (bf16[256,1408]{1,0:T(8,128)(2,1)}, bf16[256,1408]{1,0:T(8,128)(2,1)S(1)}, u32[]{:S(2)}, u32[]{:S(2)}) collective-permute-start(bf16[256,1408]{1,0:T(8,128)(2,1)} %collective-permute-done.one_a), channel_id=1, source_target_pairs={{0,2},{2,0},{4,6},{6,4},{8,10},{10,8},{12,14},{14,12},{16,18},{18,... | collective-permute-start | bytes 2162696 | tf_op jit(solution)/shard_map/ppermute | solution.py:681
  99.9 14.1 %collective-permute-start.6 = (bf16[224,1408]{1,0:T(8,128)(2,1)}, bf16[224,1408]{1,0:T(8,128)(2,1)S(1)}, u32[]{:S(2)}, u32[]{:S(2)}) collective-permute-start(bf16[224,1408]{1,0:T(8,128)(2,1)} %collective-permute-done.2.one_m), channel_id=1, source_target_pairs={{0,2},{2,0},{4,6},{6,4},{8,10},{10,8},{12,14},{14,12},{16,18},{18,... | collective-permute-start | bytes 1892360 | tf_op jit(solution)/shard_map/ppermute | solution.py:681
  105.1 9.0 %copy-start.9 = (bf16[240,1024]{1,0:T(8,128)(2,1)}, bf16[240,1024]{1,0:T(8,128)(2,1)S(1)}, u32[]{:S(2)}) copy-start(bf16[240,1024]{1,0:T(8,128)(2,1)S(1)} %collective-permute-done.9.three_r) | copy-start | bytes 1474564
  105.1 8.9 %collective-permute-start.8 = (bf16[240,1024]{1,0:T(8,128)(2,1)}, bf16[240,1024]{1,0:T(8,128)(2,1)S(1)}, u32[]{:S(2)}, u32[]{:S(2)}) collective-permute-start(bf16[240,1024]{1,0:T(8,128)(2,1)} %collective-permute-done.3.three_q), channel_id=1, source_target_pairs={{0,2},{2,0},{4,6},{6,4},{8,10},{10,8},{12,14},{14,12},{16,18},{18,... | collective-permute-start | bytes 1474568 | tf_op jit(solution)/shard_map/ppermute | solution.py:681
  114.0 1.1 copy-start.6
  114.0 1.3 copy-start.10
  114.0 1.5 %copy-start.8 = (bf16[224,1408]{1,0:T(8,128)(2,1)}, bf16[224,1408]{1,0:T(8,128)(2,1)S(1)}, u32[]{:S(2)}) copy-start(bf16[224,1408]{1,0:T(8,128)(2,1)S(1)} %collective-permute-done.6.two_m) | copy-start | bytes 1892356
  115.5 0.9 copy-start.7
  116.4 5.9 %collective-permute-start.10 = (bf16[544,1408]{1,0:T(8,128)(2,1)}, bf16[544,1408]{1,0:T(8,128)(2,1)S(1)}, u32[]{:S(2)}, u32[]{:S(2)}) collective-permute-start(bf16[544,1408]{1,0:T(8,128)(2,1)} %copy-done.6), channel_id=1, source_target_pairs={{0,2},{2,0},{4,6},{6,4},{8,10},{10,8},{12,14},{14,12},{16,18},{18,... | collective-permute-start | bytes 4595720 | tf_op jit(solution)/shard_map/ppermute | solution.py:690
  116.5 5.9 %collective-permute-start.11 = (bf16[240,1024]{1,0:T(8,128)(2,1)}, bf16[240,1024]{1,0:T(8,128)(2,1)S(1)}, u32[]{:S(2)}, u32[]{:S(2)}) collective-permute-start(bf16[240,1024]{1,0:T(8,128)(2,1)} %copy-done.9), channel_id=1, source_target_pairs={{0,2},{2,0},{4,6},{6,4},{8,10},{10,8},{12,14},{14,12},{16,18},{18,... | collective-permute-start | bytes 1474568 | tf_op jit(solution)/shard_map/ppermute | solution.py:691
  121.1 8.3 %collective-permute-start.12 = (bf16[256,512]{1,0:T(8,128)(2,1)S(1)}, bf16[256,512]{1,0:T(8,128)(2,1)S(1)}, u32[]{:S(2)}, u32[]{:S(2)}) collective-permute-start(bf16[256,512]{1,0:T(8,128)(2,1)S(1)} %get-tuple-element.101), channel_id=1, source_target_pairs={{0,1},{1,0},{2,3},{3,2},{4,5},{5,4},{6,7},{7,6},{8,9},{9,8},{10,11... | collective-permute-start | bytes 786440 | tf_op jit(solution)/shard_map/ppermute | solution.py:722
  122.3 7.1 %copy-start = (bf16[512,1024]{1,0:T(8,128)(2,1)S(1)}, bf16[512,1024]{1,0:T(8,128)(2,1)}, u32[]{:S(2)}) copy-start(bf16[512,1024]{1,0:T(8,128)(2,1)} %tok_ref.1) | copy-start | bytes 3145732
  122.3 7.1 %copy-start.4 = (f32[1024]{0:T(1024)S(1)}, f32[1024]{0:T(1024)}, u32[]{:S(2)}) copy-start(f32[1024]{0:T(1024)} %param.41) | copy-start | bytes 12292

commit v10 on v9

--- a/solution.py
+++ b/solution.py
@@ -73,14 +73,17 @@
 def project_queries(*refs, reqs, draft, heads, cut):
     copies = []
     if cut:
-        side, gate_up_w, down_w, out_w, *refs, sems = refs
+        side, gate_up_w, down_w, out_w, *refs, q_ref, q_sem, sems = refs
         *refs, first_ref, quarter_ref = refs
+        refs += [q_ref, q_sem]
         copies = run_copies(
             first_pairs(side, gate_up_w, down_w, out_w, first_ref, quarter_ref), sems
         )
-    tok_ref, gain_ref, w_ref, normed_ref, q_ref, turned_ref = refs
-    normed_ref[...] = rms_norm(tok_ref[...], gain_ref[...])
-    q_ref[...] = jnp.dot(normed_ref[...], w_ref[...], preferred_element_type=F32).astype(BF16)
+    tok_ref, gain_ref, w_ref, q_hbm, turned_ref, q_ref, q_sem = refs
+    normed = rms_norm(tok_ref[...], gain_ref[...])
+    q_ref[...] = jnp.dot(normed, w_ref[...], preferred_element_type=F32).astype(BF16)
+    copies.append(pltpu.make_async_copy(q_ref, q_hbm, q_sem.at[0]))
+    copies[-1].start()
     span = heads * draft
     for r in range(reqs):
         rows = slice(r * draft, (r + 1) * draft)
@@ -93,8 +96,8 @@
         copy.wait()
 
 
-def project_keys(normed_ref, wk_ref, wv_ref, k_ref, v_ref):
-    normed = normed_ref[...]
+def project_keys(tok_ref, gain_ref, wk_ref, wv_ref, k_ref, v_ref):
+    normed = rms_norm(tok_ref[...], gain_ref[...])
     k_ref[...] = jnp.dot(normed, wk_ref[...], preferred_element_type=F32).astype(BF16)
     v_ref[...] = jnp.dot(normed, wv_ref[...], preferred_element_type=F32).astype(BF16)
 
@@ -503,7 +506,7 @@
     grp = lax.axis_size("grp")
     depth, out_depth = w_down.shape[0] // 4, width // 4
     first, middle = model // 4, model * 7 // 32
-    near = (depth + out_depth) // 2 // 48 * 48
+    near = depth * 6 // 11 // EXTRA * EXTRA
     split = (depth, out_depth, first // 2, middle, (model - first - middle) // 2)
     pieces = 2 if grp == 2 and n % 4 == 0 and not any(size % EXTRA for size in split) else 1
     quarter = lax.rem(lax.axis_index("req"), 4)
@@ -512,17 +515,17 @@
 
     cut, units = pieces == 2, w_down.shape[0]
     cuts = ((first, units), (depth + out_depth, model)) if cut else ()
-    normed, queries, turned, *shares = pl.pallas_call(
+    queries, turned, *shares = pl.pallas_call(
         functools.partial(project_queries, reqs=reqs, draft=draft, heads=heads, cut=cut),
         out_shape=(
-            HBM((group_rows, model), BF16),
             HBM((group_rows, width), BF16),
             jax.ShapeDtypeStruct((reqs * HD, LANES), BF16),
         )
         + tuple(VMEM(shape, BF16) for shape in cuts),
         in_specs=([whole(SMEM)] + [whole(HBM)] * 3) * cut + [whole()] * 3,
-        out_specs=(whole(),) * (3 + len(cuts)),
-        scratch_shapes=[pltpu.SemaphoreType.DMA((4,))] * cut,
+        out_specs=(whole(HBM),) + (whole(),) * (1 + len(cuts)),
+        scratch_shapes=[pltpu.VMEM((group_rows, width), BF16), pltpu.SemaphoreType.DMA((1,))]
+        + [pltpu.SemaphoreType.DMA((4,))] * cut,
         compiler_params=params(14),
         cost_estimate=cost(
             2 * group_rows * model * width, 2 * model * (2 * group_rows + width)
@@ -554,7 +557,7 @@
         cost_estimate=cost(0, 4 * n * ask_block * LANES),
         name="pack_queries",
     )(codes, *keep_in(HBM, cache_len), turned)
-    packed, normed, late = lax.optimization_barrier((packed, normed, w_gate_up))
+    packed, late_tokens, late = lax.optimization_barrier((packed, tokens, w_gate_up))
     asked = lax.all_to_all(packed, "req", split_axis=0, concat_axis=0, tiled=True)
 
     if pieces == 2:
@@ -572,14 +575,14 @@
     keys, values = pl.pallas_call(
         project_keys,
         out_shape=(HBM((group_rows, width), BF16),) * 2,
-        in_specs=[whole()] * 3,
+        in_specs=[whole()] * 4,
         out_specs=(whole(),) * 2,
         compiler_params=params(12),
         cost_estimate=cost(
             4 * group_rows * model * width, 2 * model * (group_rows + 2 * width)
         ),
         name="project_keys",
-    )(*keep_in(HBM, normed, w_key, w_value))
+    )(*keep_in(HBM, late_tokens, norm_attn.reshape(1, -1), w_key, w_value))
 
     row_block = pl.BlockSpec((draft, width), lambda r, *_: (r, 0))
     fixed_block = pl.BlockSpec((fixed_count, width), lambda r, *_: (0, 0))
@@ -654,7 +657,7 @@
     answers = pl.pallas_call(
         functools.partial(
             page_attention, n=n, cap=cap, draft=draft, heads=heads, page_len=page_len,
-            scale=scale, group=2,
+            scale=scale, group=math.gcd(n, 4),
         ),
         out_shape=HBM((n * block, LANES), BF16),
         in_specs=[whole(), whole(HBM)],

time: 138 us -> 137 us (level)
  Pallas kernels: 75.3 us -> 78.7 us
  waiting for transfers between devices: 23.1 us -> 20.4 us
    ppermute x1, waiting for transfers between devices: 0.01 us -> 6.08 us  [on_device(): one_m = lax.ppermute(half_mid, 'grp', swap)]
    ppermute x1, waiting for transfers between devices: 4.65 us -> 0.86 us  [on_device(): one_q = lax.ppermute(quarters, 'grp', swap)]
    pallas_call x1, Pallas kernels: 18 us -> 21.6 us  [on_device(): pl.pallas_call(functools.partial(update_memory, reqs=reqs, draft=draft, h...]
    ppermute x1, waiting for transfers between devices: 3.93 us -> 0.78 us  [on_device(): three_q = lax.ppermute(one_q[:near], 'req', other_chip)]
    all_to_all x1, starting transfers between devices: 7.49 us -> 5.41 us  [on_device(): lax.all_to_all(answers, 'req', split_axis=0, concat_axis=0, tiled=True)]
    ppermute x1, waiting for transfers between devices: 8.91 us -> 6.88 us  [on_device(): one_b = lax.ppermute(half_last, 'grp', swap)]
    slice x0 -> x1, local copies, waits for them, and re-layouts: none -> 1.79 us  [on_device(): three_q = lax.ppermute(one_q[:near], 'req', other_chip)]
  transfers between devices with their start and end apart: 16 -> 16, of which waited for: 5 -> 6; matrix products, arithmetic and copies ran while one was open for 2% -> 2% of each run, Pallas kernels for 50% -> 52%
where the time goes in v10:
time: 137 us
  Pallas kernels  78.7 us (57%)
  starting transfers between devices  30.2 us (22%)
  waiting for transfers between devices  20.4 us (15%)
  local copies, waits for them, and re-layouts  5.95 us (4%)
    pallas_call x1, Pallas kernels, on_device(): pl.pallas_call(functools.partial(update_memory, reqs=reqs, draft=draft, h...  21.6 us
    pallas_call x1, Pallas kernels, on_device(): pl.pallas_call(functools.partial(local_attention, heads=heads, draft=draf...  18.2 us
    all_to_all x1, starting transfers between devices, on_device(): lax.all_to_all(label, 'req', split_axis=0, concat_axis=0, tiled=True)  7.39 us
    pallas_call x1, Pallas kernels, on_device(): pl.pallas_call(feed_forward, out_shape=jax.ShapeDtypeStruct((rows, model)...  7.31 us
    pallas_call x1, Pallas kernels, on_device(): pl.pallas_call(functools.partial(page_attention, n=n, cap=cap, draft=draf...  7.11 us
    ppermute x1, waiting for transfers between devices, on_device(): one_b = lax.ppermute(half_last, 'grp', swap)  6.88 us
    pallas_call x1, Pallas kernels, on_device(): pl.pallas_call(stage_weights, out_shape=(VMEM((2,) + w_out.shape, BF16),...  6.71 us
    ppermute x1, waiting for transfers between devices, on_device(): one_m = lax.ppermute(half_mid, 'grp', swap)  6.08 us
  transfers between devices with their start and end apart: 16, of which 6 were waited for; matrix products, arithmetic and copies ran while one was open for 2% of the time, Pallas kernels for 52%

profile of v10, /device:TPU:0, one launch (start us, length us, event | category | flops | bytes accessed | tf_op | source)
XLA Modules:
  0.0 136.8 jit_solution(11705034143051363708)
XLA Ops:
  0.6 0.7 fusion.1
  1.3 0.7 reshape.20
  2.0 7.4 %all-to-all-start = ((s32[16,1,3]{2,1,0:T(1,128)}), s32[16,1,3]{2,1,0:T(1,128)S(1)}, u32[]{:S(2)}, u32[]{:S(2)}) async-start(s32[16,1,3]{2,1,0:T(1,128)} %bitcast.3), calls=%async_computation | async-start | bytes 16384 | tf_op jit(solution)/shard_map/all_to_all | solution.py:504
  9.4 0.1 pad_add_fusion.refs_0_.side
  9.5 4.5 %project_queries.1 = (bf16[512,512]{1,0:T(8,128)(2,1)}, bf16[2048,128]{1,0:T(8,128)(2,1)S(1)}, bf16[256,1408]{1,0:T(8,128)(2,1)}, bf16[480,1024]{1,0:T(8,128)(2,1)}) custom-call(s32[3]{0:T(128)S(1)} %pad_add_fusion.refs_0_.side, bf16[2,1024,1408]{2,1,0:T(8,128)(2,1)} %gate_up_w.2, bf16[1408,1024]{1,0:T(8,128)(2,1)} %down_w.1, bf16[512,1024]{1,0:T(8,128)(2,1)} %out_w.1, ...), custom_call_target="tpu_custom_call" | custom-call | flops 10737418240 | bytes 62914560 | tf_op jit(solution)/shard_map/project_queries/pallas_call | solution.py:518
  14.0 1.6 %collective-permute-start = (bf16[256,1408]{1,0:T(8,128)(2,1)}, bf16[256,1408]{1,0:T(8,128)(2,1)}, u32[]{:S(2)}, u32[]{:S(2)}) collective-permute-start(bf16[256,1408]{1,0:T(8,128)(2,1)} %get-tuple-element.70), channel_id=1, source_target_pairs={{0,1},{1,0},{2,3},{3,2},{4,5},{5,4},{6,7},{7,6},{8,9},{9,8},{10,11... | collective-permute-start | bytes 2162696 | tf_op jit(solution)/shard_map/ppermute | solution.py:544
  15.5 0.6 collective-permute-start.1
  16.1 0.0 all-to-all-done.codes
  16.1 2.2 %pack_queries.1 = bf16[6400,128]{1,0:T(8,128)(2,1)} custom-call(s32[16,1,3]{2,1,0:T(1,128)S(1)} %all-to-all-done.codes, s32[16]{0:T(128)} %lengths.1, bf16[2048,128]{1,0:T(8,128)(2,1)S(1)} %get-tuple-element.60.turned_ref), custom_call_target="tpu_custom_call" | custom-call | bytes 65536000 | tf_op jit(solution)/shard_map/pack_queries/pallas_call | solution.py:547
  18.3 6.0 %all-to-all-start.1 = ((bf16[16,400,128]{2,1,0:T(8,128)(2,1)}), bf16[16,400,128]{2,1,0:T(8,128)(2,1)S(1)}, u32[]{:S(2)}, u32[]{:S(2)}) async-start(bf16[16,400,128]{2,1,0:T(8,128)(2,1)} %bitcast.19), calls=%async_computation.1 | async-start | bytes 3276800 | tf_op jit(solution)/shard_map/all_to_all | solution.py:561
  24.3 0.0 copy-start.1
  24.3 0.0 copy-start.2
  24.3 0.0 copy-start.3
  24.3 0.0 copy-start.5
  24.3 4.1 %project_keys.1 = (bf16[512,512]{1,0:T(8,128)(2,1)}, bf16[512,512]{1,0:T(8,128)(2,1)}) custom-call(bf16[512,1024]{1,0:T(8,128)(2,1)} %tok_ref.2, f32[1,1024]{1,0:T(1,128)} %bitcast.22, bf16[1024,512]{1,0:T(8,128)(2,1)} %wk_ref.1, bf16[1024,512]{1,0:T(8,128)(2,1)} %wv_ref.1), custom_call_target="tpu_custom_call" | custom-call | flops 21474836480 | bytes 62914560 | tf_op jit(solution)/shard_map/project_keys/pallas_call | solution.py:575
  28.4 21.6 %update_memory.1 = (f32[16,4,128,128]{3,2,1,0:T(8,128)}, f32[16,4,128,128]{3,2,1,0:T(8,128)}) custom-call(s32[8,16]{1,0:T(8,128)S(1)} %bitcast.17, s32[16]{0:T(128)S(1)} %copy-done.5, s32[8,4,16]{2,1,0:T(4,128)S(1)} %bitcast.15, s32[8,4,16]{2,1,0:T(4,128)S(1)} %bitcast.16, bf16[512,512]{1,0:T(8,128)(2,1)} %get-tuple-element.63.k_ref, ...), custom_call_target="tpu_custom_call" | custom-call | flops 18790481920 | bytes 335544320 | tf_op jit(solution)/shard_map/update_memory/pallas_call | solution.py:615
  50.0 3.0 %cut_last.1 = (bf16[224,1408]{1,0:T(8,128)(2,1)}, bf16[544,1408]{1,0:T(8,128)(2,1)S(1)}) custom-call(s32[3]{0:T(128)S(1)} %pad_add_fusion.refs_0_.side, bf16[2,1024,1408]{2,1,0:T(8,128)(2,1)} %gate_up_w.2), custom_call_target="tpu_custom_call" | custom-call | bytes 86507520 | tf_op jit(solution)/shard_map/cut_last/pallas_call | solution.py:564
  53.0 0.0 collective-permute-done.one_a
  53.0 0.9 collective-permute-done.1.one_q
  53.9 1.8 %slice.6 = bf16[192,1024]{1,0:T(8,128)(2,1)} slice(bf16[480,1024]{1,0:T(8,128)(2,1)} %collective-permute-done.1.one_q), slice={[0:192], [0:1024]} | slice | bytes 786432 | tf_op jit(solution)/shard_map/slice | solution.py:652
  55.7 1.7 %collective-permute-start.3 = (bf16[192,1024]{1,0:T(8,128)(2,1)}, bf16[192,1024]{1,0:T(8,128)(2,1)}, u32[]{:S(2)}, u32[]{:S(2)}) collective-permute-start(bf16[192,1024]{1,0:T(8,128)(2,1)} %slice.6), channel_id=1, source_target_pairs={{0,4},{2,6},{4,0},{6,2},{8,12},{10,14},{12,8},{14,10},{16,20},{18,... | collective-permute-start | bytes 1179656 | tf_op jit(solution)/shard_map/ppermute | solution.py:652
  57.3 1.5 %collective-permute-start.2 = (bf16[224,1408]{1,0:T(8,128)(2,1)}, bf16[224,1408]{1,0:T(8,128)(2,1)}, u32[]{:S(2)}, u32[]{:S(2)}) collective-permute-start(bf16[224,1408]{1,0:T(8,128)(2,1)} %get-tuple-element.75), channel_id=1, source_target_pairs={{0,1},{1,0},{2,3},{3,2},{4,5},{5,4},{6,7},{7,6},{8,9},{9,8},{10,11... | collective-permute-start | bytes 1892360 | tf_op jit(solution)/shard_map/ppermute | solution.py:650
  58.8 0.0 all-to-all-done.1
  58.8 7.1 %page_attention.1 = bf16[6400,128]{1,0:T(8,128)(2,1)} custom-call(bf16[6400,128]{1,0:T(8,128)(2,1)S(1)} %bitcast.14, bf16[48,2,128,512]{3,2,1,0:T(8,128)(2,1)} %kv_hbm.1), custom_call_target="tpu_custom_call" | custom-call | flops 8053063680 | bytes 317194240 | tf_op jit(solution)/shard_map/page_attention/pallas_call | solution.py:657
  65.9 0.8 collective-permute-done.3.three_q
  66.7 6.1 %collective-permute-done.2.one_m = bf16[224,1408]{1,0:T(8,128)(2,1)} collective-permute-done((bf16[224,1408]{1,0:T(8,128)(2,1)}, bf16[224,1408]{1,0:T(8,128)(2,1)}, u32[]{:S(2)}, u32[]{:S(2)}) %collective-permute-start.2) | collective-permute-done | bytes 630816 | tf_op jit(solution)/shard_map/ppermute | solution.py:650
  72.8 5.4 %all-to-all-start.2 = ((bf16[16,400,128]{2,1,0:T(8,128)(2,1)}), bf16[16,400,128]{2,1,0:T(8,128)(2,1)S(1)}, u32[]{:S(2)}, u32[]{:S(2)}) async-start(bf16[16,400,128]{2,1,0:T(8,128)(2,1)} %bitcast.20), calls=%async_computation.2 | async-start | bytes 3276800 | tf_op jit(solution)/shard_map/all_to_all | solution.py:686
  78.2 1.6 %collective-permute-start.4 = (bf16[544,1408]{1,0:T(8,128)(2,1)S(1)}, bf16[544,1408]{1,0:T(8,128)(2,1)S(1)}, u32[]{:S(2)}, u32[]{:S(2)}) collective-permute-start(bf16[544,1408]{1,0:T(8,128)(2,1)S(1)} %get-tuple-element.78), channel_id=1, source_target_pairs={{0,1},{1,0},{2,3},{3,2},{4,5},{5,4},{6,7},{7,6},{8,9},{9,8},{10,11... | collective-permute-start | bytes 4595720 | tf_op jit(solution)/shard_map/ppermute | solution.py:651
  79.8 1.1 slice.7
  80.9 2.0 %collective-permute-start.9 = (bf16[288,1024]{1,0:T(8,128)(2,1)S(1)}, bf16[288,1024]{1,0:T(8,128)(2,1)S(1)}, u32[]{:S(2)}, u32[]{:S(2)}) collective-permute-start(bf16[288,1024]{1,0:T(8,128)(2,1)S(1)} %slice.7), channel_id=1, source_target_pairs={{0,4},{2,6},{4,0},{6,2},{8,12},{10,14},{12,8},{14,10},{16,20},{18,... | collective-permute-start | bytes 1769480 | tf_op jit(solution)/shard_map/ppermute | solution.py:653
  82.9 0.0 collective-permute-start.7
  82.9 0.5 collective-permute-start.5
  83.4 18.2 %local_attention.1 = (f32[2048,128]{1,0:T(8,128)}, f32[2048,128]{1,0:T(8,128)}, f32[16,128]{1,0:T(8,128)S(1)}, f32[16,128]{1,0:T(8,128)S(1)}) custom-call(bf16[512,512]{1,0:T(8,128)(2,1)} %get-tuple-element.81.q_ref, bf16[512,512]{1,0:T(8,128)(2,1)} %get-tuple-element.63.k_ref, bf16[512,512]{1,0:T(8,128)(2,1)} %get-tuple-element.64.v_ref, ...), custom_call_target="tpu_custom_call" | custom-call | flops 20 | bytes 20 | tf_op jit(solution)/shard_map/local_attention/pallas_call | solution.py:591
  101.5 0.0 collective-permute-start.6
  101.5 5.7 %collective-permute-done.9.three_r = bf16[288,1024]{1,0:T(8,128)(2,1)S(1)} collective-permute-done((bf16[288,1024]{1,0:T(8,128)(2,1)S(1)}, bf16[288,1024]{1,0:T(8,128)(2,1)S(1)}, u32[]{:S(2)}, u32[]{:S(2)}) %collective-permute-start.9) | collective-permute-done | bytes 589856 | tf_op jit(solution)/shard_map/ppermute | solution.py:653
  107.2 0.0 collective-permute-start.8
  107.3 6.9 %collective-permute-done.4.one_b = bf16[544,1408]{1,0:T(8,128)(2,1)S(1)} collective-permute-done((bf16[544,1408]{1,0:T(8,128)(2,1)S(1)}, bf16[544,1408]{1,0:T(8,128)(2,1)S(1)}, u32[]{:S(2)}, u32[]{:S(2)}) %collective-permute-start.4) | collective-permute-done | bytes 1531936 | tf_op jit(solution)/shard_map/ppermute | solution.py:651
  114.2 1.1 copy-done.6
  115.3 0.1 copy-done.10
  115.4 0.2 copy-done.8
  115.6 0.9 copy-done.7
  116.5 0.5 collective-permute-start.11
  117.0 4.1 %combine.1 = (bf16[256,512]{1,0:T(8,128)(2,1)S(1)}, bf16[256,512]{1,0:T(8,128)(2,1)S(1)}) custom-call(s32[16,1,3]{2,1,0:T(1,128)S(1)} %all-to-all-done.codes, s32[3]{0:T(128)S(1)} %pad_add_fusion.refs_0_.side, bf16[6400,128]{1,0:T(8,128)(2,1)S(1)} %bitcast.13, f32[2048,128]{1,0:T(8,128)} %get-tuple-element.91.o_hbm, f32[2048,128]{1,0:T(8,128)} %get-tuple-element.92.ret_hbm, ...), custom_call_target="tpu_custom_call" | custom-call | flops 125829120 | bytes 74711040 | tf_op jit(solution)/shard_map/combine/pallas_call | solution.py:696
  121.1 1.6 %collective-permute-start.12 = (bf16[256,512]{1,0:T(8,128)(2,1)S(1)}, bf16[256,512]{1,0:T(8,128)(2,1)S(1)}, u32[]{:S(2)}, u32[]{:S(2)}) collective-permute-start(bf16[256,512]{1,0:T(8,128)(2,1)S(1)} %get-tuple-element.99), channel_id=1, source_target_pairs={{0,1},{1,0},{2,3},{3,2},{4,5},{5,4},{6,7},{7,6},{8,9},{9,8},{10,11... | collective-permute-start | bytes 786440 | tf_op jit(solution)/shard_map/ppermute | solution.py:725
  122.7 0.0 copy-start.4
  122.7 6.7 %stage_weights.1 = (bf16[2,512,1024]{2,1,0:T(8,128)(2,1)S(1)}, bf16[2,2,1024,1408]{3,2,1,0:T(8,128)(2,1)S(1)}, bf16[2,1408,1024]{2,1,0:T(8,128)(2,1)S(1)}) custom-call(s32[3]{0:T(128)S(1)} %pad_add_fusion.refs_0_.side, bf16[512,1024]{1,0:T(8,128)(2,1)} %out_w.1, bf16[2,1024,1408]{2,1,0:T(8,128)(2,1)} %gate_up_w.2, bf16[1408,1024]{1,0:T(8,128)(2,1)} %down_w.1, ...), custom_call_target="tpu_custom_call" | custom-call | bytes 387973120 | tf_op jit(solution)/shard_map/stage_weights/pallas_call | solution.py:727
  129.4 0.1 collective-permute-done.12.theirs_ref
  129.5 7.3 %feed_forward.1 = bf16[256,1024]{1,0:T(8,128)(2,1)} custom-call(s32[3]{0:T(128)S(1)} %pad_add_fusion.refs_0_.side, bf16[512,1024]{1,0:T(8,128)(2,1)S(1)} %copy-done, bf16[256,512]{1,0:T(8,128)(2,1)S(1)} %get-tuple-element.98.mine_ref, bf16[256,512]{1,0:T(8,128)(2,1)S(1)} %collective-permute-done.12.theirs_ref, f32[1,1024]{1,0:T(1,128)S(1)} %bitcast.18, ...), custom_call_target="tpu_custom_call" | custom-call | flops 99321118720 | bytes 387973120 | tf_op jit(solution)/shard_map/feed_forward/pallas_call | solution.py:749
  (21 shorter events, 0.0 us)
Async XLA Ops:
  2.0 14.1 %all-to-all-start = ((s32[16,1,3]{2,1,0:T(1,128)}), s32[16,1,3]{2,1,0:T(1,128)S(1)}, u32[]{:S(2)}, u32[]{:S(2)}) async-start(s32[16,1,3]{2,1,0:T(1,128)} %bitcast.3), calls=%async_computation | async-start | bytes 16384 | tf_op jit(solution)/shard_map/all_to_all | solution.py:504
  14.0 39.0 %collective-permute-start = (bf16[256,1408]{1,0:T(8,128)(2,1)}, bf16[256,1408]{1,0:T(8,128)(2,1)}, u32[]{:S(2)}, u32[]{:S(2)}) collective-permute-start(bf16[256,1408]{1,0:T(8,128)(2,1)} %get-tuple-element.70), channel_id=1, source_target_pairs={{0,1},{1,0},{2,3},{3,2},{4,5},{5,4},{6,7},{7,6},{8,9},{9,8},{10,11... | collective-permute-start | bytes 2162696 | tf_op jit(solution)/shard_map/ppermute | solution.py:544
  15.5 38.3 %collective-permute-start.1 = (bf16[480,1024]{1,0:T(8,128)(2,1)}, bf16[480,1024]{1,0:T(8,128)(2,1)}, u32[]{:S(2)}, u32[]{:S(2)}) collective-permute-start(bf16[480,1024]{1,0:T(8,128)(2,1)} %get-tuple-element.71), channel_id=1, source_target_pairs={{0,1},{1,0},{2,3},{3,2},{4,5},{5,4},{6,7},{7,6},{8,9},{9,8},{10,11... | collective-permute-start | bytes 2949128 | tf_op jit(solution)/shard_map/ppermute | solution.py:545
  18.3 40.5 %all-to-all-start.1 = ((bf16[16,400,128]{2,1,0:T(8,128)(2,1)}), bf16[16,400,128]{2,1,0:T(8,128)(2,1)S(1)}, u32[]{:S(2)}, u32[]{:S(2)}) async-start(bf16[16,400,128]{2,1,0:T(8,128)(2,1)} %bitcast.19), calls=%async_computation.1 | async-start | bytes 3276800 | tf_op jit(solution)/shard_map/all_to_all | solution.py:561
  24.3 4.1 %copy-start.1 = (s32[16,8,4]{0,2,1:T(4,128)S(1)}, s32[16,8,4]{0,2,1:T(4,128)}, u32[]{:S(2)}) copy-start(s32[16,8,4]{0,2,1:T(4,128)} %param.39) | copy-start | bytes 6148
  24.3 4.1 %copy-start.2 = (s32[16,8,4]{0,2,1:T(4,128)S(1)}, s32[16,8,4]{0,2,1:T(4,128)}, u32[]{:S(2)}) copy-start(s32[16,8,4]{0,2,1:T(4,128)} %param.40) | copy-start | bytes 6148
  24.3 4.1 %copy-start.3 = (s32[16,8]{0,1:T(8,128)S(1)}, s32[16,8]{0,1:T(8,128)}, u32[]{:S(2)}) copy-start(s32[16,8]{0,1:T(8,128)} %param.35) | copy-start | bytes 1540
  24.3 4.1 %copy-start.5 = (s32[16]{0:T(128)S(1)}, s32[16]{0:T(128)}, u32[]{:S(2)}) copy-start(s32[16]{0:T(128)} %count.1) | copy-start | bytes 196
  55.7 11.1 %collective-permute-start.3 = (bf16[192,1024]{1,0:T(8,128)(2,1)}, bf16[192,1024]{1,0:T(8,128)(2,1)}, u32[]{:S(2)}, u32[]{:S(2)}) collective-permute-start(bf16[192,1024]{1,0:T(8,128)(2,1)} %slice.6), channel_id=1, source_target_pairs={{0,4},{2,6},{4,0},{6,2},{8,12},{10,14},{12,8},{14,10},{16,20},{18,... | collective-permute-start | bytes 1179656 | tf_op jit(solution)/shard_map/ppermute | solution.py:652
  57.3 15.5 %collective-permute-start.2 = (bf16[224,1408]{1,0:T(8,128)(2,1)}, bf16[224,1408]{1,0:T(8,128)(2,1)}, u32[]{:S(2)}, u32[]{:S(2)}) collective-permute-start(bf16[224,1408]{1,0:T(8,128)(2,1)} %get-tuple-element.75), channel_id=1, source_target_pairs={{0,1},{1,0},{2,3},{3,2},{4,5},{5,4},{6,7},{7,6},{8,9},{9,8},{10,11... | collective-permute-start | bytes 1892360 | tf_op jit(solution)/shard_map/ppermute | solution.py:650
  72.8 43.7 %all-to-all-start.2 = ((bf16[16,400,128]{2,1,0:T(8,128)(2,1)}), bf16[16,400,128]{2,1,0:T(8,128)(2,1)S(1)}, u32[]{:S(2)}, u32[]{:S(2)}) async-start(bf16[16,400,128]{2,1,0:T(8,128)(2,1)} %bitcast.20), calls=%async_computation.2 | async-start | bytes 3276800 | tf_op jit(solution)/shard_map/all_to_all | solution.py:686
  78.2 35.9 %collective-permute-start.4 = (bf16[544,1408]{1,0:T(8,128)(2,1)S(1)}, bf16[544,1408]{1,0:T(8,128)(2,1)S(1)}, u32[]{:S(2)}, u32[]{:S(2)}) collective-permute-start(bf16[544,1408]{1,0:T(8,128)(2,1)S(1)} %get-tuple-element.78), channel_id=1, source_target_pairs={{0,1},{1,0},{2,3},{3,2},{4,5},{5,4},{6,7},{7,6},{8,9},{9,8},{10,11... | collective-permute-start | bytes 4595720 | tf_op jit(solution)/shard_map/ppermute | solution.py:651
  80.9 26.4 %collective-permute-start.9 = (bf16[288,1024]{1,0:T(8,128)(2,1)S(1)}, bf16[288,1024]{1,0:T(8,128)(2,1)S(1)}, u32[]{:S(2)}, u32[]{:S(2)}) collective-permute-start(bf16[288,1024]{1,0:T(8,128)(2,1)S(1)} %slice.7), channel_id=1, source_target_pairs={{0,4},{2,6},{4,0},{6,2},{8,12},{10,14},{12,8},{14,10},{16,20},{18,... | collective-permute-start | bytes 1769480 | tf_op jit(solution)/shard_map/ppermute | solution.py:653
  82.9 33.6 %collective-permute-start.7 = (bf16[480,1024]{1,0:T(8,128)(2,1)}, bf16[480,1024]{1,0:T(8,128)(2,1)}, u32[]{:S(2)}, u32[]{:S(2)}) collective-permute-start(bf16[480,1024]{1,0:T(8,128)(2,1)} %collective-permute-done.1.one_q), channel_id=1, source_target_pairs={{0,2},{2,0},{4,6},{6,4},{8,10},{10,8},{12,14},{14,12},{16,18},{18,... | collective-permute-start | bytes 2949128 | tf_op jit(solution)/shard_map/ppermute | solution.py:684
  82.9 31.3 %collective-permute-start.5 = (bf16[256,1408]{1,0:T(8,128)(2,1)}, bf16[256,1408]{1,0:T(8,128)(2,1)S(1)}, u32[]{:S(2)}, u32[]{:S(2)}) collective-permute-start(bf16[256,1408]{1,0:T(8,128)(2,1)} %collective-permute-done.one_a), channel_id=1, source_target_pairs={{0,2},{2,0},{4,6},{6,4},{8,10},{10,8},{12,14},{14,12},{16,18},{18,... | collective-permute-start | bytes 2162696 | tf_op jit(solution)/shard_map/ppermute | solution.py:684
  101.5 12.6 %collective-permute-start.6 = (bf16[224,1408]{1,0:T(8,128)(2,1)}, bf16[224,1408]{1,0:T(8,128)(2,1)S(1)}, u32[]{:S(2)}, u32[]{:S(2)}) collective-permute-start(bf16[224,1408]{1,0:T(8,128)(2,1)} %collective-permute-done.2.one_m), channel_id=1, source_target_pairs={{0,2},{2,0},{4,6},{6,4},{8,10},{10,8},{12,14},{14,12},{16,18},{18,... | collective-permute-start | bytes 1892360 | tf_op jit(solution)/shard_map/ppermute | solution.py:684
  107.2 6.9 %copy-start.9 = (bf16[288,1024]{1,0:T(8,128)(2,1)}, bf16[288,1024]{1,0:T(8,128)(2,1)S(1)}, u32[]{:S(2)}) copy-start(bf16[288,1024]{1,0:T(8,128)(2,1)S(1)} %collective-permute-done.9.three_r) | copy-start | bytes 1769476
  107.2 6.9 %collective-permute-start.8 = (bf16[192,1024]{1,0:T(8,128)(2,1)}, bf16[192,1024]{1,0:T(8,128)(2,1)S(1)}, u32[]{:S(2)}, u32[]{:S(2)}) collective-permute-start(bf16[192,1024]{1,0:T(8,128)(2,1)} %collective-permute-done.3.three_q), channel_id=1, source_target_pairs={{0,2},{2,0},{4,6},{6,4},{8,10},{10,8},{12,14},{14,12},{16,18},{18,... | collective-permute-start | bytes 1179656 | tf_op jit(solution)/shard_map/ppermute | solution.py:684
  114.1 1.1 copy-start.6
  114.1 1.2 copy-start.10
  114.1 1.4 %copy-start.8 = (bf16[224,1408]{1,0:T(8,128)(2,1)}, bf16[224,1408]{1,0:T(8,128)(2,1)S(1)}, u32[]{:S(2)}) copy-start(bf16[224,1408]{1,0:T(8,128)(2,1)S(1)} %collective-permute-done.6.two_m) | copy-start | bytes 1892356
  115.6 0.9 copy-start.7
  116.5 6.2 %collective-permute-start.10 = (bf16[544,1408]{1,0:T(8,128)(2,1)}, bf16[544,1408]{1,0:T(8,128)(2,1)S(1)}, u32[]{:S(2)}, u32[]{:S(2)}) collective-permute-start(bf16[544,1408]{1,0:T(8,128)(2,1)} %copy-done.6), channel_id=1, source_target_pairs={{0,2},{2,0},{4,6},{6,4},{8,10},{10,8},{12,14},{14,12},{16,18},{18,... | collective-permute-start | bytes 4595720 | tf_op jit(solution)/shard_map/ppermute | solution.py:693
  116.5 6.2 %collective-permute-start.11 = (bf16[288,1024]{1,0:T(8,128)(2,1)}, bf16[288,1024]{1,0:T(8,128)(2,1)S(1)}, u32[]{:S(2)}, u32[]{:S(2)}) collective-permute-start(bf16[288,1024]{1,0:T(8,128)(2,1)} %copy-done.9), channel_id=1, source_target_pairs={{0,2},{2,0},{4,6},{6,4},{8,10},{10,8},{12,14},{14,12},{16,18},{18,... | collective-permute-start | bytes 1769480 | tf_op jit(solution)/shard_map/ppermute | solution.py:694
  121.1 8.4 %collective-permute-start.12 = (bf16[256,512]{1,0:T(8,128)(2,1)S(1)}, bf16[256,512]{1,0:T(8,128)(2,1)S(1)}, u32[]{:S(2)}, u32[]{:S(2)}) collective-permute-start(bf16[256,512]{1,0:T(8,128)(2,1)S(1)} %get-tuple-element.99), channel_id=1, source_target_pairs={{0,1},{1,0},{2,3},{3,2},{4,5},{5,4},{6,7},{7,6},{8,9},{9,8},{10,11... | collective-permute-start | bytes 786440 | tf_op jit(solution)/shard_map/ppermute | solution.py:725
  122.7 6.8 %copy-start = (bf16[512,1024]{1,0:T(8,128)(2,1)S(1)}, bf16[512,1024]{1,0:T(8,128)(2,1)}, u32[]{:S(2)}) copy-start(bf16[512,1024]{1,0:T(8,128)(2,1)} %tok_ref.2) | copy-start | bytes 3145732
  122.7 6.8 %copy-start.4 = (f32[1024]{0:T(1024)S(1)}, f32[1024]{0:T(1024)}, u32[]{:S(2)}) copy-start(f32[1024]{0:T(1024)} %param.41) | copy-start | bytes 12292

commit v11 on v10

--- a/solution.py
+++ b/solution.py
@@ -505,7 +505,7 @@
 
     grp = lax.axis_size("grp")
     depth, out_depth = w_down.shape[0] // 4, width // 4
-    first, middle = model // 4, model * 7 // 32
+    first, middle = model // 4, model * 6 // 32
     near = depth * 6 // 11 // EXTRA * EXTRA
     split = (depth, out_depth, first // 2, middle, (model - first - middle) // 2)
     pieces = 2 if grp == 2 and n % 4 == 0 and not any(size % EXTRA for size in split) else 1
@@ -642,8 +642,8 @@
     )
 
     if pieces == 2:
-        memory_out, momentum_out, half_mid, half_last, one_a, one_q = lax.optimization_barrier(
-            (memory_out, momentum_out, half_mid, half_last, one_a, one_q)
+        memory_out, momentum_out, half_last, one_a, one_q = lax.optimization_barrier(
+            (memory_out, momentum_out, half_last, one_a, one_q)
         )
         other_core = [(i, i ^ 1) for i in range(n)]
         other_chip = [(i, i ^ 2) for i in range(n)]

time: 137 us -> 136 us (level)
  waiting for transfers between devices: 20.4 us -> 18 us
  starting transfers between devices: 30.2 us -> 31.8 us
    ppermute x1, waiting for transfers between devices: 6.08 us -> 0.2 us  [on_device(): one_m = lax.ppermute(half_mid, 'grp', swap)]
    ppermute x1, waiting for transfers between devices: 6.88 us -> 8.81 us  [on_device(): one_b = lax.ppermute(half_last, 'grp', swap)]
where the time goes in v11:
time: 136 us; the launch traced here: 135 us
  Pallas kernels  77.5 us (57%)
  starting transfers between devices  31.8 us (23%)
  waiting for transfers between devices  18 us (13%)
  local copies, waits for them, and re-layouts  6 us (4%)
    pallas_call x1, Pallas kernels, on_device(): pl.pallas_call(functools.partial(update_memory, reqs=reqs, draft=draft, h...  20.4 us
    pallas_call x1, Pallas kernels, on_device(): pl.pallas_call(functools.partial(local_attention, heads=heads, draft=draf...  18.2 us
    ppermute x1, waiting for transfers between devices, on_device(): one_b = lax.ppermute(half_last, 'grp', swap)  8.81 us
    all_to_all x1, starting transfers between devices, on_device(): lax.all_to_all(label, 'req', split_axis=0, concat_axis=0, tiled=True)  7.39 us
    pallas_call x1, Pallas kernels, on_device(): pl.pallas_call(feed_forward, out_shape=jax.ShapeDtypeStruct((rows, model)...  7.31 us
    pallas_call x1, Pallas kernels, on_device(): pl.pallas_call(functools.partial(page_attention, n=n, cap=cap, draft=draf...  7.12 us
    pallas_call x1, Pallas kernels, on_device(): pl.pallas_call(stage_weights, out_shape=(VMEM((2,) + w_out.shape, BF16),...  6.69 us
    all_to_all x1, starting transfers between devices, on_device(): lax.all_to_all(answers, 'req', split_axis=0, concat_axis=0, tiled=True)  6.68 us
  transfers between devices with their start and end apart: 16, of which 6 were waited for; matrix products, arithmetic and copies ran while one was open for 2% of the time, Pallas kernels for 52%

profile of v11, /device:TPU:0, one launch (start us, length us, event | category | flops | bytes accessed | tf_op | source)
XLA Modules:
  0.0 134.9 jit_solution(5971287833210632)
XLA Ops:
  0.6 0.7 fusion.1
  1.3 0.7 reshape.20
  2.0 7.4 %all-to-all-start = ((s32[16,1,3]{2,1,0:T(1,128)}), s32[16,1,3]{2,1,0:T(1,128)S(1)}, u32[]{:S(2)}, u32[]{:S(2)}) async-start(s32[16,1,3]{2,1,0:T(1,128)} %bitcast.3), calls=%async_computation | async-start | bytes 16384 | tf_op jit(solution)/shard_map/all_to_all | solution.py:504
  9.4 0.1 pad_add_fusion.refs_0_.side
  9.5 4.5 %project_queries.1 = (bf16[512,512]{1,0:T(8,128)(2,1)}, bf16[2048,128]{1,0:T(8,128)(2,1)S(1)}, bf16[256,1408]{1,0:T(8,128)(2,1)}, bf16[480,1024]{1,0:T(8,128)(2,1)}) custom-call(s32[3]{0:T(128)S(1)} %pad_add_fusion.refs_0_.side, bf16[2,1024,1408]{2,1,0:T(8,128)(2,1)} %gate_up_w.2, bf16[1408,1024]{1,0:T(8,128)(2,1)} %down_w.1, bf16[512,1024]{1,0:T(8,128)(2,1)} %out_w.1, ...), custom_call_target="tpu_custom_call" | custom-call | flops 10737418240 | bytes 62914560 | tf_op jit(solution)/shard_map/project_queries/pallas_call | solution.py:518
  14.0 1.6 %collective-permute-start = (bf16[256,1408]{1,0:T(8,128)(2,1)}, bf16[256,1408]{1,0:T(8,128)(2,1)}, u32[]{:S(2)}, u32[]{:S(2)}) collective-permute-start(bf16[256,1408]{1,0:T(8,128)(2,1)} %get-tuple-element.68), channel_id=1, source_target_pairs={{0,1},{1,0},{2,3},{3,2},{4,5},{5,4},{6,7},{7,6},{8,9},{9,8},{10,11... | collective-permute-start | bytes 2162696 | tf_op jit(solution)/shard_map/ppermute | solution.py:544
  15.6 0.6 collective-permute-start.1
  16.1 0.0 all-to-all-done.codes
  16.1 2.2 %pack_queries.1 = bf16[6400,128]{1,0:T(8,128)(2,1)} custom-call(s32[16,1,3]{2,1,0:T(1,128)S(1)} %all-to-all-done.codes, s32[16]{0:T(128)} %lengths.1, bf16[2048,128]{1,0:T(8,128)(2,1)S(1)} %get-tuple-element.59.turned_ref), custom_call_target="tpu_custom_call" | custom-call | bytes 65536000 | tf_op jit(solution)/shard_map/pack_queries/pallas_call | solution.py:547
  18.3 6.0 %all-to-all-start.1 = ((bf16[16,400,128]{2,1,0:T(8,128)(2,1)}), bf16[16,400,128]{2,1,0:T(8,128)(2,1)S(1)}, u32[]{:S(2)}, u32[]{:S(2)}) async-start(bf16[16,400,128]{2,1,0:T(8,128)(2,1)} %bitcast.19), calls=%async_computation.1 | async-start | bytes 3276800 | tf_op jit(solution)/shard_map/all_to_all | solution.py:561
  24.3 3.0 %cut_last.1 = (bf16[192,1408]{1,0:T(8,128)(2,1)}, bf16[576,1408]{1,0:T(8,128)(2,1)S(1)}) custom-call(s32[3]{0:T(128)S(1)} %pad_add_fusion.refs_0_.side, bf16[2,1024,1408]{2,1,0:T(8,128)(2,1)} %gate_up_w.2), custom_call_target="tpu_custom_call" | custom-call | bytes 86507520 | tf_op jit(solution)/shard_map/cut_last/pallas_call | solution.py:564
  27.3 0.0 copy-start.1
  27.3 0.0 copy-start.2
  27.3 0.0 copy-start.3
  27.3 0.0 copy-start.5
  27.3 1.6 %collective-permute-start.2 = (bf16[192,1408]{1,0:T(8,128)(2,1)}, bf16[192,1408]{1,0:T(8,128)(2,1)}, u32[]{:S(2)}, u32[]{:S(2)}) collective-permute-start(bf16[192,1408]{1,0:T(8,128)(2,1)} %get-tuple-element.73), channel_id=1, source_target_pairs={{0,1},{1,0},{2,3},{3,2},{4,5},{5,4},{6,7},{7,6},{8,9},{9,8},{10,11... | collective-permute-start | bytes 1622024 | tf_op jit(solution)/shard_map/ppermute | solution.py:650
  28.9 4.1 %project_keys.1 = (bf16[512,512]{1,0:T(8,128)(2,1)}, bf16[512,512]{1,0:T(8,128)(2,1)}) custom-call(bf16[512,1024]{1,0:T(8,128)(2,1)} %tok_ref.2, f32[1,1024]{1,0:T(1,128)} %bitcast.22, bf16[1024,512]{1,0:T(8,128)(2,1)} %wk_ref.1, bf16[1024,512]{1,0:T(8,128)(2,1)} %wv_ref.1), custom_call_target="tpu_custom_call" | custom-call | flops 21474836480 | bytes 62914560 | tf_op jit(solution)/shard_map/project_keys/pallas_call | solution.py:575
  33.0 20.4 %update_memory.1 = (f32[16,4,128,128]{3,2,1,0:T(8,128)}, f32[16,4,128,128]{3,2,1,0:T(8,128)}) custom-call(s32[8,16]{1,0:T(8,128)S(1)} %bitcast.17, s32[16]{0:T(128)S(1)} %copy-done.5, s32[8,4,16]{2,1,0:T(4,128)S(1)} %bitcast.15, s32[8,4,16]{2,1,0:T(4,128)S(1)} %bitcast.16, bf16[512,512]{1,0:T(8,128)(2,1)} %get-tuple-element.62.k_ref, ...), custom_call_target="tpu_custom_call" | custom-call | flops 18790481920 | bytes 335544320 | tf_op jit(solution)/shard_map/update_memory/pallas_call | solution.py:615
  53.4 0.0 collective-permute-done.one_a
  53.4 1.1 collective-permute-done.1.one_q
  54.4 1.8 %slice.6 = bf16[192,1024]{1,0:T(8,128)(2,1)} slice(bf16[480,1024]{1,0:T(8,128)(2,1)} %collective-permute-done.1.one_q), slice={[0:192], [0:1024]} | slice | bytes 786432 | tf_op jit(solution)/shard_map/slice | solution.py:652
  56.2 1.9 %collective-permute-start.3 = (bf16[192,1024]{1,0:T(8,128)(2,1)}, bf16[192,1024]{1,0:T(8,128)(2,1)}, u32[]{:S(2)}, u32[]{:S(2)}) collective-permute-start(bf16[192,1024]{1,0:T(8,128)(2,1)} %slice.6), channel_id=1, source_target_pairs={{0,4},{2,6},{4,0},{6,2},{8,12},{10,14},{12,8},{14,10},{16,20},{18,... | collective-permute-start | bytes 1179656 | tf_op jit(solution)/shard_map/ppermute | solution.py:652
  58.1 0.0 all-to-all-done.1
  58.1 7.1 %page_attention.1 = bf16[6400,128]{1,0:T(8,128)(2,1)} custom-call(bf16[6400,128]{1,0:T(8,128)(2,1)S(1)} %bitcast.14, bf16[48,2,128,512]{3,2,1,0:T(8,128)(2,1)} %kv_hbm.1), custom_call_target="tpu_custom_call" | custom-call | flops 8053063680 | bytes 317194240 | tf_op jit(solution)/shard_map/page_attention/pallas_call | solution.py:657
  65.3 0.2 collective-permute-done.2.one_m
  65.5 2.1 %collective-permute-done.3.three_q = bf16[192,1024]{1,0:T(8,128)(2,1)} collective-permute-done((bf16[192,1024]{1,0:T(8,128)(2,1)}, bf16[192,1024]{1,0:T(8,128)(2,1)}, u32[]{:S(2)}, u32[]{:S(2)}) %collective-permute-start.3) | collective-permute-done | bytes 393248 | tf_op jit(solution)/shard_map/ppermute | solution.py:652
  67.6 6.7 %all-to-all-start.2 = ((bf16[16,400,128]{2,1,0:T(8,128)(2,1)}), bf16[16,400,128]{2,1,0:T(8,128)(2,1)S(1)}, u32[]{:S(2)}, u32[]{:S(2)}) async-start(bf16[16,400,128]{2,1,0:T(8,128)(2,1)} %bitcast.20), calls=%async_computation.2 | async-start | bytes 3276800 | tf_op jit(solution)/shard_map/all_to_all | solution.py:686
  74.3 1.6 %collective-permute-start.4 = (bf16[576,1408]{1,0:T(8,128)(2,1)S(1)}, bf16[576,1408]{1,0:T(8,128)(2,1)S(1)}, u32[]{:S(2)}, u32[]{:S(2)}) collective-permute-start(bf16[576,1408]{1,0:T(8,128)(2,1)S(1)} %get-tuple-element.76), channel_id=1, source_target_pairs={{0,1},{1,0},{2,3},{3,2},{4,5},{5,4},{6,7},{7,6},{8,9},{9,8},{10,11... | collective-permute-start | bytes 4866056 | tf_op jit(solution)/shard_map/ppermute | solution.py:651
  75.9 1.1 slice.7
  77.0 2.0 %collective-permute-start.9 = (bf16[288,1024]{1,0:T(8,128)(2,1)S(1)}, bf16[288,1024]{1,0:T(8,128)(2,1)S(1)}, u32[]{:S(2)}, u32[]{:S(2)}) collective-permute-start(bf16[288,1024]{1,0:T(8,128)(2,1)S(1)} %slice.7), channel_id=1, source_target_pairs={{0,4},{2,6},{4,0},{6,2},{8,12},{10,14},{12,8},{14,10},{16,20},{18,... | collective-permute-start | bytes 1769480 | tf_op jit(solution)/shard_map/ppermute | solution.py:653
  78.9 0.5 collective-permute-start.5
  79.5 18.2 %local_attention.1 = (f32[2048,128]{1,0:T(8,128)}, f32[2048,128]{1,0:T(8,128)}, f32[16,128]{1,0:T(8,128)S(1)}, f32[16,128]{1,0:T(8,128)S(1)}) custom-call(bf16[512,512]{1,0:T(8,128)(2,1)} %get-tuple-element.79.q_ref, bf16[512,512]{1,0:T(8,128)(2,1)} %get-tuple-element.62.k_ref, bf16[512,512]{1,0:T(8,128)(2,1)} %get-tuple-element.63.v_ref, ...), custom_call_target="tpu_custom_call" | custom-call | flops 20 | bytes 20 | tf_op jit(solution)/shard_map/local_attention/pallas_call | solution.py:591
  97.6 0.0 collective-permute-start.6
  97.6 5.7 %collective-permute-done.9.three_r = bf16[288,1024]{1,0:T(8,128)(2,1)S(1)} collective-permute-done((bf16[288,1024]{1,0:T(8,128)(2,1)S(1)}, bf16[288,1024]{1,0:T(8,128)(2,1)S(1)}, u32[]{:S(2)}, u32[]{:S(2)}) %collective-permute-start.9) | collective-permute-done | bytes 589856 | tf_op jit(solution)/shard_map/ppermute | solution.py:653
  103.3 0.0 collective-permute-start.8
  103.3 8.8 %collective-permute-done.4.one_b = bf16[576,1408]{1,0:T(8,128)(2,1)S(1)} collective-permute-done((bf16[576,1408]{1,0:T(8,128)(2,1)S(1)}, bf16[576,1408]{1,0:T(8,128)(2,1)S(1)}, u32[]{:S(2)}, u32[]{:S(2)}) %collective-permute-start.4) | collective-permute-done | bytes 1622048 | tf_op jit(solution)/shard_map/ppermute | solution.py:651
  112.2 0.0 collective-permute-done.6.two_m
  112.2 1.1 copy-done.6
  113.3 0.1 copy-done.10
  113.4 0.2 copy-done.9
  113.6 0.9 copy-done.7
  114.6 0.5 collective-permute-start.11
  115.1 4.1 %combine.1 = (bf16[256,512]{1,0:T(8,128)(2,1)S(1)}, bf16[256,512]{1,0:T(8,128)(2,1)S(1)}) custom-call(s32[16,1,3]{2,1,0:T(1,128)S(1)} %all-to-all-done.codes, s32[3]{0:T(128)S(1)} %pad_add_fusion.refs_0_.side, bf16[6400,128]{1,0:T(8,128)(2,1)S(1)} %bitcast.13, f32[2048,128]{1,0:T(8,128)} %get-tuple-element.89.o_hbm, f32[2048,128]{1,0:T(8,128)} %get-tuple-element.90.ret_hbm, ...), custom_call_target="tpu_custom_call" | custom-call | flops 125829120 | bytes 74711040 | tf_op jit(solution)/shard_map/combine/pallas_call | solution.py:696
  119.2 1.6 %collective-permute-start.12 = (bf16[256,512]{1,0:T(8,128)(2,1)S(1)}, bf16[256,512]{1,0:T(8,128)(2,1)S(1)}, u32[]{:S(2)}, u32[]{:S(2)}) collective-permute-start(bf16[256,512]{1,0:T(8,128)(2,1)S(1)} %get-tuple-element.97), channel_id=1, source_target_pairs={{0,1},{1,0},{2,3},{3,2},{4,5},{5,4},{6,7},{7,6},{8,9},{9,8},{10,11... | collective-permute-start | bytes 786440 | tf_op jit(solution)/shard_map/ppermute | solution.py:725
  120.8 0.0 copy-start.4
  120.8 6.7 %stage_weights.1 = (bf16[2,512,1024]{2,1,0:T(8,128)(2,1)S(1)}, bf16[2,2,1024,1408]{3,2,1,0:T(8,128)(2,1)S(1)}, bf16[2,1408,1024]{2,1,0:T(8,128)(2,1)S(1)}) custom-call(s32[3]{0:T(128)S(1)} %pad_add_fusion.refs_0_.side, bf16[512,1024]{1,0:T(8,128)(2,1)} %out_w.1, bf16[2,1024,1408]{2,1,0:T(8,128)(2,1)} %gate_up_w.2, bf16[1408,1024]{1,0:T(8,128)(2,1)} %down_w.1, ...), custom_call_target="tpu_custom_call" | custom-call | bytes 387973120 | tf_op jit(solution)/shard_map/stage_weights/pallas_call | solution.py:727
  127.5 0.1 collective-permute-done.12.theirs_ref
  127.6 7.3 %feed_forward.1 = bf16[256,1024]{1,0:T(8,128)(2,1)} custom-call(s32[3]{0:T(128)S(1)} %pad_add_fusion.refs_0_.side, bf16[512,1024]{1,0:T(8,128)(2,1)S(1)} %copy-done, bf16[256,512]{1,0:T(8,128)(2,1)S(1)} %get-tuple-element.96.mine_ref, bf16[256,512]{1,0:T(8,128)(2,1)S(1)} %collective-permute-done.12.theirs_ref, f32[1,1024]{1,0:T(1,128)S(1)} %bitcast.18, ...), custom_call_target="tpu_custom_call" | custom-call | flops 99321118720 | bytes 387973120 | tf_op jit(solution)/shard_map/feed_forward/pallas_call | solution.py:749
  (21 shorter events, 0.0 us)
Async XLA Ops:
  2.0 14.1 %all-to-all-start = ((s32[16,1,3]{2,1,0:T(1,128)}), s32[16,1,3]{2,1,0:T(1,128)S(1)}, u32[]{:S(2)}, u32[]{:S(2)}) async-start(s32[16,1,3]{2,1,0:T(1,128)} %bitcast.3), calls=%async_computation | async-start | bytes 16384 | tf_op jit(solution)/shard_map/all_to_all | solution.py:504
  14.0 39.4 %collective-permute-start = (bf16[256,1408]{1,0:T(8,128)(2,1)}, bf16[256,1408]{1,0:T(8,128)(2,1)}, u32[]{:S(2)}, u32[]{:S(2)}) collective-permute-start(bf16[256,1408]{1,0:T(8,128)(2,1)} %get-tuple-element.68), channel_id=1, source_target_pairs={{0,1},{1,0},{2,3},{3,2},{4,5},{5,4},{6,7},{7,6},{8,9},{9,8},{10,11... | collective-permute-start | bytes 2162696 | tf_op jit(solution)/shard_map/ppermute | solution.py:544
  15.6 38.9 %collective-permute-start.1 = (bf16[480,1024]{1,0:T(8,128)(2,1)}, bf16[480,1024]{1,0:T(8,128)(2,1)}, u32[]{:S(2)}, u32[]{:S(2)}) collective-permute-start(bf16[480,1024]{1,0:T(8,128)(2,1)} %get-tuple-element.69), channel_id=1, source_target_pairs={{0,1},{1,0},{2,3},{3,2},{4,5},{5,4},{6,7},{7,6},{8,9},{9,8},{10,11... | collective-permute-start | bytes 2949128 | tf_op jit(solution)/shard_map/ppermute | solution.py:545
  18.3 39.8 %all-to-all-start.1 = ((bf16[16,400,128]{2,1,0:T(8,128)(2,1)}), bf16[16,400,128]{2,1,0:T(8,128)(2,1)S(1)}, u32[]{:S(2)}, u32[]{:S(2)}) async-start(bf16[16,400,128]{2,1,0:T(8,128)(2,1)} %bitcast.19), calls=%async_computation.1 | async-start | bytes 3276800 | tf_op jit(solution)/shard_map/all_to_all | solution.py:561
  27.3 5.7 %copy-start.1 = (s32[16,8,4]{0,2,1:T(4,128)S(1)}, s32[16,8,4]{0,2,1:T(4,128)}, u32[]{:S(2)}) copy-start(s32[16,8,4]{0,2,1:T(4,128)} %param.39) | copy-start | bytes 6148
  27.3 5.7 %copy-start.2 = (s32[16,8,4]{0,2,1:T(4,128)S(1)}, s32[16,8,4]{0,2,1:T(4,128)}, u32[]{:S(2)}) copy-start(s32[16,8,4]{0,2,1:T(4,128)} %param.40) | copy-start | bytes 6148
  27.3 5.7 %copy-start.3 = (s32[16,8]{0,1:T(8,128)S(1)}, s32[16,8]{0,1:T(8,128)}, u32[]{:S(2)}) copy-start(s32[16,8]{0,1:T(8,128)} %param.35) | copy-start | bytes 1540
  27.3 5.7 %copy-start.5 = (s32[16]{0:T(128)S(1)}, s32[16]{0:T(128)}, u32[]{:S(2)}) copy-start(s32[16]{0:T(128)} %count.1) | copy-start | bytes 196
  27.3 38.2 %collective-permute-start.2 = (bf16[192,1408]{1,0:T(8,128)(2,1)}, bf16[192,1408]{1,0:T(8,128)(2,1)}, u32[]{:S(2)}, u32[]{:S(2)}) collective-permute-start(bf16[192,1408]{1,0:T(8,128)(2,1)} %get-tuple-element.73), channel_id=1, source_target_pairs={{0,1},{1,0},{2,3},{3,2},{4,5},{5,4},{6,7},{7,6},{8,9},{9,8},{10,11... | collective-permute-start | bytes 1622024 | tf_op jit(solution)/shard_map/ppermute | solution.py:650
  56.2 11.4 %collective-permute-start.3 = (bf16[192,1024]{1,0:T(8,128)(2,1)}, bf16[192,1024]{1,0:T(8,128)(2,1)}, u32[]{:S(2)}, u32[]{:S(2)}) collective-permute-start(bf16[192,1024]{1,0:T(8,128)(2,1)} %slice.6), channel_id=1, source_target_pairs={{0,4},{2,6},{4,0},{6,2},{8,12},{10,14},{12,8},{14,10},{16,20},{18,... | collective-permute-start | bytes 1179656 | tf_op jit(solution)/shard_map/ppermute | solution.py:652
  67.6 47.0 %all-to-all-start.2 = ((bf16[16,400,128]{2,1,0:T(8,128)(2,1)}), bf16[16,400,128]{2,1,0:T(8,128)(2,1)S(1)}, u32[]{:S(2)}, u32[]{:S(2)}) async-start(bf16[16,400,128]{2,1,0:T(8,128)(2,1)} %bitcast.20), calls=%async_computation.2 | async-start | bytes 3276800 | tf_op jit(solution)/shard_map/all_to_all | solution.py:686
  74.3 37.8 %collective-permute-start.4 = (bf16[576,1408]{1,0:T(8,128)(2,1)S(1)}, bf16[576,1408]{1,0:T(8,128)(2,1)S(1)}, u32[]{:S(2)}, u32[]{:S(2)}) collective-permute-start(bf16[576,1408]{1,0:T(8,128)(2,1)S(1)} %get-tuple-element.76), channel_id=1, source_target_pairs={{0,1},{1,0},{2,3},{3,2},{4,5},{5,4},{6,7},{7,6},{8,9},{9,8},{10,11... | collective-permute-start | bytes 4866056 | tf_op jit(solution)/shard_map/ppermute | solution.py:651
  77.0 26.4 %collective-permute-start.9 = (bf16[288,1024]{1,0:T(8,128)(2,1)S(1)}, bf16[288,1024]{1,0:T(8,128)(2,1)S(1)}, u32[]{:S(2)}, u32[]{:S(2)}) collective-permute-start(bf16[288,1024]{1,0:T(8,128)(2,1)S(1)} %slice.7), channel_id=1, source_target_pairs={{0,4},{2,6},{4,0},{6,2},{8,12},{10,14},{12,8},{14,10},{16,20},{18,... | collective-permute-start | bytes 1769480 | tf_op jit(solution)/shard_map/ppermute | solution.py:653
  78.9 35.6 %collective-permute-start.7 = (bf16[480,1024]{1,0:T(8,128)(2,1)}, bf16[480,1024]{1,0:T(8,128)(2,1)}, u32[]{:S(2)}, u32[]{:S(2)}) collective-permute-start(bf16[480,1024]{1,0:T(8,128)(2,1)} %collective-permute-done.1.one_q), channel_id=1, source_target_pairs={{0,2},{2,0},{4,6},{6,4},{8,10},{10,8},{12,14},{14,12},{16,18},{18,... | collective-permute-start | bytes 2949128 | tf_op jit(solution)/shard_map/ppermute | solution.py:684
  78.9 33.2 %collective-permute-start.5 = (bf16[256,1408]{1,0:T(8,128)(2,1)}, bf16[256,1408]{1,0:T(8,128)(2,1)S(1)}, u32[]{:S(2)}, u32[]{:S(2)}) collective-permute-start(bf16[256,1408]{1,0:T(8,128)(2,1)} %collective-permute-done.one_a), channel_id=1, source_target_pairs={{0,2},{2,0},{4,6},{6,4},{8,10},{10,8},{12,14},{14,12},{16,18},{18,... | collective-permute-start | bytes 2162696 | tf_op jit(solution)/shard_map/ppermute | solution.py:684
  97.6 14.6 %collective-permute-start.6 = (bf16[192,1408]{1,0:T(8,128)(2,1)}, bf16[192,1408]{1,0:T(8,128)(2,1)S(1)}, u32[]{:S(2)}, u32[]{:S(2)}) collective-permute-start(bf16[192,1408]{1,0:T(8,128)(2,1)} %collective-permute-done.2.one_m), channel_id=1, source_target_pairs={{0,2},{2,0},{4,6},{6,4},{8,10},{10,8},{12,14},{14,12},{16,18},{18,... | collective-permute-start | bytes 1622024 | tf_op jit(solution)/shard_map/ppermute | solution.py:684
  103.3 8.9 %copy-start.8 = (bf16[288,1024]{1,0:T(8,128)(2,1)}, bf16[288,1024]{1,0:T(8,128)(2,1)S(1)}, u32[]{:S(2)}) copy-start(bf16[288,1024]{1,0:T(8,128)(2,1)S(1)} %collective-permute-done.9.three_r) | copy-start | bytes 1769476
  103.3 8.8 %collective-permute-start.8 = (bf16[192,1024]{1,0:T(8,128)(2,1)}, bf16[192,1024]{1,0:T(8,128)(2,1)S(1)}, u32[]{:S(2)}, u32[]{:S(2)}) collective-permute-start(bf16[192,1024]{1,0:T(8,128)(2,1)} %collective-permute-done.3.three_q), channel_id=1, source_target_pairs={{0,2},{2,0},{4,6},{6,4},{8,10},{10,8},{12,14},{14,12},{16,18},{18,... | collective-permute-start | bytes 1179656 | tf_op jit(solution)/shard_map/ppermute | solution.py:684
  112.1 1.2 copy-start.6
  112.2 1.3 copy-start.10
  112.2 1.5 %copy-start.9 = (bf16[192,1408]{1,0:T(8,128)(2,1)}, bf16[192,1408]{1,0:T(8,128)(2,1)S(1)}, u32[]{:S(2)}) copy-start(bf16[192,1408]{1,0:T(8,128)(2,1)S(1)} %collective-permute-done.6.two_m) | copy-start | bytes 1622020
  113.6 0.9 copy-start.7
  114.6 6.2 %collective-permute-start.10 = (bf16[576,1408]{1,0:T(8,128)(2,1)}, bf16[576,1408]{1,0:T(8,128)(2,1)S(1)}, u32[]{:S(2)}, u32[]{:S(2)}) collective-permute-start(bf16[576,1408]{1,0:T(8,128)(2,1)} %copy-done.6), channel_id=1, source_target_pairs={{0,2},{2,0},{4,6},{6,4},{8,10},{10,8},{12,14},{14,12},{16,18},{18,... | collective-permute-start | bytes 4866056 | tf_op jit(solution)/shard_map/ppermute | solution.py:693
  114.6 6.2 %collective-permute-start.11 = (bf16[288,1024]{1,0:T(8,128)(2,1)}, bf16[288,1024]{1,0:T(8,128)(2,1)S(1)}, u32[]{:S(2)}, u32[]{:S(2)}) collective-permute-start(bf16[288,1024]{1,0:T(8,128)(2,1)} %copy-done.8), channel_id=1, source_target_pairs={{0,2},{2,0},{4,6},{6,4},{8,10},{10,8},{12,14},{14,12},{16,18},{18,... | collective-permute-start | bytes 1769480 | tf_op jit(solution)/shard_map/ppermute | solution.py:694
  119.2 8.4 %collective-permute-start.12 = (bf16[256,512]{1,0:T(8,128)(2,1)S(1)}, bf16[256,512]{1,0:T(8,128)(2,1)S(1)}, u32[]{:S(2)}, u32[]{:S(2)}) collective-permute-start(bf16[256,512]{1,0:T(8,128)(2,1)S(1)} %get-tuple-element.97), channel_id=1, source_target_pairs={{0,1},{1,0},{2,3},{3,2},{4,5},{5,4},{6,7},{7,6},{8,9},{9,8},{10,11... | collective-permute-start | bytes 786440 | tf_op jit(solution)/shard_map/ppermute | solution.py:725
  120.8 6.8 %copy-start = (bf16[512,1024]{1,0:T(8,128)(2,1)S(1)}, bf16[512,1024]{1,0:T(8,128)(2,1)}, u32[]{:S(2)}) copy-start(bf16[512,1024]{1,0:T(8,128)(2,1)} %tok_ref.2) | copy-start | bytes 3145732
  120.8 6.8 %copy-start.4 = (f32[1024]{0:T(1024)S(1)}, f32[1024]{0:T(1024)}, u32[]{:S(2)}) copy-start(f32[1024]{0:T(1024)} %param.41) | copy-start | bytes 12292

commit v12 on v11

--- a/solution.py
+++ b/solution.py
@@ -407,15 +407,15 @@
 
 
 def stage_weights(
-    side, out_w, gate_up_w, down_w, one_a, one_m, one_b, one_q, two_a, two_m, two_q, three_q,
-    three_r, four_q, two_b, four_r, out_all, gate_up_all, down_all, sems,
+    side, out_w, gate_up_w, down_w, one_a, one_m, one_q, two_a, two_m, two_q, three_q,
+    three_r, four_q, four_r, out_all, gate_up_own, gate_up_peer, down_all, sems,
 ):
     width, depth = out_w.shape[0] // 4, down_w.shape[0] // 4
-    pairs = [(gate_up_w, gate_up_all.at[0]), (down_w, down_all.at[0]), (out_w, out_all.at[0])]
-    for half, parts in ((side[1], (one_a, one_m, one_b)), (1 - side[1], (two_a, two_m, two_b))):
+    pairs = [(gate_up_w, gate_up_own), (down_w, down_all.at[0]), (out_w, out_all.at[0])]
+    for half, parts in ((side[1], (one_a, one_m)), (1 - side[1], (two_a, two_m))):
         at = 0
         for part in parts:
-            pairs.append((part, gate_up_all.at[1, half, pl.ds(at, part.shape[0])]))
+            pairs.append((part, gate_up_peer.at[half, pl.ds(at, part.shape[0])]))
             at += part.shape[0]
     core, chip = side[1], side[2] // 2
     near = three_q.shape[0]
@@ -435,23 +435,40 @@
 
 
 def feed_forward(
-    side, tok_ref, mine_ref, theirs_ref, gain_ref, out_w, gate_up_w, down_w, out_ref,
-    residual, hidden,
+    side, tok_ref, mine_ref, theirs_ref, gain_ref, out_w, own_w, peer_w, down_w, one_b, two_b,
+    out_ref, residual, ffn_in, hidden,
 ):
     rows = mine_ref.shape[0]
-    units = gate_up_w.shape[3]
+    units = own_w.shape[2]
+    first = peer_w.shape[1]
     tokens = tok_ref[pl.ds(pl.multiple_of(side[0] * rows, rows), rows), :].astype(F32)
     summed = tokens + jnp.dot(mine_ref[...], out_w[0], preferred_element_type=F32)
     summed = summed + jnp.dot(theirs_ref[...], out_w[1], preferred_element_type=F32)
     residual[...] = summed.astype(BF16)
-    ffn_in = rms_norm(residual[...], gain_ref[...])
+    ffn_in[...] = rms_norm(residual[...], gain_ref[...])
     step = 256
-    for half in range(2):
-        for first in range(0, units, step):
-            cols = slice(first, min(first + step, units))
-            gate = jnp.dot(ffn_in, gate_up_w[half, 0, :, cols], preferred_element_type=F32)
-            up = jnp.dot(ffn_in, gate_up_w[half, 1, :, cols], preferred_element_type=F32)
-            hidden[half, :, cols] = (gate / (1.0 + jnp.exp(-gate)) * up).astype(BF16)
+
+    def gated(gate, up):
+        return (gate / (1.0 + jnp.exp(-gate)) * up).astype(BF16)
+
+    for at in range(0, units, step):
+        cols = slice(at, min(at + step, units))
+        gate = jnp.dot(ffn_in[...], own_w[0, :, cols], preferred_element_type=F32)
+        up = jnp.dot(ffn_in[...], own_w[1, :, cols], preferred_element_type=F32)
+        hidden[0, :, cols] = gated(gate, up)
+
+    def peer(gate_tail, up_tail):
+        for at in range(0, units, step):
+            cols = slice(at, min(at + step, units))
+            gate, up = (
+                jnp.dot(ffn_in[:, :first], peer_w[half, :, cols], preferred_element_type=F32)
+                + jnp.dot(ffn_in[:, first:], tail[:, cols], preferred_element_type=F32)
+                for half, tail in enumerate((gate_tail, up_tail))
+            )
+            hidden[1, :, cols] = gated(gate, up)
+
+    pl.when(side[1] == 0)(functools.partial(peer, one_b, two_b))
+    pl.when(side[1] == 1)(functools.partial(peer, two_b, one_b))
     for at in range(0, out_ref.shape[1], step):
         cols = slice(at, at + step)
         total = residual[:, cols].astype(F32)
@@ -685,12 +702,9 @@
         )
     returned = lax.all_to_all(answers, "req", split_axis=0, concat_axis=0, tiled=True)
     if pieces == 2:
-        returned, one_b, two_a, two_m, two_q, four_q, three_r, own, retrieved = (
-            lax.optimization_barrier(
-                (returned, one_b, two_a, two_m, two_q, four_q, three_r, own, retrieved)
-            )
-        )
-        two_b = lax.ppermute(one_b, "req", other_core)
+        returned, two_a, two_m, two_q, four_q, three_r, own, retrieved = lax.optimization_barrier(
+            (returned, two_a, two_m, two_q, four_q, three_r, own, retrieved)
+        )
         four_r = lax.ppermute(three_r, "req", other_core)
     rows = group_rows // grp
     mixed = pl.pallas_call(
@@ -723,35 +737,37 @@
     if pieces == 2:
         mine, asked_for = mixed
         theirs = lax.ppermute(asked_for, "grp", swap)
-        mine, two_b, four_r = lax.optimization_barrier((mine, two_b, four_r))
-        out_near, gate_up_near, down_near = pl.pallas_call(
+        mine, four_r, one_b = lax.optimization_barrier((mine, four_r, one_b))
+        two_b = lax.ppermute(one_b, "req", other_core)
+        out_near, own_near, peer_near, down_near = pl.pallas_call(
             stage_weights,
             out_shape=(
                 VMEM((2,) + w_out.shape, BF16),
-                VMEM((2,) + w_gate_up.shape, BF16),
+                VMEM(w_gate_up.shape, BF16),
+                VMEM((2, first + middle, units), BF16),
                 VMEM((2,) + w_down.shape, BF16),
             ),
-            in_specs=[whole(SMEM)] + [whole(pl.ANY)] * 15,
-            out_specs=(whole(),) * 3,
-            scratch_shapes=[pltpu.SemaphoreType.DMA((19,))],
+            in_specs=[whole(SMEM)] + [whole(pl.ANY)] * 13,
+            out_specs=(whole(),) * 4,
+            scratch_shapes=[pltpu.SemaphoreType.DMA((17,))],
             compiler_params=params(2),
             cost_estimate=cost(0, 2 * model * (2 * width + 6 * units)),
             name="stage_weights",
         )(
             side,
             *keep_in(
-                HBM, w_out, w_gate_up, w_down, one_a, one_m, one_b, one_q, two_a, two_m, two_q,
-                three_q, three_r, four_q,
+                HBM, w_out, w_gate_up, w_down, one_a, one_m, one_q, two_a, two_m, two_q, three_q,
+                three_r, four_q,
             ),
-            two_b,
             four_r,
         )
         layer_out = pl.pallas_call(
             feed_forward,
             out_shape=jax.ShapeDtypeStruct((rows, model), BF16),
-            in_specs=[whole(SMEM)] + [whole()] * 7,
+            in_specs=[whole(SMEM)] + [whole()] * 10,
             out_specs=whole(),
             scratch_shapes=[
+                pltpu.VMEM((rows, model), BF16),
                 pltpu.VMEM((rows, model), BF16),
                 pltpu.VMEM((2, rows, units), BF16),
             ],
@@ -762,7 +778,7 @@
             name="feed_forward",
         )(
             side, tokens, mine, theirs, norm_ffn.reshape(1, -1),
-            *keep_in(VMEM, out_near, gate_up_near, down_near),
+            *keep_in(VMEM, out_near, own_near, peer_near, down_near, one_b, two_b),
         )
         return (layer_out, memory_out, momentum_out)
 

time: 136 us -> 134 us (0.985)
  the two profiles are of different devices: /device:TPU:0 before, /device:TPU:16 now
where the time goes in v12:
time: 134 us; the launch traced here: 133 us
  Pallas kernels  80.5 us (60%)
  starting transfers between devices  27.7 us (21%)
  waiting for transfers between devices  17.9 us (13%)
  local copies, waits for them, and re-layouts  5.46 us (4%)
    pallas_call x1, Pallas kernels, on_device(): pl.pallas_call(functools.partial(update_memory, reqs=reqs, draft=draft, h...  22.1 us
    pallas_call x1, Pallas kernels, on_device(): pl.pallas_call(functools.partial(local_attention, heads=heads, draft=draf...  18.2 us
    pallas_call x1, Pallas kernels, on_device(): pl.pallas_call(feed_forward, out_shape=jax.ShapeDtypeStruct((rows, model)...  9.19 us
    ppermute x1, waiting for transfers between devices, on_device(): three_r = lax.ppermute(one_q[near:], 'req', other_chip)  7.85 us
    pallas_call x1, Pallas kernels, on_device(): pl.pallas_call(functools.partial(page_attention, n=n, cap=cap, draft=draf...  7.11 us
    all_to_all x1, starting transfers between devices, on_device(): lax.all_to_all(label, 'req', split_axis=0, concat_axis=0, tiled=True)  6.18 us
    pallas_call x1, Pallas kernels, on_device(): pl.pallas_call(stage_weights, out_shape=(VMEM((2,) + w_out.shape, BF16),...  6.09 us
    all_to_all x1, starting transfers between devices, on_device(): lax.all_to_all(packed, 'req', split_axis=0, concat_axis=0, tiled=True)  6.03 us
  transfers between devices with their start and end apart: 16, of which 5 were waited for; matrix products, arithmetic and copies ran while one was open for 2% of the time, Pallas kernels for 54%

profile of v12, /device:TPU:16, one launch (start us, length us, event | category | flops | bytes accessed | tf_op | source)
XLA Modules:
  0.0 133.1 jit_solution(8134755907734724345)
XLA Ops:
  0.6 0.7 fusion.1
  1.3 0.7 reshape.20
  2.0 6.2 %all-to-all-start = ((s32[16,1,3]{2,1,0:T(1,128)}), s32[16,1,3]{2,1,0:T(1,128)S(1)}, u32[]{:S(2)}, u32[]{:S(2)}) async-start(s32[16,1,3]{2,1,0:T(1,128)} %bitcast.3), calls=%async_computation | async-start | bytes 16384 | tf_op jit(solution)/shard_map/all_to_all | solution.py:521
  8.2 0.1 pad_add_fusion.refs_0_.side
  8.3 4.5 %project_queries.1 = (bf16[512,512]{1,0:T(8,128)(2,1)}, bf16[2048,128]{1,0:T(8,128)(2,1)S(1)}, bf16[256,1408]{1,0:T(8,128)(2,1)}, bf16[480,1024]{1,0:T(8,128)(2,1)}) custom-call(s32[3]{0:T(128)S(1)} %pad_add_fusion.refs_0_.side, bf16[2,1024,1408]{2,1,0:T(8,128)(2,1)} %gate_up_w.2, bf16[1408,1024]{1,0:T(8,128)(2,1)} %down_w.1, bf16[512,1024]{1,0:T(8,128)(2,1)} %out_w.1, ...), custom_call_target="tpu_custom_call" | custom-call | flops 10737418240 | bytes 62914560 | tf_op jit(solution)/shard_map/project_queries/pallas_call | solution.py:535
  12.8 1.6 %collective-permute-start = (bf16[256,1408]{1,0:T(8,128)(2,1)}, bf16[256,1408]{1,0:T(8,128)(2,1)}, u32[]{:S(2)}, u32[]{:S(2)}) collective-permute-start(bf16[256,1408]{1,0:T(8,128)(2,1)} %get-tuple-element.68), channel_id=1, source_target_pairs={{0,1},{1,0},{2,3},{3,2},{4,5},{5,4},{6,7},{7,6},{8,9},{9,8},{10,11... | collective-permute-start | bytes 2162696 | tf_op jit(solution)/shard_map/ppermute | solution.py:561
  14.4 0.5 collective-permute-start.1
  14.9 2.2 %pack_queries.1 = bf16[6400,128]{1,0:T(8,128)(2,1)} custom-call(s32[16,1,3]{2,1,0:T(1,128)S(1)} %all-to-all-done.codes, s32[16]{0:T(128)} %lengths.1, bf16[2048,128]{1,0:T(8,128)(2,1)S(1)} %get-tuple-element.59.turned_ref), custom_call_target="tpu_custom_call" | custom-call | bytes 65536000 | tf_op jit(solution)/shard_map/pack_queries/pallas_call | solution.py:564
  17.1 6.0 %all-to-all-start.1 = ((bf16[16,400,128]{2,1,0:T(8,128)(2,1)}), bf16[16,400,128]{2,1,0:T(8,128)(2,1)S(1)}, u32[]{:S(2)}, u32[]{:S(2)}) async-start(bf16[16,400,128]{2,1,0:T(8,128)(2,1)} %bitcast.19), calls=%async_computation.1 | async-start | bytes 3276800 | tf_op jit(solution)/shard_map/all_to_all | solution.py:578
  23.1 3.0 %cut_last.1 = (bf16[192,1408]{1,0:T(8,128)(2,1)}, bf16[576,1408]{1,0:T(8,128)(2,1)S(1)}) custom-call(s32[3]{0:T(128)S(1)} %pad_add_fusion.refs_0_.side, bf16[2,1024,1408]{2,1,0:T(8,128)(2,1)} %gate_up_w.2), custom_call_target="tpu_custom_call" | custom-call | bytes 86507520 | tf_op jit(solution)/shard_map/cut_last/pallas_call | solution.py:581
  26.1 0.0 copy-start.1
  26.1 0.0 copy-start.2
  26.1 0.0 copy-start.3
  26.1 0.0 copy-start.5
  26.1 1.6 %collective-permute-start.2 = (bf16[192,1408]{1,0:T(8,128)(2,1)}, bf16[192,1408]{1,0:T(8,128)(2,1)}, u32[]{:S(2)}, u32[]{:S(2)}) collective-permute-start(bf16[192,1408]{1,0:T(8,128)(2,1)} %get-tuple-element.73), channel_id=1, source_target_pairs={{0,1},{1,0},{2,3},{3,2},{4,5},{5,4},{6,7},{7,6},{8,9},{9,8},{10,11... | collective-permute-start | bytes 1622024 | tf_op jit(solution)/shard_map/ppermute | solution.py:667
  27.7 4.1 %project_keys.1 = (bf16[512,512]{1,0:T(8,128)(2,1)}, bf16[512,512]{1,0:T(8,128)(2,1)}) custom-call(bf16[512,1024]{1,0:T(8,128)(2,1)} %tok_ref.2, f32[1,1024]{1,0:T(1,128)} %bitcast.22, bf16[1024,512]{1,0:T(8,128)(2,1)} %wk_ref.1, bf16[1024,512]{1,0:T(8,128)(2,1)} %wv_ref.1), custom_call_target="tpu_custom_call" | custom-call | flops 21474836480 | bytes 62914560 | tf_op jit(solution)/shard_map/project_keys/pallas_call | solution.py:592
  31.8 22.1 %update_memory.1 = (f32[16,4,128,128]{3,2,1,0:T(8,128)}, f32[16,4,128,128]{3,2,1,0:T(8,128)}) custom-call(s32[8,16]{1,0:T(8,128)S(1)} %bitcast.17, s32[16]{0:T(128)S(1)} %copy-done.5, s32[8,4,16]{2,1,0:T(4,128)S(1)} %bitcast.15, s32[8,4,16]{2,1,0:T(4,128)S(1)} %bitcast.16, bf16[512,512]{1,0:T(8,128)(2,1)} %get-tuple-element.62.k_ref, ...), custom_call_target="tpu_custom_call" | custom-call | flops 18790481920 | bytes 335544320 | tf_op jit(solution)/shard_map/update_memory/pallas_call | solution.py:632
  53.9 0.0 collective-permute-done.1.one_q
  53.9 1.8 %slice.6 = bf16[192,1024]{1,0:T(8,128)(2,1)} slice(bf16[480,1024]{1,0:T(8,128)(2,1)} %collective-permute-done.1.one_q), slice={[0:192], [0:1024]} | slice | bytes 786432 | tf_op jit(solution)/shard_map/slice | solution.py:669
  55.7 1.3 collective-permute-start.3
  57.0 4.0 %all-to-all-done.1 = bf16[16,400,128]{2,1,0:T(8,128)(2,1)S(1)} async-done(((bf16[16,400,128]{2,1,0:T(8,128)(2,1)}), bf16[16,400,128]{2,1,0:T(8,128)(2,1)S(1)}, u32[]{:S(2)}, u32[]{:S(2)}) %all-to-all-start.1) | async-done | bytes 1638432 | tf_op jit(solution)/shard_map/all_to_all | solution.py:578
  61.0 7.1 %page_attention.1 = bf16[6400,128]{1,0:T(8,128)(2,1)} custom-call(bf16[6400,128]{1,0:T(8,128)(2,1)S(1)} %bitcast.14, bf16[48,2,128,512]{3,2,1,0:T(8,128)(2,1)} %kv_hbm.1), custom_call_target="tpu_custom_call" | custom-call | flops 8053063680 | bytes 317194240 | tf_op jit(solution)/shard_map/page_attention/pallas_call | solution.py:674
  68.2 0.0 collective-permute-done.2.one_m
  68.2 4.9 %all-to-all-start.2 = ((bf16[16,400,128]{2,1,0:T(8,128)(2,1)}), bf16[16,400,128]{2,1,0:T(8,128)(2,1)S(1)}, u32[]{:S(2)}, u32[]{:S(2)}) async-start(bf16[16,400,128]{2,1,0:T(8,128)(2,1)} %bitcast.20), calls=%async_computation.2 | async-start | bytes 3276800 | tf_op jit(solution)/shard_map/all_to_all | solution.py:703
  73.1 1.5 %collective-permute-start.10 = (bf16[576,1408]{1,0:T(8,128)(2,1)S(1)}, bf16[576,1408]{1,0:T(8,128)(2,1)}, u32[]{:S(2)}, u32[]{:S(2)}) collective-permute-start(bf16[576,1408]{1,0:T(8,128)(2,1)S(1)} %get-tuple-element.94), channel_id=1, source_target_pairs={{0,1},{1,0},{2,3},{3,2},{4,5},{5,4},{6,7},{7,6},{8,9},{9,8},{10,11... | collective-permute-start | bytes 4866056 | tf_op jit(solution)/shard_map/ppermute | solution.py:668
  74.6 1.1 slice.7
  75.7 1.5 %collective-permute-start.8 = (bf16[288,1024]{1,0:T(8,128)(2,1)S(1)}, bf16[288,1024]{1,0:T(8,128)(2,1)S(1)}, u32[]{:S(2)}, u32[]{:S(2)}) collective-permute-start(bf16[288,1024]{1,0:T(8,128)(2,1)S(1)} %slice.7), channel_id=1, source_target_pairs={{0,4},{2,6},{4,0},{6,2},{8,12},{10,14},{12,8},{14,10},{16,20},{18,... | collective-permute-start | bytes 1769480 | tf_op jit(solution)/shard_map/ppermute | solution.py:670
  77.2 0.0 collective-permute-start.6
  77.2 0.5 collective-permute-start.4
  77.7 18.2 %local_attention.1 = (f32[2048,128]{1,0:T(8,128)}, f32[2048,128]{1,0:T(8,128)}, f32[16,128]{1,0:T(8,128)S(1)}, f32[16,128]{1,0:T(8,128)S(1)}) custom-call(bf16[512,512]{1,0:T(8,128)(2,1)} %get-tuple-element.78.q_ref, bf16[512,512]{1,0:T(8,128)(2,1)} %get-tuple-element.62.k_ref, bf16[512,512]{1,0:T(8,128)(2,1)} %get-tuple-element.63.v_ref, ...), custom_call_target="tpu_custom_call" | custom-call | flops 20 | bytes 20 | tf_op jit(solution)/shard_map/local_attention/pallas_call | solution.py:608
  95.9 0.0 collective-permute-start.5
  95.9 7.8 %collective-permute-done.8.three_r = bf16[288,1024]{1,0:T(8,128)(2,1)S(1)} collective-permute-done((bf16[288,1024]{1,0:T(8,128)(2,1)S(1)}, bf16[288,1024]{1,0:T(8,128)(2,1)S(1)}, u32[]{:S(2)}, u32[]{:S(2)}) %collective-permute-start.8) | collective-permute-done | bytes 589856 | tf_op jit(solution)/shard_map/ppermute | solution.py:670
  103.8 0.0 collective-permute-start.7
  103.8 1.9 %collective-permute-done.7.four_q = bf16[192,1024]{1,0:T(8,128)(2,1)S(1)} collective-permute-done((bf16[192,1024]{1,0:T(8,128)(2,1)}, bf16[192,1024]{1,0:T(8,128)(2,1)S(1)}, u32[]{:S(2)}, u32[]{:S(2)}) %collective-permute-start.7) | collective-permute-done | bytes 393248 | tf_op jit(solution)/shard_map/ppermute | solution.py:701
  105.7 0.0 collective-permute-done.5.two_m
  105.7 0.0 collective-permute-done.4.two_a
  105.7 0.7 copy-done.9
  106.4 0.2 copy-done.8
  106.7 0.9 copy-done.6
  107.6 3.3 %all-to-all-done.2 = bf16[16,400,128]{2,1,0:T(8,128)(2,1)S(1)} async-done(((bf16[16,400,128]{2,1,0:T(8,128)(2,1)}), bf16[16,400,128]{2,1,0:T(8,128)(2,1)S(1)}, u32[]{:S(2)}, u32[]{:S(2)}) %all-to-all-start.2) | async-done | bytes 1638432 | tf_op jit(solution)/shard_map/all_to_all | solution.py:703
  110.9 0.0 collective-permute-start.9
  110.9 4.1 %combine.1 = (bf16[256,512]{1,0:T(8,128)(2,1)S(1)}, bf16[256,512]{1,0:T(8,128)(2,1)S(1)}) custom-call(s32[16,1,3]{2,1,0:T(1,128)S(1)} %all-to-all-done.codes, s32[3]{0:T(128)S(1)} %pad_add_fusion.refs_0_.side, bf16[6400,128]{1,0:T(8,128)(2,1)S(1)} %bitcast.13, f32[2048,128]{1,0:T(8,128)} %get-tuple-element.88.o_hbm, f32[2048,128]{1,0:T(8,128)} %get-tuple-element.89.ret_hbm, ...), custom_call_target="tpu_custom_call" | custom-call | flops 125829120 | bytes 74711040 | tf_op jit(solution)/shard_map/combine/pallas_call | solution.py:710
  115.0 0.0 collective-permute-done.10.one_b
  115.0 0.6 collective-permute-start.12
  115.6 1.5 %collective-permute-start.11 = (bf16[256,512]{1,0:T(8,128)(2,1)S(1)}, bf16[256,512]{1,0:T(8,128)(2,1)S(1)}, u32[]{:S(2)}, u32[]{:S(2)}) collective-permute-start(bf16[256,512]{1,0:T(8,128)(2,1)S(1)} %get-tuple-element.96), channel_id=1, source_target_pairs={{0,1},{1,0},{2,3},{3,2},{4,5},{5,4},{6,7},{7,6},{8,9},{9,8},{10,11... | collective-permute-start | bytes 786440 | tf_op jit(solution)/shard_map/ppermute | solution.py:739
  117.1 6.1 %stage_weights.1 = (bf16[2,512,1024]{2,1,0:T(8,128)(2,1)S(1)}, bf16[2,1024,1408]{2,1,0:T(8,128)(2,1)S(1)}, bf16[2,448,1408]{2,1,0:T(8,128)(2,1)S(1)}, bf16[2,1408,1024]{2,1,0:T(8,128)(2,1)S(1)}) custom-call(s32[3]{0:T(128)S(1)} %pad_add_fusion.refs_0_.side, bf16[512,1024]{1,0:T(8,128)(2,1)} %out_w.1, bf16[2,1024,1408]{2,1,0:T(8,128)(2,1)} %gate_up_w.2, ...), custom_call_target="tpu_custom_call" | custom-call | bytes 387973120 | tf_op jit(solution)/shard_map/stage_weights/pallas_call | solution.py:742
  123.2 0.7 collective-permute-done.11.theirs_ref
  123.9 9.2 %feed_forward.1 = bf16[256,1024]{1,0:T(8,128)(2,1)} custom-call(s32[3]{0:T(128)S(1)} %pad_add_fusion.refs_0_.side, bf16[512,1024]{1,0:T(8,128)(2,1)S(1)} %copy-done, bf16[256,512]{1,0:T(8,128)(2,1)S(1)} %get-tuple-element.95.mine_ref, bf16[256,512]{1,0:T(8,128)(2,1)S(1)} %collective-permute-done.11.theirs_ref, f32[1,1024]{1,0:T(1,128)S(1)} %bitcast.18, ...), custom_call_target="tpu_custom_call" | custom-call | flops 99321118720 | bytes 387973120 | tf_op jit(solution)/shard_map/feed_forward/pallas_call | solution.py:764
  (19 shorter events, 0.0 us)
Async XLA Ops:
  2.0 12.9 %all-to-all-start = ((s32[16,1,3]{2,1,0:T(1,128)}), s32[16,1,3]{2,1,0:T(1,128)S(1)}, u32[]{:S(2)}, u32[]{:S(2)}) async-start(s32[16,1,3]{2,1,0:T(1,128)} %bitcast.3), calls=%async_computation | async-start | bytes 16384 | tf_op jit(solution)/shard_map/all_to_all | solution.py:521
  12.8 41.1 %collective-permute-start = (bf16[256,1408]{1,0:T(8,128)(2,1)}, bf16[256,1408]{1,0:T(8,128)(2,1)}, u32[]{:S(2)}, u32[]{:S(2)}) collective-permute-start(bf16[256,1408]{1,0:T(8,128)(2,1)} %get-tuple-element.68), channel_id=1, source_target_pairs={{0,1},{1,0},{2,3},{3,2},{4,5},{5,4},{6,7},{7,6},{8,9},{9,8},{10,11... | collective-permute-start | bytes 2162696 | tf_op jit(solution)/shard_map/ppermute | solution.py:561
  14.4 39.6 %collective-permute-start.1 = (bf16[480,1024]{1,0:T(8,128)(2,1)}, bf16[480,1024]{1,0:T(8,128)(2,1)}, u32[]{:S(2)}, u32[]{:S(2)}) collective-permute-start(bf16[480,1024]{1,0:T(8,128)(2,1)} %get-tuple-element.69), channel_id=1, source_target_pairs={{0,1},{1,0},{2,3},{3,2},{4,5},{5,4},{6,7},{7,6},{8,9},{9,8},{10,11... | collective-permute-start | bytes 2949128 | tf_op jit(solution)/shard_map/ppermute | solution.py:562
  17.1 44.0 %all-to-all-start.1 = ((bf16[16,400,128]{2,1,0:T(8,128)(2,1)}), bf16[16,400,128]{2,1,0:T(8,128)(2,1)S(1)}, u32[]{:S(2)}, u32[]{:S(2)}) async-start(bf16[16,400,128]{2,1,0:T(8,128)(2,1)} %bitcast.19), calls=%async_computation.1 | async-start | bytes 3276800 | tf_op jit(solution)/shard_map/all_to_all | solution.py:578
  26.1 5.7 %copy-start.1 = (s32[16,8,4]{0,2,1:T(4,128)S(1)}, s32[16,8,4]{0,2,1:T(4,128)}, u32[]{:S(2)}) copy-start(s32[16,8,4]{0,2,1:T(4,128)} %param.39) | copy-start | bytes 6148
  26.1 5.7 %copy-start.2 = (s32[16,8,4]{0,2,1:T(4,128)S(1)}, s32[16,8,4]{0,2,1:T(4,128)}, u32[]{:S(2)}) copy-start(s32[16,8,4]{0,2,1:T(4,128)} %param.40) | copy-start | bytes 6148
  26.1 5.7 %copy-start.3 = (s32[16,8]{0,1:T(8,128)S(1)}, s32[16,8]{0,1:T(8,128)}, u32[]{:S(2)}) copy-start(s32[16,8]{0,1:T(8,128)} %param.35) | copy-start | bytes 1540
  26.1 5.7 %copy-start.5 = (s32[16]{0:T(128)S(1)}, s32[16]{0:T(128)}, u32[]{:S(2)}) copy-start(s32[16]{0:T(128)} %count.1) | copy-start | bytes 196
  26.1 42.0 %collective-permute-start.2 = (bf16[192,1408]{1,0:T(8,128)(2,1)}, bf16[192,1408]{1,0:T(8,128)(2,1)}, u32[]{:S(2)}, u32[]{:S(2)}) collective-permute-start(bf16[192,1408]{1,0:T(8,128)(2,1)} %get-tuple-element.73), channel_id=1, source_target_pairs={{0,1},{1,0},{2,3},{3,2},{4,5},{5,4},{6,7},{7,6},{8,9},{9,8},{10,11... | collective-permute-start | bytes 1622024 | tf_op jit(solution)/shard_map/ppermute | solution.py:667
  55.7 12.5 %collective-permute-start.3 = (bf16[192,1024]{1,0:T(8,128)(2,1)}, bf16[192,1024]{1,0:T(8,128)(2,1)}, u32[]{:S(2)}, u32[]{:S(2)}) collective-permute-start(bf16[192,1024]{1,0:T(8,128)(2,1)} %slice.6), channel_id=1, source_target_pairs={{0,4},{2,6},{4,0},{6,2},{8,12},{10,14},{12,8},{14,10},{16,20},{18,... | collective-permute-start | bytes 1179656 | tf_op jit(solution)/shard_map/ppermute | solution.py:669
  68.2 42.7 %all-to-all-start.2 = ((bf16[16,400,128]{2,1,0:T(8,128)(2,1)}), bf16[16,400,128]{2,1,0:T(8,128)(2,1)S(1)}, u32[]{:S(2)}, u32[]{:S(2)}) async-start(bf16[16,400,128]{2,1,0:T(8,128)(2,1)} %bitcast.20), calls=%async_computation.2 | async-start | bytes 3276800 | tf_op jit(solution)/shard_map/all_to_all | solution.py:703
  73.1 41.9 %collective-permute-start.10 = (bf16[576,1408]{1,0:T(8,128)(2,1)S(1)}, bf16[576,1408]{1,0:T(8,128)(2,1)}, u32[]{:S(2)}, u32[]{:S(2)}) collective-permute-start(bf16[576,1408]{1,0:T(8,128)(2,1)S(1)} %get-tuple-element.94), channel_id=1, source_target_pairs={{0,1},{1,0},{2,3},{3,2},{4,5},{5,4},{6,7},{7,6},{8,9},{9,8},{10,11... | collective-permute-start | bytes 4866056 | tf_op jit(solution)/shard_map/ppermute | solution.py:668
  75.7 28.1 %collective-permute-start.8 = (bf16[288,1024]{1,0:T(8,128)(2,1)S(1)}, bf16[288,1024]{1,0:T(8,128)(2,1)S(1)}, u32[]{:S(2)}, u32[]{:S(2)}) collective-permute-start(bf16[288,1024]{1,0:T(8,128)(2,1)S(1)} %slice.7), channel_id=1, source_target_pairs={{0,4},{2,6},{4,0},{6,2},{8,12},{10,14},{12,8},{14,10},{16,20},{18,... | collective-permute-start | bytes 1769480 | tf_op jit(solution)/shard_map/ppermute | solution.py:670
  77.2 30.4 %collective-permute-start.6 = (bf16[480,1024]{1,0:T(8,128)(2,1)}, bf16[480,1024]{1,0:T(8,128)(2,1)}, u32[]{:S(2)}, u32[]{:S(2)}) collective-permute-start(bf16[480,1024]{1,0:T(8,128)(2,1)} %collective-permute-done.1.one_q), channel_id=1, source_target_pairs={{0,2},{2,0},{4,6},{6,4},{8,10},{10,8},{12,14},{14,12},{16,18},{18,... | collective-permute-start | bytes 2949128 | tf_op jit(solution)/shard_map/ppermute | solution.py:701
  77.2 28.5 %collective-permute-start.4 = (bf16[256,1408]{1,0:T(8,128)(2,1)}, bf16[256,1408]{1,0:T(8,128)(2,1)S(1)}, u32[]{:S(2)}, u32[]{:S(2)}) collective-permute-start(bf16[256,1408]{1,0:T(8,128)(2,1)} %collective-permute-done.one_a), channel_id=1, source_target_pairs={{0,2},{2,0},{4,6},{6,4},{8,10},{10,8},{12,14},{14,12},{16,18},{18,... | collective-permute-start | bytes 2162696 | tf_op jit(solution)/shard_map/ppermute | solution.py:701
  95.9 9.8 %collective-permute-start.5 = (bf16[192,1408]{1,0:T(8,128)(2,1)}, bf16[192,1408]{1,0:T(8,128)(2,1)S(1)}, u32[]{:S(2)}, u32[]{:S(2)}) collective-permute-start(bf16[192,1408]{1,0:T(8,128)(2,1)} %collective-permute-done.2.one_m), channel_id=1, source_target_pairs={{0,2},{2,0},{4,6},{6,4},{8,10},{10,8},{12,14},{14,12},{16,18},{18,... | collective-permute-start | bytes 1622024 | tf_op jit(solution)/shard_map/ppermute | solution.py:701
  103.8 2.0 %copy-start.7 = (bf16[288,1024]{1,0:T(8,128)(2,1)}, bf16[288,1024]{1,0:T(8,128)(2,1)S(1)}, u32[]{:S(2)}) copy-start(bf16[288,1024]{1,0:T(8,128)(2,1)S(1)} %collective-permute-done.8.three_r) | copy-start | bytes 1769476
  103.8 1.9 %collective-permute-start.7 = (bf16[192,1024]{1,0:T(8,128)(2,1)}, bf16[192,1024]{1,0:T(8,128)(2,1)S(1)}, u32[]{:S(2)}, u32[]{:S(2)}) collective-permute-start(bf16[192,1024]{1,0:T(8,128)(2,1)} %collective-permute-done.3.three_q), channel_id=1, source_target_pairs={{0,2},{2,0},{4,6},{6,4},{8,10},{10,8},{12,14},{14,12},{16,18},{18,... | collective-permute-start | bytes 1179656 | tf_op jit(solution)/shard_map/ppermute | solution.py:701
  105.7 0.7 copy-start.9
  105.7 1.0 copy-start.8
  106.7 0.9 copy-start.6
  110.9 4.1 %collective-permute-start.9 = (bf16[288,1024]{1,0:T(8,128)(2,1)}, bf16[288,1024]{1,0:T(8,128)(2,1)S(1)}, u32[]{:S(2)}, u32[]{:S(2)}) collective-permute-start(bf16[288,1024]{1,0:T(8,128)(2,1)} %copy-done.7), channel_id=1, source_target_pairs={{0,2},{2,0},{4,6},{6,4},{8,10},{10,8},{12,14},{14,12},{16,18},{18,... | collective-permute-start | bytes 1769480 | tf_op jit(solution)/shard_map/ppermute | solution.py:708
  115.0 8.9 %collective-permute-start.12 = (bf16[576,1408]{1,0:T(8,128)(2,1)}, bf16[576,1408]{1,0:T(8,128)(2,1)S(1)}, u32[]{:S(2)}, u32[]{:S(2)}) collective-permute-start(bf16[576,1408]{1,0:T(8,128)(2,1)} %collective-permute-done.10.one_b), channel_id=1, source_target_pairs={{0,2},{2,0},{4,6},{6,4},{8,10},{10,8},{12,14},{14,12},{16,18},{18,... | collective-permute-start | bytes 4866056 | tf_op jit(solution)/shard_map/ppermute | solution.py:741
  115.6 8.3 %copy-start = (bf16[512,1024]{1,0:T(8,128)(2,1)S(1)}, bf16[512,1024]{1,0:T(8,128)(2,1)}, u32[]{:S(2)}) copy-start(bf16[512,1024]{1,0:T(8,128)(2,1)} %tok_ref.2) | copy-start | bytes 3145732
  115.6 8.3 %copy-start.4 = (f32[1024]{0:T(1024)S(1)}, f32[1024]{0:T(1024)}, u32[]{:S(2)}) copy-start(f32[1024]{0:T(1024)} %param.41) | copy-start | bytes 12292
  115.6 8.3 %collective-permute-start.11 = (bf16[256,512]{1,0:T(8,128)(2,1)S(1)}, bf16[256,512]{1,0:T(8,128)(2,1)S(1)}, u32[]{:S(2)}, u32[]{:S(2)}) collective-permute-start(bf16[256,512]{1,0:T(8,128)(2,1)S(1)} %get-tuple-element.96), channel_id=1, source_target_pairs={{0,1},{1,0},{2,3},{3,2},{4,5},{5,4},{6,7},{7,6},{8,9},{9,8},{10,11... | collective-permute-start | bytes 786440 | tf_op jit(solution)/shard_map/ppermute | solution.py:739
